TPU v7x, 32 devices: a whole 2x2x4 slice. The times are simulated.
32 devices in a mesh: dp: 16 (over z, y, x), head: 2 (over core).
Axes of the slice: x: 2, y: 2, z: 4, core: 2. Of those that a mesh axis runs over, the one named last changes fastest.
Arguments:
- block_in: bfloat16 [4096, 2048], P('dp'), may hold values from -6 to 6
- out_grad: bfloat16 [4096, 2048], P('dp'), may hold values from -6 to 6
- attn_gain: float32 [2048], replicated, may hold values from 0.5 to 1.5
- mlp_gain: float32 [2048], replicated, may hold values from 0.5 to 1.5
- w_query: bfloat16 [2048, 2048], P(None, 'head'), may hold values from -0.25 to 0.25
- w_key: bfloat16 [2048, 2048], P(None, 'head'), may hold values from -0.125 to 0.125
- w_value: bfloat16 [2048, 2048], P(None, 'head'), may hold values from -0.125 to 0.125
- w_forget: bfloat16 [2048, 256], P(None, 'head'), may hold values from -0.125 to 0.125
- w_output: bfloat16 [2048, 2048], P(None, 'head'), may hold values from -0.375 to 0.375
- w_gate: bfloat16 [2048, 5632], P('dp', 'head'), may hold values from -0.125 to 0.125
- w_up: bfloat16 [2048, 5632], P('dp', 'head'), may hold values from -0.125 to 0.125
- w_down: bfloat16 [2048, 5632], P('dp', 'head'), may hold values from -0.15625 to 0.15625
- doc_starts: int32 [16, 3], P('dp'), may hold values from 1 to 255, as said below
Outputs:
- block_out: bfloat16 [4096, 2048], P('dp')
- block_in_grad: float32 [4096, 2048], P('dp')
- attn_gain_grad: float32 [2048], P('dp')
- mlp_gain_grad: float32 [2048], P('dp')
- w_query_grad: float32 [2048, 2048], P('dp', 'head')
- w_key_grad: float32 [2048, 2048], P('dp', 'head')
- w_value_grad: float32 [2048, 2048], P('dp', 'head')
- w_forget_grad: float32 [2048, 256], P('dp', 'head')
- w_output_grad: float32 [2048, 2048], P('dp', 'head')
- w_gate_grad: float32 [2048, 5632], P('dp', 'head')
- w_up_grad: float32 [2048, 5632], P('dp', 'head')
- w_down_grad: float32 [2048, 5632], P('dp', 'head')
Inputs may be any that keep to these rules, and one draw needn't show every extreme that they name: `doc_starts`: each row holds 3 distinct positions in increasing order, from 1 to 255; position 0 always begins a document.
All inputs are finite; a program needn't handle non-finite values.
Results may differ from a plain program's by a relative error of at most 0.015.
Values may be sent and summed in bfloat16 or wider, within the bound.
No kernel may reach another device: no remote copies, remote signals or barrier semaphores. Data moves between devices by JAX's collectives and lax.ppermute only.
A program may use at most 256 MiB of HBM per device.

v0:
```python
from functools import partial
import math

import jax
import jax.numpy as jnp
from jax import lax
from jax.sharding import PartitionSpec as P

DK = 512
DV = 512
M = 64


eps = 1e-06
tau_inv = 0.125
highest_precision = lax.Precision.HIGHEST


def matmul_plain(left, right):
    return jnp.dot(left, right, preferred_element_type=jnp.float32)


def matmul_rt(left, right):
    return lax.dot_general(
        left, right, (((1,), (1,)), ((), ())), preferred_element_type=jnp.float32
    )


def matmul_lt(left, right):
    return lax.dot_general(
        left, right, (((0,), (0,)), ((), ())), preferred_element_type=jnp.float32
    )


def rms_scale(values):
    return lax.rsqrt(jnp.mean(values * values, axis=-1, keepdims=True) + eps)


def norm_back(values, scale, gain, upstream):
    gain_grad = jnp.sum(upstream * values * scale, axis=0)
    weighted = upstream * gain
    input_grad = scale * weighted - values * (scale * scale * scale) * jnp.mean(
        weighted * values, axis=-1, keepdims=True
    )
    return (gain_grad, input_grad)


def silu_slope(values):
    sigmoid_val = jax.nn.sigmoid(values)
    return sigmoid_val * (1.0 + values * (1.0 - sigmoid_val))


def slot_block(state_triple, block_data):
    slot_key_state, slot_value_state, last_segment = state_triple
    query_matrix, key_matrix, value_matrix, log_keep, segment = block_data
    cumulative = jnp.cumsum(log_keep, axis=0)
    carried_state = (
        jnp.exp(cumulative) * (segment == last_segment).astype(jnp.float32)[:, None, None]
    )
    length = segment.shape[0]
    steps_idx = jnp.arange(length)
    allowed = (steps_idx[None, :] <= steps_idx[:, None]) & (segment[None, :] == segment[:, None])
    spread = cumulative[:, None] - cumulative[None, :]
    decays = jnp.exp(jnp.where(allowed[:, :, None, None], spread, -jnp.inf))
    written = decays * (1.0 - jnp.exp(log_keep))[None]
    affinity = jnp.einsum("thd,jhd->htj", query_matrix, key_matrix, precision=highest_precision)
    logit_scores = carried_state * jnp.einsum(
        "ebo,peo->peb", slot_key_state, query_matrix, precision=highest_precision
    )
    logit_scores = logit_scores + jnp.einsum(
        "htj,tjhm->thm", affinity, written, precision=highest_precision
    )
    probability_full = jax.nn.softmax(logit_scores, axis=-1)
    mixing = jnp.einsum("thm,tjhm->htj", probability_full, written, precision=highest_precision)
    block_output = jnp.einsum(
        "zin,inc->zic",
        probability_full * carried_state,
        slot_value_state,
        precision=highest_precision,
    )
    block_output = block_output + jnp.einsum(
        "htj,jhd->thd", mixing, value_matrix, precision=highest_precision
    )
    trailing_weights = written[-1]
    slot_key_state = carried_state[-1][:, :, None] * slot_key_state + jnp.einsum(
        "oes,oev->esv", trailing_weights, key_matrix, precision=highest_precision
    )
    slot_value_state = carried_state[-1][:, :, None] * slot_value_state + jnp.einsum(
        "oes,oev->esv", trailing_weights, value_matrix, precision=highest_precision
    )
    return ((slot_key_state, slot_value_state, segment[-1]), block_output)


def attend(query_matrix, key_matrix, value_matrix, log_keep, segment):
    length = query_matrix.shape[0]
    head_count = query_matrix.shape[1]
    block_len = math.gcd(length, 64)
    block_count = length // block_len

    def arrange(values):
        return values.reshape((block_count, block_len) + values.shape[1:])

    initial = (
        jnp.zeros((head_count, M, DK), jnp.float32),
        jnp.zeros((head_count, M, DV), jnp.float32),
        jnp.zeros((), jnp.int32),
    )
    scaled = query_matrix * (1.0 / math.sqrt(DK))
    unused, outputs = lax.scan(
        jax.checkpoint(slot_block),
        initial,
        (
            arrange(scaled),
            arrange(key_matrix),
            arrange(value_matrix),
            arrange(log_keep),
            arrange(segment),
        ),
    )
    return outputs.reshape(length, head_count, DV)


def on_device(
    block_in,
    out_grad,
    attn_gain,
    mlp_gain,
    w_query,
    w_key,
    w_value,
    w_forget,
    w_output,
    w_gate,
    w_up,
    w_down,
    doc_starts,
):
    length = block_in.shape[0]
    head_local = w_query.shape[1] // DK
    inputs_f = block_in.astype(jnp.float32)
    scale_one = rms_scale(inputs_f)
    normed = (inputs_f * scale_one * attn_gain).astype(jnp.bfloat16)
    query_pre = matmul_plain(normed, w_query)
    key_pre = matmul_plain(normed, w_key)
    value_pre = matmul_plain(normed, w_value)
    forget_pre = matmul_plain(normed, w_forget)
    query_matrix = jax.nn.silu(query_pre).astype(jnp.bfloat16)
    key_matrix = jax.nn.silu(key_pre).astype(jnp.bfloat16)
    value_matrix = jax.nn.silu(value_pre).astype(jnp.bfloat16)
    log_keep = jax.nn.log_sigmoid(forget_pre) * tau_inv
    positions = jnp.arange(length, dtype=jnp.int32)
    segment = jnp.sum((positions[:, None] >= doc_starts[0][None, :]).astype(jnp.int32), axis=1)
    mixed_heads, core_pull = jax.vjp(
        partial(attend, segment=segment),
        query_matrix.astype(jnp.float32).reshape(length, head_local, DK),
        key_matrix.astype(jnp.float32).reshape(length, head_local, DK),
        value_matrix.astype(jnp.float32).reshape(length, head_local, DV),
        log_keep.reshape(length, head_local, M),
    )
    mixed_flat = mixed_heads.reshape(length, head_local * DV).astype(jnp.bfloat16)
    branch = lax.psum(matmul_rt(mixed_flat, w_output), "head")
    hidden = inputs_f + branch
    scale_two = rms_scale(hidden)
    normed_two = (hidden * scale_two * mlp_gain).astype(jnp.bfloat16)
    full_gate, full_up, full_down = (
        lax.all_gather(w_gate, "dp", axis=0, tiled=True),
        lax.all_gather(w_up, "dp", axis=0, tiled=True),
        lax.all_gather(w_down, "dp", axis=0, tiled=True),
    )
    gate_act = matmul_plain(normed_two, full_gate)
    up_act = matmul_plain(normed_two, full_up)
    inner_act = (jax.nn.silu(gate_act) * up_act).astype(jnp.bfloat16)
    mlp_part = matmul_rt(inner_act, full_down)
    mlp_out = lax.psum(mlp_part, "head")
    result = (hidden + mlp_out).astype(jnp.bfloat16)
    inner_grad = matmul_plain(out_grad, full_down)
    gate_grad = (inner_grad * up_act * silu_slope(gate_act)).astype(jnp.bfloat16)
    up_grad = (inner_grad * jax.nn.silu(gate_act)).astype(jnp.bfloat16)
    normed_two_part = matmul_rt(gate_grad, full_gate) + matmul_rt(up_grad, full_up)
    normed_two_grad = lax.psum(normed_two_part, "head")
    mlp_gain_part, hidden_grad = norm_back(hidden, scale_two, mlp_gain, normed_two_grad)
    hidden_grad = hidden_grad + out_grad.astype(jnp.float32)
    mlp_grads = (
        lax.psum_scatter(matmul_lt(normed_two, gate_grad), "dp", scatter_dimension=0, tiled=True),
        lax.psum_scatter(matmul_lt(normed_two, up_grad), "dp", scatter_dimension=0, tiled=True),
        lax.psum_scatter(matmul_lt(out_grad, inner_act), "dp", scatter_dimension=0, tiled=True),
    )
    branch_grad = hidden_grad.astype(jnp.bfloat16)
    output_grad = matmul_lt(branch_grad, mixed_flat)
    mixed_grad = matmul_plain(branch_grad, w_output)
    query_grad, key_grad, value_grad, log_grad = core_pull(
        mixed_grad.reshape(length, head_local, DV)
    )
    query_pre_grad = (query_grad.reshape(length, -1) * silu_slope(query_pre)).astype(jnp.bfloat16)
    key_pre_grad = (key_grad.reshape(length, -1) * silu_slope(key_pre)).astype(jnp.bfloat16)
    value_pre_grad = (value_grad.reshape(length, -1) * silu_slope(value_pre)).astype(jnp.bfloat16)
    forget_pre_grad = (log_grad.reshape(length, -1) * tau_inv * jax.nn.sigmoid(-forget_pre)).astype(
        jnp.bfloat16
    )
    normed_part = matmul_rt(query_pre_grad, w_query) + matmul_rt(key_pre_grad, w_key)
    normed_part = (
        normed_part + matmul_rt(value_pre_grad, w_value) + matmul_rt(forget_pre_grad, w_forget)
    )
    normed_grad = lax.psum(normed_part, "head")
    attn_gain_part, input_grad = norm_back(inputs_f, scale_one, attn_gain, normed_grad)
    input_grad = input_grad + hidden_grad
    shares = (
        lax.psum_scatter(matmul_lt(normed, query_pre_grad), "dp", scatter_dimension=0, tiled=True),
        lax.psum_scatter(matmul_lt(normed, key_pre_grad), "dp", scatter_dimension=0, tiled=True),
        lax.psum_scatter(matmul_lt(normed, value_pre_grad), "dp", scatter_dimension=0, tiled=True),
        lax.psum_scatter(matmul_lt(normed, forget_pre_grad), "dp", scatter_dimension=0, tiled=True),
        lax.psum_scatter(output_grad, "dp", scatter_dimension=0, tiled=True),
        lax.psum_scatter(attn_gain_part, "dp", scatter_dimension=0, tiled=True),
        lax.psum_scatter(mlp_gain_part, "dp", scatter_dimension=0, tiled=True),
    )
    return (
        result,
        input_grad,
        shares[5],
        shares[6],
        shares[0],
        shares[1],
        shares[2],
        shares[3],
        shares[4],
        mlp_grads[0],
        mlp_grads[1],
        mlp_grads[2],
    )


def solution(mesh):
    placed = (
        P("dp", None),
        P("dp", None),
        P(),
        P(),
        P(None, "head"),
        P(None, "head"),
        P(None, "head"),
        P(None, "head"),
        P(None, "head"),
        P("dp", "head"),
        P("dp", "head"),
        P("dp", "head"),
        P("dp", None),
    )
    return jax.shard_map(
        on_device,
        mesh=mesh,
        in_specs=placed,
        out_specs=(
            P("dp", None),
            P("dp", None),
            P("dp"),
            P("dp"),
            P("dp", "head"),
            P("dp", "head"),
            P("dp", "head"),
            P("dp", "head"),
            P("dp", "head"),
            P("dp", "head"),
            P("dp", "head"),
            P("dp", "head"),
        ),
        check_vma=False,
    )
```

profile of v0, /device:TPU:0, one launch (start us, length us, event | category | flops | bytes accessed | tf_op | source)
XLA Modules:
  0.0 3181.7 jit_solution(3647508772836407878)
XLA Ops:
  11.0 2.4 fusion.118
  15.1 4.8 fusion.111
  23.2 4.8 fusion.112
  31.3 4.9 convert_multiply_fusion.5
  39.5 101.2 %while.49 = (s32[]{:T(128)}, f32[2,64,512]{2,1,0:T(8,128)S(1)}, f32[2,64,512]{2,1,0:T(8,128)S(1)}, s32[]{:T(128)}, bf16[4,64,2,512]{3,1,2,0:T(8,128)(2,1)}, /*in...) while((s32[]{:T(128)}, f32[2,64,512]{2,1,0:T(8,128)S(1)}, ...), condition=%wide.region_6.7_spmd.clone, body=%wide.region_2.6_spmd.clone.sunk | while | flops 320614592 | bytes 12804115 | solution.py:109
  44.1 6.9 fusion.304
  57.8 4.1 fusion.308
  69.3 6.9 fusion.304
  82.9 4.1 fusion.308
  94.4 6.9 fusion.304
  108.1 4.1 fusion.308
  119.6 6.9 fusion.304
  133.2 4.1 fusion.308
  143.2 4.8 fusion.142
  149.9 22.4 all-reduce.11.cloned.1.call-done
  175.8 119.5 %all-gather.4.cloned.1.call-done = bf16[2048,2816]{1,0:T(8,128)(2,1)} async-done(((bf16[128,2816]{1,0:T(8,128)(2,1)}), bf16[2048,2816]{1,0:T(8,128)(2,1)}) %all-gather.4.cloned.1.call-update) | async-done | bytes 11534352 | tf_op jit(solution)/shard_map/all_gather | solution.py:166
  295.2 9.0 fusion.143
  304.3 133.0 %all-gather.6.cloned.1.call-done = bf16[2048,2816]{1,0:T(8,128)(2,1)} async-done(((bf16[128,2816]{1,0:T(8,128)(2,1)}), bf16[2048,2816]{1,0:T(8,128)(2,1)}) %all-gather.6.cloned.1.call-update) | async-done | bytes 11534352 | tf_op jit(solution)/shard_map/all_gather | solution.py:167
  437.3 9.0 fusion.144
  446.2 133.0 %all-gather.8.cloned.1.call-done = bf16[2048,2816]{1,0:T(8,128)(2,1)} async-done(((bf16[128,2816]{1,0:T(8,128)(2,1)}), bf16[2048,2816]{1,0:T(8,128)(2,1)}) %all-gather.8.cloned.1.call-update) | async-done | bytes 11534352 | tf_op jit(solution)/shard_map/all_gather | solution.py:168
  579.3 11.2 multiply_convert_fusion
  590.5 9.8 fusion.146
  600.4 6.0 convolution_add_fusion.10
  606.5 9.9 fusion.145
  616.4 9.6 all-reduce.13.cloned.1.call-done
  626.1 3.5 multiply_reduce_fusion.6
  640.1 248.0 %while.50 = (s32[]{:T(128)}, f32[2,64,512]{2,1,0:T(8,128)}, f32[2,64,512]{2,1,0:T(8,128)}, f32[4,64,2,512]{3,1,2,0:T(8,128)}, f32[4,64,2,512]{3,2,1,0:T(2,128)},...) while((s32[]{:T(128)}, f32[2,64,512]{2,1,0:T(8,128)}, ...), condition=%wide.region_23.24_spmd.clone, body=%wide.region_12.23_spmd.clone.sunk | while | flops 733630336 | bytes 24650808 | solution.py:109
  650.9 4.7 fusion.345
  657.6 6.0 fusion.347
  677.4 5.0 multiply_reduce_fusion.13
  689.7 5.6 fusion.356
  713.3 4.7 fusion.345
  719.9 6.0 fusion.347
  739.8 5.0 multiply_reduce_fusion.13
  752.0 5.6 fusion.356
  775.6 4.7 fusion.345
  782.3 6.0 fusion.347
  802.1 5.0 multiply_reduce_fusion.13
  814.3 5.6 fusion.356
  837.9 4.7 fusion.345
  844.6 6.0 fusion.347
  864.4 5.0 multiply_reduce_fusion.13
  876.7 5.6 fusion.356
  892.5 2.6 fusion.147
  900.1 3.6 convolution_add_fusion.9
  907.4 14.6 convolution_bitcast_fusion.6
  924.3 5.4 fusion.125
  929.9 5.1 fusion.123
  935.1 4.7 fusion.121
  940.9 6.2 fusion.113
  948.3 10.8 fusion.148
  959.2 10.7 fusion.149
  971.9 2.1 fusion.110
  974.0 83.4 %all-reduce.5 = (f32[2048]{0:T(1024)S(1)}, f32[2048]{0:T(1024)S(1)}) all-reduce(f32[2048]{0:T(1024)S(1)} %get-tuple-element.745, f32[2048]{0:T(1024)S(1)} %copy-done.49), channel_id=2, replica_groups=mesh['dp'=16,'head'=2] {'dp'}, use_global_device_ids=true, to_apply=%region_27.28.clone | all-reduce | flops 4096 | bytes 32768
  1058.6 5.9 fusion.107
  1064.5 334.4 %reduce-scatter.23.cloned.1.call-done = f32[128,2816]{0,1:T(8,128)} async-done(((f32[2048,2816]{0,1:T(8,128)}), f32[128,2816]{0,1:T(8,128)}) %reduce-scatter.23.cloned.1.call-update) | async-done | bytes 1441808 | tf_op jit(solution)/shard_map/reduce_scatter | solution.py:186
  1398.9 2.9 copy.147
  1401.8 85.5 %reduce-scatter.15.cloned.1.call-done = f32[128,128]{1,0:T(8,128)} async-done(((f32[2048,128]{1,0:T(8,128)}), f32[128,128]{1,0:T(8,128)}) %reduce-scatter.15.cloned.1.call-update) | async-done | bytes 65552 | tf_op jit(solution)/shard_map/reduce_scatter | solution.py:211
  1487.3 177.0 %reduce-scatter.9.cloned.1.call-done = f32[128,1024]{1,0:T(8,128)} async-done(((f32[2048,1024]{1,0:T(8,128)}), f32[128,1024]{1,0:T(8,128)}) %reduce-scatter.9.cloned.1.call-update) | async-done | bytes 524304 | tf_op jit(solution)/shard_map/reduce_scatter | solution.py:208
  1664.3 183.0 %reduce-scatter.11.cloned.1.call-done = f32[128,1024]{1,0:T(8,128)} async-done(((f32[2048,1024]{1,0:T(8,128)}), f32[128,1024]{1,0:T(8,128)}) %reduce-scatter.11.cloned.1.call-update) | async-done | bytes 524304 | tf_op jit(solution)/shard_map/reduce_scatter | solution.py:209
  1847.3 183.0 %reduce-scatter.13.cloned.1.call-done = f32[128,1024]{1,0:T(8,128)} async-done(((f32[2048,1024]{1,0:T(8,128)}), f32[128,1024]{1,0:T(8,128)}) %reduce-scatter.13.cloned.1.call-update) | async-done | bytes 524304 | tf_op jit(solution)/shard_map/reduce_scatter | solution.py:210
  2030.3 183.0 %reduce-scatter.17.cloned.1.call-done = f32[128,1024]{1,0:T(8,128)} async-done(((f32[2048,1024]{1,0:T(8,128)}), f32[128,1024]{1,0:T(8,128)}) %reduce-scatter.17.cloned.1.call-update) | async-done | bytes 524304 | tf_op jit(solution)/shard_map/reduce_scatter | solution.py:212
  2213.3 478.3 %reduce-scatter.19.cloned.1.call-done = f32[128,2816]{1,0:T(8,128)} async-done(((f32[2048,2816]{1,0:T(8,128)}), f32[128,2816]{1,0:T(8,128)}) %reduce-scatter.19.cloned.1.call-update) | async-done | bytes 1441808 | tf_op jit(solution)/shard_map/reduce_scatter | solution.py:184
  2691.6 482.5 %reduce-scatter.21.cloned.1.call-done = f32[128,2816]{1,0:T(8,128)} async-done(((f32[2048,2816]{1,0:T(8,128)}), f32[128,2816]{1,0:T(8,128)}) %reduce-scatter.21.cloned.1.call-update) | async-done | bytes 1441808 | tf_op jit(solution)/shard_map/reduce_scatter | solution.py:185
  (644 shorter events, 267.0 us)
Async XLA Ops:
  8.0 7.0 copy-start.1
  8.0 7.0 copy-start.38
  8.0 6.3 copy-start.53
  8.1 164.2 %all-reduce.11.cloned.1.call-start = ((), (), s32[]{:S(2)}) async-start(), calls=%async_computation.8 | async-start | bytes 4194304 | tf_op jit(solution)/shard_map/psum | solution.py:161
  11.0 20.3 copy-start.44
  57.8 4.1 copy-start.33
  82.9 4.1 copy-start.33
  108.1 4.1 copy-start.33
  133.2 4.1 copy-start.33
  148.1 147.2 %all-gather.4.cloned.1.call-start = ((), (), s32[]{:S(2)}) async-start(), calls=%async_computation.9 | async-start | bytes 12255232 | tf_op jit(solution)/shard_map/all_gather | solution.py:166
  148.6 288.6 %all-gather.6.cloned.1.call-start = ((), (), s32[]{:S(2)}) async-start(), calls=%async_computation.10 | async-start | bytes 12255232 | tf_op jit(solution)/shard_map/all_gather | solution.py:167
  149.2 26.3 copy-start.46
  149.2 430.0 %all-gather.8.cloned.1.call-start = ((), (), s32[]{:S(2)}) async-start(), calls=%async_computation.11 | async-start | bytes 12255232 | tf_op jit(solution)/shard_map/all_gather | solution.py:168
  149.8 476.2 %all-reduce.13.cloned.1.call-start = ((), (), s32[]{:S(2)}) async-start(), calls=%async_computation.12 | async-start | bytes 4194304 | tf_op jit(solution)/shard_map/psum | solution.py:180
  175.8 261.5 %copy-start.16 = (bf16[256,2048]{1,0:T(8,128)(2,1)}, bf16[256,2048]{1,0:T(8,128)(2,1)S(1)}, u32[]{:S(2)}) copy-start(bf16[256,2048]{1,0:T(8,128)(2,1)S(1)} %multiply_convert_fusion.3) | copy-start | bytes 3145732
  579.3 21.1 slice-start
  579.3 21.1 slice-start.1
  590.5 9.8 copy-start.37
  590.5 9.8 copy-start.36
  590.5 9.9 slice-start.2
  606.4 365.4 %all-reduce.15.cloned.1.call-start = ((), (), s32[]{:S(2)}) async-start(), calls=%async_computation.21 | async-start | bytes 8388608 | tf_op jit(solution)/shard_map/psum | solution.py:174
  606.5 23.1 copy-start.25
  647.9 7.8 copy-start.8
  657.6 6.0 copy-start.24
  666.5 7.1 copy-start.10
  667.8 6.5 copy-start.13
  669.2 5.1 copy-start.5
  688.7 7.0 copy-start.35
  689.6 6.9 copy-start.15
  708.3 9.7 copy-start.8
  719.9 6.0 copy-start.24
  728.8 7.2 copy-start.10
  730.1 6.5 copy-start.13
  731.6 5.1 copy-start.5
  751.0 7.0 copy-start.35
  752.0 6.9 copy-start.15
  770.7 9.7 copy-start.8
  782.3 6.0 copy-start.24
  791.2 7.2 copy-start.10
  792.5 6.5 copy-start.13
  793.9 5.1 copy-start.5
  813.4 7.0 copy-start.35
  814.3 6.9 copy-start.15
  833.0 9.7 copy-start.8
  844.6 6.0 copy-start.24
  853.5 7.2 copy-start.10
  854.8 6.5 copy-start.13
  856.2 5.1 copy-start.5
  875.7 7.0 copy-start.35
  876.6 6.9 copy-start.15
  892.5 3.8 copy-start.28
  900.1 3.6 copy-start.29
  900.1 3.6 copy-start.40
  900.1 4.1 copy-start.26
  907.3 491.6 %reduce-scatter.23.cloned.1.call-start = ((), (), s32[]{:S(2)}) async-start(), calls=%async_computation.20 | async-start | bytes 24510464 | tf_op jit(solution)/shard_map/reduce_scatter | solution.py:186
  922.0 565.3 %reduce-scatter.15.cloned.1.call-start = ((), (), s32[]{:S(2)}) async-start(), calls=%async_computation.16 | async-start | bytes 1114112 | tf_op jit(solution)/shard_map/reduce_scatter | solution.py:211
  924.2 740.1 %reduce-scatter.9.cloned.1.call-start = ((), (), s32[]{:S(2)}) async-start(), calls=%async_computation.13 | async-start | bytes 8912896 | tf_op jit(solution)/shard_map/reduce_scatter | solution.py:208
  929.7 917.6 %reduce-scatter.11.cloned.1.call-start = ((), (), s32[]{:S(2)}) async-start(), calls=%async_computation.14 | async-start | bytes 8912896 | tf_op jit(solution)/shard_map/reduce_scatter | solution.py:209
  935.0 1095.2 %reduce-scatter.13.cloned.1.call-start = ((), (), s32[]{:S(2)}) async-start(), calls=%async_computation.15 | async-start | bytes 8912896 | tf_op jit(solution)/shard_map/reduce_scatter | solution.py:210
  939.9 1273.4 %reduce-scatter.17.cloned.1.call-start = ((), (), s32[]{:S(2)}) async-start(), calls=%async_computation.17 | async-start | bytes 8912896 | tf_op jit(solution)/shard_map/reduce_scatter | solution.py:212
  947.1 1744.5 %reduce-scatter.19.cloned.1.call-start = ((), (), s32[]{:S(2)}) async-start(), calls=%async_computation.18 | async-start | bytes 24510464 | tf_op jit(solution)/shard_map/reduce_scatter | solution.py:184
  959.2 2214.9 %reduce-scatter.21.cloned.1.call-start = ((), (), s32[]{:S(2)}) async-start(), calls=%async_computation.19 | async-start | bytes 24510464 | tf_op jit(solution)/shard_map/reduce_scatter | solution.py:185
  970.0 4.0 copy-start.49
  970.0 88.6 %copy-start.50 = (f32[256]{0:T(256)S(1)}, f32[256]{0:T(256)}, u32[]{:S(2)}) copy-start(f32[256]{0:T(256)} %get-tuple-element.837) | copy-start | bytes 3076
  (74 other events, 166.2 us)
Sparse Core Ops, SparseCore 0:
  148.2 23.9 all-reduce.10
  606.5 19.4 all-reduce.12
  907.4 29.5 all-reduce.14
Sparse Core Ops, SparseCore 1:
  151.3 143.9 all-gather.3
  297.8 139.3 all-gather.5
  439.9 139.3 all-gather.7
  922.1 476.8 reduce-scatter.22
  1401.7 85.5 reduce-scatter.14
  1490.2 174.1 reduce-scatter.8
  1667.1 180.2 reduce-scatter.10
  1850.0 180.2 reduce-scatter.12
  2033.0 180.2 reduce-scatter.16
  2216.2 475.4 reduce-scatter.18
  2694.4 479.7 reduce-scatter.20
where the time goes:
time: 3200 us; the launch traced here: 3180 us
  waiting for transfers between devices  2530 us (79%)
  matrix products  306 us (10%)
  local copies, waits for them, and re-layouts  142 us (4%)
  other arithmetic  101 us (3%)
  blocking collectives  83.4 us (3%)
    reduce_scatter x1, waiting for transfers between devices, on_device(): lax.psum_scatter(matmul_lt(normed_two, up_grad), 'dp', scatter_dimension=...  483 us
    reduce_scatter x1, waiting for transfers between devices, on_device(): lax.psum_scatter(matmul_lt(normed_two, gate_grad), 'dp', scatter_dimensio...  478 us
    reduce_scatter x1, waiting for transfers between devices, on_device(): lax.psum_scatter(matmul_lt(out_grad, inner_act), 'dp', scatter_dimension=...  334 us
    reduce_scatter x1, waiting for transfers between devices, on_device(): lax.psum_scatter(output_grad, 'dp', scatter_dimension=0, tiled=True)  183 us
    reduce_scatter x1, waiting for transfers between devices, on_device(): lax.psum_scatter(matmul_lt(normed, value_pre_grad), 'dp', scatter_dimensi...  183 us
    reduce_scatter x1, waiting for transfers between devices, on_device(): lax.psum_scatter(matmul_lt(normed, key_pre_grad), 'dp', scatter_dimension...  183 us
    reduce_scatter x1, waiting for transfers between devices, on_device(): lax.psum_scatter(matmul_lt(normed, query_pre_grad), 'dp', scatter_dimensi...  177 us
    all_gather x1, waiting for transfers between devices, on_device(): lax.all_gather(w_down, 'dp', axis=0, tiled=True)  133 us
  transfers between devices with their start and end apart: 14, of which 13 were waited for; matrix products, arithmetic and copies ran while one was open for 3% of the time, Pallas kernels for 0%

commit v1 on v0

v1 whole, which is shorter than its diff:
```python
import math
from functools import partial
import jax
import jax.numpy as jnp
from jax import lax
from jax.experimental import pallas as pl
from jax.experimental.pallas import tpu as pltpu
from jax.sharding import PartitionSpec as P

DK = 512
DV = 512
M = 64
B = 16
f32 = jnp.float32
bf16 = jnp.bfloat16


def nn(a, b):
    return jnp.dot(a.astype(bf16), b.astype(bf16), preferred_element_type=f32)


def nt(a, b):
    return lax.dot_general(
        a.astype(bf16), b.astype(bf16), (((1,), (1,)), ((), ())), preferred_element_type=f32
    )


def tn(a, b):
    return lax.dot_general(
        a.astype(bf16), b.astype(bf16), (((0,), (0,)), ((), ())), preferred_element_type=f32
    )


def nn3(a, b):
    ah, bh = a.astype(bf16), b.astype(bf16)
    al, bl = (a - ah.astype(f32)).astype(bf16), (b - bh.astype(f32)).astype(bf16)
    return nn(ah, bh) + (nn(al, bh) + nn(ah, bl))


def shift_up(x, s):
    return pltpu.roll(x, x.shape[0] - s, 0)


def shift_down(x, s):
    return pltpu.roll(x, s, 0)


def segment_at(pos, starts):
    seg = jnp.zeros(pos.shape, jnp.int32)
    for s in starts:
        seg = seg + (pos >= s).astype(jnp.int32)
    return seg


def same_document(t, j, starts):
    ok = None
    for s in starts:
        same = (t >= s) == (j >= s)
        ok = same if ok is None else ok & same
    return ok


def level_sizes(length):
    sizes = []
    h = length // 2
    while h >= B:
        sizes.append(h)
        h //= 2
    return sizes


def row_pick(x, size, row):
    n, lanes = x.shape
    x3 = x.reshape(n // size, size, lanes)
    return jnp.broadcast_to(x3[:, row : row + 1, :], x3.shape).reshape(n, lanes)


class Common:
    def __init__(self, la, starts):
        length, lanes = la.shape
        self.length, self.lanes = length, lanes
        rows = lax.broadcasted_iota(jnp.int32, (length, lanes), 0)
        self.rows = rows
        self.lane_head = lax.broadcasted_iota(jnp.int32, (length, lanes), 1) // M
        c = la
        s = 1
        while s < length:
            c = c + jnp.where(rows >= s, shift_down(c, s), 0.0)
            s *= 2
        self.c = c
        self.alpha = jnp.exp(la)
        self.om = 1.0 - self.alpha
        self.levels = level_sizes(length)
        self.x = []
        for h in self.levels:
            mid = row_pick(c, 2 * h, h - 1)
            self.x.append(jnp.exp(-jnp.abs(c - mid)))
        t = lax.broadcasted_iota(jnp.int32, (length, length), 0)
        j = lax.broadcasted_iota(jnp.int32, (length, length), 1)
        same = same_document(t, j, starts)
        self.masks = [
            same & ((t // (2 * h)) == (j // (2 * h))) & ((t & h) != 0) & ((j & h) == 0)
            for h in self.levels
        ]
        tc = lax.broadcasted_iota(jnp.int32, (length, B), 0)
        off = lax.broadcasted_iota(jnp.int32, (length, B), 1)
        jc = (tc - tc % B) + off
        self.mask_c = same_document(tc, jc, starts) & (jc <= tc)

    def by_head(self, parts):
        out = parts[0]
        for i in range(1, len(parts)):
            out = jnp.where(self.lane_head == i, parts[i], out)
        return out

    def only(self, x, i):
        return jnp.where(self.lane_head == i, x, 0.0)

    def decay_from(self, jj):
        return jnp.exp(jnp.minimum(self.c - row_pick(self.c, B, jj), 0.0))

    def om_at(self, jj):
        return row_pick(self.om, B, jj)


def blocks(x):
    return x.reshape(x.shape[0] // B, B, x.shape[1])


def block_nt(a, b):
    r = lax.dot_general(
        blocks(a.astype(bf16)),
        blocks(b.astype(bf16)),
        (((2,), (2,)), ((0,), (0,))),
        preferred_element_type=f32,
    )
    return r.reshape(a.shape[0], B)


def block_nn(a, b):
    r = lax.dot_general(
        blocks(a.astype(bf16)),
        blocks(b.astype(bf16)),
        (((2,), (1,)), ((0,), (0,))),
        preferred_element_type=f32,
    )
    return r.reshape(a.shape[0], b.shape[1])


def block_tn(a, b):
    at = jnp.swapaxes(blocks(a), 1, 2).astype(bf16)
    r = lax.dot_general(
        at, blocks(b.astype(bf16)), (((2,), (1,)), ((0,), (0,))), preferred_element_type=f32
    )
    return r.reshape(a.shape[0], b.shape[1])


def collect(lanes, heads):
    r = lax.broadcasted_iota(jnp.int32, (B * lanes, heads * 128), 0)
    col = lax.broadcasted_iota(jnp.int32, (B * lanes, heads * 128), 1)
    jj, head = r // lanes, (r % lanes) // M
    return jnp.where(col == head * 128 + jj, 1.0, 0.0).astype(bf16)


def wide(x, jj):
    return jnp.broadcast_to(x[:, jj : jj + 1], (x.shape[0], 128))


def forward_math(q, k, v, la, starts):
    heads = q.shape[1] // DK
    scale = 1.0 / math.sqrt(DK)
    cm = Common(la, starts)
    qs = [q[:, i * DK : (i + 1) * DK] for i in range(heads)]
    ks = [k[:, i * DK : (i + 1) * DK] for i in range(heads)]
    vs = [v[:, i * DV : (i + 1) * DV] for i in range(heads)]
    aff = [nt(qs[i], ks[i]) * scale for i in range(heads)]
    affc = [jnp.where(cm.mask_c, block_nt(qs[i], ks[i]) * scale, 0.0) for i in range(heads)]
    s = jnp.zeros_like(la)
    parts = []
    for x, mask in zip(cm.x, cm.masks):
        g = x * cm.om
        part = x * cm.by_head([nn3(jnp.where(mask, aff[i], 0.0), g) for i in range(heads)])
        parts.append(part)
        s = s + part
    for jj in range(B):
        s = s + cm.by_head([wide(affc[i], jj) for i in range(heads)]) * (
            cm.decay_from(jj) * cm.om_at(jj)
        )
    top = cm.by_head(
        [
            jnp.max(jnp.where(cm.lane_head == i, s, -jnp.inf), axis=1, keepdims=True)
            for i in range(heads)
        ]
    )
    e = jnp.exp(s - top)
    total = cm.by_head([jnp.sum(cm.only(e, i), axis=1, keepdims=True) for i in range(heads)])
    p = e / total
    mix = [jnp.zeros((cm.length, cm.length), f32) for _ in range(heads)]
    for x, mask in zip(cm.x, cm.masks):
        g = x * cm.om
        px = p * x
        for i in range(heads):
            mix[i] = mix[i] + jnp.where(mask, nt(cm.only(px, i), g), 0.0)
    mix = [m.astype(bf16) for m in mix]
    pieces = [(p * (cm.decay_from(jj) * cm.om_at(jj))).astype(bf16) for jj in range(B)]
    mixc = nn(jnp.concatenate(pieces, axis=1), collect(cm.lanes, heads))
    mixc = [
        jnp.where(cm.mask_c, mixc[:, i * 128 : i * 128 + B], 0.0) for i in range(heads)
    ]
    outs = [nn(mix[i], vs[i]) + block_nn(mixc[i], vs[i]) for i in range(heads)]
    return outs, p, parts, mix, mixc


def backward_math(q, k, v, la, starts, p, parts, mix, mixc, dout):
    heads = q.shape[1] // DK
    scale = 1.0 / math.sqrt(DK)
    cm = Common(la, starts)
    qs = [q[:, i * DK : (i + 1) * DK] for i in range(heads)]
    ks = [k[:, i * DK : (i + 1) * DK] for i in range(heads)]
    vs = [v[:, i * DV : (i + 1) * DV] for i in range(heads)]
    dos = [dout[:, i * DV : (i + 1) * DV].astype(bf16) for i in range(heads)]
    aff = [nt(qs[i], ks[i]) * scale for i in range(heads)]
    affc = [jnp.where(cm.mask_c, block_nt(qs[i], ks[i]) * scale, 0.0) for i in range(heads)]
    dmix = [nt(dos[i], vs[i]) for i in range(heads)]
    dmixc = [jnp.where(cm.mask_c, block_nt(dos[i], vs[i]), 0.0) for i in range(heads)]
    dp = jnp.zeros_like(la)
    dparts = []
    for x, mask in zip(cm.x, cm.masks):
        g = x * cm.om
        part = x * cm.by_head([nn3(jnp.where(mask, dmix[i], 0.0), g) for i in range(heads)])
        dparts.append(part)
        dp = dp + part
    for jj in range(B):
        dp = dp + cm.by_head([wide(dmixc[i], jj) for i in range(heads)]) * (
            cm.decay_from(jj) * cm.om_at(jj)
        )
    pdp = p * dp
    inner = cm.by_head([jnp.sum(cm.only(pdp, i), axis=1, keepdims=True) for i in range(heads)])
    ds = pdp - p * inner
    daff = [jnp.zeros((cm.length, cm.length), f32) for _ in range(heads)]
    dla = jnp.zeros_like(la)
    reach = jnp.zeros_like(la)
    for n, h in enumerate(cm.levels):
        x, mask = cm.x[n], cm.masks[n]
        g = x * cm.om
        dsx, px = ds * x, p * x
        both = jnp.concatenate([dsx, px], axis=0).astype(bf16)
        cols = []
        for i in range(heads):
            daff[i] = daff[i] + jnp.where(mask, nt(cm.only(dsx, i), g), 0.0)
            left = jnp.concatenate(
                [jnp.where(mask, aff[i], 0.0), jnp.where(mask, dmix[i], 0.0)], axis=0
            )
            cols.append(tn(left, both))
        r = x * cm.by_head(cols)
        reach = reach + r
        right = (cm.rows & h) != 0
        flow = jnp.where(right, ds * parts[n] + p * dparts[n], cm.om * r)
        s = 1
        while s < h:
            flow = flow + jnp.where((cm.rows & (h - 1)) < h - s, shift_up(flow, s), 0.0)
            s *= 2
        dla = dla + jnp.where(right, flow, row_pick(flow, h, 0) - flow)
    flow = jnp.zeros_like(la)
    near = jnp.zeros_like(la)
    pieces = []
    for jj in range(B):
        w = cm.decay_from(jj)
        omj = cm.om_at(jj)
        aj = cm.by_head([wide(affc[i], jj) for i in range(heads)])
        dj = cm.by_head([wide(dmixc[i], jj) for i in range(heads)])
        pieces.append((ds * (w * omj)).astype(bf16))
        z = w * (aj * ds + dj * p)
        flow = flow + omj * z
        z3 = blocks(z)
        tot = jnp.broadcast_to(jnp.sum(z3, axis=1, keepdims=True), z3.shape).reshape(z.shape)
        near = jnp.where((cm.rows & (B - 1)) == jj, tot, near)
    flow = flow - cm.om * near
    s = 1
    while s < B:
        flow = flow + jnp.where((cm.rows & (B - 1)) < B - s, shift_up(flow, s), 0.0)
        s *= 2
    dla = dla + flow - cm.alpha * (reach + near)
    daffc = nn(jnp.concatenate(pieces, axis=1), collect(cm.lanes, heads))
    daffc = [
        jnp.where(cm.mask_c, daffc[:, i * 128 : i * 128 + B], 0.0) for i in range(heads)
    ]
    dq, dk, dv = [], [], []
    for i in range(heads):
        da = daff[i].astype(bf16)
        dq.append((nn(da, ks[i]) + block_nn(daffc[i], ks[i])) * scale)
        dk.append((tn(da, qs[i]) + block_tn(daffc[i], qs[i])) * scale)
        dv.append(tn(mix[i], dos[i]) + block_tn(mixc[i], dos[i]))
    return dq, dk, dv, dla


def head_split(outs, ref, width):
    for i, x in enumerate(outs):
        ref[:, i * width : (i + 1) * width] = x.astype(ref.dtype)


def forward_kernel(starts_ref, q_ref, k_ref, v_ref, la_ref, o_ref, p_ref, parts_ref, mix_ref, mixc_ref):
    starts = [starts_ref[0, n] for n in range(starts_ref.shape[1])]
    outs, p, parts, mix, mixc = forward_math(
        q_ref[...], k_ref[...], v_ref[...], la_ref[...], starts
    )
    head_split(outs, o_ref, DV)
    p_ref[...] = p
    for n, x in enumerate(parts):
        parts_ref[n] = x
    for i in range(len(mix)):
        mix_ref[i] = mix[i]
        mixc_ref[i] = mixc[i].astype(bf16)


def backward_kernel(
    starts_ref, q_ref, k_ref, v_ref, la_ref, p_ref, parts_ref, mix_ref, mixc_ref, do_ref,
    dq_ref, dk_ref, dv_ref, dla_ref,
):
    starts = [starts_ref[0, n] for n in range(starts_ref.shape[1])]
    heads = mix_ref.shape[0]
    dq, dk, dv, dla = backward_math(
        q_ref[...],
        k_ref[...],
        v_ref[...],
        la_ref[...],
        starts,
        p_ref[...],
        [parts_ref[n] for n in range(parts_ref.shape[0])],
        [mix_ref[i] for i in range(heads)],
        [mixc_ref[i] for i in range(heads)],
        do_ref[...],
    )
    head_split(dq, dq_ref, DK)
    head_split(dk, dk_ref, DK)
    head_split(dv, dv_ref, DV)
    dla_ref[...] = dla


SMEM = pl.BlockSpec(memory_space=pltpu.SMEM)
VMEM = pl.BlockSpec(memory_space=pltpu.VMEM)


def attend_forward(q, k, v, la, starts):
    length, lanes = la.shape
    heads = q.shape[1] // DK
    sds = jax.ShapeDtypeStruct
    return pl.pallas_call(
        forward_kernel,
        out_shape=(
            sds((length, heads * DV), bf16),
            sds((length, lanes), f32),
            sds((len(level_sizes(length)), length, lanes), f32),
            sds((heads, length, length), bf16),
            sds((heads, length, B), bf16),
        ),
        in_specs=[SMEM] + [VMEM] * 4,
        out_specs=(VMEM,) * 5,
        cost_estimate=pl.CostEstimate(
            flops=4 * 10**9, transcendentals=10**6, bytes_accessed=4 * 10**6
        ),
        name="slot_forward",
    )(starts, q, k, v, la)


def attend_backward(q, k, v, la, starts, saved, dout):
    length, lanes = la.shape
    sds = jax.ShapeDtypeStruct
    return pl.pallas_call(
        backward_kernel,
        out_shape=(
            sds(q.shape, f32),
            sds(k.shape, f32),
            sds(v.shape, f32),
            sds((length, lanes), f32),
        ),
        in_specs=[SMEM] + [VMEM] * 9,
        out_specs=(VMEM,) * 4,
        cost_estimate=pl.CostEstimate(
            flops=12 * 10**9, transcendentals=10**6, bytes_accessed=8 * 10**6
        ),
        name="slot_backward",
    )(starts, q, k, v, la, *saved, dout)


eps = 1e-06
tau_inv = 0.125
INNER = 4
LAP = (0, 1, 3, 2)


def rms_scale(values):
    return lax.rsqrt(jnp.mean(values * values, axis=-1, keepdims=True) + eps)


def norm_back(values, scale, gain, upstream):
    gain_grad = jnp.sum(upstream * values * scale, axis=0)
    weighted = upstream * gain
    input_grad = scale * weighted - values * (scale * scale * scale) * jnp.mean(
        weighted * values, axis=-1, keepdims=True
    )
    return (gain_grad, input_grad)


def silu_slope(values):
    sigmoid_val = jax.nn.sigmoid(values)
    return sigmoid_val * (1.0 + values * (1.0 - sigmoid_val))


class Grid:
    def __init__(self, dp):
        self.dp = dp
        self.outer = dp // INNER
        self.rows = [[o * INNER + i for i in LAP] for o in range(self.outer)]
        self.cols = [[o * INNER + i for o in range(self.outer)] for i in range(INNER)]
        self.gathered = [o * INNER + i for i in LAP for o in range(self.outer)]
        walk = [0]
        for n, i in enumerate((1, 3, 2)):
            column = [o * INNER + i for o in range(self.outer)]
            walk += column if n % 2 == 0 else column[::-1]
        walk += [o * INNER for o in range(self.outer - 1, 0, -1)]
        self.walk = walk


def reorder(x, order):
    n = len(order)
    size = x.shape[-1] // n
    return jnp.concatenate([x[..., b * size : (b + 1) * size] for b in order], axis=-1)


def inverse(order):
    back = [0] * len(order)
    for n, b in enumerate(order):
        back[b] = n
    return back


def swap(x):
    return lax.ppermute(x, "head", [(0, 1), (1, 0)])


def half_of(x, which):
    size = x.shape[0] // 2
    return lax.dynamic_slice_in_dim(x, which * size, size, 0)


def join(mine, other, core):
    size = mine.shape[0]
    out = jnp.zeros((2 * size,) + mine.shape[1:], mine.dtype)
    out = lax.dynamic_update_slice_in_dim(out, mine, core * size, 0)
    return lax.dynamic_update_slice_in_dim(out, other, (1 - core) * size, 0)


def spread_columns(w, grid, place):
    rows, size = w.shape[0], w.shape[1] // grid.outer
    if grid.outer > 4:
        return lax.all_to_all(w, "dp", 1, 0, tiled=True, axis_index_groups=grid.cols)
    out = jnp.zeros((grid.outer, rows, size), w.dtype)
    for s in range(grid.outer):
        mate = place ^ s
        piece = lax.dynamic_slice_in_dim(w, mate * size, size, 1)
        if s:
            pairs = [
                (o * INNER + i, (o ^ s) * INNER + i) for o in range(grid.outer) for i in range(INNER)
            ]
            piece = lax.ppermute(piece, "dp", pairs)
        out = lax.dynamic_update_slice_in_dim(out, piece[None], mate, 0)
    return out.reshape(grid.outer * rows, size)


def gather_rows(w, grid):
    return lax.all_gather(w, "dp", axis=0, tiled=True, axis_index_groups=grid.rows)


def scatter_rows(g, grid):
    g = lax.psum_scatter(
        g, "dp", scatter_dimension=0, tiled=True, axis_index_groups=grid.rows
    )
    return lax.all_to_all(g, "dp", 0, 1, tiled=True, axis_index_groups=grid.cols)


def gather_tokens(x, grid):
    x = reorder(x, grid.gathered)
    own = lax.all_gather(x, "dp", axis=0, tiled=True, axis_index_groups=grid.cols)
    return jnp.concatenate([own, swap(own)], axis=0)


def scatter_tokens(x, grid):
    size = x.shape[0] // 2
    other = swap(x[size:].astype(bf16))
    mine = (x[:size] + other.astype(f32)).astype(bf16)
    mine = lax.psum_scatter(
        mine, "dp", scatter_dimension=0, tiled=True, axis_index_groups=grid.cols
    )
    return reorder(mine.astype(f32), inverse(grid.gathered))


def on_device(
    block_in,
    out_grad,
    attn_gain,
    mlp_gain,
    w_query,
    w_key,
    w_value,
    w_forget,
    w_output,
    w_gate,
    w_up,
    w_down,
    doc_starts,
    grid,
):
    core = lax.axis_index("head")
    place = lax.axis_index("dp") // INNER
    cot_half = half_of(out_grad, core)
    cot_all = gather_tokens(cot_half, grid)
    full_gate = gather_rows(spread_columns(w_gate, grid, place), grid)
    full_up = gather_rows(spread_columns(w_up, grid, place), grid)
    full_down = gather_rows(spread_columns(w_down, grid, place), grid)

    inputs_f = block_in.astype(f32)
    scale_one = rms_scale(inputs_f)
    normed = (inputs_f * scale_one * attn_gain).astype(bf16)
    query_pre = nn(normed, w_query)
    key_pre = nn(normed, w_key)
    value_pre = nn(normed, w_value)
    forget_pre = nn(normed, w_forget)
    query = jax.nn.silu(query_pre).astype(bf16)
    key = jax.nn.silu(key_pre).astype(bf16)
    value = jax.nn.silu(value_pre).astype(bf16)
    log_keep = jax.nn.log_sigmoid(forget_pre) * tau_inv
    mixed, *saved = attend_forward(query, key, value, log_keep, doc_starts)

    branch = nt(mixed, w_output)
    hidden = half_of(inputs_f, core) + half_of(branch, core) + swap(half_of(branch, 1 - core))
    scale_two = rms_scale(hidden)
    normed_two = (hidden * scale_two * mlp_gain).astype(bf16)
    tokens = gather_tokens(normed_two, grid)

    gate_act = nn(tokens, full_gate)
    up_act = nn(tokens, full_up)
    inner_grad = nn(cot_all, full_down)
    gate_grad = (inner_grad * up_act * silu_slope(gate_act)).astype(bf16)
    up_grad = (inner_grad * jax.nn.silu(gate_act)).astype(bf16)
    inner_act = (jax.nn.silu(gate_act) * up_act).astype(bf16)
    normed_two_grad = scatter_tokens(nt(gate_grad, full_gate) + nt(up_grad, full_up), grid)
    mlp_out = scatter_tokens(nt(inner_act, full_down), grid)
    result = (hidden + mlp_out).astype(bf16)
    result = join(result, swap(result), core)

    mlp_gain_part, hidden_grad = norm_back(hidden, scale_two, mlp_gain, normed_two_grad)
    hidden_grad = hidden_grad + cot_half.astype(f32)
    branch_half = hidden_grad.astype(bf16)
    branch_grad = join(branch_half, swap(branch_half), core)
    mixed_grad = nn(branch_grad, w_output).astype(bf16)

    gate_sum = scatter_rows(tn(tokens, gate_grad).astype(bf16), grid).astype(f32)
    up_sum = scatter_rows(tn(tokens, up_grad).astype(bf16), grid).astype(f32)
    down_sum = scatter_rows(tn(cot_all, inner_act).astype(bf16), grid).astype(f32)

    def walk_sum(g):
        return lax.psum_scatter(
            g.astype(bf16), "dp", scatter_dimension=0, tiled=True, axis_index_groups=[grid.walk]
        ).astype(f32)

    output_sum = walk_sum(tn(reorder(branch_grad, grid.walk), mixed))
    query_grad, key_grad, value_grad, log_grad = attend_backward(
        query, key, value, log_keep, doc_starts, saved, mixed_grad
    )
    query_pre_grad = (query_grad * silu_slope(query_pre)).astype(bf16)
    key_pre_grad = (key_grad * silu_slope(key_pre)).astype(bf16)
    value_pre_grad = (value_grad * silu_slope(value_pre)).astype(bf16)
    forget_pre_grad = (log_grad * tau_inv * jax.nn.sigmoid(-forget_pre)).astype(bf16)
    pre_grads = (query_pre_grad, key_pre_grad, value_pre_grad, forget_pre_grad)
    sums = walk_sum(tn(reorder(normed, grid.walk), jnp.concatenate(pre_grads, axis=1)))
    normed_part = nt(query_pre_grad, w_query) + nt(key_pre_grad, w_key)
    normed_part = normed_part + nt(value_pre_grad, w_value) + nt(forget_pre_grad, w_forget)
    normed_grad = half_of(normed_part, core) + swap(half_of(normed_part, 1 - core))
    attn_gain_part, input_grad = norm_back(
        half_of(inputs_f, core), half_of(scale_one, core), attn_gain, normed_grad
    )
    input_grad = input_grad + hidden_grad
    input_grad = join(input_grad, swap(input_grad), core)

    gains = jnp.stack([attn_gain_part, mlp_gain_part])
    gains = gains + swap(gains)
    gains = jnp.swapaxes(gains.reshape(2, grid.dp, -1), 0, 1)
    gains = jnp.sum(lax.all_to_all(gains, "dp", 0, 0, tiled=True), axis=0)

    widths = [g.shape[1] for g in pre_grads]
    ends = [sum(widths[: n + 1]) for n in range(4)]
    query_sum, key_sum, value_sum, forget_sum = (
        sums[:, e - w : e] for e, w in zip(ends, widths)
    )
    return (
        result,
        input_grad,
        gains[0],
        gains[1],
        query_sum,
        key_sum,
        value_sum,
        forget_sum,
        output_sum,
        gate_sum,
        up_sum,
        down_sum,
    )


def solution(mesh):
    placed = (
        P("dp", None),
        P("dp", None),
        P(),
        P(),
        P(None, "head"),
        P(None, "head"),
        P(None, "head"),
        P(None, "head"),
        P(None, "head"),
        P("dp", "head"),
        P("dp", "head"),
        P("dp", "head"),
        P("dp", None),
    )
    return jax.shard_map(
        partial(on_device, grid=Grid(mesh.shape["dp"])),
        mesh=mesh,
        in_specs=placed,
        out_specs=(P("dp", None), P("dp", None), P("dp"), P("dp")) + (P("dp", "head"),) * 8,
        check_vma=False,
    )
```

time: 3200 us -> 772 us (0.24)
  waiting for transfers between devices: 2530 us -> 416 us
  matrix products: 306 us -> 102 us
  blocking collectives: 83.4 us -> 0 us
  other arithmetic: 101 us -> 33.1 us
  starting transfers between devices: 0.77 us -> 55.3 us
    reduce_scatter x8 -> x7, waiting for transfers between devices: 2110 us -> 214 us  [the longest x2 132 us: walk_sum(): lax.psum_scatter(g.astype(bf16), 'dp', scatter_dimension=0, tiled=True, a...]
    all_gather x3 -> x5, waiting for transfers between devices: 385 us -> 91.6 us  [the longest x3 87.1 us: gather_rows(): lax.all_gather(w, 'dp', axis=0, tiled=True, axis_index_groups=grid.rows)]
    dot_general x120 -> x21, matrix products: 306 us -> 102 us  [the longest x8 41.6 us: nn(): return jnp.dot(a.astype(bf16), b.astype(bf16), preferred_element_type=f32)]
    unnamed x1 -> x0, blocking collectives: 83.4 us -> none
    ppermute x0 -> x19, waiting for transfers between devices: none -> 71.8 us  [the longest x9 66.3 us: spread_columns(): piece = lax.ppermute(piece, 'dp', pairs)]
    unnamed x83 -> x169, local copies, waits for them, and re-layouts: 20.4 us -> 77.5 us
    all_to_all x0 -> x4, waiting for transfers between devices: none -> 39.1 us  [the longest x3 39.1 us: scatter_rows(): lax.all_to_all(g, 'dp', 0, 1, tiled=True, axis_index_groups=grid.cols)]
    ppermute x0 -> x19, starting transfers between devices: none -> 37.2 us  [the longest x9 35.9 us: spread_columns(): piece = lax.ppermute(piece, 'dp', pairs)]
  transfers between devices with their start and end apart: 14 -> 35, of which waited for: 13 -> 19; matrix products, arithmetic and copies ran while one was open for 3% -> 26% of each run, Pallas kernels for 0% -> 1%
where the time goes in v1:
time: 772 us; the launch traced here: 759 us
  waiting for transfers between devices  416 us (54%)
  local copies, waits for them, and re-layouts  121 us (16%)
  matrix products  102 us (13%)
  starting transfers between devices  55.3 us (7%)
  other arithmetic  33.1 us (4%)
  Pallas kernels  15.7 us (2%)
  between operations  15.3 us (2%)
    reduce_scatter x2, waiting for transfers between devices, walk_sum(): lax.psum_scatter(g.astype(bf16), 'dp', scatter_dimension=0, tiled=True, a...  132 us
    all_gather x3, waiting for transfers between devices, gather_rows(): lax.all_gather(w, 'dp', axis=0, tiled=True, axis_index_groups=grid.rows)  87.1 us
    unnamed x169, local copies, waits for them, and re-layouts  77.5 us
    ppermute x9, waiting for transfers between devices, spread_columns(): piece = lax.ppermute(piece, 'dp', pairs)  66.3 us
    reduce_scatter x2, waiting for transfers between devices, scatter_tokens(): lax.psum_scatter(mine, 'dp', scatter_dimension=0, tiled=True, axis_index_...  54.4 us
    dot_general x8, matrix products, nn(): return jnp.dot(a.astype(bf16), b.astype(bf16), preferred_element_type=f32)  41.6 us
    all_to_all x3, waiting for transfers between devices, scatter_rows(): lax.all_to_all(g, 'dp', 0, 1, tiled=True, axis_index_groups=grid.cols)  39.1 us
    ppermute x9, starting transfers between devices, spread_columns(): piece = lax.ppermute(piece, 'dp', pairs)  35.9 us
  transfers between devices with their start and end apart: 35, of which 19 were waited for; matrix products, arithmetic and copies ran while one was open for 26% of the time, Pallas kernels for 1%

profile of v1, /device:TPU:0, one launch (start us, length us, event | category | flops | bytes accessed | tf_op | source)
XLA Modules:
  0.0 758.8 jit_solution(12829213524078213233)
XLA Ops:
  10.4 4.7 multiply_convert_fusion.10
  15.1 2.4 multiply_convert_fusion.9
  17.6 2.5 multiply_convert_fusion.8
  21.2 6.4 slot_forward.1
  27.5 5.0 fusion.15
  32.5 2.4 constant_dynamic-slice_fusion.10
  48.9 2.1 copy-done.15
  64.3 2.6 collective-permute-start.8
  66.9 2.6 collective-permute-start.9
  70.6 15.5 %collective-permute-done.8 = bf16[128,704]{1,0:T(8,128)(2,1)} collective-permute-done((bf16[128,704]{1,0:T(8,128)(2,1)}, bf16[128,704]{1,0:T(8,128)(2,1)}, u32[]{:S(2)}, u32[]{:S(2)}) %collective-permute-start.8) | collective-permute-done | bytes 180256 | tf_op jit(solution)/shard_map/ppermute | solution.py:466
  87.0 2.4 collective-permute-done.9
  90.4 5.9 collective-permute-done.10
  99.7 13.7 %collective-permute-start.5 = (bf16[128,704]{1,0:T(8,128)(2,1)S(1)}, bf16[128,704]{1,0:T(8,128)(2,1)S(1)}, u32[]{:S(2)}, u32[]{:S(2)}) collective-permute-start(bf16[128,704]{1,0:T(8,128)(2,1)S(1)} %get-tuple-element.82), channel_id=1, source_target_pairs={{0,8},{2,10},{4,12},{6,14},{8,0},{10,2},{12,4},{14,6},{16,24},{18,... | collective-permute-start | bytes 540680 | tf_op jit(solution)/shard_map/ppermute | solution.py:466
  113.5 2.3 collective-permute-start.7
  116.9 4.0 collective-permute-done.5
  120.9 17.5 %collective-permute-done.6 = bf16[128,704]{1,0:T(8,128)(2,1)S(1)} collective-permute-done((bf16[128,704]{1,0:T(8,128)(2,1)S(1)}, bf16[128,704]{1,0:T(8,128)(2,1)S(1)}, u32[]{:S(2)}, u32[]{:S(2)}) %collective-permute-start.6) | collective-permute-done | bytes 180256 | tf_op jit(solution)/shard_map/ppermute | solution.py:466
  140.9 12.2 %collective-permute-start.2 = (bf16[128,704]{1,0:T(8,128)(2,1)S(1)}, bf16[128,704]{1,0:T(8,128)(2,1)S(1)}, u32[]{:S(2)}, u32[]{:S(2)}) collective-permute-start(bf16[128,704]{1,0:T(8,128)(2,1)S(1)} %get-tuple-element.79), channel_id=1, source_target_pairs={{0,8},{2,10},{4,12},{6,14},{8,0},{10,2},{12,4},{14,6},{16,24},{18,... | collective-permute-start | bytes 540680 | tf_op jit(solution)/shard_map/ppermute | solution.py:466
  153.1 2.4 collective-permute-start.4
  156.7 8.6 %collective-permute-done.2 = bf16[128,704]{1,0:T(8,128)(2,1)S(1)} collective-permute-done((bf16[128,704]{1,0:T(8,128)(2,1)S(1)}, bf16[128,704]{1,0:T(8,128)(2,1)S(1)}, u32[]{:S(2)}, u32[]{:S(2)}) %collective-permute-start.2) | collective-permute-done | bytes 180256 | tf_op jit(solution)/shard_map/ppermute | solution.py:466
  165.3 12.2 %collective-permute-done.3 = bf16[128,704]{1,0:T(8,128)(2,1)S(1)} collective-permute-done((bf16[128,704]{1,0:T(8,128)(2,1)S(1)}, bf16[128,704]{1,0:T(8,128)(2,1)S(1)}, u32[]{:S(2)}, u32[]{:S(2)}) %collective-permute-start.3) | collective-permute-done | bytes 180256 | tf_op jit(solution)/shard_map/ppermute | solution.py:466
  179.1 4.4 all-gather.6.cloned.1.call-done
  183.6 3.3 constant_dynamic-update-slice_fusion.51
  188.4 3.2 constant_dynamic-update-slice_fusion.50
  191.6 30.0 %all-gather.12.cloned.1.call-done = bf16[2048,704]{1,0:T(8,128)(2,1)} async-done(((bf16[512,704]{1,0:T(8,128)(2,1)}), bf16[2048,704]{1,0:T(8,128)(2,1)}) %all-gather.12.cloned.1.call-update) | async-done | bytes 2883600 | tf_op jit(solution)/shard_map/all_gather | solution.py:472
  221.6 7.9 %fusion.18 = f32[1024,704]{0,1:T(8,128)} fusion(bf16[1024,2048]{1,0:T(8,128)(2,1)} %constant_dynamic-update-slice_fusion.50, bf16[2048,704]{1,0:T(8,128)(2,1)} %all-gather.12.cloned.1.call-done), kind=kOutput, calls=%fused_computation.200 | convolution fusion | flops 2952790016 | bytes 9961472 | tf_op jit(solution)/shard_map/dot_general | solution.py:19
  229.5 3.5 constant_dynamic-update-slice_fusion.16
  233.0 26.8 %all-gather.10.cloned.1.call-done = bf16[2048,704]{1,0:T(8,128)(2,1)} async-done(((bf16[512,704]{1,0:T(8,128)(2,1)}), bf16[2048,704]{1,0:T(8,128)(2,1)}) %all-gather.10.cloned.1.call-update) | async-done | bytes 2883600 | tf_op jit(solution)/shard_map/all_gather | solution.py:472
  259.8 7.9 %fusion.16 = f32[1024,704]{0,1:T(8,128)} fusion(bf16[1024,2048]{1,0:T(8,128)(2,1)} %constant_dynamic-update-slice_fusion.16, bf16[2048,704]{1,0:T(8,128)(2,1)} %all-gather.10.cloned.1.call-done), kind=kOutput, calls=%fused_computation.198 | convolution fusion | flops 2952790016 | bytes 9961472 | tf_op jit(solution)/shard_map/dot_general | solution.py:19
  267.7 30.3 %all-gather.8.cloned.1.call-done = bf16[2048,704]{1,0:T(8,128)(2,1)} async-done(((bf16[512,704]{1,0:T(8,128)(2,1)}), bf16[2048,704]{1,0:T(8,128)(2,1)}) %all-gather.8.cloned.1.call-update) | async-done | bytes 2883600 | tf_op jit(solution)/shard_map/all_gather | solution.py:472
  298.0 10.4 %multiply_convert_fusion.1 = (bf16[1024,704]{0,1:T(8,128)(2,1)S(1)}, bf16[1024,704]{0,1:T(8,128)(2,1)S(1)}, bf16[1024,704]{0,1:T(8,128)(2,1)}) fusion(f32[1024,704]{0,1:T(8,128)} %fusion.18, f32[1024,704]{0,1:T(8,128)} %fusion.16, bf16[1024,2048]{1,0:T(8,128)(2,1)} %constant_dynamic-update-slice_fusion.16, bf16[2048,704]{1,0:T(8,128)(2,1)} %all-gather.8.cloned.1.call-done), kind=kOutput, calls=%fused_computation.13 | convolution fusion | flops 2963603456 | bytes 17170432 | tf_op jit(solution)/shard_map/dot_general | solution.py:19
  308.4 3.7 fusion.19
  312.2 3.6 convolution_add_fusion
  316.2 4.1 collective-permute-done.14
  320.3 2.1 fusion
  322.5 7.4 convolution_convert_fusion.4
  330.0 7.5 convolution_convert_fusion.3
  337.7 7.4 convolution_convert_fusion.2
  345.2 5.9 fusion.17
  351.1 3.3 copy-done.4
  356.1 10.1 %reduce-scatter.10.cloned.1.call-done = bf16[128,2048]{1,0:T(8,128)(2,1)} async-done(((bf16[512,2048]{1,0:T(8,128)(2,1)}), bf16[128,2048]{1,0:T(8,128)(2,1)}) %reduce-scatter.10.cloned.1.call-update) | async-done | bytes 524304 | tf_op jit(solution)/shard_map/reduce_scatter | solution.py:492
  372.1 3.7 fusion.1
  375.9 1.9 constant_dynamic-update-slice_fusion.100
  390.9 3.4 convolution_convert_fusion.1
  404.7 4.6 convolution_convert_fusion.5.do_ref
  409.3 9.3 %slot_backward.1 = (f32[256,1024]{1,0:T(8,128)}, f32[256,1024]{1,0:T(8,128)}, f32[256,1024]{1,0:T(8,128)}, f32[256,128]{1,0:T(8,128)}) custom-call(s32[1,3]{1,0:T(1,128)} %starts_ref.3, bf16[256,1024]{1,0:T(8,128)(2,1)} %get-tuple-element.88.q_ref, bf16[256,1024]{1,0:T(8,128)(2,1)} %get-tuple-element.90.k_ref, bf16[256,1024]{1,0:T(8,128)(2,1)} %get-tuple-element.92.v_ref, ...), custom_call_target="tpu_custom_call" | custom-call | flops 12000000000 | bytes 8000000 | tf_op jit(solution)/shard_map/slot_backward/pallas_call | solution.py:369
  421.4 2.5 multiply_convert_fusion.4
  423.9 9.9 %convolution_convert_fusion = bf16[2048,3200]{1,0:T(8,128)(2,1)} fusion(bf16[256,2048]{1,0:T(8,128)(2,1)} %constant_dynamic-update-slice_fusion.68, bf16[256,128]{1,0:T(8,128)(2,1)S(1)} %multiply_convert_fusion.11, bf16[256,1024]{1,0:T(8,128)(2,1)S(1)} %get-tuple-element.96, bf16[256,1024]{1,0:T(8,128)(2,1)S(1)} %get-tuple-element.97, ...), kind=kOutput, calls=%fused_computation | convolution fusion | flops 3368550400 | bytes 15794176 | tf_op jit(solution)/shard_map/dot_general | solution.py:29
  434.5 2.1 copy_bitcast_fusion.2
  436.6 3.6 all-to-all-start.1
  440.2 2.1 copy_bitcast_fusion.1
  442.3 27.2 %reduce-scatter.20.cloned.1.call-done = bf16[512,704]{0,1:T(8,128)(2,1)} async-done(((bf16[2048,704]{0,1:T(8,128)(2,1)}), bf16[512,704]{0,1:T(8,128)(2,1)}) %reduce-scatter.20.cloned.1.call-update) | async-done | bytes 720912 | tf_op jit(solution)/shard_map/reduce_scatter | solution.py:476
  469.6 2.1 copy_bitcast_fusion
  471.7 44.3 %reduce-scatter.8.cloned.1.call-done = bf16[128,2048]{1,0:T(8,128)(2,1)} async-done(((bf16[512,2048]{1,0:T(8,128)(2,1)}), bf16[128,2048]{1,0:T(8,128)(2,1)}) %reduce-scatter.8.cloned.1.call-update) | async-done | bytes 524304 | tf_op jit(solution)/shard_map/reduce_scatter | solution.py:492
  524.2 3.7 fusion.20
  535.5 4.2 all-to-all-start.2
  546.0 21.4 %all-to-all-done.2 = bf16[4,128,704]{1,2,0:T(8,128)(2,1)} async-done(((bf16[4,128,704]{1,2,0:T(8,128)(2,1)}), bf16[4,128,704]{1,2,0:T(8,128)(2,1)}, u32[]{:S(2)}, u32[]{:S(2)}) %all-to-all-start.2) | async-done | bytes 720928 | tf_op jit(solution)/shard_map/all_to_all | solution.py:479
  567.5 4.2 all-to-all-start.3
  571.9 3.3 constant_dynamic-update-slice_fusion.99
  576.4 2.2 constant_dynamic-update-slice_fusion.103
  581.2 17.7 %all-to-all-done.3 = bf16[4,128,704]{1,2,0:T(8,128)(2,1)} async-done(((bf16[4,128,704]{1,2,0:T(8,128)(2,1)}), bf16[4,128,704]{1,2,0:T(8,128)(2,1)}, u32[]{:S(2)}, u32[]{:S(2)}) %all-to-all-start.3) | async-done | bytes 720928 | tf_op jit(solution)/shard_map/all_to_all | solution.py:479
  598.9 4.6 all-to-all-start
  612.0 2.4 constant_dynamic-update-slice_fusion.98
  616.2 131.9 %reduce-scatter.12.cloned.1.call-done = bf16[128,3200]{1,0:T(8,128)(2,1)} async-done(((bf16[2048,3200]{1,0:T(8,128)(2,1)}), bf16[128,3200]{1,0:T(8,128)(2,1)}) %reduce-scatter.12.cloned.1.call-update) | async-done | bytes 819216 | tf_op jit(solution)/shard_map/reduce_scatter | solution.py:563
  748.1 2.3 fusion.14
  (281 shorter events, 118.7 us)
Async XLA Ops:
  7.2 12.9 %copy-start = (bf16[2048,128]{1,0:T(8,128)(2,1)S(1)}, bf16[2048,128]{1,0:T(8,128)(2,1)}, u32[]{:S(2)}) copy-start(bf16[2048,128]{1,0:T(8,128)(2,1)} %param.20) | copy-start | bytes 1572868
  7.2 171.8 %all-gather.14.cloned.1.call-start = ((), (), s32[]{:S(2)}) async-start(), calls=%async_computation.16 | async-start | bytes 2621440 | tf_op jit(solution)/shard_map/all_gather | solution.py:484
  8.8 6.3 copy-start.29
  10.4 4.8 copy-start.8
  15.1 2.5 copy-start.10
  32.5 16.1 %copy-start.3 = (bf16[256,2048]{1,0:T(8,128)(2,1)S(1)}, bf16[256,2048]{1,0:T(8,128)(2,1)}, u32[]{:S(2)}) copy-start(bf16[256,2048]{1,0:T(8,128)(2,1)} %param.13) | copy-start | bytes 3145732
  34.9 14.0 %collective-permute-start = (f32[128,2048]{1,0:T(8,128)}, f32[128,2048]{1,0:T(8,128)}, u32[]{:S(2)}, u32[]{:S(2)}) collective-permute-start(f32[128,2048]{1,0:T(8,128)} %constant_dynamic-slice_fusion.10), channel_id=1, source_target_pairs={{0,1},{1,0},{2,3},{3,2},{4,5},{5,4},{6,7},{7,6},{8,9},{9,8},{10,11... | collective-permute-start | bytes 3145736 | tf_op jit(solution)/shard_map/ppermute | solution.py:439
  48.5 135.0 %all-gather.6.cloned.1.call-start = ((), (), s32[]{:S(2)}) async-start(), calls=%async_computation.11 | async-start | bytes 2621440 | tf_op jit(solution)/shard_map/all_gather | solution.py:484
  48.6 2.4 copy-start.15
  48.8 4.3 copy-start.1
  48.9 4.1 copy-start.27
  48.9 14.4 %copy-start.24 = (bf16[128,2816]{1,0:T(8,128)(2,1)S(1)}, bf16[128,2816]{1,0:T(8,128)(2,1)}, u32[]{:S(2)}) copy-start(bf16[128,2816]{1,0:T(8,128)(2,1)} %param.24) | copy-start | bytes 2162692
  52.9 16.5 %copy-start.31 = (f32[128]{0:T(128)}, f32[128]{0:T(128)S(1)}, u32[]{:S(2)}) copy-start(f32[128]{0:T(128)S(1)} %get-tuple-element.87) | copy-start | bytes 1540
  63.1 158.5 %all-gather.12.cloned.1.call-start = ((), (), s32[]{:S(2)}) async-start(), calls=%async_computation.14 | async-start | bytes 3932160 | tf_op jit(solution)/shard_map/all_gather | solution.py:472
  64.3 21.8 %collective-permute-start.8 = (bf16[128,704]{1,0:T(8,128)(2,1)}, bf16[128,704]{1,0:T(8,128)(2,1)}, u32[]{:S(2)}, u32[]{:S(2)}) collective-permute-start(bf16[128,704]{1,0:T(8,128)(2,1)} %get-tuple-element.76), channel_id=1, source_target_pairs={{0,8},{2,10},{4,12},{6,14},{8,0},{10,2},{12,4},{14,6},{16,24},{18,... | collective-permute-start | bytes 540680 | tf_op jit(solution)/shard_map/ppermute | solution.py:466
  66.9 22.6 %collective-permute-start.9 = (bf16[128,704]{1,0:T(8,128)(2,1)}, bf16[128,704]{1,0:T(8,128)(2,1)}, u32[]{:S(2)}, u32[]{:S(2)}) collective-permute-start(bf16[128,704]{1,0:T(8,128)(2,1)} %get-tuple-element.77), channel_id=1, source_target_pairs={{0,16},{2,18},{4,20},{6,22},{8,24},{10,26},{12,28},{14,30},{16,0},... | collective-permute-start | bytes 540680 | tf_op jit(solution)/shard_map/ppermute | solution.py:466
  69.4 26.9 %collective-permute-start.10 = (bf16[128,704]{1,0:T(8,128)(2,1)}, bf16[128,704]{1,0:T(8,128)(2,1)}, u32[]{:S(2)}, u32[]{:S(2)}) collective-permute-start(bf16[128,704]{1,0:T(8,128)(2,1)} %get-tuple-element.75), channel_id=1, source_target_pairs={{0,24},{2,26},{4,28},{6,30},{8,16},{10,18},{12,20},{14,22},{16,8},... | collective-permute-start | bytes 540680 | tf_op jit(solution)/shard_map/ppermute | solution.py:466
  98.2 161.6 %all-gather.10.cloned.1.call-start = ((), (), s32[]{:S(2)}) async-start(), calls=%async_computation.13 | async-start | bytes 3932160 | tf_op jit(solution)/shard_map/all_gather | solution.py:472
  99.7 21.3 %collective-permute-start.5 = (bf16[128,704]{1,0:T(8,128)(2,1)S(1)}, bf16[128,704]{1,0:T(8,128)(2,1)S(1)}, u32[]{:S(2)}, u32[]{:S(2)}) collective-permute-start(bf16[128,704]{1,0:T(8,128)(2,1)S(1)} %get-tuple-element.82), channel_id=1, source_target_pairs={{0,8},{2,10},{4,12},{6,14},{8,0},{10,2},{12,4},{14,6},{16,24},{18,... | collective-permute-start | bytes 540680 | tf_op jit(solution)/shard_map/ppermute | solution.py:466
  113.3 25.2 %collective-permute-start.6 = (bf16[128,704]{1,0:T(8,128)(2,1)S(1)}, bf16[128,704]{1,0:T(8,128)(2,1)S(1)}, u32[]{:S(2)}, u32[]{:S(2)}) collective-permute-start(bf16[128,704]{1,0:T(8,128)(2,1)S(1)} %get-tuple-element.83), channel_id=1, source_target_pairs={{0,16},{2,18},{4,20},{6,22},{8,24},{10,26},{12,28},{14,30},{16,0},... | collective-permute-start | bytes 540680 | tf_op jit(solution)/shard_map/ppermute | solution.py:466
  113.5 25.0 %collective-permute-start.7 = (bf16[128,704]{1,0:T(8,128)(2,1)S(1)}, bf16[128,704]{1,0:T(8,128)(2,1)S(1)}, u32[]{:S(2)}, u32[]{:S(2)}) collective-permute-start(bf16[128,704]{1,0:T(8,128)(2,1)S(1)} %get-tuple-element.81), channel_id=1, source_target_pairs={{0,24},{2,26},{4,28},{6,30},{8,16},{10,18},{12,20},{14,22},{16,8},... | collective-permute-start | bytes 540680 | tf_op jit(solution)/shard_map/ppermute | solution.py:466
  139.5 158.5 %all-gather.8.cloned.1.call-start = ((), (), s32[]{:S(2)}) async-start(), calls=%async_computation.12 | async-start | bytes 3932160 | tf_op jit(solution)/shard_map/all_gather | solution.py:472
  140.9 24.4 %collective-permute-start.2 = (bf16[128,704]{1,0:T(8,128)(2,1)S(1)}, bf16[128,704]{1,0:T(8,128)(2,1)S(1)}, u32[]{:S(2)}, u32[]{:S(2)}) collective-permute-start(bf16[128,704]{1,0:T(8,128)(2,1)S(1)} %get-tuple-element.79), channel_id=1, source_target_pairs={{0,8},{2,10},{4,12},{6,14},{8,0},{10,2},{12,4},{14,6},{16,24},{18,... | collective-permute-start | bytes 540680 | tf_op jit(solution)/shard_map/ppermute | solution.py:466
  153.1 24.4 %collective-permute-start.3 = (bf16[128,704]{1,0:T(8,128)(2,1)S(1)}, bf16[128,704]{1,0:T(8,128)(2,1)S(1)}, u32[]{:S(2)}, u32[]{:S(2)}) collective-permute-start(bf16[128,704]{1,0:T(8,128)(2,1)S(1)} %get-tuple-element.80), channel_id=1, source_target_pairs={{0,16},{2,18},{4,20},{6,22},{8,24},{10,26},{12,28},{14,30},{16,0},... | collective-permute-start | bytes 540680 | tf_op jit(solution)/shard_map/ppermute | solution.py:466
  153.1 24.5 %collective-permute-start.4 = (bf16[128,704]{1,0:T(8,128)(2,1)S(1)}, bf16[128,704]{1,0:T(8,128)(2,1)S(1)}, u32[]{:S(2)}, u32[]{:S(2)}) collective-permute-start(bf16[128,704]{1,0:T(8,128)(2,1)S(1)} %get-tuple-element.78), channel_id=1, source_target_pairs={{0,24},{2,26},{4,28},{6,30},{8,16},{10,18},{12,20},{14,22},{16,8},... | collective-permute-start | bytes 540680 | tf_op jit(solution)/shard_map/ppermute | solution.py:466
  178.5 187.7 %reduce-scatter.10.cloned.1.call-start = ((), (), s32[]{:S(2)}) async-start(), calls=%async_computation.17 | async-start | bytes 2621440 | tf_op jit(solution)/shard_map/reduce_scatter | solution.py:492
  179.0 9.3 %collective-permute-start.13 = (bf16[512,2048]{1,0:T(8,128)(2,1)}, bf16[512,2048]{1,0:T(8,128)(2,1)}, u32[]{:S(2)}, u32[]{:S(2)}) collective-permute-start(bf16[512,2048]{1,0:T(8,128)(2,1)} %all-gather.14.cloned.1.call-done), channel_id=1, source_target_pairs={{0,1},{1,0},{2,3},{3,2},{4,5},{5,4},{6,7},{7,6},{8,9},{9,8},{10,11... | collective-permute-start | bytes 6291464 | tf_op jit(solution)/shard_map/ppermute | solution.py:439
  183.6 3.4 copy-start.19
  183.6 46.0 %collective-permute-start.1 = (bf16[512,2048]{1,0:T(8,128)(2,1)}, bf16[512,2048]{1,0:T(8,128)(2,1)}, u32[]{:S(2)}, u32[]{:S(2)}) collective-permute-start(bf16[512,2048]{1,0:T(8,128)(2,1)} %all-gather.6.cloned.1.call-done), channel_id=1, source_target_pairs={{0,1},{1,0},{2,3},{3,2},{4,5},{5,4},{6,7},{7,6},{8,9},{9,8},{10,11... | collective-permute-start | bytes 6291464 | tf_op jit(solution)/shard_map/ppermute | solution.py:439
  298.0 10.5 %copy-start.34 = (bf16[2048,704]{1,0:T(8,128)(2,1)S(1)}, bf16[2048,704]{1,0:T(8,128)(2,1)}, u32[]{:S(2)}) copy-start(bf16[2048,704]{1,0:T(8,128)(2,1)} %all-gather.10.cloned.1.call-done) | copy-start | bytes 8650756
  308.4 3.8 copy-start.37
  308.4 3.8 copy-start.36
  308.4 3.8 copy-start.35
  316.1 4.2 collective-permute-start.14
  322.5 112.1 %reduce-scatter.16.cloned.1.call-start = ((), (), s32[]{:S(2)}) async-start(), calls=%async_computation.20 | async-start | bytes 3604480 | tf_op jit(solution)/shard_map/reduce_scatter | solution.py:476
  329.9 110.3 %reduce-scatter.18.cloned.1.call-start = ((), (), s32[]{:S(2)}) async-start(), calls=%async_computation.21 | async-start | bytes 3604480 | tf_op jit(solution)/shard_map/reduce_scatter | solution.py:476
  337.5 132.1 %reduce-scatter.20.cloned.1.call-start = ((), (), s32[]{:S(2)}) async-start(), calls=%async_computation.22 | async-start | bytes 3604480 | tf_op jit(solution)/shard_map/reduce_scatter | solution.py:476
  345.1 170.8 %reduce-scatter.8.cloned.1.call-start = ((), (), s32[]{:S(2)}) async-start(), calls=%async_computation.15 | async-start | bytes 2621440 | tf_op jit(solution)/shard_map/reduce_scatter | solution.py:492
  351.0 3.3 copy-start.4
  354.4 13.4 %copy-start.32 = (f32[128]{0:T(128)S(1)}, f32[128]{0:T(128)}, u32[]{:S(2)}) copy-start(f32[128]{0:T(128)} %copy-done.31) | copy-start | bytes 1540
  356.0 15.1 %collective-permute-start.11 = (bf16[512,2048]{1,0:T(8,128)(2,1)}, bf16[512,2048]{1,0:T(8,128)(2,1)}, u32[]{:S(2)}, u32[]{:S(2)}) collective-permute-start(bf16[512,2048]{1,0:T(8,128)(2,1)} %slice.597), channel_id=1, source_target_pairs={{0,1},{1,0},{2,3},{3,2},{4,5},{5,4},{6,7},{7,6},{8,9},{9,8},{10,11... | collective-permute-start | bytes 6291464 | tf_op jit(solution)/shard_map/ppermute | solution.py:439
  367.6 4.5 copy-start.5
  371.1 4.8 collective-permute-start.15
  375.8 15.1 %copy-start.26 = (bf16[256,1024]{1,0:T(8,128)(2,1)S(1)}, bf16[256,1024]{1,0:T(8,128)(2,1)}, u32[]{:S(2)}) copy-start(bf16[256,1024]{1,0:T(8,128)(2,1)} %get-tuple-element.21) | copy-start | bytes 1572868
  375.9 238.5 %reduce-scatter.14.cloned.1.call-start = ((), (), s32[]{:S(2)}) async-start(), calls=%async_computation.19 | async-start | bytes 4456448 | tf_op jit(solution)/shard_map/reduce_scatter | solution.py:563
  394.3 353.8 %reduce-scatter.12.cloned.1.call-start = ((), (), s32[]{:S(2)}) async-start(), calls=%async_computation.18 | async-start | bytes 13926400 | tf_op jit(solution)/shard_map/reduce_scatter | solution.py:563
  409.3 10.4 %copy-start.23 = (f32[256,1024]{1,0:T(8,128)S(1)}, f32[256,1024]{1,0:T(8,128)}, u32[]{:S(2)}) copy-start(f32[256,1024]{1,0:T(8,128)} %get-tuple-element.89) | copy-start | bytes 3145732
  418.6 2.8 copy-start.21
  418.6 2.8 copy-start.22
  421.3 2.5 copy-start.16
  436.6 98.9 %all-to-all-start.1 = ((bf16[4,128,704]{1,2,0:T(8,128)(2,1)}), bf16[4,128,704]{1,2,0:T(8,128)(2,1)S(1)}, u32[]{:S(2)}, u32[]{:S(2)}) async-start(bf16[4,128,704]{1,2,0:T(8,128)(2,1)} %copy_bitcast_fusion.2), calls=%async_computation.6 | async-start | bytes 1441792 | tf_op jit(solution)/shard_map/all_to_all | solution.py:479
  515.9 8.3 %copy-start.17 = (bf16[256,1024]{1,0:T(8,128)(2,1)S(1)}, bf16[256,1024]{1,0:T(8,128)(2,1)}, u32[]{:S(2)}) copy-start(bf16[256,1024]{1,0:T(8,128)(2,1)} %copy-done.16) | copy-start | bytes 1572868
  517.1 17.8 %copy-start.6 = (f32[128,2048]{1,0:T(8,128)}, f32[128,2048]{1,0:T(8,128)S(1)}, u32[]{:S(2)}) copy-start(f32[128,2048]{1,0:T(8,128)S(1)} %convert_element_type.128) | copy-start | bytes 3145732
  524.2 3.7 copy-start.9
  527.9 2.3 copy-start.11
  533.2 11.0 %copy-start.28 = (f32[2048]{0:T(1024)S(1)}, f32[2048]{0:T(1024)}, u32[]{:S(2)}) copy-start(f32[2048]{0:T(1024)} %param.15) | copy-start | bytes 24580
  534.3 9.9 %collective-permute-start.16 = (f32[128,2048]{1,0:T(8,128)}, f32[128,2048]{1,0:T(8,128)S(1)}, u32[]{:S(2)}, u32[]{:S(2)}) collective-permute-start(f32[128,2048]{1,0:T(8,128)} %constant_dynamic-slice_fusion), channel_id=1, source_target_pairs={{0,1},{1,0},{2,3},{3,2},{4,5},{5,4},{6,7},{7,6},{8,9},{9,8},{10,11... | collective-permute-start | bytes 3145736 | tf_op jit(solution)/shard_map/ppermute | solution.py:439
  535.5 31.9 %all-to-all-start.2 = ((bf16[4,128,704]{1,2,0:T(8,128)(2,1)}), bf16[4,128,704]{1,2,0:T(8,128)(2,1)}, u32[]{:S(2)}, u32[]{:S(2)}) async-start(bf16[4,128,704]{1,2,0:T(8,128)(2,1)} %copy_bitcast_fusion.1), calls=%async_computation.8 | async-start | bytes 1441792 | tf_op jit(solution)/shard_map/all_to_all | solution.py:479
  567.5 31.4 %all-to-all-start.3 = ((bf16[4,128,704]{1,2,0:T(8,128)(2,1)}), bf16[4,128,704]{1,2,0:T(8,128)(2,1)}, u32[]{:S(2)}, u32[]{:S(2)}) async-start(bf16[4,128,704]{1,2,0:T(8,128)(2,1)} %copy_bitcast_fusion), calls=%async_computation.10 | async-start | bytes 1441792 | tf_op jit(solution)/shard_map/all_to_all | solution.py:479
  575.2 3.4 copy-start.18
  575.2 36.8 %collective-permute-start.17 = (f32[128,2048]{1,0:T(8,128)}, f32[128,2048]{1,0:T(8,128)}, u32[]{:S(2)}, u32[]{:S(2)}) collective-permute-start(f32[128,2048]{1,0:T(8,128)} %get-tuple-element.59), channel_id=1, source_target_pairs={{0,1},{1,0},{2,3},{3,2},{4,5},{5,4},{6,7},{7,6},{8,9},{9,8},{10,11... | collective-permute-start | bytes 3145736 | tf_op jit(solution)/shard_map/ppermute | solution.py:439
  578.6 24.8 %collective-permute-start.12 = (bf16[128,2048]{1,0:T(8,128)(2,1)S(1)}, bf16[128,2048]{1,0:T(8,128)(2,1)S(1)}, u32[]{:S(2)}, u32[]{:S(2)}) collective-permute-start(bf16[128,2048]{1,0:T(8,128)(2,1)S(1)} %get-tuple-element.66), channel_id=1, source_target_pairs={{0,1},{1,0},{2,3},{3,2},{4,5},{5,4},{6,7},{7,6},{8,9},{9,8},{10,11... | collective-permute-start | bytes 1572872 | tf_op jit(solution)/shard_map/ppermute | solution.py:439
  579.0 1.6 collective-permute-start.18
  598.9 12.6 %all-to-all-start = ((f32[16,2,128]{2,1,0:T(2,128)}), f32[16,2,128]{2,1,0:T(2,128)S(1)}, u32[]{:S(2)}, u32[]{:S(2)}) async-start(f32[16,2,128]{2,1,0:T(2,128)} %add_bitcast_fusion), calls=%async_computation.2 | async-start | bytes 32768 | tf_op jit(solution)/shard_map/all_to_all | solution.py:589
  (9 other events, 8.9 us)
Sparse Core Ops, SparseCore 0:
  48.7 64.9 all-gather.13
  115.8 67.7 all-gather.5
  185.7 35.8 all-gather.11
  223.6 36.1 all-gather.9
  261.8 36.1 all-gather.7
  322.6 43.6 reduce-scatter.9
  368.5 31.5 reduce-scatter.15
  402.4 32.3 reduce-scatter.17
  437.2 32.3 reduce-scatter.19
  472.3 43.5 reduce-scatter.7
  518.2 88.0 reduce-scatter.13
  608.5 139.5 reduce-scatter.11

commit v2 on v1

--- a/solution.py
+++ b/solution.py
@@ -394,7 +394,7 @@
 
 
 def norm_back(values, scale, gain, upstream):
-    gain_grad = jnp.sum(upstream * values * scale, axis=0)
+    gain_grad = jnp.sum(upstream * values * scale, axis=0, keepdims=True)
     weighted = upstream * gain
     input_grad = scale * weighted - values * (scale * scale * scale) * jnp.mean(
         weighted * values, axis=-1, keepdims=True
@@ -411,20 +411,17 @@
     def __init__(self, dp):
         self.dp = dp
         self.outer = dp // INNER
-        self.rows = [[o * INNER + i for i in LAP] for o in range(self.outer)]
+        self.laps = [[o * INNER + i for i in LAP] for o in range(self.outer)]
+        self.rows = [[o * INNER + i for i in range(INNER)] for o in range(self.outer)]
         self.cols = [[o * INNER + i for o in range(self.outer)] for i in range(INNER)]
         self.gathered = [o * INNER + i for i in LAP for o in range(self.outer)]
-        walk = [0]
-        for n, i in enumerate((1, 3, 2)):
-            column = [o * INNER + i for o in range(self.outer)]
-            walk += column if n % 2 == 0 else column[::-1]
-        walk += [o * INNER for o in range(self.outer - 1, 0, -1)]
-        self.walk = walk
+        self.natural = inverse(self.gathered)
+        self.up = [(d, d + INNER) for d in range(dp - INNER)]
+        self.down = [(d + INNER, d) for d in range(dp - INNER)]
 
 
 def reorder(x, order):
-    n = len(order)
-    size = x.shape[-1] // n
+    size = x.shape[-1] // len(order)
     return jnp.concatenate([x[..., b * size : (b + 1) * size] for b in order], axis=-1)
 
 
@@ -451,48 +448,150 @@
     return lax.dynamic_update_slice_in_dim(out, other, (1 - core) * size, 0)
 
 
-def spread_columns(w, grid, place):
-    rows, size = w.shape[0], w.shape[1] // grid.outer
-    if grid.outer > 4:
-        return lax.all_to_all(w, "dp", 1, 0, tiled=True, axis_index_groups=grid.cols)
-    out = jnp.zeros((grid.outer, rows, size), w.dtype)
-    for s in range(grid.outer):
-        mate = place ^ s
-        piece = lax.dynamic_slice_in_dim(w, mate * size, size, 1)
-        if s:
-            pairs = [
-                (o * INNER + i, (o ^ s) * INNER + i) for o in range(grid.outer) for i in range(INNER)
-            ]
-            piece = lax.ppermute(piece, "dp", pairs)
-        out = lax.dynamic_update_slice_in_dim(out, piece[None], mate, 0)
-    return out.reshape(grid.outer * rows, size)
-
-
-def gather_rows(w, grid):
-    return lax.all_gather(w, "dp", axis=0, tiled=True, axis_index_groups=grid.rows)
-
-
-def scatter_rows(g, grid):
-    g = lax.psum_scatter(
-        g, "dp", scatter_dimension=0, tiled=True, axis_index_groups=grid.rows
-    )
-    return lax.all_to_all(g, "dp", 0, 1, tiled=True, axis_index_groups=grid.cols)
-
-
-def gather_tokens(x, grid):
-    x = reorder(x, grid.gathered)
-    own = lax.all_gather(x, "dp", axis=0, tiled=True, axis_index_groups=grid.cols)
+def on_rows(kernel, name, core, halves, wholes, outs):
+    rows = halves[0].shape[0] // 2
+    specs = [pl.BlockSpec((rows, x.shape[1]), lambda i, c: (c[0], 0)) for x in halves]
+    specs += [pl.BlockSpec(x.shape, lambda i, c: (0, 0)) for x in wholes]
+    return pl.pallas_call(
+        kernel,
+        out_shape=outs,
+        grid_spec=pltpu.PrefetchScalarGridSpec(
+            num_scalar_prefetch=1,
+            grid=(1,),
+            in_specs=specs,
+            out_specs=[pl.BlockSpec(x.shape, lambda i, c: (0, 0)) for x in outs],
+        ),
+        name=name,
+    )(core.reshape(1), *halves, *wholes)
+
+
+def aligned(grid, width):
+    return (width // grid.dp) % 128 == 0
+
+
+def put_in_order(x, order, grid, inside):
+    return reorder(x, order) if aligned(grid, x.shape[1]) == inside else x
+
+
+def cotangent_rows(out_grad, core, grid):
+    rows, width = out_grad.shape
+
+    def kernel(core_ref, cot_ref, out_ref):
+        out_ref[...] = put_in_order(cot_ref[...], grid.gathered, grid, True)
+
+    outs = [jax.ShapeDtypeStruct((rows // 2, width), bf16)]
+    (x,) = on_rows(kernel, "cotangent_rows", core, [out_grad], [], outs)
+    return put_in_order(x, grid.gathered, grid, False)
+
+
+def second_norm(block_in, mine, other, gain, core, grid):
+    rows, width = mine.shape
+
+    def kernel(core_ref, in_ref, mine_ref, other_ref, gain_ref, hidden_ref, normed_ref):
+        hidden = in_ref[...].astype(f32) + (mine_ref[...] + other_ref[...])
+        hidden_ref[...] = hidden
+        normed = (hidden * rms_scale(hidden) * gain_ref[...]).astype(bf16)
+        normed_ref[...] = put_in_order(normed, grid.gathered, grid, True)
+
+    outs = [jax.ShapeDtypeStruct((rows, width), f32), jax.ShapeDtypeStruct((rows, width), bf16)]
+    hidden, normed = on_rows(
+        kernel, "second_norm", core, [block_in], [mine, other, gain[None]], outs
+    )
+    return hidden, put_in_order(normed, grid.gathered, grid, False)
+
+
+def second_norm_back(out_grad, hidden, gain, parts, core, grid):
+    rows, width = hidden.shape
+    parts = [put_in_order(x, grid.natural, grid, False) for x in parts]
+
+    def kernel(core_ref, cot_ref, hidden_ref, gain_ref, *refs):
+        upstream = sum(x[...].astype(f32) for x in refs[: len(parts)])
+        upstream = put_in_order(upstream, grid.natural, grid, True)
+        grad_ref, low_ref, gain_grad_ref = refs[len(parts) :]
+        hidden = hidden_ref[...]
+        gain_grad, grad = norm_back(hidden, rms_scale(hidden), gain_ref[...], upstream)
+        grad = grad + cot_ref[...].astype(f32)
+        grad_ref[...] = grad
+        low_ref[...] = grad.astype(bf16)
+        gain_grad_ref[...] = gain_grad
+
+    sds = jax.ShapeDtypeStruct
+    outs = [sds((rows, width), f32), sds((rows, width), bf16), sds((1, width), f32)]
+    return on_rows(
+        kernel, "second_norm_back", core, [out_grad], [hidden, gain[None], *parts], outs
+    )
+
+
+def first_norm_back(block_in, grad, gain, mine, other, core):
+    rows, width = grad.shape
+
+    def kernel(core_ref, in_ref, grad_ref, gain_ref, mine_ref, other_ref, out_ref, gain_grad_ref):
+        inputs = in_ref[...].astype(f32)
+        upstream = mine_ref[...] + other_ref[...]
+        gain_grad, out = norm_back(inputs, rms_scale(inputs), gain_ref[...], upstream)
+        out_ref[...] = out + grad_ref[...]
+        gain_grad_ref[...] = gain_grad
+
+    sds = jax.ShapeDtypeStruct
+    outs = [sds((rows, width), f32), sds((1, width), f32)]
+    return on_rows(
+        kernel, "first_norm_back", core, [block_in], [grad, gain[None], mine, other], outs
+    )
+
+
+def block_result(block_in, hidden, parts, core, grid):
+    rows, width = hidden.shape
+    parts = [put_in_order(x, grid.natural, grid, False) for x in parts]
+
+    def kernel(core_ref, in_ref, hidden_ref, *refs):
+        out = sum(x[...].astype(f32) for x in refs[: len(parts)])
+        out = put_in_order(out, grid.natural, grid, True)
+        refs[-1][...] = (hidden_ref[...] + out).astype(bf16)
+
+    outs = [jax.ShapeDtypeStruct((rows, width), bf16)]
+    (x,) = on_rows(kernel, "block_result", core, [block_in], [hidden, *parts], outs)
+    return x
+
+
+def exchange(x, split, concat, groups):
+    return lax.all_to_all(x, "dp", split, concat, tiled=True, axis_index_groups=groups)
+
+
+def gather_along(x, grid, place):
+    n = grid.outer
+    above = below = x
+    from_below, from_above = [], []
+    for _ in range(n - 1):
+        below = lax.ppermute(below, "dp", grid.up)
+        above = lax.ppermute(above, "dp", grid.down)
+        from_below.append(below)
+        from_above.append(above)
+    blocks = [x]
+    for k in range(1, n):
+        blocks.append(jnp.where(place + k < n, from_above[k - 1], from_below[n - 1 - k]))
+    return jnp.concatenate(blocks, axis=0)
+
+
+def gather_tokens(x, grid, place):
+    own = gather_along(x, grid, place)
     return jnp.concatenate([own, swap(own)], axis=0)
 
 
 def scatter_tokens(x, grid):
-    size = x.shape[0] // 2
-    other = swap(x[size:].astype(bf16))
-    mine = (x[:size] + other.astype(f32)).astype(bf16)
-    mine = lax.psum_scatter(
-        mine, "dp", scatter_dimension=0, tiled=True, axis_index_groups=grid.cols
-    )
-    return reorder(mine.astype(f32), inverse(grid.gathered))
+    n = grid.outer
+    size = x.shape[0] // (2 * n)
+    block = [x[k * size : (k + 1) * size] for k in range(2 * n)]
+    order = [k for s in range(1, n) for k in (n - s, s)]
+    order = list(dict.fromkeys(order)) + [0]
+    swapped = {k: swap(block[n + k].astype(bf16)) for k in order}
+    own = {k: block[k] + swapped[k].astype(f32) for k in order}
+    up = down = None
+    for k in range(n - 1):
+        send = own[n - 1 - k] if up is None else own[n - 1 - k] + up.astype(f32)
+        up = lax.ppermute(send.astype(bf16), "dp", grid.up)
+        send = own[1 + k] if down is None else own[1 + k] + down.astype(f32)
+        down = lax.ppermute(send.astype(bf16), "dp", grid.down)
+    return own[0], up, down
 
 
 def on_device(
@@ -513,15 +612,20 @@
 ):
     core = lax.axis_index("head")
     place = lax.axis_index("dp") // INNER
-    cot_half = half_of(out_grad, core)
-    cot_all = gather_tokens(cot_half, grid)
-    full_gate = gather_rows(spread_columns(w_gate, grid, place), grid)
-    full_up = gather_rows(spread_columns(w_up, grid, place), grid)
-    full_down = gather_rows(spread_columns(w_down, grid, place), grid)
+    width = block_in.shape[1]
+
+    def columns(w):
+        return exchange(w, 1, 0, grid.cols)
+
+    def gather_rows(w):
+        return lax.all_gather(w, "dp", axis=0, tiled=True, axis_index_groups=grid.laps)
+
+    gate_piece, up_piece, down_piece = columns(w_gate), columns(w_up), columns(w_down)
 
     inputs_f = block_in.astype(f32)
-    scale_one = rms_scale(inputs_f)
-    normed = (inputs_f * scale_one * attn_gain).astype(bf16)
+    normed = (inputs_f * rms_scale(inputs_f) * attn_gain).astype(bf16)
+    normed, gate_piece = lax.optimization_barrier((normed, gate_piece))
+    full_gate = gather_rows(gate_piece)
     query_pre = nn(normed, w_query)
     key_pre = nn(normed, w_key)
     value_pre = nn(normed, w_value)
@@ -530,13 +634,46 @@
     key = jax.nn.silu(key_pre).astype(bf16)
     value = jax.nn.silu(value_pre).astype(bf16)
     log_keep = jax.nn.log_sigmoid(forget_pre) * tau_inv
+    query, up_piece = lax.optimization_barrier((query, up_piece))
+    full_up = gather_rows(up_piece)
     mixed, *saved = attend_forward(query, key, value, log_keep, doc_starts)
 
-    branch = nt(mixed, w_output)
-    hidden = half_of(inputs_f, core) + half_of(branch, core) + swap(half_of(branch, 1 - core))
-    scale_two = rms_scale(hidden)
-    normed_two = (hidden * scale_two * mlp_gain).astype(bf16)
-    tokens = gather_tokens(normed_two, grid)
+    branch_other = swap(nt(half_of(mixed, 1 - core), w_output))
+    branch_mine = nt(half_of(mixed, core), w_output)
+    hidden, normed_two = second_norm(block_in, branch_mine, branch_other, mlp_gain, core, grid)
+    normed_two, down_piece = lax.optimization_barrier((normed_two, down_piece))
+    full_down = gather_rows(down_piece)
+    tokens = gather_tokens(normed_two, grid, place)
+    cot_rows = cotangent_rows(out_grad, core, grid)
+    cot_rows, tokens = lax.optimization_barrier((cot_rows, tokens))
+    cot_all = gather_tokens(cot_rows, grid, place)
+
+    def plane_tokens(half):
+        own = lax.all_gather(half, "dp", axis=0, tiled=True, axis_index_groups=grid.rows)
+        return own, swap(own)
+
+    def plane_columns(parts):
+        rows = parts[0].shape[0]
+        x = jnp.concatenate([p.reshape(rows, INNER, -1) for p in parts], axis=2)
+        size = x.shape[2]
+        x = exchange(x.reshape(rows, INNER * size), 1, 0, grid.rows)
+        x = x.reshape(INNER, 2, rows // 2, size)
+        return tuple(
+            lax.dynamic_index_in_dim(x, c, 1, keepdims=False).reshape(-1, size)
+            for c in (core, 1 - core)
+        )
+
+    def plane_grad(left, right):
+        g = (tn(left[0], right[0]) + tn(left[1], right[1])).astype(bf16)
+        g = lax.psum_scatter(
+            g, "dp", scatter_dimension=0, tiled=True, axis_index_groups=grid.cols
+        )
+        size = g.shape[1]
+        g = exchange(g, 0, 1, grid.rows).reshape(-1, INNER, size)
+        return g.astype(f32)
+
+    normed_plane = plane_tokens(half_of(normed, core))
+    mixed_plane = plane_columns([mixed])
 
     gate_act = nn(tokens, full_gate)
     up_act = nn(tokens, full_up)
@@ -544,27 +681,26 @@
     gate_grad = (inner_grad * up_act * silu_slope(gate_act)).astype(bf16)
     up_grad = (inner_grad * jax.nn.silu(gate_act)).astype(bf16)
     inner_act = (jax.nn.silu(gate_act) * up_act).astype(bf16)
-    normed_two_grad = scatter_tokens(nt(gate_grad, full_gate) + nt(up_grad, full_up), grid)
-    mlp_out = scatter_tokens(nt(inner_act, full_down), grid)
-    result = (hidden + mlp_out).astype(bf16)
+    back_parts = scatter_tokens(nt(gate_grad, full_gate) + nt(up_grad, full_up), grid)
+    hidden_grad, low_half, mlp_gain_part = second_norm_back(
+        out_grad, hidden, mlp_gain, back_parts, core, grid
+    )
+    branch_grad = join(low_half, swap(low_half), core)
+    mixed_grad = nn(branch_grad, w_output).astype(bf16)
+
+    def scatter_rows(g):
+        return lax.psum_scatter(
+            g.astype(bf16), "dp", scatter_dimension=0, tiled=True, axis_index_groups=grid.laps
+        )
+
+    down_rows = scatter_rows(tn(cot_all, inner_act))
+    gate_rows = scatter_rows(tn(tokens, gate_grad))
+    up_rows = scatter_rows(tn(tokens, up_grad))
+    out_parts = scatter_tokens(nt(inner_act, full_down), grid)
+    result = block_result(block_in, hidden, out_parts, core, grid)
     result = join(result, swap(result), core)
 
-    mlp_gain_part, hidden_grad = norm_back(hidden, scale_two, mlp_gain, normed_two_grad)
-    hidden_grad = hidden_grad + cot_half.astype(f32)
-    branch_half = hidden_grad.astype(bf16)
-    branch_grad = join(branch_half, swap(branch_half), core)
-    mixed_grad = nn(branch_grad, w_output).astype(bf16)
-
-    gate_sum = scatter_rows(tn(tokens, gate_grad).astype(bf16), grid).astype(f32)
-    up_sum = scatter_rows(tn(tokens, up_grad).astype(bf16), grid).astype(f32)
-    down_sum = scatter_rows(tn(cot_all, inner_act).astype(bf16), grid).astype(f32)
-
-    def walk_sum(g):
-        return lax.psum_scatter(
-            g.astype(bf16), "dp", scatter_dimension=0, tiled=True, axis_index_groups=[grid.walk]
-        ).astype(f32)
-
-    output_sum = walk_sum(tn(reorder(branch_grad, grid.walk), mixed))
+    output_sum = plane_grad(plane_tokens(low_half), mixed_plane)
     query_grad, key_grad, value_grad, log_grad = attend_backward(
         query, key, value, log_keep, doc_starts, saved, mixed_grad
     )
@@ -573,26 +709,32 @@
     value_pre_grad = (value_grad * silu_slope(value_pre)).astype(bf16)
     forget_pre_grad = (log_grad * tau_inv * jax.nn.sigmoid(-forget_pre)).astype(bf16)
     pre_grads = (query_pre_grad, key_pre_grad, value_pre_grad, forget_pre_grad)
-    sums = walk_sum(tn(reorder(normed, grid.walk), jnp.concatenate(pre_grads, axis=1)))
-    normed_part = nt(query_pre_grad, w_query) + nt(key_pre_grad, w_key)
-    normed_part = normed_part + nt(value_pre_grad, w_value) + nt(forget_pre_grad, w_forget)
-    normed_grad = half_of(normed_part, core) + swap(half_of(normed_part, 1 - core))
-    attn_gain_part, input_grad = norm_back(
-        half_of(inputs_f, core), half_of(scale_one, core), attn_gain, normed_grad
-    )
-    input_grad = input_grad + hidden_grad
+    sums = plane_grad(normed_plane, plane_columns(pre_grads))
+    ends = [0]
+    for g in pre_grads:
+        ends.append(ends[-1] + g.shape[1] // INNER)
+    query_sum, key_sum, value_sum, forget_sum = (
+        sums[:, :, a:b].reshape(sums.shape[0], -1) for a, b in zip(ends, ends[1:])
+    )
+
+    def normed_part(which):
+        q, k, v, f = (half_of(g, which) for g in pre_grads)
+        return nt(q, w_query) + nt(k, w_key) + nt(v, w_value) + nt(f, w_forget)
+
+    part_other = swap(normed_part(1 - core))
+    input_grad, attn_gain_part = first_norm_back(
+        block_in, hidden_grad, attn_gain, normed_part(core), part_other, core
+    )
     input_grad = join(input_grad, swap(input_grad), core)
 
-    gains = jnp.stack([attn_gain_part, mlp_gain_part])
+    gains = jnp.concatenate([attn_gain_part, mlp_gain_part], axis=0)
     gains = gains + swap(gains)
     gains = jnp.swapaxes(gains.reshape(2, grid.dp, -1), 0, 1)
     gains = jnp.sum(lax.all_to_all(gains, "dp", 0, 0, tiled=True), axis=0)
 
-    widths = [g.shape[1] for g in pre_grads]
-    ends = [sum(widths[: n + 1]) for n in range(4)]
-    query_sum, key_sum, value_sum, forget_sum = (
-        sums[:, e - w : e] for e, w in zip(ends, widths)
-    )
+    def to_columns(g):
+        return exchange(g, 0, 1, grid.cols).astype(f32)
+
     return (
         result,
         input_grad,
@@ -602,10 +744,10 @@
         key_sum,
         value_sum,
         forget_sum,
-        output_sum,
-        gate_sum,
-        up_sum,
-        down_sum,
+        output_sum.reshape(output_sum.shape[0], -1),
+        to_columns(gate_rows),
+        to_columns(up_rows),
+        to_columns(down_rows),
     )
 
 

time: 772 us -> 699 us (0.905)
  the two profiles are of different devices: /device:TPU:0 before, /device:TPU:16 now
where the time goes in v2:
time: 699 us; the launch traced here: 693 us
  waiting for transfers between devices  283 us (40%)
  starting transfers between devices  139 us (20%)
  matrix products  112 us (16%)
  local copies, waits for them, and re-layouts  71.9 us (10%)
  other arithmetic  39.7 us (6%)
  Pallas kernels  31.6 us (5%)
  between operations  15.5 us (2%)
    all_to_all x10, waiting for transfers between devices, exchange(): lax.all_to_all(x, 'dp', split, concat, tiled=True, axis_index_groups=groups)  96.5 us
    ppermute x6, waiting for transfers between devices, scatter_tokens(): up = lax.ppermute(send.astype(bf16), 'dp', grid.up)  76.8 us
    all_to_all x10, starting transfers between devices, exchange(): lax.all_to_all(x, 'dp', split, concat, tiled=True, axis_index_groups=groups)  62.6 us
    ppermute x6, waiting for transfers between devices, gather_along(): below = lax.ppermute(below, 'dp', grid.up)  54.5 us
    dot_general x13, matrix products, nt(): lax.dot_general(a.astype(bf16), b.astype(bf16), (((1,), (1,)), ((), ())),...  41.1 us
    dot_general x8, matrix products, nn(): return jnp.dot(a.astype(bf16), b.astype(bf16), preferred_element_type=f32)  40.9 us
    dot_general x7, matrix products, tn(): lax.dot_general(a.astype(bf16), b.astype(bf16), (((0,), (0,)), ((), ())),...  30 us
    unnamed x120, local copies, waits for them, and re-layouts  27 us
  transfers between devices with their start and end apart: 63, of which 27 were waited for; matrix products, arithmetic and copies ran while one was open for 27% of the time, Pallas kernels for 5%

profile of v2, /device:TPU:16, one launch (start us, length us, event | category | flops | bytes accessed | tf_op | source)
XLA Modules:
  0.0 693.1 jit_solution(15835663938971211257)
XLA Ops:
  9.6 5.2 all-to-all-start
  18.5 11.8 %all-to-all-done = bf16[128,4,704]{0,2,1:T(8,128)(2,1)S(1)} async-done(((bf16[128,4,704]{0,2,1:T(8,128)(2,1)}), bf16[128,4,704]{0,2,1:T(8,128)(2,1)S(1)}, u32[]{:S(2)}, u32[]{:S(2)}) %all-to-all-start) | async-done | bytes 720928 | tf_op jit(solution)/shard_map/all_to_all | solution.py:557
  30.2 7.4 %all-to-all-start.1 = ((bf16[128,4,704]{0,2,1:T(8,128)(2,1)}), bf16[128,4,704]{0,2,1:T(8,128)(2,1)}, u32[]{:S(2)}, u32[]{:S(2)}) async-start(bf16[128,4,704]{0,2,1:T(8,128)(2,1)} %bitcast.3), calls=%async_computation.1 | async-start | bytes 1441792 | tf_op jit(solution)/shard_map/all_to_all | solution.py:557
  38.9 4.6 multiply_convert_fusion.8
  43.5 9.2 %all-to-all-done.1 = bf16[128,4,704]{0,2,1:T(8,128)(2,1)} async-done(((bf16[128,4,704]{0,2,1:T(8,128)(2,1)}), bf16[128,4,704]{0,2,1:T(8,128)(2,1)}, u32[]{:S(2)}, u32[]{:S(2)}) %all-to-all-start.1) | async-done | bytes 720928 | tf_op jit(solution)/shard_map/all_to_all | solution.py:557
  52.7 6.8 all-to-all-start.2
  63.0 4.7 multiply_convert_fusion.7
  70.2 6.4 slot_forward.1
  76.7 4.8 fusion.22
  82.4 4.7 fusion.24.mine_ref
  96.1 10.6 %collective-permute-done.2 = bf16[128,2048]{1,0:T(8,128)(2,1)S(1)} collective-permute-done((bf16[128,2048]{1,0:T(8,128)(2,1)}, bf16[128,2048]{1,0:T(8,128)(2,1)S(1)}, u32[]{:S(2)}, u32[]{:S(2)}) %collective-permute-start.2) | collective-permute-done | bytes 524320 | tf_op jit(solution)/shard_map/ppermute | solution.py:565
  106.6 3.3 collective-permute-start.3
  112.5 9.6 %collective-permute-done.3 = bf16[128,2048]{1,0:T(8,128)(2,1)} collective-permute-done((bf16[128,2048]{1,0:T(8,128)(2,1)S(1)}, bf16[128,2048]{1,0:T(8,128)(2,1)}, u32[]{:S(2)}, u32[]{:S(2)}) %collective-permute-start.3) | collective-permute-done | bytes 524320 | tf_op jit(solution)/shard_map/ppermute | solution.py:565
  122.1 3.3 collective-permute-start.4
  129.3 7.6 %collective-permute-done.4 = bf16[128,2048]{1,0:T(8,128)(2,1)} collective-permute-done((bf16[128,2048]{1,0:T(8,128)(2,1)}, bf16[128,2048]{1,0:T(8,128)(2,1)}, u32[]{:S(2)}, u32[]{:S(2)}) %collective-permute-start.4) | collective-permute-done | bytes 524320 | tf_op jit(solution)/shard_map/ppermute | solution.py:565
  154.5 3.9 collective-permute-start.19
  158.4 10.0 %collective-permute-done.20 = bf16[128,2048]{1,0:T(8,128)(2,1)S(1)} collective-permute-done((bf16[128,2048]{1,0:T(8,128)(2,1)S(1)}, bf16[128,2048]{1,0:T(8,128)(2,1)S(1)}, u32[]{:S(2)}, u32[]{:S(2)}) %collective-permute-start.20) | collective-permute-done | bytes 524320 | tf_op jit(solution)/shard_map/ppermute | solution.py:565
  170.7 3.6 collective-permute-start.23
  174.3 9.4 %collective-permute-done.21 = bf16[128,2048]{1,0:T(8,128)(2,1)} collective-permute-done((bf16[128,2048]{1,0:T(8,128)(2,1)S(1)}, bf16[128,2048]{1,0:T(8,128)(2,1)}, u32[]{:S(2)}, u32[]{:S(2)}) %collective-permute-start.21) | collective-permute-done | bytes 524320 | tf_op jit(solution)/shard_map/ppermute | solution.py:565
  187.0 3.9 collective-permute-start.24
  191.0 7.3 %collective-permute-done.22 = bf16[128,2048]{1,0:T(8,128)(2,1)} collective-permute-done((bf16[128,2048]{1,0:T(8,128)(2,1)}, bf16[128,2048]{1,0:T(8,128)(2,1)}, u32[]{:S(2)}, u32[]{:S(2)}) %collective-permute-start.22) | collective-permute-done | bytes 524320 | tf_op jit(solution)/shard_map/ppermute | solution.py:565
  204.9 8.0 %fusion.46 = f32[1024,704]{0,1:T(8,128)} fusion(bf16[1024,2048]{1,0:T(8,128)(2,1)} %constant_dynamic-update-slice_fusion, bf16[2048,704]{0,1:T(8,128)(2,1)} %all-gather.8.cloned.1.call-done), kind=kOutput, calls=%fused_computation.137 | convolution fusion | flops 2952790016 | bytes 9961472 | tf_op jit(solution)/shard_map/dot_general | solution.py:19
  212.9 7.9 %fusion.45 = f32[1024,704]{0,1:T(8,128)} fusion(bf16[1024,2048]{1,0:T(8,128)(2,1)} %constant_dynamic-update-slice_fusion, bf16[2048,704]{0,1:T(8,128)(2,1)} %all-gather.6.cloned.1.call-done), kind=kOutput, calls=%fused_computation.136 | convolution fusion | flops 2952790016 | bytes 9961472 | tf_op jit(solution)/shard_map/dot_general | solution.py:19
  223.9 10.1 %multiply_convert_fusion = (bf16[1024,704]{0,1:T(8,128)(2,1)S(1)}, bf16[1024,704]{0,1:T(8,128)(2,1)S(1)}, bf16[1024,704]{0,1:T(8,128)(2,1)}) fusion(f32[1024,704]{0,1:T(8,128)} %fusion.45, f32[1024,704]{0,1:T(8,128)} %fusion.46, bf16[1024,2048]{1,0:T(8,128)(2,1)} %constant_dynamic-update-slice_fusion.5, bf16[2048,704]{0,1:T(8,128)(2,1)} %all-gather.10.cloned.1.call-done), kind=kOutput, calls=%fused_computation.5 | convolution fusion | flops 2963603456 | bytes 17170432 | tf_op jit(solution)/shard_map/dot_general | solution.py:19
  234.0 3.7 fusion.47
  237.7 3.6 fusion.44
  248.0 13.0 %collective-permute-done.33 = bf16[128,2048]{1,0:T(8,128)(2,1)S(1)} collective-permute-done((bf16[128,2048]{1,0:T(8,128)(2,1)S(1)}, bf16[128,2048]{1,0:T(8,128)(2,1)S(1)}, u32[]{:S(2)}, u32[]{:S(2)}) %collective-permute-start.33) | collective-permute-done | bytes 524320 | tf_op jit(solution)/shard_map/ppermute | solution.py:593
  265.4 12.1 %collective-permute-done.34 = bf16[128,2048]{1,0:T(8,128)(2,1)} collective-permute-done((bf16[128,2048]{1,0:T(8,128)(2,1)}, bf16[128,2048]{1,0:T(8,128)(2,1)}, u32[]{:S(2)}, u32[]{:S(2)}) %collective-permute-start.34) | collective-permute-done | bytes 524320 | tf_op jit(solution)/shard_map/ppermute | solution.py:593
  277.6 3.4 add_convert_fusion.1
  282.8 12.5 %collective-permute-done.30 = bf16[128,2048]{1,0:T(8,128)(2,1)S(1)} collective-permute-done((bf16[128,2048]{1,0:T(8,128)(2,1)S(1)}, bf16[128,2048]{1,0:T(8,128)(2,1)S(1)}, u32[]{:S(2)}, u32[]{:S(2)}) %collective-permute-start.30) | collective-permute-done | bytes 524320 | tf_op jit(solution)/shard_map/ppermute | solution.py:591
  298.9 3.6 collective-permute-start.35
  302.6 7.8 %collective-permute-done.31 = bf16[128,2048]{1,0:T(8,128)(2,1)S(1)} collective-permute-done((bf16[128,2048]{1,0:T(8,128)(2,1)S(1)}, bf16[128,2048]{1,0:T(8,128)(2,1)S(1)}, u32[]{:S(2)}, u32[]{:S(2)}) %collective-permute-start.31) | collective-permute-done | bytes 524320 | tf_op jit(solution)/shard_map/ppermute | solution.py:591
  314.3 10.3 %collective-permute-done.32.refs_1_ = bf16[128,2048]{1,0:T(8,128)(2,1)S(1)} collective-permute-done((bf16[128,2048]{1,0:T(8,128)(2,1)S(1)}, bf16[128,2048]{1,0:T(8,128)(2,1)S(1)}, u32[]{:S(2)}, u32[]{:S(2)}) %collective-permute-start.32) | collective-permute-done | bytes 524320 | tf_op jit(solution)/shard_map/ppermute | solution.py:591
  325.3 3.9 second_norm_back.1
  329.3 7.5 %convolution_convert_fusion = bf16[2048,704]{0,1:T(8,128)(2,1)} fusion(bf16[1024,704]{0,1:T(8,128)(2,1)} %get-tuple-element.116, bf16[1024,2048]{1,0:T(8,128)(2,1)} %constant_dynamic-update-slice_fusion.5), kind=kOutput, calls=%fused_computation.2 | convolution fusion | flops 2954231808 | bytes 8519680 | tf_op jit(solution)/shard_map/dot_general | solution.py:29
  338.3 6.7 convolution_convert_fusion.2
  346.3 7.7 %fusion.43 = (bf16[1024,2048]{1,0:T(8,128)(2,1)S(1)}, f32[1024,2048]{1,0:T(8,128)}) fusion(bf16[1024,704]{0,1:T(8,128)(2,1)S(1)} %copy-done.51, bf16[2048,704]{0,1:T(8,128)(2,1)} %all-gather.10.cloned.1.call-done), kind=kOutput, calls=%fused_computation.134 | convolution fusion | flops 2954887168 | bytes 16908288 | tf_op jit(solution)/shard_map/dot_general | solution.py:23
  355.9 4.5 convolution_convert_fusion.1
  366.3 3.6 all-to-all-start.6
  369.9 12.6 %all-to-all-done.6 = bf16[256,4,256]{2,0,1:T(8,128)(2,1)S(1)} async-done(((bf16[256,4,256]{2,0,1:T(8,128)(2,1)}), bf16[256,4,256]{2,0,1:T(8,128)(2,1)S(1)}, u32[]{:S(2)}, u32[]{:S(2)}) %all-to-all-start.6) | async-done | bytes 524320 | tf_op jit(solution)/shard_map/all_to_all | solution.py:557
  392.2 9.4 %slot_backward.1 = (f32[256,1024]{1,0:T(8,128)}, f32[256,1024]{1,0:T(8,128)}, f32[256,1024]{1,0:T(8,128)}, f32[256,128]{1,0:T(8,128)}) custom-call(s32[1,3]{1,0:T(1,128)} %starts_ref.3, bf16[256,1024]{1,0:T(8,128)(2,1)} %get-tuple-element.37.q_ref, bf16[256,1024]{1,0:T(8,128)(2,1)} %get-tuple-element.136.k_ref, bf16[256,1024]{1,0:T(8,128)(2,1)} %get-tuple-element.138.v_ref, ...), custom_call_target="tpu_custom_call" | custom-call | flops 12000000000 | bytes 8000000 | tf_op jit(solution)/shard_map/slot_backward/pallas_call | solution.py:369
  410.2 3.6 all-to-all-start.4
  418.2 3.9 fusion.16
  424.6 27.8 %all-to-all-done.4 = bf16[256,4,800]{0,2,1:T(8,128)(2,1)S(1)} async-done(((bf16[256,4,800]{0,2,1:T(8,128)(2,1)}), bf16[256,4,800]{0,2,1:T(8,128)(2,1)S(1)}, u32[]{:S(2)}, u32[]{:S(2)}) %all-to-all-start.4) | async-done | bytes 1638432 | tf_op jit(solution)/shard_map/all_to_all | solution.py:557
  453.6 3.6 reshape.143
  457.2 3.4 constant_dynamic-slice_fusion.2
  464.6 5.3 add_convert_fusion
  471.2 3.9 convolution_add_fusion.3
  483.9 3.9 first_norm_back.1
  488.6 3.6 add_convert_fusion.5
  492.2 4.2 collective-permute-start.12
  497.0 5.1 all-to-all-start.3
  504.3 22.5 %all-to-all-done.3 = f32[16,2,128]{2,1,0:T(2,128)S(1)} async-done(((f32[16,2,128]{2,1,0:T(2,128)}), f32[16,2,128]{2,1,0:T(2,128)S(1)}, u32[]{:S(2)}, u32[]{:S(2)}) %all-to-all-start.3) | async-done | bytes 16416 | tf_op jit(solution)/shard_map/all_to_all | solution.py:733
  526.8 5.8 all-to-all-start.10
  534.8 3.4 collective-permute-start.13
  540.3 26.1 %all-to-all-done.10 = bf16[4,128,704]{1,2,0:T(8,128)(2,1)S(1)} async-done(((bf16[4,128,704]{1,2,0:T(8,128)(2,1)}), bf16[4,128,704]{1,2,0:T(8,128)(2,1)S(1)}, u32[]{:S(2)}, u32[]{:S(2)}) %all-to-all-start.10) | async-done | bytes 720928 | tf_op jit(solution)/shard_map/all_to_all | solution.py:557
  566.4 6.7 all-to-all-start.8
  575.6 29.2 %collective-permute-done.13 = bf16[128,2048]{1,0:T(8,128)(2,1)} collective-permute-done((bf16[128,2048]{1,0:T(8,128)(2,1)}, bf16[128,2048]{1,0:T(8,128)(2,1)}, u32[]{:S(2)}, u32[]{:S(2)}) %collective-permute-start.13) | collective-permute-done | bytes 524320 | tf_op jit(solution)/shard_map/ppermute | solution.py:591
  611.2 3.5 all-to-all-done.8
  614.8 16.5 %all-to-all-start.9 = ((bf16[4,128,704]{1,2,0:T(8,128)(2,1)}), bf16[4,128,704]{1,2,0:T(8,128)(2,1)S(1)}, u32[]{:S(2)}, u32[]{:S(2)}) async-start(bf16[4,128,704]{1,2,0:T(8,128)(2,1)} %copy_bitcast_fusion.5), calls=%async_computation.13 | async-start | bytes 1441792 | tf_op jit(solution)/shard_map/all_to_all | solution.py:557
  631.6 17.1 %collective-permute-done.14.refs_1_ = bf16[128,2048]{1,0:T(8,128)(2,1)} collective-permute-done((bf16[128,2048]{1,0:T(8,128)(2,1)}, bf16[128,2048]{1,0:T(8,128)(2,1)}, u32[]{:S(2)}, u32[]{:S(2)}) %collective-permute-start.14) | collective-permute-done | bytes 524320 | tf_op jit(solution)/shard_map/ppermute | solution.py:591
  658.7 3.4 all-to-all-start.7
  664.3 3.6 all-to-all-done.7
  668.0 3.5 all-to-all-start.5
  (295 shorter events, 177.8 us)
Async XLA Ops:
  9.6 20.6 %all-to-all-start = ((bf16[128,4,704]{0,2,1:T(8,128)(2,1)}), bf16[128,4,704]{0,2,1:T(8,128)(2,1)S(1)}, u32[]{:S(2)}, u32[]{:S(2)}) async-start(bf16[128,4,704]{0,2,1:T(8,128)(2,1)} %bitcast.1), calls=%async_computation | async-start | bytes 1441792 | tf_op jit(solution)/shard_map/all_to_all | solution.py:557
  30.2 22.4 %all-to-all-start.1 = ((bf16[128,4,704]{0,2,1:T(8,128)(2,1)}), bf16[128,4,704]{0,2,1:T(8,128)(2,1)}, u32[]{:S(2)}, u32[]{:S(2)}) async-start(bf16[128,4,704]{0,2,1:T(8,128)(2,1)} %bitcast.3), calls=%async_computation.1 | async-start | bytes 1441792 | tf_op jit(solution)/shard_map/all_to_all | solution.py:557
  52.7 28.8 %all-to-all-start.2 = ((bf16[128,4,704]{0,2,1:T(8,128)(2,1)}), bf16[128,4,704]{0,2,1:T(8,128)(2,1)S(1)}, u32[]{:S(2)}, u32[]{:S(2)}) async-start(bf16[128,4,704]{0,2,1:T(8,128)(2,1)} %bitcast.6), calls=%async_computation.2 | async-start | bytes 1441792 | tf_op jit(solution)/shard_map/all_to_all | solution.py:557
  59.5 145.4 %all-gather.8.cloned.1.call-start = ((), (), s32[]{:S(2)}) async-start(), calls=%async_computation.17 | async-start | bytes 3604480 | tf_op jit(solution)/shard_map/all_gather | solution.py:621
  61.6 151.3 %all-gather.6.cloned.1.call-start = ((), (), s32[]{:S(2)}) async-start(), calls=%async_computation.16 | async-start | bytes 3604480 | tf_op jit(solution)/shard_map/all_gather | solution.py:621
  81.5 5.6 collective-permute-start
  90.2 16.4 %collective-permute-start.2 = (bf16[128,2048]{1,0:T(8,128)(2,1)}, bf16[128,2048]{1,0:T(8,128)(2,1)S(1)}, u32[]{:S(2)}, u32[]{:S(2)}) collective-permute-start(bf16[128,2048]{1,0:T(8,128)(2,1)} %get-tuple-element.41), channel_id=1, source_target_pairs={{0,8},{2,10},{4,12},{6,14},{8,16},{10,18},{12,20},{14,22},{16,24},... | collective-permute-start | bytes 1572872 | tf_op jit(solution)/shard_map/ppermute | solution.py:565
  93.6 16.4 %collective-permute-start.1 = (bf16[128,2048]{1,0:T(8,128)(2,1)}, bf16[128,2048]{1,0:T(8,128)(2,1)S(1)}, u32[]{:S(2)}, u32[]{:S(2)}) collective-permute-start(bf16[128,2048]{1,0:T(8,128)(2,1)} %get-tuple-element.41), channel_id=1, source_target_pairs={{8,0},{10,2},{12,4},{14,6},{16,8},{18,10},{20,12},{22,14},{24,16},... | collective-permute-start | bytes 1572872 | tf_op jit(solution)/shard_map/ppermute | solution.py:566
  106.6 15.5 %collective-permute-start.3 = (bf16[128,2048]{1,0:T(8,128)(2,1)S(1)}, bf16[128,2048]{1,0:T(8,128)(2,1)}, u32[]{:S(2)}, u32[]{:S(2)}) collective-permute-start(bf16[128,2048]{1,0:T(8,128)(2,1)S(1)} %collective-permute-done.2), channel_id=1, source_target_pairs={{0,8},{2,10},{4,12},{6,14},{8,16},{10,18},{12,20},{14,22},{16,24},... | collective-permute-start | bytes 1572872 | tf_op jit(solution)/shard_map/ppermute | solution.py:565
  110.0 16.6 %collective-permute-start.5 = (bf16[128,2048]{1,0:T(8,128)(2,1)S(1)}, bf16[128,2048]{1,0:T(8,128)(2,1)}, u32[]{:S(2)}, u32[]{:S(2)}) collective-permute-start(bf16[128,2048]{1,0:T(8,128)(2,1)S(1)} %collective-permute-done.1), channel_id=1, source_target_pairs={{8,0},{10,2},{12,4},{14,6},{16,8},{18,10},{20,12},{22,14},{24,16},... | collective-permute-start | bytes 1572872 | tf_op jit(solution)/shard_map/ppermute | solution.py:566
  122.1 14.8 %collective-permute-start.4 = (bf16[128,2048]{1,0:T(8,128)(2,1)}, bf16[128,2048]{1,0:T(8,128)(2,1)}, u32[]{:S(2)}, u32[]{:S(2)}) collective-permute-start(bf16[128,2048]{1,0:T(8,128)(2,1)} %collective-permute-done.3), channel_id=1, source_target_pairs={{0,8},{2,10},{4,12},{6,14},{8,16},{10,18},{12,20},{14,22},{16,24},... | collective-permute-start | bytes 1572872 | tf_op jit(solution)/shard_map/ppermute | solution.py:565
  125.5 98.4 %all-gather.10.cloned.1.call-start = ((), (), s32[]{:S(2)}) async-start(), calls=%async_computation.18 | async-start | bytes 3604480 | tf_op jit(solution)/shard_map/all_gather | solution.py:621
  126.6 14.6 %collective-permute-start.6 = (bf16[128,2048]{1,0:T(8,128)(2,1)}, bf16[128,2048]{1,0:T(8,128)(2,1)S(1)}, u32[]{:S(2)}, u32[]{:S(2)}) collective-permute-start(bf16[128,2048]{1,0:T(8,128)(2,1)} %collective-permute-done.5), channel_id=1, source_target_pairs={{8,0},{10,2},{12,4},{14,6},{16,8},{18,10},{20,12},{22,14},{24,16},... | collective-permute-start | bytes 1572872 | tf_op jit(solution)/shard_map/ppermute | solution.py:566
  144.9 4.5 collective-permute-start.7
  152.6 15.9 %collective-permute-start.20 = (bf16[128,2048]{1,0:T(8,128)(2,1)S(1)}, bf16[128,2048]{1,0:T(8,128)(2,1)S(1)}, u32[]{:S(2)}, u32[]{:S(2)}) collective-permute-start(bf16[128,2048]{1,0:T(8,128)(2,1)S(1)} %copy-done.10), channel_id=1, source_target_pairs={{0,8},{2,10},{4,12},{6,14},{8,16},{10,18},{12,20},{14,22},{16,24},... | collective-permute-start | bytes 1572872 | tf_op jit(solution)/shard_map/ppermute | solution.py:565
  154.5 16.2 %collective-permute-start.19 = (bf16[128,2048]{1,0:T(8,128)(2,1)S(1)}, bf16[128,2048]{1,0:T(8,128)(2,1)}, u32[]{:S(2)}, u32[]{:S(2)}) collective-permute-start(bf16[128,2048]{1,0:T(8,128)(2,1)S(1)} %copy-done.10), channel_id=1, source_target_pairs={{8,0},{10,2},{12,4},{14,6},{16,8},{18,10},{20,12},{22,14},{24,16},... | collective-permute-start | bytes 1572872 | tf_op jit(solution)/shard_map/ppermute | solution.py:566
  168.5 15.2 %collective-permute-start.21 = (bf16[128,2048]{1,0:T(8,128)(2,1)S(1)}, bf16[128,2048]{1,0:T(8,128)(2,1)}, u32[]{:S(2)}, u32[]{:S(2)}) collective-permute-start(bf16[128,2048]{1,0:T(8,128)(2,1)S(1)} %collective-permute-done.20), channel_id=1, source_target_pairs={{0,8},{2,10},{4,12},{6,14},{8,16},{10,18},{12,20},{14,22},{16,24},... | collective-permute-start | bytes 1572872 | tf_op jit(solution)/shard_map/ppermute | solution.py:565
  170.7 16.3 %collective-permute-start.23 = (bf16[128,2048]{1,0:T(8,128)(2,1)}, bf16[128,2048]{1,0:T(8,128)(2,1)}, u32[]{:S(2)}, u32[]{:S(2)}) collective-permute-start(bf16[128,2048]{1,0:T(8,128)(2,1)} %collective-permute-done.19), channel_id=1, source_target_pairs={{8,0},{10,2},{12,4},{14,6},{16,8},{18,10},{20,12},{22,14},{24,16},... | collective-permute-start | bytes 1572872 | tf_op jit(solution)/shard_map/ppermute | solution.py:566
  183.7 14.6 %collective-permute-start.22 = (bf16[128,2048]{1,0:T(8,128)(2,1)}, bf16[128,2048]{1,0:T(8,128)(2,1)}, u32[]{:S(2)}, u32[]{:S(2)}) collective-permute-start(bf16[128,2048]{1,0:T(8,128)(2,1)} %collective-permute-done.21), channel_id=1, source_target_pairs={{0,8},{2,10},{4,12},{6,14},{8,16},{10,18},{12,20},{14,22},{16,24},... | collective-permute-start | bytes 1572872 | tf_op jit(solution)/shard_map/ppermute | solution.py:565
  186.1 197.2 %all-gather.12.cloned.1.call-start = ((), (), s32[]{:S(2)}) async-start(), calls=%async_computation.19 | async-start | bytes 2621440 | tf_op jit(solution)/shard_map/all_gather | solution.py:652
  187.0 15.4 %collective-permute-start.24 = (bf16[128,2048]{1,0:T(8,128)(2,1)}, bf16[128,2048]{1,0:T(8,128)(2,1)S(1)}, u32[]{:S(2)}, u32[]{:S(2)}) collective-permute-start(bf16[128,2048]{1,0:T(8,128)(2,1)} %collective-permute-done.23), channel_id=1, source_target_pairs={{8,0},{10,2},{12,4},{14,6},{16,8},{18,10},{20,12},{22,14},{24,16},... | collective-permute-start | bytes 1572872 | tf_op jit(solution)/shard_map/ppermute | solution.py:566
  204.9 15.9 %collective-permute-start.25 = (bf16[512,2048]{1,0:T(8,128)(2,1)}, bf16[512,2048]{1,0:T(8,128)(2,1)}, u32[]{:S(2)}, u32[]{:S(2)}) collective-permute-start(bf16[512,2048]{1,0:T(8,128)(2,1)} %pad_maximum_fusion.1), channel_id=1, source_target_pairs={{0,1},{1,0},{2,3},{3,2},{4,5},{5,4},{6,7},{7,6},{8,9},{9,8},{10,11... | collective-permute-start | bytes 6291464 | tf_op jit(solution)/shard_map/ppermute | solution.py:436
  242.7 2.0 collective-permute-start.27
  243.2 4.7 collective-permute-start.28
  244.9 16.1 %collective-permute-start.33 = (bf16[128,2048]{1,0:T(8,128)(2,1)S(1)}, bf16[128,2048]{1,0:T(8,128)(2,1)S(1)}, u32[]{:S(2)}, u32[]{:S(2)}) collective-permute-start(bf16[128,2048]{1,0:T(8,128)(2,1)S(1)} %fusion.12), channel_id=1, source_target_pairs={{8,0},{10,2},{12,4},{14,6},{16,8},{18,10},{20,12},{22,14},{24,16},... | collective-permute-start | bytes 1572872 | tf_op jit(solution)/shard_map/ppermute | solution.py:593
  247.4 18.0 %collective-permute-start.26 = (bf16[128,2048]{1,0:T(8,128)(2,1)}, bf16[128,2048]{1,0:T(8,128)(2,1)}, u32[]{:S(2)}, u32[]{:S(2)}) collective-permute-start(bf16[128,2048]{1,0:T(8,128)(2,1)} %get-tuple-element.120), channel_id=1, source_target_pairs={{0,1},{1,0},{2,3},{3,2},{4,5},{5,4},{6,7},{7,6},{8,9},{9,8},{10,11... | collective-permute-start | bytes 1572872 | tf_op jit(solution)/shard_map/ppermute | solution.py:436
  247.5 17.9 %collective-permute-start.29 = (bf16[128,2048]{1,0:T(8,128)(2,1)}, bf16[128,2048]{1,0:T(8,128)(2,1)}, u32[]{:S(2)}, u32[]{:S(2)}) collective-permute-start(bf16[128,2048]{1,0:T(8,128)(2,1)} %get-tuple-element.118), channel_id=1, source_target_pairs={{0,1},{1,0},{2,3},{3,2},{4,5},{5,4},{6,7},{7,6},{8,9},{9,8},{10,11... | collective-permute-start | bytes 1572872 | tf_op jit(solution)/shard_map/ppermute | solution.py:436
  262.0 15.5 %collective-permute-start.34 = (bf16[128,2048]{1,0:T(8,128)(2,1)}, bf16[128,2048]{1,0:T(8,128)(2,1)}, u32[]{:S(2)}, u32[]{:S(2)}) collective-permute-start(bf16[128,2048]{1,0:T(8,128)(2,1)} %add_convert_fusion.2), channel_id=1, source_target_pairs={{8,0},{10,2},{12,4},{14,6},{16,8},{18,10},{20,12},{22,14},{24,16},... | collective-permute-start | bytes 1572872 | tf_op jit(solution)/shard_map/ppermute | solution.py:593
  265.4 126.7 %all-gather.14.cloned.1.call-start = ((), (), s32[]{:S(2)}) async-start(), calls=%async_computation.21 | async-start | bytes 2621440 | tf_op jit(solution)/shard_map/all_gather | solution.py:652
  280.9 14.4 %collective-permute-start.30 = (bf16[128,2048]{1,0:T(8,128)(2,1)S(1)}, bf16[128,2048]{1,0:T(8,128)(2,1)S(1)}, u32[]{:S(2)}, u32[]{:S(2)}) collective-permute-start(bf16[128,2048]{1,0:T(8,128)(2,1)S(1)} %get-tuple-element.109), channel_id=1, source_target_pairs={{0,8},{2,10},{4,12},{6,14},{8,16},{10,18},{12,20},{14,22},{16,24},... | collective-permute-start | bytes 1572872 | tf_op jit(solution)/shard_map/ppermute | solution.py:591
  296.7 13.6 %collective-permute-start.31 = (bf16[128,2048]{1,0:T(8,128)(2,1)S(1)}, bf16[128,2048]{1,0:T(8,128)(2,1)S(1)}, u32[]{:S(2)}, u32[]{:S(2)}) collective-permute-start(bf16[128,2048]{1,0:T(8,128)(2,1)S(1)} %add_convert_fusion.4), channel_id=1, source_target_pairs={{0,8},{2,10},{4,12},{6,14},{8,16},{10,18},{12,20},{14,22},{16,24},... | collective-permute-start | bytes 1572872 | tf_op jit(solution)/shard_map/ppermute | solution.py:591
  298.9 15.3 %collective-permute-start.35 = (bf16[128,2048]{1,0:T(8,128)(2,1)S(1)}, bf16[128,2048]{1,0:T(8,128)(2,1)S(1)}, u32[]{:S(2)}, u32[]{:S(2)}) collective-permute-start(bf16[128,2048]{1,0:T(8,128)(2,1)S(1)} %get-tuple-element.108), channel_id=1, source_target_pairs={{8,0},{10,2},{12,4},{14,6},{16,8},{18,10},{20,12},{22,14},{24,16},... | collective-permute-start | bytes 1572872 | tf_op jit(solution)/shard_map/ppermute | solution.py:593
  311.7 12.8 %collective-permute-start.32 = (bf16[128,2048]{1,0:T(8,128)(2,1)S(1)}, bf16[128,2048]{1,0:T(8,128)(2,1)S(1)}, u32[]{:S(2)}, u32[]{:S(2)}) collective-permute-start(bf16[128,2048]{1,0:T(8,128)(2,1)S(1)} %add_convert_fusion.3), channel_id=1, source_target_pairs={{0,8},{2,10},{4,12},{6,14},{8,16},{10,18},{12,20},{14,22},{16,24},... | collective-permute-start | bytes 1572872 | tf_op jit(solution)/shard_map/ppermute | solution.py:591
  329.3 172.9 %reduce-scatter.14.cloned.1.call-start = ((), (), s32[]{:S(2)}) async-start(), calls=%async_computation.25 | async-start | bytes 3604480 | tf_op jit(solution)/shard_map/reduce_scatter | solution.py:692
  336.8 201.4 %reduce-scatter.10.cloned.1.call-start = ((), (), s32[]{:S(2)}) async-start(), calls=%async_computation.23 | async-start | bytes 3604480 | tf_op jit(solution)/shard_map/reduce_scatter | solution.py:692
  345.0 264.2 %reduce-scatter.12.cloned.1.call-start = ((), (), s32[]{:S(2)}) async-start(), calls=%async_computation.24 | async-start | bytes 3604480 | tf_op jit(solution)/shard_map/reduce_scatter | solution.py:692
  355.2 5.4 collective-permute-start.9
  360.5 23.3 %collective-permute-start.10 = (bf16[128,2048]{1,0:T(8,128)(2,1)}, bf16[128,2048]{1,0:T(8,128)(2,1)S(1)}, u32[]{:S(2)}, u32[]{:S(2)}) collective-permute-start(bf16[128,2048]{1,0:T(8,128)(2,1)} %get-tuple-element.123), channel_id=1, source_target_pairs={{0,1},{1,0},{2,3},{3,2},{4,5},{5,4},{6,7},{7,6},{8,9},{9,8},{10,11... | collective-permute-start | bytes 1572872 | tf_op jit(solution)/shard_map/ppermute | solution.py:436
  363.0 21.4 %collective-permute-start.15 = (bf16[128,2048]{1,0:T(8,128)(2,1)}, bf16[128,2048]{1,0:T(8,128)(2,1)S(1)}, u32[]{:S(2)}, u32[]{:S(2)}) collective-permute-start(bf16[128,2048]{1,0:T(8,128)(2,1)} %fusion.10), channel_id=1, source_target_pairs={{8,0},{10,2},{12,4},{14,6},{16,8},{18,10},{20,12},{22,14},{24,16},... | collective-permute-start | bytes 1572872 | tf_op jit(solution)/shard_map/ppermute | solution.py:593
  366.3 16.3 %all-to-all-start.6 = ((bf16[256,4,256]{2,0,1:T(8,128)(2,1)}), bf16[256,4,256]{2,0,1:T(8,128)(2,1)S(1)}, u32[]{:S(2)}, u32[]{:S(2)}) async-start(bf16[256,4,256]{2,0,1:T(8,128)(2,1)} %bitcast.145), calls=%async_computation.7 | async-start | bytes 1048576 | tf_op jit(solution)/shard_map/all_to_all | solution.py:557
  383.3 81.4 %collective-permute-start.40 = (bf16[512,2048]{1,0:T(8,128)(2,1)}, bf16[512,2048]{1,0:T(8,128)(2,1)}, u32[]{:S(2)}, u32[]{:S(2)}) collective-permute-start(bf16[512,2048]{1,0:T(8,128)(2,1)} %all-gather.12.cloned.1.call-done), channel_id=1, source_target_pairs={{0,1},{1,0},{2,3},{3,2},{4,5},{5,4},{6,7},{7,6},{8,9},{9,8},{10,11... | collective-permute-start | bytes 6291464 | tf_op jit(solution)/shard_map/ppermute | solution.py:436
  383.3 105.3 %collective-permute-start.11 = (bf16[128,2048]{1,0:T(8,128)(2,1)}, bf16[128,2048]{1,0:T(8,128)(2,1)}, u32[]{:S(2)}, u32[]{:S(2)}) collective-permute-start(bf16[128,2048]{1,0:T(8,128)(2,1)} %get-tuple-element.122), channel_id=1, source_target_pairs={{0,1},{1,0},{2,3},{3,2},{4,5},{5,4},{6,7},{7,6},{8,9},{9,8},{10,11... | collective-permute-start | bytes 1572872 | tf_op jit(solution)/shard_map/ppermute | solution.py:436
  383.8 104.8 %collective-permute-start.8 = (bf16[128,2048]{1,0:T(8,128)(2,1)}, bf16[128,2048]{1,0:T(8,128)(2,1)}, u32[]{:S(2)}, u32[]{:S(2)}) collective-permute-start(bf16[128,2048]{1,0:T(8,128)(2,1)} %get-tuple-element.124), channel_id=1, source_target_pairs={{0,1},{1,0},{2,3},{3,2},{4,5},{5,4},{6,7},{7,6},{8,9},{9,8},{10,11... | collective-permute-start | bytes 1572872 | tf_op jit(solution)/shard_map/ppermute | solution.py:436
  383.8 6.1 collective-permute-start.36
  387.1 101.5 %collective-permute-start.16 = (bf16[128,2048]{1,0:T(8,128)(2,1)}, bf16[128,2048]{1,0:T(8,128)(2,1)}, u32[]{:S(2)}, u32[]{:S(2)}) collective-permute-start(bf16[128,2048]{1,0:T(8,128)(2,1)} %add_convert_fusion.6), channel_id=1, source_target_pairs={{8,0},{10,2},{12,4},{14,6},{16,8},{18,10},{20,12},{22,14},{24,16},... | collective-permute-start | bytes 1572872 | tf_op jit(solution)/shard_map/ppermute | solution.py:593
  392.1 21.8 %collective-permute-start.41 = (bf16[512,2048]{1,0:T(8,128)(2,1)}, bf16[512,2048]{1,0:T(8,128)(2,1)}, u32[]{:S(2)}, u32[]{:S(2)}) collective-permute-start(bf16[512,2048]{1,0:T(8,128)(2,1)} %all-gather.14.cloned.1.call-done), channel_id=1, source_target_pairs={{0,1},{1,0},{2,3},{3,2},{4,5},{5,4},{6,7},{7,6},{8,9},{9,8},{10,11... | collective-permute-start | bytes 6291464 | tf_op jit(solution)/shard_map/ppermute | solution.py:436
  410.2 42.2 %all-to-all-start.4 = ((bf16[256,4,800]{0,2,1:T(8,128)(2,1)}), bf16[256,4,800]{0,2,1:T(8,128)(2,1)S(1)}, u32[]{:S(2)}, u32[]{:S(2)}) async-start(bf16[256,4,800]{0,2,1:T(8,128)(2,1)} %pad_maximum_fusion.2), calls=%async_computation.4 | async-start | bytes 3276800 | tf_op jit(solution)/shard_map/all_to_all | solution.py:557
  413.8 244.9 %reduce-scatter.8.cloned.1.call-start = ((), (), s32[]{:S(2)}) async-start(), calls=%async_computation.22 | async-start | bytes 1310720 | tf_op jit(solution)/shard_map/reduce_scatter | solution.py:668
  418.1 244.0 %reduce-scatter.6.cloned.1.call-start = ((), (), s32[]{:S(2)}) async-start(), calls=%async_computation.20 | async-start | bytes 4096000 | tf_op jit(solution)/shard_map/reduce_scatter | solution.py:668
  475.5 7.4 %collective-permute-start.37 = (f32[128,2048]{1,0:T(8,128)S(1)}, f32[128,2048]{1,0:T(8,128)S(1)}, u32[]{:S(2)}, u32[]{:S(2)}) collective-permute-start(f32[128,2048]{1,0:T(8,128)S(1)} %convolution_add_fusion.2), channel_id=1, source_target_pairs={{0,1},{1,0},{2,3},{3,2},{4,5},{5,4},{6,7},{7,6},{8,9},{9,8},{10,11... | collective-permute-start | bytes 3145736 | tf_op jit(solution)/shard_map/ppermute | solution.py:436
  488.5 7.9 %collective-permute-start.39 = (f32[2,2048]{1,0:T(2,128)S(1)}, f32[2,2048]{1,0:T(2,128)S(1)}, u32[]{:S(2)}, u32[]{:S(2)}) collective-permute-start(f32[2,2048]{1,0:T(2,128)S(1)} %pad_maximum_fusion.3), channel_id=1, source_target_pairs={{0,1},{1,0},{2,3},{3,2},{4,5},{5,4},{6,7},{7,6},{8,9},{9,8},{10,11... | collective-permute-start | bytes 49160 | tf_op jit(solution)/shard_map/ppermute | solution.py:436
  492.2 40.4 %collective-permute-start.12 = (bf16[128,2048]{1,0:T(8,128)(2,1)}, bf16[128,2048]{1,0:T(8,128)(2,1)S(1)}, u32[]{:S(2)}, u32[]{:S(2)}) collective-permute-start(bf16[128,2048]{1,0:T(8,128)(2,1)} %get-tuple-element.111), channel_id=1, source_target_pairs={{0,8},{2,10},{4,12},{6,14},{8,16},{10,18},{12,20},{14,22},{16,24},... | collective-permute-start | bytes 1572872 | tf_op jit(solution)/shard_map/ppermute | solution.py:591
  497.0 29.7 %all-to-all-start.3 = ((f32[16,2,128]{2,1,0:T(2,128)}), f32[16,2,128]{2,1,0:T(2,128)S(1)}, u32[]{:S(2)}, u32[]{:S(2)}) async-start(f32[16,2,128]{2,1,0:T(2,128)} %add_bitcast_fusion), calls=%async_computation.3 | async-start | bytes 32768 | tf_op jit(solution)/shard_map/all_to_all | solution.py:733
  526.8 39.6 %all-to-all-start.10 = ((bf16[4,128,704]{1,2,0:T(8,128)(2,1)}), bf16[4,128,704]{1,2,0:T(8,128)(2,1)S(1)}, u32[]{:S(2)}, u32[]{:S(2)}) async-start(bf16[4,128,704]{1,2,0:T(8,128)(2,1)} %copy_bitcast_fusion.4), calls=%async_computation.15 | async-start | bytes 1441792 | tf_op jit(solution)/shard_map/all_to_all | solution.py:557
  532.5 72.3 %copy-start.27 = (bf16[128,2048]{1,0:T(8,128)(2,1)S(1)}, bf16[128,2048]{1,0:T(8,128)(2,1)}, u32[]{:S(2)}) copy-start(bf16[128,2048]{1,0:T(8,128)(2,1)} %copy-done.26) | copy-start | bytes 1572868
  534.8 70.0 %collective-permute-start.13 = (bf16[128,2048]{1,0:T(8,128)(2,1)}, bf16[128,2048]{1,0:T(8,128)(2,1)}, u32[]{:S(2)}, u32[]{:S(2)}) collective-permute-start(bf16[128,2048]{1,0:T(8,128)(2,1)} %add_convert_fusion.8), channel_id=1, source_target_pairs={{0,8},{2,10},{4,12},{6,14},{8,16},{10,18},{12,20},{14,22},{16,24},... | collective-permute-start | bytes 1572872 | tf_op jit(solution)/shard_map/ppermute | solution.py:591
  566.4 48.3 %all-to-all-start.8 = ((bf16[4,128,704]{1,2,0:T(8,128)(2,1)}), bf16[4,128,704]{1,2,0:T(8,128)(2,1)S(1)}, u32[]{:S(2)}, u32[]{:S(2)}) async-start(bf16[4,128,704]{1,2,0:T(8,128)(2,1)} %copy_bitcast_fusion.6), calls=%async_computation.11 | async-start | bytes 1441792 | tf_op jit(solution)/shard_map/all_to_all | solution.py:557
  573.1 58.5 %collective-permute-start.17 = (bf16[128,2048]{1,0:T(8,128)(2,1)}, bf16[128,2048]{1,0:T(8,128)(2,1)S(1)}, u32[]{:S(2)}, u32[]{:S(2)}) collective-permute-start(bf16[128,2048]{1,0:T(8,128)(2,1)} %get-tuple-element.110), channel_id=1, source_target_pairs={{8,0},{10,2},{12,4},{14,6},{16,8},{18,10},{20,12},{22,14},{24,16},... | collective-permute-start | bytes 1572872 | tf_op jit(solution)/shard_map/ppermute | solution.py:593
  607.2 41.5 %collective-permute-start.14 = (bf16[128,2048]{1,0:T(8,128)(2,1)}, bf16[128,2048]{1,0:T(8,128)(2,1)}, u32[]{:S(2)}, u32[]{:S(2)}) collective-permute-start(bf16[128,2048]{1,0:T(8,128)(2,1)} %add_convert_fusion.7), channel_id=1, source_target_pairs={{0,8},{2,10},{4,12},{6,14},{8,16},{10,18},{12,20},{14,22},{16,24},... | collective-permute-start | bytes 1572872 | tf_op jit(solution)/shard_map/ppermute | solution.py:591
  614.8 43.9 %all-to-all-start.9 = ((bf16[4,128,704]{1,2,0:T(8,128)(2,1)}), bf16[4,128,704]{1,2,0:T(8,128)(2,1)S(1)}, u32[]{:S(2)}, u32[]{:S(2)}) async-start(bf16[4,128,704]{1,2,0:T(8,128)(2,1)} %copy_bitcast_fusion.5), calls=%async_computation.13 | async-start | bytes 1441792 | tf_op jit(solution)/shard_map/all_to_all | solution.py:557
  651.7 3.5 collective-permute-start.18
  651.7 20.3 %collective-permute-start.38 = (f32[128,2048]{1,0:T(8,128)}, f32[128,2048]{1,0:T(8,128)}, u32[]{:S(2)}, u32[]{:S(2)}) collective-permute-start(f32[128,2048]{1,0:T(8,128)} %get-tuple-element.57), channel_id=1, source_target_pairs={{0,1},{1,0},{2,3},{3,2},{4,5},{5,4},{6,7},{7,6},{8,9},{9,8},{10,11... | collective-permute-start | bytes 3145736 | tf_op jit(solution)/shard_map/ppermute | solution.py:436
  658.7 9.3 %all-to-all-start.7 = ((bf16[4,128,256]{2,1,0:T(8,128)(2,1)}), bf16[4,128,256]{2,1,0:T(8,128)(2,1)S(1)}, u32[]{:S(2)}, u32[]{:S(2)}) async-start(bf16[4,128,256]{2,1,0:T(8,128)(2,1)} %bitcast.164), calls=%async_computation.9 | async-start | bytes 524288 | tf_op jit(solution)/shard_map/all_to_all | solution.py:557
  668.0 14.1 %all-to-all-start.5 = ((bf16[4,128,800]{1,2,0:T(8,128)(2,1)}), bf16[4,128,800]{1,2,0:T(8,128)(2,1)S(1)}, u32[]{:S(2)}, u32[]{:S(2)}) async-start(bf16[4,128,800]{1,2,0:T(8,128)(2,1)} %copy_bitcast_fusion), calls=%async_computation.6 | async-start | bytes 1638400 | tf_op jit(solution)/shard_map/all_to_all | solution.py:557
  (53 other events, 450.0 us)
Sparse Core Ops, SparseCore 0:
  61.8 34.8 all-gather.7
  125.6 34.0 all-gather.5
  186.2 34.1 all-gather.9
  265.5 36.8 all-gather.11
  329.4 35.4 all-gather.13
  367.1 35.6 reduce-scatter.13
  405.0 49.9 reduce-scatter.9
  457.3 32.3 reduce-scatter.11
  492.6 33.7 reduce-scatter.7
  528.5 101.8 reduce-scatter.5

commit v3 on v2

--- a/solution.py
+++ b/solution.py
@@ -557,27 +557,33 @@
     return lax.all_to_all(x, "dp", split, concat, tiled=True, axis_index_groups=groups)
 
 
-def gather_along(x, grid, place):
+def tie(*values):
+    return lax.optimization_barrier(values)
+
+
+def gather_along(x, grid, place, beside=()):
     n = grid.outer
     above = below = x
-    from_below, from_above = [], []
-    for _ in range(n - 1):
+    from_below, from_above, done = [], [], []
+    for k in range(n - 1):
         below = lax.ppermute(below, "dp", grid.up)
         above = lax.ppermute(above, "dp", grid.down)
+        extra = beside[k] if k < len(beside) else ()
+        below, above, *extra = tie(below, above, *extra)
         from_below.append(below)
         from_above.append(above)
+        done += extra
     blocks = [x]
     for k in range(1, n):
         blocks.append(jnp.where(place + k < n, from_above[k - 1], from_below[n - 1 - k]))
-    return jnp.concatenate(blocks, axis=0)
-
-
-def gather_tokens(x, grid, place):
-    own = gather_along(x, grid, place)
+    return jnp.concatenate(blocks, axis=0), done
+
+
+def with_other_core(own):
     return jnp.concatenate([own, swap(own)], axis=0)
 
 
-def scatter_tokens(x, grid):
+def scatter_tokens(x, grid, beside=()):
     n = grid.outer
     size = x.shape[0] // (2 * n)
     block = [x[k * size : (k + 1) * size] for k in range(2 * n)]
@@ -586,12 +592,26 @@
     swapped = {k: swap(block[n + k].astype(bf16)) for k in order}
     own = {k: block[k] + swapped[k].astype(f32) for k in order}
     up = down = None
+    done = []
     for k in range(n - 1):
-        send = own[n - 1 - k] if up is None else own[n - 1 - k] + up.astype(f32)
-        up = lax.ppermute(send.astype(bf16), "dp", grid.up)
-        send = own[1 + k] if down is None else own[1 + k] + down.astype(f32)
-        down = lax.ppermute(send.astype(bf16), "dp", grid.down)
-    return own[0], up, down
+        up = own[n - 1 - k] if up is None else own[n - 1 - k] + up.astype(f32)
+        down = own[1 + k] if down is None else own[1 + k] + down.astype(f32)
+        up = lax.ppermute(up.astype(bf16), "dp", grid.up)
+        down = lax.ppermute(down.astype(bf16), "dp", grid.down)
+        extra = beside[k] if k < len(beside) else ()
+        up, down, *extra = tie(up, down, *extra)
+        done += extra
+    return (own[0], up, down), done
+
+
+def plane_gather(x, grid, inner):
+    out = jnp.zeros((INNER,) + x.shape, x.dtype)
+    for k in range(INNER):
+        y = x
+        if k:
+            y = lax.ppermute(x, "dp", [(d, d ^ k) for d in range(grid.dp)])
+        out = lax.dynamic_update_slice_in_dim(out, y[None], inner ^ k, 0)
+    return out.reshape(INNER * x.shape[0], x.shape[1])
 
 
 def on_device(
@@ -612,7 +632,7 @@
 ):
     core = lax.axis_index("head")
     place = lax.axis_index("dp") // INNER
-    width = block_in.shape[1]
+    inner = lax.axis_index("dp") % INNER
 
     def columns(w):
         return exchange(w, 1, 0, grid.cols)
@@ -624,32 +644,27 @@
 
     inputs_f = block_in.astype(f32)
     normed = (inputs_f * rms_scale(inputs_f) * attn_gain).astype(bf16)
-    normed, gate_piece = lax.optimization_barrier((normed, gate_piece))
+    query_pre = nn(normed, w_query)
+    later, query_pre, gate_piece = tie(normed, query_pre, gate_piece)
     full_gate = gather_rows(gate_piece)
-    query_pre = nn(normed, w_query)
-    key_pre = nn(normed, w_key)
-    value_pre = nn(normed, w_value)
-    forget_pre = nn(normed, w_forget)
+    key_pre = nn(later, w_key)
+    value_pre = nn(later, w_value)
+    forget_pre = nn(later, w_forget)
     query = jax.nn.silu(query_pre).astype(bf16)
     key = jax.nn.silu(key_pre).astype(bf16)
     value = jax.nn.silu(value_pre).astype(bf16)
     log_keep = jax.nn.log_sigmoid(forget_pre) * tau_inv
-    query, up_piece = lax.optimization_barrier((query, up_piece))
+    key, value, log_keep, up_piece = tie(key, value, log_keep, up_piece)
     full_up = gather_rows(up_piece)
     mixed, *saved = attend_forward(query, key, value, log_keep, doc_starts)
 
     branch_other = swap(nt(half_of(mixed, 1 - core), w_output))
     branch_mine = nt(half_of(mixed, core), w_output)
+    branch_mine, down_piece = tie(branch_mine, down_piece)
+    full_down = gather_rows(down_piece)
     hidden, normed_two = second_norm(block_in, branch_mine, branch_other, mlp_gain, core, grid)
-    normed_two, down_piece = lax.optimization_barrier((normed_two, down_piece))
-    full_down = gather_rows(down_piece)
-    tokens = gather_tokens(normed_two, grid, place)
-    cot_rows = cotangent_rows(out_grad, core, grid)
-    cot_rows, tokens = lax.optimization_barrier((cot_rows, tokens))
-    cot_all = gather_tokens(cot_rows, grid, place)
-
     def plane_tokens(half):
-        own = lax.all_gather(half, "dp", axis=0, tiled=True, axis_index_groups=grid.rows)
+        own = plane_gather(half, grid, inner)
         return own, swap(own)
 
     def plane_columns(parts):
@@ -663,53 +678,81 @@
             for c in (core, 1 - core)
         )
 
-    def plane_grad(left, right):
-        g = (tn(left[0], right[0]) + tn(left[1], right[1])).astype(bf16)
-        g = lax.psum_scatter(
+    def plane_product(left, right):
+        return (tn(left[0], right[0]) + tn(left[1], right[1])).astype(bf16)
+
+    def plane_sum(g):
+        return lax.psum_scatter(
             g, "dp", scatter_dimension=0, tiled=True, axis_index_groups=grid.cols
         )
+
+    def from_plane(g):
         size = g.shape[1]
-        g = exchange(g, 0, 1, grid.rows).reshape(-1, INNER, size)
-        return g.astype(f32)
-
+        return exchange(g, 0, 1, grid.rows).reshape(-1, INNER, size).astype(f32)
+
+    cot_rows = cotangent_rows(out_grad, core, grid)
+    own, (cot_rows, full_gate, full_up) = gather_along(
+        normed_two, grid, place, ((cot_rows,), (full_gate,), (full_up,))
+    )
+    tokens = with_other_core(own)
+    own, (gate_act, up_act, full_down) = gather_along(
+        cot_rows, grid, place, ((nn(tokens, full_gate),), (nn(tokens, full_up),), (full_down,))
+    )
+    cot_all = with_other_core(own)
+
+    def scatter_rows(g):
+        return lax.psum_scatter(
+            g, "dp", scatter_dimension=0, tiled=True, axis_index_groups=grid.laps
+        )
+
+    mixed_plane = plane_columns([mixed])
     normed_plane = plane_tokens(half_of(normed, core))
-    mixed_plane = plane_columns([mixed])
-
-    gate_act = nn(tokens, full_gate)
-    up_act = nn(tokens, full_up)
     inner_grad = nn(cot_all, full_down)
     gate_grad = (inner_grad * up_act * silu_slope(gate_act)).astype(bf16)
     up_grad = (inner_grad * jax.nn.silu(gate_act)).astype(bf16)
     inner_act = (jax.nn.silu(gate_act) * up_act).astype(bf16)
-    back_parts = scatter_tokens(nt(gate_grad, full_gate) + nt(up_grad, full_up), grid)
+    back_parts, (down_rows, gate_rows, mixed_own, mixed_rest, up_rows, *normed_plane) = scatter_tokens(
+        nt(gate_grad, full_gate) + nt(up_grad, full_up),
+        grid,
+        (
+            (tn(cot_all, inner_act).astype(bf16),),
+            (tn(tokens, gate_grad).astype(bf16), *mixed_plane),
+            (tn(tokens, up_grad).astype(bf16), *normed_plane),
+        ),
+    )
+    mixed_plane = (mixed_own, mixed_rest)
+    down_rows, gate_rows, up_rows = (scatter_rows(g) for g in (down_rows, gate_rows, up_rows))
     hidden_grad, low_half, mlp_gain_part = second_norm_back(
         out_grad, hidden, mlp_gain, back_parts, core, grid
     )
     branch_grad = join(low_half, swap(low_half), core)
     mixed_grad = nn(branch_grad, w_output).astype(bf16)
-
-    def scatter_rows(g):
-        return lax.psum_scatter(
-            g.astype(bf16), "dp", scatter_dimension=0, tiled=True, axis_index_groups=grid.laps
-        )
-
-    down_rows = scatter_rows(tn(cot_all, inner_act))
-    gate_rows = scatter_rows(tn(tokens, gate_grad))
-    up_rows = scatter_rows(tn(tokens, up_grad))
-    out_parts = scatter_tokens(nt(inner_act, full_down), grid)
-    result = block_result(block_in, hidden, out_parts, core, grid)
-    result = join(result, swap(result), core)
-
-    output_sum = plane_grad(plane_tokens(low_half), mixed_plane)
-    query_grad, key_grad, value_grad, log_grad = attend_backward(
-        query, key, value, log_keep, doc_starts, saved, mixed_grad
-    )
+    mixed_grad, down_rows, later_act = tie(mixed_grad, down_rows, inner_act)
+    saved_grads = attend_backward(query, key, value, log_keep, doc_starts, saved, mixed_grad)
+    query_grad, key_grad, value_grad, log_grad = saved_grads
     query_pre_grad = (query_grad * silu_slope(query_pre)).astype(bf16)
     key_pre_grad = (key_grad * silu_slope(key_pre)).astype(bf16)
     value_pre_grad = (value_grad * silu_slope(value_pre)).astype(bf16)
     forget_pre_grad = (log_grad * tau_inv * jax.nn.sigmoid(-forget_pre)).astype(bf16)
     pre_grads = (query_pre_grad, key_pre_grad, value_pre_grad, forget_pre_grad)
-    sums = plane_grad(normed_plane, plane_columns(pre_grads))
+
+    query_pre_grad, gate_rows = tie(query_pre_grad, gate_rows)
+    pre_grads = (query_pre_grad,) + pre_grads[1:]
+    out_parts, (query_pre_grad, *grad_columns) = scatter_tokens(
+        nt(later_act, full_down), grid, ((query_pre_grad,), tuple(plane_columns(pre_grads)))
+    )
+    pre_grads = (query_pre_grad,) + pre_grads[1:]
+    output_grad = plane_product(plane_tokens(low_half), mixed_plane)
+    pre_grad, up_rows, output_grad = tie(
+        plane_product(normed_plane, grad_columns), up_rows, output_grad
+    )
+    output_sum = from_plane(plane_sum(output_grad))
+    sums = plane_sum(pre_grad)
+
+    result = block_result(block_in, hidden, out_parts, core, grid)
+    result = join(result, swap(result), core)
+
+    sums = from_plane(sums)
     ends = [0]
     for g in pre_grads:
         ends.append(ends[-1] + g.shape[1] // INNER)

time: 699 us -> 703 us (level)
  the two profiles are of different devices: /device:TPU:16 before, /device:TPU:0 now
where the time goes in v3:
time: 703 us; the launch traced here: 689 us
  waiting for transfers between devices  298 us (42%)
  matrix products  98.7 us (14%)
  starting transfers between devices  93.6 us (13%)
  local copies, waits for them, and re-layouts  81.1 us (12%)
  other arithmetic  48.7 us (7%)
  Pallas kernels  31.9 us (5%)
  blocking collectives  21.7 us (3%)
  between operations  15.4 us (2%)
    all_to_all x9, waiting for transfers between devices, exchange(): lax.all_to_all(x, 'dp', split, concat, tiled=True, axis_index_groups=groups)  87.9 us
    ppermute x6, waiting for transfers between devices, plane_gather(): y = lax.ppermute(x, 'dp', [(d, d ^ k) for d in range(grid.dp)])  71.3 us
    dot_general x13, matrix products, nt(): lax.dot_general(a.astype(bf16), b.astype(bf16), (((1,), (1,)), ((), ())),...  43.3 us
    ppermute x6, waiting for transfers between devices, scatter_tokens(): up = lax.ppermute(up.astype(bf16), 'dp', grid.up)  38.4 us
    all_to_all x9, starting transfers between devices, exchange(): lax.all_to_all(x, 'dp', split, concat, tiled=True, axis_index_groups=groups)  37.1 us
    ppermute x6, waiting for transfers between devices, gather_along(): below = lax.ppermute(below, 'dp', grid.up)  30.9 us
    dot_general x8, matrix products, nn(): return jnp.dot(a.astype(bf16), b.astype(bf16), preferred_element_type=f32)  30.3 us
    ppermute x6, waiting for transfers between devices, scatter_tokens(): down = lax.ppermute(down.astype(bf16), 'dp', grid.down)  25.2 us
  transfers between devices with their start and end apart: 66, of which 42 were waited for; matrix products, arithmetic and copies ran while one was open for 27% of the time, Pallas kernels for 5%

profile of v3, /device:TPU:0, one launch (start us, length us, event | category | flops | bytes accessed | tf_op | source)
XLA Modules:
  0.0 689.4 jit_solution(2030089653666588110)
XLA Ops:
  9.6 6.3 all-to-all-start
  20.0 14.7 %all-to-all-done = bf16[128,4,704]{0,2,1:T(8,128)(2,1)} async-done(((bf16[128,4,704]{0,2,1:T(8,128)(2,1)}), bf16[128,4,704]{0,2,1:T(8,128)(2,1)}, u32[]{:S(2)}, u32[]{:S(2)}) %all-to-all-start) | async-done | bytes 720928 | tf_op jit(solution)/shard_map/all_to_all | solution.py:557
  39.1 21.7 %all_to_all.156 = bf16[128,4,704]{0,2,1:T(8,128)(2,1)S(1)} all-to-all(bf16[128,4,704]{0,2,1:T(8,128)(2,1)} %bitcast.172), channel_id=1, replica_groups={{0,8,16,24},{2,10,18,26},{4,12,20,28},{6,14,22,30},{1,9,17,25},{3,11,19..., dimensions={1} | all-to-all | bytes 1441792 | tf_op jit(solution)/shard_map/all_to_all | solution.py:557
  62.9 4.8 multiply_convert_fusion.7
  72.4 4.2 all-to-all-start.2
  77.9 6.5 slot_forward.1
  84.4 4.9 fusion.17
  89.3 5.4 all-to-all-done.2
  96.7 4.7 fusion.19.mine_ref
  110.0 7.8 %collective-permute-done.1 = bf16[128,2048]{1,0:T(8,128)(2,1)S(1)} collective-permute-done((bf16[128,2048]{1,0:T(8,128)(2,1)}, bf16[128,2048]{1,0:T(8,128)(2,1)S(1)}, u32[]{:S(2)}, u32[]{:S(2)}) %collective-permute-start.1) | collective-permute-done | bytes 524320 | tf_op jit(solution)/shard_map/ppermute | solution.py:569
  117.8 4.0 collective-permute-done.2
  125.5 7.5 %collective-permute-done.5 = bf16[128,2048]{1,0:T(8,128)(2,1)S(1)} collective-permute-done((bf16[128,2048]{1,0:T(8,128)(2,1)S(1)}, bf16[128,2048]{1,0:T(8,128)(2,1)S(1)}, u32[]{:S(2)}, u32[]{:S(2)}) %collective-permute-start.5) | collective-permute-done | bytes 524320 | tf_op jit(solution)/shard_map/ppermute | solution.py:569
  146.9 4.9 collective-permute-done.8
  167.3 7.2 %fusion.41 = f32[1024,704]{0,1:T(8,128)} fusion(bf16[1024,2048]{1,0:T(8,128)(2,1)} %constant_dynamic-update-slice_fusion, bf16[2048,704]{0,1:T(8,128)(2,1)S(1)} %copy-done.12), kind=kOutput, calls=%fused_computation.142 | convolution fusion | flops 2952790016 | bytes 9961472 | tf_op jit(solution)/shard_map/dot_general | solution.py:19
  180.9 4.9 fusion.42
  185.8 4.2 collective-permute-done.10
  190.0 5.0 collective-permute-done.11
  198.9 8.0 %collective-permute-done.12 = bf16[128,2048]{1,0:T(8,128)(2,1)S(1)} collective-permute-done((bf16[128,2048]{1,0:T(8,128)(2,1)}, bf16[128,2048]{1,0:T(8,128)(2,1)S(1)}, u32[]{:S(2)}, u32[]{:S(2)}) %collective-permute-start.12) | collective-permute-done | bytes 524320 | tf_op jit(solution)/shard_map/ppermute | solution.py:569
  217.4 4.1 collective-permute-done.14
  228.2 3.5 fusion.44
  231.7 3.6 fusion.38
  244.3 4.5 convolution_convert_fusion.2
  248.8 5.3 collective-permute-done.19
  254.0 4.9 collective-permute-done.20
  259.9 3.7 all-to-all-start.3
  263.6 14.8 %all-to-all-done.3 = bf16[256,4,256]{2,0,1:T(8,128)(2,1)S(1)} async-done(((bf16[256,4,256]{2,0,1:T(8,128)(2,1)}), bf16[256,4,256]{2,0,1:T(8,128)(2,1)S(1)}, u32[]{:S(2)}, u32[]{:S(2)}) %all-to-all-start.3) | async-done | bytes 524320 | tf_op jit(solution)/shard_map/all_to_all | solution.py:557
  286.0 4.6 convolution_convert_fusion.1
  290.6 4.7 collective-permute-done.21
  295.3 4.7 collective-permute-done.22
  306.1 22.5 %collective-permute-done.25 = bf16[128,2048]{1,0:T(8,128)(2,1)S(1)} collective-permute-done((bf16[128,2048]{1,0:T(8,128)(2,1)}, bf16[128,2048]{1,0:T(8,128)(2,1)S(1)}, u32[]{:S(2)}, u32[]{:S(2)}) %collective-permute-start.25) | collective-permute-done | bytes 524320 | tf_op jit(solution)/shard_map/ppermute | solution.py:612
  332.6 17.8 %collective-permute-done.27 = bf16[128,2048]{1,0:T(8,128)(2,1)S(1)} collective-permute-done((bf16[128,2048]{1,0:T(8,128)(2,1)}, bf16[128,2048]{1,0:T(8,128)(2,1)S(1)}, u32[]{:S(2)}, u32[]{:S(2)}) %collective-permute-start.27) | collective-permute-done | bytes 524320 | tf_op jit(solution)/shard_map/ppermute | solution.py:612
  351.7 4.6 collective-permute-done.15
  356.3 3.7 add_convert_fusion.5
  362.7 4.5 convolution_convert_fusion
  367.3 5.8 collective-permute-done.23.refs_1_
  373.1 4.1 collective-permute-done.24.refs_2_
  378.0 3.9 second_norm_back.1
  388.8 11.0 %collective-permute-done.44 = bf16[128,2048]{1,0:T(8,128)(2,1)} collective-permute-done((bf16[128,2048]{1,0:T(8,128)(2,1)}, bf16[128,2048]{1,0:T(8,128)(2,1)}, u32[]{:S(2)}, u32[]{:S(2)}) %collective-permute-start.44) | collective-permute-done | bytes 524320 | tf_op jit(solution)/shard_map/ppermute | solution.py:612
  403.0 16.7 %collective-permute-done.46 = bf16[128,2048]{1,0:T(8,128)(2,1)} collective-permute-done((bf16[128,2048]{1,0:T(8,128)(2,1)}, bf16[128,2048]{1,0:T(8,128)(2,1)}, u32[]{:S(2)}, u32[]{:S(2)}) %collective-permute-start.46) | collective-permute-done | bytes 524320 | tf_op jit(solution)/shard_map/ppermute | solution.py:612
  426.1 9.2 %fusion.39 = (bf16[1024,2048]{1,0:T(8,128)(2,1)S(1)}, f32[1024,2048]{1,0:T(8,128)}) fusion(bf16[1024,704]{0,1:T(8,128)(2,1)} %copy-done.25, bf16[2048,704]{0,1:T(8,128)(2,1)} %all-gather.8.cloned.1.call-done), kind=kOutput, calls=%fused_computation.140 | convolution fusion | flops 2954887168 | bytes 16908288 | tf_op jit(solution)/shard_map/dot_general | solution.py:23
  437.2 9.7 %slot_backward.1 = (f32[256,1024]{1,0:T(8,128)}, f32[256,1024]{1,0:T(8,128)}, f32[256,1024]{1,0:T(8,128)}, f32[256,128]{1,0:T(8,128)}) custom-call(s32[1,3]{1,0:T(1,128)} %starts_ref.3, bf16[256,1024]{1,0:T(8,128)(2,1)} %multiply_convert_fusion.8.q_ref, bf16[256,1024]{1,0:T(8,128)(2,1)} %get-tuple-element.87.k_ref, ...), custom_call_target="tpu_custom_call" | custom-call | flops 12000000000 | bytes 8000000 | tf_op jit(solution)/shard_map/slot_backward/pallas_call | solution.py:369
  461.3 4.4 all-to-all-start.4
  476.5 5.6 collective-permute-done.34
  482.1 5.1 collective-permute-done.35
  503.0 4.5 collective-permute-done.37
  507.4 3.6 fusion.46
  511.1 3.6 add_convert_fusion
  516.8 4.4 all-to-all-start.10
  521.2 3.8 fusion.10
  535.5 18.8 %all-to-all-done.10 = bf16[4,128,704]{1,2,0:T(8,128)(2,1)} async-done(((bf16[4,128,704]{1,2,0:T(8,128)(2,1)}), bf16[4,128,704]{1,2,0:T(8,128)(2,1)}, u32[]{:S(2)}, u32[]{:S(2)}) %all-to-all-start.10) | async-done | bytes 720928 | tf_op jit(solution)/shard_map/all_to_all | solution.py:557
  554.3 3.5 all-to-all-start.8
  557.8 4.0 convolution_add_fusion.6
  563.1 3.9 first_norm_back.1
  570.3 25.3 %all-to-all-done.8 = bf16[4,128,704]{1,2,0:T(8,128)(2,1)S(1)} async-done(((bf16[4,128,704]{1,2,0:T(8,128)(2,1)}), bf16[4,128,704]{1,2,0:T(8,128)(2,1)S(1)}, u32[]{:S(2)}, u32[]{:S(2)}) %all-to-all-start.8) | async-done | bytes 720928 | tf_op jit(solution)/shard_map/all_to_all | solution.py:557
  595.5 3.8 all-to-all-start.5
  600.3 6.7 all-to-all-done.5
  607.0 3.5 all-to-all-start.9
  610.5 4.3 add_convert_fusion.1
  614.8 4.7 collective-permute-start.38
  629.0 17.0 %collective-permute-done.38.refs_1_ = bf16[128,2048]{1,0:T(8,128)(2,1)} collective-permute-done((bf16[128,2048]{1,0:T(8,128)(2,1)}, bf16[128,2048]{1,0:T(8,128)(2,1)}, u32[]{:S(2)}, u32[]{:S(2)}) %collective-permute-start.38) | collective-permute-done | bytes 524320 | tf_op jit(solution)/shard_map/ppermute | solution.py:599
  654.5 3.6 all-to-all-start.7
  660.3 3.9 all-to-all-done.7
  664.2 3.5 all-to-all-start.6
  673.4 5.1 all-to-all-done.6
  (321 shorter events, 228.8 us)
Async XLA Ops:
  9.6 25.2 %all-to-all-start = ((bf16[128,4,704]{0,2,1:T(8,128)(2,1)}), bf16[128,4,704]{0,2,1:T(8,128)(2,1)}, u32[]{:S(2)}, u32[]{:S(2)}) async-start(bf16[128,4,704]{0,2,1:T(8,128)(2,1)} %bitcast.1), calls=%async_computation | async-start | bytes 1441792 | tf_op jit(solution)/shard_map/all_to_all | solution.py:557
  15.9 121.3 %all-gather.4.cloned.1.call-start = ((), (), s32[]{:S(2)}) async-start(), calls=%async_computation.16 | async-start | bytes 3604480 | tf_op jit(solution)/shard_map/all_gather | solution.py:641
  36.8 106.8 %all-gather.6.cloned.1.call-start = ((), (), s32[]{:S(2)}) async-start(), calls=%async_computation.17 | async-start | bytes 3604480 | tf_op jit(solution)/shard_map/all_gather | solution.py:641
  72.4 22.3 %all-to-all-start.2 = ((bf16[128,4,704]{0,2,1:T(8,128)(2,1)}), bf16[128,4,704]{0,2,1:T(8,128)(2,1)}, u32[]{:S(2)}, u32[]{:S(2)}) async-start(bf16[128,4,704]{0,2,1:T(8,128)(2,1)} %bitcast.171), calls=%async_computation.2 | async-start | bytes 1441792 | tf_op jit(solution)/shard_map/all_to_all | solution.py:557
  76.6 122.3 %all-gather.8.cloned.1.call-start = ((), (), s32[]{:S(2)}) async-start(), calls=%async_computation.18 | async-start | bytes 3604480 | tf_op jit(solution)/shard_map/all_gather | solution.py:641
  89.3 12.2 %collective-permute-start = (f32[128,2048]{1,0:T(8,128)}, f32[128,2048]{1,0:T(8,128)S(1)}, u32[]{:S(2)}, u32[]{:S(2)}) collective-permute-start(f32[128,2048]{1,0:T(8,128)} %fusion.17), channel_id=1, source_target_pairs={{0,1},{1,0},{2,3},{3,2},{4,5},{5,4},{6,7},{7,6},{8,9},{9,8},{10,11... | collective-permute-start | bytes 3145736 | tf_op jit(solution)/shard_map/ppermute | solution.py:436
  105.5 12.3 %collective-permute-start.1 = (bf16[128,2048]{1,0:T(8,128)(2,1)}, bf16[128,2048]{1,0:T(8,128)(2,1)S(1)}, u32[]{:S(2)}, u32[]{:S(2)}) collective-permute-start(bf16[128,2048]{1,0:T(8,128)(2,1)} %get-tuple-element.93), channel_id=1, source_target_pairs={{0,8},{2,10},{4,12},{6,14},{8,16},{10,18},{12,20},{14,22},{16,24},... | collective-permute-start | bytes 1572872 | tf_op jit(solution)/shard_map/ppermute | solution.py:569
  106.8 15.1 %collective-permute-start.2 = (bf16[128,2048]{1,0:T(8,128)(2,1)}, bf16[128,2048]{1,0:T(8,128)(2,1)S(1)}, u32[]{:S(2)}, u32[]{:S(2)}) collective-permute-start(bf16[128,2048]{1,0:T(8,128)(2,1)} %get-tuple-element.93), channel_id=1, source_target_pairs={{8,0},{10,2},{12,4},{14,6},{16,8},{18,10},{20,12},{22,14},{24,16},... | collective-permute-start | bytes 1572872 | tf_op jit(solution)/shard_map/ppermute | solution.py:570
  121.9 11.2 %collective-permute-start.5 = (bf16[128,2048]{1,0:T(8,128)(2,1)S(1)}, bf16[128,2048]{1,0:T(8,128)(2,1)S(1)}, u32[]{:S(2)}, u32[]{:S(2)}) collective-permute-start(bf16[128,2048]{1,0:T(8,128)(2,1)S(1)} %collective-permute-done.1), channel_id=1, source_target_pairs={{0,8},{2,10},{4,12},{6,14},{8,16},{10,18},{12,20},{14,22},{16,24},... | collective-permute-start | bytes 1572872 | tf_op jit(solution)/shard_map/ppermute | solution.py:569
  124.2 13.1 %collective-permute-start.6 = (bf16[128,2048]{1,0:T(8,128)(2,1)S(1)}, bf16[128,2048]{1,0:T(8,128)(2,1)}, u32[]{:S(2)}, u32[]{:S(2)}) collective-permute-start(bf16[128,2048]{1,0:T(8,128)(2,1)S(1)} %collective-permute-done.2), channel_id=1, source_target_pairs={{8,0},{10,2},{12,4},{14,6},{16,8},{18,10},{20,12},{22,14},{24,16},... | collective-permute-start | bytes 1572872 | tf_op jit(solution)/shard_map/ppermute | solution.py:570
  137.3 9.6 %collective-permute-start.7 = (bf16[128,2048]{1,0:T(8,128)(2,1)}, bf16[128,2048]{1,0:T(8,128)(2,1)}, u32[]{:S(2)}, u32[]{:S(2)}) collective-permute-start(bf16[128,2048]{1,0:T(8,128)(2,1)} %copy-done.40), channel_id=1, source_target_pairs={{0,8},{2,10},{4,12},{6,14},{8,16},{10,18},{12,20},{14,22},{16,24},... | collective-permute-start | bytes 1572872 | tf_op jit(solution)/shard_map/ppermute | solution.py:569
  140.4 11.4 %collective-permute-start.8 = (bf16[128,2048]{1,0:T(8,128)(2,1)}, bf16[128,2048]{1,0:T(8,128)(2,1)}, u32[]{:S(2)}, u32[]{:S(2)}) collective-permute-start(bf16[128,2048]{1,0:T(8,128)(2,1)} %collective-permute-done.6), channel_id=1, source_target_pairs={{8,0},{10,2},{12,4},{14,6},{16,8},{18,10},{20,12},{22,14},{24,16},... | collective-permute-start | bytes 1572872 | tf_op jit(solution)/shard_map/ppermute | solution.py:570
  159.4 4.5 collective-permute-start.9
  159.4 266.7 %reduce-scatter.6.cloned.1.call-start = ((), (), s32[]{:S(2)}) async-start(), calls=%async_computation.19 | async-start | bytes 3604480 | tf_op jit(solution)/shard_map/reduce_scatter | solution.py:704
  159.5 15.0 %collective-permute-start.3 = (bf16[128,2048]{1,0:T(8,128)(2,1)S(1)}, bf16[128,2048]{1,0:T(8,128)(2,1)S(1)}, u32[]{:S(2)}, u32[]{:S(2)}) collective-permute-start(bf16[128,2048]{1,0:T(8,128)(2,1)S(1)} %copy-done.8), channel_id=1, source_target_pairs={{0,8},{2,10},{4,12},{6,14},{8,16},{10,18},{12,20},{14,22},{16,24},... | collective-permute-start | bytes 1572872 | tf_op jit(solution)/shard_map/ppermute | solution.py:569
  161.1 16.2 %collective-permute-start.4 = (bf16[128,2048]{1,0:T(8,128)(2,1)S(1)}, bf16[128,2048]{1,0:T(8,128)(2,1)S(1)}, u32[]{:S(2)}, u32[]{:S(2)}) collective-permute-start(bf16[128,2048]{1,0:T(8,128)(2,1)S(1)} %copy-done.8), channel_id=1, source_target_pairs={{8,0},{10,2},{12,4},{14,6},{16,8},{18,10},{20,12},{22,14},{24,16},... | collective-permute-start | bytes 1572872 | tf_op jit(solution)/shard_map/ppermute | solution.py:570
  177.3 12.7 %collective-permute-start.10 = (bf16[128,2048]{1,0:T(8,128)(2,1)S(1)}, bf16[128,2048]{1,0:T(8,128)(2,1)}, u32[]{:S(2)}, u32[]{:S(2)}) collective-permute-start(bf16[128,2048]{1,0:T(8,128)(2,1)S(1)} %collective-permute-done.3), channel_id=1, source_target_pairs={{0,8},{2,10},{4,12},{6,14},{8,16},{10,18},{12,20},{14,22},{16,24},... | collective-permute-start | bytes 1572872 | tf_op jit(solution)/shard_map/ppermute | solution.py:569
  179.6 15.4 %collective-permute-start.11 = (bf16[128,2048]{1,0:T(8,128)(2,1)S(1)}, bf16[128,2048]{1,0:T(8,128)(2,1)}, u32[]{:S(2)}, u32[]{:S(2)}) collective-permute-start(bf16[128,2048]{1,0:T(8,128)(2,1)S(1)} %collective-permute-done.4), channel_id=1, source_target_pairs={{8,0},{10,2},{12,4},{14,6},{16,8},{18,10},{20,12},{22,14},{24,16},... | collective-permute-start | bytes 1572872 | tf_op jit(solution)/shard_map/ppermute | solution.py:570
  195.0 11.9 %collective-permute-start.12 = (bf16[128,2048]{1,0:T(8,128)(2,1)}, bf16[128,2048]{1,0:T(8,128)(2,1)S(1)}, u32[]{:S(2)}, u32[]{:S(2)}) collective-permute-start(bf16[128,2048]{1,0:T(8,128)(2,1)} %collective-permute-done.10), channel_id=1, source_target_pairs={{0,8},{2,10},{4,12},{6,14},{8,16},{10,18},{12,20},{14,22},{16,24},... | collective-permute-start | bytes 1572872 | tf_op jit(solution)/shard_map/ppermute | solution.py:569
  196.4 14.7 %collective-permute-start.13 = (bf16[128,2048]{1,0:T(8,128)(2,1)}, bf16[128,2048]{1,0:T(8,128)(2,1)}, u32[]{:S(2)}, u32[]{:S(2)}) collective-permute-start(bf16[128,2048]{1,0:T(8,128)(2,1)} %collective-permute-done.11), channel_id=1, source_target_pairs={{8,0},{10,2},{12,4},{14,6},{16,8},{18,10},{20,12},{22,14},{24,16},... | collective-permute-start | bytes 1572872 | tf_op jit(solution)/shard_map/ppermute | solution.py:570
  217.3 4.2 collective-permute-start.14
  236.9 2.5 collective-permute-start.18
  240.7 13.3 %collective-permute-start.19 = (bf16[128,2048]{1,0:T(8,128)(2,1)}, bf16[128,2048]{1,0:T(8,128)(2,1)}, u32[]{:S(2)}, u32[]{:S(2)}) collective-permute-start(bf16[128,2048]{1,0:T(8,128)(2,1)} %get-tuple-element.221), channel_id=1, source_target_pairs={{0,8},{2,10},{4,12},{6,14},{8,16},{10,18},{12,20},{14,22},{16,24},... | collective-permute-start | bytes 1572872 | tf_op jit(solution)/shard_map/ppermute | solution.py:599
  242.8 16.2 %collective-permute-start.20 = (bf16[128,2048]{1,0:T(8,128)(2,1)}, bf16[128,2048]{1,0:T(8,128)(2,1)}, u32[]{:S(2)}, u32[]{:S(2)}) collective-permute-start(bf16[128,2048]{1,0:T(8,128)(2,1)} %get-tuple-element.220), channel_id=1, source_target_pairs={{8,0},{10,2},{12,4},{14,6},{16,8},{18,10},{20,12},{22,14},{24,16},... | collective-permute-start | bytes 1572872 | tf_op jit(solution)/shard_map/ppermute | solution.py:600
  259.0 20.2 %collective-permute-start.17 = (bf16[128,2048]{1,0:T(8,128)(2,1)}, bf16[128,2048]{1,0:T(8,128)(2,1)}, u32[]{:S(2)}, u32[]{:S(2)}) collective-permute-start(bf16[128,2048]{1,0:T(8,128)(2,1)} %get-tuple-element.229), channel_id=1, source_target_pairs={{0,1},{1,0},{2,3},{3,2},{4,5},{5,4},{6,7},{7,6},{8,9},{9,8},{10,11... | collective-permute-start | bytes 1572872 | tf_op jit(solution)/shard_map/ppermute | solution.py:436
  259.9 18.4 %all-to-all-start.3 = ((bf16[256,4,256]{2,0,1:T(8,128)(2,1)}), bf16[256,4,256]{2,0,1:T(8,128)(2,1)S(1)}, u32[]{:S(2)}, u32[]{:S(2)}) async-start(bf16[256,4,256]{2,0,1:T(8,128)(2,1)} %bitcast.180), calls=%async_computation.3 | async-start | bytes 1048576 | tf_op jit(solution)/shard_map/all_to_all | solution.py:557
  263.5 193.1 %reduce-scatter.8.cloned.1.call-start = ((), (), s32[]{:S(2)}) async-start(), calls=%async_computation.20 | async-start | bytes 3604480 | tf_op jit(solution)/shard_map/reduce_scatter | solution.py:704
  282.6 12.7 %collective-permute-start.21 = (bf16[128,2048]{1,0:T(8,128)(2,1)}, bf16[128,2048]{1,0:T(8,128)(2,1)}, u32[]{:S(2)}, u32[]{:S(2)}) collective-permute-start(bf16[128,2048]{1,0:T(8,128)(2,1)} %get-tuple-element.211), channel_id=1, source_target_pairs={{0,8},{2,10},{4,12},{6,14},{8,16},{10,18},{12,20},{14,22},{16,24},... | collective-permute-start | bytes 1572872 | tf_op jit(solution)/shard_map/ppermute | solution.py:599
  284.7 15.3 %collective-permute-start.22 = (bf16[128,2048]{1,0:T(8,128)(2,1)S(1)}, bf16[128,2048]{1,0:T(8,128)(2,1)}, u32[]{:S(2)}, u32[]{:S(2)}) collective-permute-start(bf16[128,2048]{1,0:T(8,128)(2,1)S(1)} %get-tuple-element.210), channel_id=1, source_target_pairs={{8,0},{10,2},{12,4},{14,6},{16,8},{18,10},{20,12},{22,14},{24,16},... | collective-permute-start | bytes 1572872 | tf_op jit(solution)/shard_map/ppermute | solution.py:600
  300.1 214.7 %reduce-scatter.10.cloned.1.call-start = ((), (), s32[]{:S(2)}) async-start(), calls=%async_computation.21 | async-start | bytes 3604480 | tf_op jit(solution)/shard_map/reduce_scatter | solution.py:704
  302.6 26.0 %collective-permute-start.25 = (bf16[128,2048]{1,0:T(8,128)(2,1)}, bf16[128,2048]{1,0:T(8,128)(2,1)S(1)}, u32[]{:S(2)}, u32[]{:S(2)}) collective-permute-start(bf16[128,2048]{1,0:T(8,128)(2,1)} %get-tuple-element.195), channel_id=1, source_target_pairs={{0,2},{2,0},{4,6},{6,4},{8,10},{10,8},{12,14},{14,12},{16,18},{18,... | collective-permute-start | bytes 1572872 | tf_op jit(solution)/shard_map/ppermute | solution.py:612
  304.0 27.8 %collective-permute-start.26 = (bf16[128,2048]{1,0:T(8,128)(2,1)}, bf16[128,2048]{1,0:T(8,128)(2,1)S(1)}, u32[]{:S(2)}, u32[]{:S(2)}) collective-permute-start(bf16[128,2048]{1,0:T(8,128)(2,1)} %get-tuple-element.195), channel_id=1, source_target_pairs={{0,4},{2,6},{4,0},{6,2},{8,12},{10,14},{12,8},{14,10},{16,20},{18,... | collective-permute-start | bytes 1572872 | tf_op jit(solution)/shard_map/ppermute | solution.py:612
  304.4 46.0 %collective-permute-start.27 = (bf16[128,2048]{1,0:T(8,128)(2,1)}, bf16[128,2048]{1,0:T(8,128)(2,1)S(1)}, u32[]{:S(2)}, u32[]{:S(2)}) collective-permute-start(bf16[128,2048]{1,0:T(8,128)(2,1)} %get-tuple-element.195), channel_id=1, source_target_pairs={{0,6},{2,4},{4,2},{6,0},{8,14},{10,12},{12,10},{14,8},{16,22},{18,... | collective-permute-start | bytes 1572872 | tf_op jit(solution)/shard_map/ppermute | solution.py:612
  351.2 16.1 %collective-permute-start.28 = (bf16[512,2048]{1,0:T(8,128)(2,1)}, bf16[512,2048]{1,0:T(8,128)(2,1)}, u32[]{:S(2)}, u32[]{:S(2)}) collective-permute-start(bf16[512,2048]{1,0:T(8,128)(2,1)} %bitcast.177), channel_id=1, source_target_pairs={{0,1},{1,0},{2,3},{3,2},{4,5},{5,4},{6,7},{7,6},{8,9},{9,8},{10,11... | collective-permute-start | bytes 6291464 | tf_op jit(solution)/shard_map/ppermute | solution.py:436
  351.2 5.1 collective-permute-start.15
  360.1 13.0 %collective-permute-start.23 = (bf16[128,2048]{1,0:T(8,128)(2,1)S(1)}, bf16[128,2048]{1,0:T(8,128)(2,1)S(1)}, u32[]{:S(2)}, u32[]{:S(2)}) collective-permute-start(bf16[128,2048]{1,0:T(8,128)(2,1)S(1)} %get-tuple-element.218), channel_id=1, source_target_pairs={{0,8},{2,10},{4,12},{6,14},{8,16},{10,18},{12,20},{14,22},{16,24},... | collective-permute-start | bytes 1572872 | tf_op jit(solution)/shard_map/ppermute | solution.py:599
  361.4 15.9 %collective-permute-start.24 = (bf16[128,2048]{1,0:T(8,128)(2,1)S(1)}, bf16[128,2048]{1,0:T(8,128)(2,1)S(1)}, u32[]{:S(2)}, u32[]{:S(2)}) collective-permute-start(bf16[128,2048]{1,0:T(8,128)(2,1)S(1)} %get-tuple-element.217), channel_id=1, source_target_pairs={{8,0},{10,2},{12,4},{14,6},{16,8},{18,10},{20,12},{22,14},{24,16},... | collective-permute-start | bytes 1572872 | tf_op jit(solution)/shard_map/ppermute | solution.py:600
  382.0 17.8 %collective-permute-start.44 = (bf16[128,2048]{1,0:T(8,128)(2,1)}, bf16[128,2048]{1,0:T(8,128)(2,1)}, u32[]{:S(2)}, u32[]{:S(2)}) collective-permute-start(bf16[128,2048]{1,0:T(8,128)(2,1)} %get-tuple-element.121), channel_id=1, source_target_pairs={{0,2},{2,0},{4,6},{6,4},{8,10},{10,8},{12,14},{14,12},{16,18},{18,... | collective-permute-start | bytes 1572872 | tf_op jit(solution)/shard_map/ppermute | solution.py:612
  382.3 19.6 %collective-permute-start.45 = (bf16[128,2048]{1,0:T(8,128)(2,1)}, bf16[128,2048]{1,0:T(8,128)(2,1)}, u32[]{:S(2)}, u32[]{:S(2)}) collective-permute-start(bf16[128,2048]{1,0:T(8,128)(2,1)} %get-tuple-element.121), channel_id=1, source_target_pairs={{0,4},{2,6},{4,0},{6,2},{8,12},{10,14},{12,8},{14,10},{16,20},{18,... | collective-permute-start | bytes 1572872 | tf_op jit(solution)/shard_map/ppermute | solution.py:612
  384.0 35.7 %collective-permute-start.46 = (bf16[128,2048]{1,0:T(8,128)(2,1)}, bf16[128,2048]{1,0:T(8,128)(2,1)}, u32[]{:S(2)}, u32[]{:S(2)}) collective-permute-start(bf16[128,2048]{1,0:T(8,128)(2,1)} %get-tuple-element.121), channel_id=1, source_target_pairs={{0,6},{2,4},{4,2},{6,0},{8,14},{10,12},{12,10},{14,8},{16,22},{18,... | collective-permute-start | bytes 1572872 | tf_op jit(solution)/shard_map/ppermute | solution.py:612
  385.4 35.4 %collective-permute-start.29 = (bf16[128,2048]{1,0:T(8,128)(2,1)}, bf16[128,2048]{1,0:T(8,128)(2,1)}, u32[]{:S(2)}, u32[]{:S(2)}) collective-permute-start(bf16[128,2048]{1,0:T(8,128)(2,1)} %get-tuple-element.121), channel_id=1, source_target_pairs={{0,1},{1,0},{2,3},{3,2},{4,5},{5,4},{6,7},{7,6},{8,9},{9,8},{10,11... | collective-permute-start | bytes 1572872 | tf_op jit(solution)/shard_map/ppermute | solution.py:436
  420.7 51.7 %collective-permute-start.47 = (bf16[512,2048]{1,0:T(8,128)(2,1)S(1)}, bf16[512,2048]{1,0:T(8,128)(2,1)}, u32[]{:S(2)}, u32[]{:S(2)}) collective-permute-start(bf16[512,2048]{1,0:T(8,128)(2,1)S(1)} %bitcast.164), channel_id=1, source_target_pairs={{0,1},{1,0},{2,3},{3,2},{4,5},{5,4},{6,7},{7,6},{8,9},{9,8},{10,11... | collective-permute-start | bytes 6291464 | tf_op jit(solution)/shard_map/ppermute | solution.py:436
  436.7 29.1 %collective-permute-start.31 = (bf16[128,2048]{1,0:T(8,128)(2,1)}, bf16[128,2048]{1,0:T(8,128)(2,1)}, u32[]{:S(2)}, u32[]{:S(2)}) collective-permute-start(bf16[128,2048]{1,0:T(8,128)(2,1)} %get-tuple-element.227), channel_id=1, source_target_pairs={{0,1},{1,0},{2,3},{3,2},{4,5},{5,4},{6,7},{7,6},{8,9},{9,8},{10,11... | collective-permute-start | bytes 1572872 | tf_op jit(solution)/shard_map/ppermute | solution.py:436
  437.1 28.6 %collective-permute-start.33 = (bf16[128,2048]{1,0:T(8,128)(2,1)}, bf16[128,2048]{1,0:T(8,128)(2,1)}, u32[]{:S(2)}, u32[]{:S(2)}) collective-permute-start(bf16[128,2048]{1,0:T(8,128)(2,1)} %get-tuple-element.226), channel_id=1, source_target_pairs={{0,1},{1,0},{2,3},{3,2},{4,5},{5,4},{6,7},{7,6},{8,9},{9,8},{10,11... | collective-permute-start | bytes 1572872 | tf_op jit(solution)/shard_map/ppermute | solution.py:436
  453.4 33.8 %collective-permute-start.32 = (bf16[128,2048]{1,0:T(8,128)(2,1)}, bf16[128,2048]{1,0:T(8,128)(2,1)}, u32[]{:S(2)}, u32[]{:S(2)}) collective-permute-start(bf16[128,2048]{1,0:T(8,128)(2,1)} %get-tuple-element.225), channel_id=1, source_target_pairs={{0,1},{1,0},{2,3},{3,2},{4,5},{5,4},{6,7},{7,6},{8,9},{9,8},{10,11... | collective-permute-start | bytes 1572872 | tf_op jit(solution)/shard_map/ppermute | solution.py:436
  461.3 32.4 %all-to-all-start.4 = ((bf16[256,4,800]{0,2,1:T(8,128)(2,1)}), bf16[256,4,800]{0,2,1:T(8,128)(2,1)}, u32[]{:S(2)}, u32[]{:S(2)}) async-start(bf16[256,4,800]{0,2,1:T(8,128)(2,1)} %pad_maximum_fusion.2), calls=%async_computation.6 | async-start | bytes 3276800 | tf_op jit(solution)/shard_map/all_to_all | solution.py:557
  465.7 188.8 %reduce-scatter.14.cloned.1.call-start = ((), (), s32[]{:S(2)}) async-start(), calls=%async_computation.23 | async-start | bytes 1310720 | tf_op jit(solution)/shard_map/reduce_scatter | solution.py:685
  468.9 13.2 %collective-permute-start.34 = (bf16[128,2048]{1,0:T(8,128)(2,1)}, bf16[128,2048]{1,0:T(8,128)(2,1)}, u32[]{:S(2)}, u32[]{:S(2)}) collective-permute-start(bf16[128,2048]{1,0:T(8,128)(2,1)} %get-tuple-element.216), channel_id=1, source_target_pairs={{0,8},{2,10},{4,12},{6,14},{8,16},{10,18},{12,20},{14,22},{16,24},... | collective-permute-start | bytes 1572872 | tf_op jit(solution)/shard_map/ppermute | solution.py:599
  471.0 16.2 %collective-permute-start.35 = (bf16[128,2048]{1,0:T(8,128)(2,1)}, bf16[128,2048]{1,0:T(8,128)(2,1)}, u32[]{:S(2)}, u32[]{:S(2)}) collective-permute-start(bf16[128,2048]{1,0:T(8,128)(2,1)} %get-tuple-element.215), channel_id=1, source_target_pairs={{8,0},{10,2},{12,4},{14,6},{16,8},{18,10},{20,12},{22,14},{24,16},... | collective-permute-start | bytes 1572872 | tf_op jit(solution)/shard_map/ppermute | solution.py:600
  490.2 12.8 %collective-permute-start.36 = (bf16[128,2048]{1,0:T(8,128)(2,1)}, bf16[128,2048]{1,0:T(8,128)(2,1)}, u32[]{:S(2)}, u32[]{:S(2)}) collective-permute-start(bf16[128,2048]{1,0:T(8,128)(2,1)} %get-tuple-element.209), channel_id=1, source_target_pairs={{0,8},{2,10},{4,12},{6,14},{8,16},{10,18},{12,20},{14,22},{16,24},... | collective-permute-start | bytes 1572872 | tf_op jit(solution)/shard_map/ppermute | solution.py:599
  492.4 15.0 %collective-permute-start.37 = (bf16[128,2048]{1,0:T(8,128)(2,1)}, bf16[128,2048]{1,0:T(8,128)(2,1)}, u32[]{:S(2)}, u32[]{:S(2)}) collective-permute-start(bf16[128,2048]{1,0:T(8,128)(2,1)} %get-tuple-element.208), channel_id=1, source_target_pairs={{8,0},{10,2},{12,4},{14,6},{16,8},{18,10},{20,12},{22,14},{24,16},... | collective-permute-start | bytes 1572872 | tf_op jit(solution)/shard_map/ppermute | solution.py:600
  514.8 143.4 %reduce-scatter.12.cloned.1.call-start = ((), (), s32[]{:S(2)}) async-start(), calls=%async_computation.22 | async-start | bytes 4096000 | tf_op jit(solution)/shard_map/reduce_scatter | solution.py:685
  515.5 95.0 %collective-permute-start.30 = (bf16[128,2048]{1,0:T(8,128)(2,1)}, bf16[128,2048]{1,0:T(8,128)(2,1)}, u32[]{:S(2)}, u32[]{:S(2)}) collective-permute-start(bf16[128,2048]{1,0:T(8,128)(2,1)} %get-tuple-element.228), channel_id=1, source_target_pairs={{0,1},{1,0},{2,3},{3,2},{4,5},{5,4},{6,7},{7,6},{8,9},{9,8},{10,11... | collective-permute-start | bytes 1572872 | tf_op jit(solution)/shard_map/ppermute | solution.py:436
  516.8 37.4 %all-to-all-start.10 = ((bf16[4,128,704]{1,2,0:T(8,128)(2,1)}), bf16[4,128,704]{1,2,0:T(8,128)(2,1)}, u32[]{:S(2)}, u32[]{:S(2)}) async-start(bf16[4,128,704]{1,2,0:T(8,128)(2,1)} %copy_bitcast_fusion.6), calls=%async_computation.15 | async-start | bytes 1441792 | tf_op jit(solution)/shard_map/all_to_all | solution.py:557
  532.7 30.3 %collective-permute-start.41 = (f32[128,2048]{1,0:T(8,128)}, f32[128,2048]{1,0:T(8,128)}, u32[]{:S(2)}, u32[]{:S(2)}) collective-permute-start(f32[128,2048]{1,0:T(8,128)} %convolution_add_fusion.2), channel_id=1, source_target_pairs={{0,1},{1,0},{2,3},{3,2},{4,5},{5,4},{6,7},{7,6},{8,9},{9,8},{10,11... | collective-permute-start | bytes 3145736 | tf_op jit(solution)/shard_map/ppermute | solution.py:436
  554.3 41.3 %all-to-all-start.8 = ((bf16[4,128,704]{1,2,0:T(8,128)(2,1)}), bf16[4,128,704]{1,2,0:T(8,128)(2,1)S(1)}, u32[]{:S(2)}, u32[]{:S(2)}) async-start(bf16[4,128,704]{1,2,0:T(8,128)(2,1)} %copy_bitcast_fusion.8), calls=%async_computation.13 | async-start | bytes 1441792 | tf_op jit(solution)/shard_map/all_to_all | solution.py:557
  595.5 11.5 %all-to-all-start.5 = ((f32[16,2,128]{2,1,0:T(2,128)}), f32[16,2,128]{2,1,0:T(2,128)S(1)}, u32[]{:S(2)}, u32[]{:S(2)}) async-start(f32[16,2,128]{2,1,0:T(2,128)} %add_bitcast_fusion), calls=%async_computation.7 | async-start | bytes 32768 | tf_op jit(solution)/shard_map/all_to_all | solution.py:776
  607.0 47.5 %all-to-all-start.9 = ((bf16[4,128,704]{1,2,0:T(8,128)(2,1)}), bf16[4,128,704]{1,2,0:T(8,128)(2,1)S(1)}, u32[]{:S(2)}, u32[]{:S(2)}) async-start(bf16[4,128,704]{1,2,0:T(8,128)(2,1)} %copy_bitcast_fusion.7), calls=%async_computation.14 | async-start | bytes 1441792 | tf_op jit(solution)/shard_map/all_to_all | solution.py:557
  614.8 31.2 %collective-permute-start.38 = (bf16[128,2048]{1,0:T(8,128)(2,1)}, bf16[128,2048]{1,0:T(8,128)(2,1)}, u32[]{:S(2)}, u32[]{:S(2)}) collective-permute-start(bf16[128,2048]{1,0:T(8,128)(2,1)} %get-tuple-element.213), channel_id=1, source_target_pairs={{0,8},{2,10},{4,12},{6,14},{8,16},{10,18},{12,20},{14,22},{16,24},... | collective-permute-start | bytes 1572872 | tf_op jit(solution)/shard_map/ppermute | solution.py:599
  619.5 28.5 %collective-permute-start.39 = (bf16[128,2048]{1,0:T(8,128)(2,1)}, bf16[128,2048]{1,0:T(8,128)(2,1)}, u32[]{:S(2)}, u32[]{:S(2)}) collective-permute-start(bf16[128,2048]{1,0:T(8,128)(2,1)} %get-tuple-element.212), channel_id=1, source_target_pairs={{8,0},{10,2},{12,4},{14,6},{16,8},{18,10},{20,12},{22,14},{24,16},... | collective-permute-start | bytes 1572872 | tf_op jit(solution)/shard_map/ppermute | solution.py:600
  625.1 45.0 %collective-permute-start.42 = (f32[128,2048]{1,0:T(8,128)}, f32[128,2048]{1,0:T(8,128)}, u32[]{:S(2)}, u32[]{:S(2)}) collective-permute-start(f32[128,2048]{1,0:T(8,128)} %get-tuple-element.143), channel_id=1, source_target_pairs={{0,1},{1,0},{2,3},{3,2},{4,5},{5,4},{6,7},{7,6},{8,9},{9,8},{10,11... | collective-permute-start | bytes 3145736 | tf_op jit(solution)/shard_map/ppermute | solution.py:436
  651.0 16.7 %collective-permute-start.40 = (bf16[128,2048]{1,0:T(8,128)(2,1)}, bf16[128,2048]{1,0:T(8,128)(2,1)S(1)}, u32[]{:S(2)}, u32[]{:S(2)}) collective-permute-start(bf16[128,2048]{1,0:T(8,128)(2,1)} %block_result.1), channel_id=1, source_target_pairs={{0,1},{1,0},{2,3},{3,2},{4,5},{5,4},{6,7},{7,6},{8,9},{9,8},{10,11... | collective-permute-start | bytes 1572872 | tf_op jit(solution)/shard_map/ppermute | solution.py:436
  654.5 9.7 %all-to-all-start.7 = ((bf16[4,128,256]{2,1,0:T(8,128)(2,1)}), bf16[4,128,256]{2,1,0:T(8,128)(2,1)S(1)}, u32[]{:S(2)}, u32[]{:S(2)}) async-start(bf16[4,128,256]{2,1,0:T(8,128)(2,1)} %bitcast.188), calls=%async_computation.12 | async-start | bytes 524288 | tf_op jit(solution)/shard_map/all_to_all | solution.py:557
  664.2 14.3 %all-to-all-start.6 = ((bf16[4,128,800]{1,2,0:T(8,128)(2,1)}), bf16[4,128,800]{1,2,0:T(8,128)(2,1)S(1)}, u32[]{:S(2)}, u32[]{:S(2)}) async-start(bf16[4,128,800]{1,2,0:T(8,128)(2,1)} %copy_bitcast_fusion.2), calls=%async_computation.10 | async-start | bytes 1638400 | tf_op jit(solution)/shard_map/all_to_all | solution.py:557
  (62 other events, 652.2 us)
Sparse Core Ops, SparseCore 0:
  36.9 33.0 all-gather.3
  72.1 33.9 all-gather.5
  159.5 32.2 all-gather.7
  259.1 36.1 reduce-scatter.5
  300.2 51.6 reduce-scatter.7
  388.9 42.0 reduce-scatter.9
  514.9 36.9 reduce-scatter.13
  554.2 86.9 reduce-scatter.11

commit v4 on v3

--- a/solution.py
+++ b/solution.py
@@ -640,28 +640,30 @@
     def gather_rows(w):
         return lax.all_gather(w, "dp", axis=0, tiled=True, axis_index_groups=grid.laps)
 
-    gate_piece, up_piece, down_piece = columns(w_gate), columns(w_up), columns(w_down)
-
+    def column_pairs(a, b):
+        rows = a.shape[0]
+        both = [w.reshape(rows, grid.outer, -1) for w in (a, b)]
+        both = columns(jnp.concatenate(both, axis=2).reshape(rows, -1))
+        return jnp.split(both, 2, axis=1)
+
+    gate_piece, up_piece = column_pairs(w_gate, w_up)
     inputs_f = block_in.astype(f32)
     normed = (inputs_f * rms_scale(inputs_f) * attn_gain).astype(bf16)
     query_pre = nn(normed, w_query)
-    later, query_pre, gate_piece = tie(normed, query_pre, gate_piece)
-    full_gate = gather_rows(gate_piece)
-    key_pre = nn(later, w_key)
-    value_pre = nn(later, w_value)
-    forget_pre = nn(later, w_forget)
+    key_pre = nn(normed, w_key)
+    value_pre = nn(normed, w_value)
+    forget_pre = nn(normed, w_forget)
     query = jax.nn.silu(query_pre).astype(bf16)
     key = jax.nn.silu(key_pre).astype(bf16)
     value = jax.nn.silu(value_pre).astype(bf16)
     log_keep = jax.nn.log_sigmoid(forget_pre) * tau_inv
-    key, value, log_keep, up_piece = tie(key, value, log_keep, up_piece)
-    full_up = gather_rows(up_piece)
     mixed, *saved = attend_forward(query, key, value, log_keep, doc_starts)
+    mixed, gate_piece, up_piece, down_later = tie(mixed, gate_piece, up_piece, w_down)
+    full_gate, full_up = gather_rows(gate_piece), gather_rows(up_piece)
+    down_piece = columns(down_later)
 
     branch_other = swap(nt(half_of(mixed, 1 - core), w_output))
     branch_mine = nt(half_of(mixed, core), w_output)
-    branch_mine, down_piece = tie(branch_mine, down_piece)
-    full_down = gather_rows(down_piece)
     hidden, normed_two = second_norm(block_in, branch_mine, branch_other, mlp_gain, core, grid)
     def plane_tokens(half):
         own = plane_gather(half, grid, inner)
@@ -691,13 +693,26 @@
         return exchange(g, 0, 1, grid.rows).reshape(-1, INNER, size).astype(f32)
 
     cot_rows = cotangent_rows(out_grad, core, grid)
-    own, (cot_rows, full_gate, full_up) = gather_along(
-        normed_two, grid, place, ((cot_rows,), (full_gate,), (full_up,))
-    )
+    own, (cot_rows, down_piece, normed_own, normed_rest, full_gate) = gather_along(
+        normed_two,
+        grid,
+        place,
+        ((cot_rows, down_piece), plane_tokens(half_of(normed, core)), (full_gate,)),
+    )
+    normed_plane = (normed_own, normed_rest)
+    full_down = gather_rows(down_piece)
     tokens = with_other_core(own)
-    own, (gate_act, up_act, full_down) = gather_along(
-        cot_rows, grid, place, ((nn(tokens, full_gate),), (nn(tokens, full_up),), (full_down,))
-    )
+    own, (gate_act, full_up, mixed_own, mixed_rest, up_act, full_down) = gather_along(
+        cot_rows,
+        grid,
+        place,
+        (
+            (nn(tokens, full_gate), full_up),
+            plane_columns([mixed]),
+            (nn(tokens, full_up), full_down),
+        ),
+    )
+    mixed_plane = (mixed_own, mixed_rest)
     cot_all = with_other_core(own)
 
     def scatter_rows(g):
@@ -705,22 +720,22 @@
             g, "dp", scatter_dimension=0, tiled=True, axis_index_groups=grid.laps
         )
 
-    mixed_plane = plane_columns([mixed])
-    normed_plane = plane_tokens(half_of(normed, core))
+    def to_columns(g):
+        return exchange(g, 0, 1, grid.cols).astype(f32)
+
     inner_grad = nn(cot_all, full_down)
     gate_grad = (inner_grad * up_act * silu_slope(gate_act)).astype(bf16)
     up_grad = (inner_grad * jax.nn.silu(gate_act)).astype(bf16)
     inner_act = (jax.nn.silu(gate_act) * up_act).astype(bf16)
-    back_parts, (down_rows, gate_rows, mixed_own, mixed_rest, up_rows, *normed_plane) = scatter_tokens(
+    back_parts, (down_rows, gate_rows, up_rows) = scatter_tokens(
         nt(gate_grad, full_gate) + nt(up_grad, full_up),
         grid,
         (
             (tn(cot_all, inner_act).astype(bf16),),
-            (tn(tokens, gate_grad).astype(bf16), *mixed_plane),
-            (tn(tokens, up_grad).astype(bf16), *normed_plane),
+            (tn(tokens, gate_grad).astype(bf16),),
+            (tn(tokens, up_grad).astype(bf16),),
         ),
     )
-    mixed_plane = (mixed_own, mixed_rest)
     down_rows, gate_rows, up_rows = (scatter_rows(g) for g in (down_rows, gate_rows, up_rows))
     hidden_grad, low_half, mlp_gain_part = second_norm_back(
         out_grad, hidden, mlp_gain, back_parts, core, grid
@@ -736,17 +751,18 @@
     forget_pre_grad = (log_grad * tau_inv * jax.nn.sigmoid(-forget_pre)).astype(bf16)
     pre_grads = (query_pre_grad, key_pre_grad, value_pre_grad, forget_pre_grad)
 
-    query_pre_grad, gate_rows = tie(query_pre_grad, gate_rows)
+    down_sum = to_columns(down_rows)
+    query_pre_grad, gate_rows, down_sum, low_half = tie(
+        query_pre_grad, gate_rows, down_sum, low_half
+    )
     pre_grads = (query_pre_grad,) + pre_grads[1:]
     out_parts, (query_pre_grad, *grad_columns) = scatter_tokens(
         nt(later_act, full_down), grid, ((query_pre_grad,), tuple(plane_columns(pre_grads)))
     )
     pre_grads = (query_pre_grad,) + pre_grads[1:]
     output_grad = plane_product(plane_tokens(low_half), mixed_plane)
-    pre_grad, up_rows, output_grad = tie(
-        plane_product(normed_plane, grad_columns), up_rows, output_grad
-    )
-    output_sum = from_plane(plane_sum(output_grad))
+    pre_grad = plane_product(normed_plane, grad_columns)
+    pre_grad, up_rows = tie(jnp.concatenate([pre_grad, output_grad], axis=1), up_rows)
     sums = plane_sum(pre_grad)
 
     result = block_result(block_in, hidden, out_parts, core, grid)
@@ -754,9 +770,9 @@
 
     sums = from_plane(sums)
     ends = [0]
-    for g in pre_grads:
+    for g in (*pre_grads, mixed):
         ends.append(ends[-1] + g.shape[1] // INNER)
-    query_sum, key_sum, value_sum, forget_sum = (
+    query_sum, key_sum, value_sum, forget_sum, output_sum = (
         sums[:, :, a:b].reshape(sums.shape[0], -1) for a, b in zip(ends, ends[1:])
     )
 
@@ -774,9 +790,6 @@
     gains = gains + swap(gains)
     gains = jnp.swapaxes(gains.reshape(2, grid.dp, -1), 0, 1)
     gains = jnp.sum(lax.all_to_all(gains, "dp", 0, 0, tiled=True), axis=0)
-
-    def to_columns(g):
-        return exchange(g, 0, 1, grid.cols).astype(f32)
 
     return (
         result,
@@ -787,10 +800,10 @@
         key_sum,
         value_sum,
         forget_sum,
-        output_sum.reshape(output_sum.shape[0], -1),
+        output_sum,
         to_columns(gate_rows),
         to_columns(up_rows),
-        to_columns(down_rows),
+        down_sum,
     )
 
 

time: 703 us -> 646 us (0.919)
  the two profiles are of different devices: /device:TPU:0 before, /device:TPU:8 now
where the time goes in v4:
time: 646 us; the launch traced here: 638 us
  waiting for transfers between devices  212 us (33%)
  starting transfers between devices  148 us (23%)
  matrix products  102 us (16%)
  local copies, waits for them, and re-layouts  77.3 us (12%)
  other arithmetic  50.9 us (8%)
  Pallas kernels  31.7 us (5%)
  between operations  15.4 us (2%)
    ppermute x6, waiting for transfers between devices, plane_gather(): y = lax.ppermute(x, 'dp', [(d, d ^ k) for d in range(grid.dp)])  56.3 us
    all_to_all x8, waiting for transfers between devices, exchange(): lax.all_to_all(x, 'dp', split, concat, tiled=True, axis_index_groups=groups)  45.8 us
    dot_general x13, matrix products, nt(): lax.dot_general(a.astype(bf16), b.astype(bf16), (((1,), (1,)), ((), ())),...  43.5 us
    all_to_all x8, starting transfers between devices, exchange(): lax.all_to_all(x, 'dp', split, concat, tiled=True, axis_index_groups=groups)  42.1 us
    ppermute x6, waiting for transfers between devices, scatter_tokens(): up = lax.ppermute(up.astype(bf16), 'dp', grid.up)  36.2 us
    dot_general x8, matrix products, nn(): return jnp.dot(a.astype(bf16), b.astype(bf16), preferred_element_type=f32)  31.1 us
    ppermute x6, waiting for transfers between devices, gather_along(): below = lax.ppermute(below, 'dp', grid.up)  30.3 us
    dot_general x7, matrix products, tn(): lax.dot_general(a.astype(bf16), b.astype(bf16), (((0,), (0,)), ((), ())),...  27.6 us
  transfers between devices with their start and end apart: 64, of which 36 were waited for; matrix products, arithmetic and copies ran while one was open for 29% of the time, Pallas kernels for 5%

profile of v4, /device:TPU:8, one launch (start us, length us, event | category | flops | bytes accessed | tf_op | source)
XLA Modules:
  0.0 638.4 jit_solution(2182835496441718705)
XLA Ops:
  11.4 5.3 all-to-all-start
  26.3 6.4 slot_forward.1
  32.7 14.9 %all-to-all-done = bf16[128,4,1408]{0,2,1:T(8,128)(2,1)} async-done(((bf16[128,4,1408]{0,2,1:T(8,128)(2,1)}), bf16[128,4,1408]{0,2,1:T(8,128)(2,1)}, u32[]{:S(2)}, u32[]{:S(2)}) %all-to-all-start) | async-done | bytes 1441824 | tf_op jit(solution)/shard_map/all_to_all | solution.py:557
  59.3 17.1 %collective-permute-done.7 = bf16[128,2048]{1,0:T(8,128)(2,1)S(1)} collective-permute-done((bf16[128,2048]{1,0:T(8,128)(2,1)}, bf16[128,2048]{1,0:T(8,128)(2,1)S(1)}, u32[]{:S(2)}, u32[]{:S(2)}) %collective-permute-start.7) | collective-permute-done | bytes 524320 | tf_op jit(solution)/shard_map/ppermute | solution.py:612
  77.2 4.4 collective-permute-done.8
  82.4 4.7 fusion.17
  87.2 10.5 %collective-permute-done.9 = bf16[128,2048]{1,0:T(8,128)(2,1)} collective-permute-done((bf16[128,2048]{1,0:T(8,128)(2,1)}, bf16[128,2048]{1,0:T(8,128)(2,1)}, u32[]{:S(2)}, u32[]{:S(2)}) %collective-permute-start.9) | collective-permute-done | bytes 524320 | tf_op jit(solution)/shard_map/ppermute | solution.py:612
  100.7 10.1 %all-to-all-start.1 = ((bf16[128,4,704]{0,2,1:T(8,128)(2,1)}), bf16[128,4,704]{0,2,1:T(8,128)(2,1)S(1)}, u32[]{:S(2)}, u32[]{:S(2)}) async-start(bf16[128,4,704]{0,2,1:T(8,128)(2,1)} %bitcast.6), calls=%async_computation.1 | async-start | bytes 1441792 | tf_op jit(solution)/shard_map/all_to_all | solution.py:557
  110.8 9.6 %all-gather.6.cloned.1.call-start = ((), (), s32[]{:S(2)}) async-start(), calls=%async_computation.14 | async-start | bytes 3932160 | tf_op jit(solution)/shard_map/all_gather | solution.py:641
  120.5 4.7 fusion.19.mine_ref
  129.2 3.5 collective-permute-start.1
  138.1 7.5 %collective-permute-done.1 = bf16[128,2048]{1,0:T(8,128)(2,1)S(1)} collective-permute-done((bf16[128,2048]{1,0:T(8,128)(2,1)}, bf16[128,2048]{1,0:T(8,128)(2,1)S(1)}, u32[]{:S(2)}, u32[]{:S(2)}) %collective-permute-start.1) | collective-permute-done | bytes 524320 | tf_op jit(solution)/shard_map/ppermute | solution.py:569
  148.7 3.4 collective-permute-start.5
  154.6 8.9 %collective-permute-done.5 = bf16[128,2048]{1,0:T(8,128)(2,1)S(1)} collective-permute-done((bf16[128,2048]{1,0:T(8,128)(2,1)S(1)}, bf16[128,2048]{1,0:T(8,128)(2,1)S(1)}, u32[]{:S(2)}, u32[]{:S(2)}) %collective-permute-start.5) | collective-permute-done | bytes 524320 | tf_op jit(solution)/shard_map/ppermute | solution.py:569
  163.6 3.4 collective-permute-done.6
  169.2 4.4 collective-permute-start.12
  174.5 6.3 collective-permute-done.11
  192.7 3.9 all-to-all-start.2
  198.8 4.0 collective-permute-start.4
  205.9 7.1 %fusion.41 = f32[1024,704]{0,1:T(8,128)} fusion(bf16[1024,2048]{1,0:T(8,128)(2,1)} %constant_dynamic-update-slice_fusion, bf16[2048,704]{1,0:T(8,128)(2,1)S(1)} %copy-done.16), kind=kOutput, calls=%fused_computation.141 | convolution fusion | flops 2952790016 | bytes 9961472 | tf_op jit(solution)/shard_map/dot_general | solution.py:19
  216.6 4.0 collective-permute-start.15
  222.2 7.6 %collective-permute-done.14 = bf16[128,2048]{1,0:T(8,128)(2,1)S(1)} collective-permute-done((bf16[128,2048]{1,0:T(8,128)(2,1)S(1)}, bf16[128,2048]{1,0:T(8,128)(2,1)S(1)}, u32[]{:S(2)}, u32[]{:S(2)}) %collective-permute-start.14) | collective-permute-done | bytes 524320 | tf_op jit(solution)/shard_map/ppermute | solution.py:569
  233.8 4.7 collective-permute-start.17
  238.6 8.0 %fusion.42 = f32[1024,704]{0,1:T(8,128)} fusion(bf16[1024,2048]{1,0:T(8,128)(2,1)} %constant_dynamic-update-slice_fusion, bf16[2048,704]{1,0:T(8,128)(2,1)} %all-gather.6.cloned.1.call-done), kind=kOutput, calls=%fused_computation.142 | convolution fusion | flops 2952790016 | bytes 9961472 | tf_op jit(solution)/shard_map/dot_general | solution.py:19
  252.8 4.1 collective-permute-done.18
  261.5 3.4 multiply_convert_fusion
  264.8 3.5 fusion.44
  268.4 5.5 fusion.39
  281.2 4.7 collective-permute-start.24
  285.9 4.5 convolution_convert_fusion.2
  290.4 5.0 collective-permute-done.23
  304.4 4.7 collective-permute-start.26
  309.1 6.7 %convolution_convert_fusion.1 = bf16[2048,704]{0,1:T(8,128)(2,1)} fusion(bf16[1024,704]{0,1:T(8,128)(2,1)S(1)} %get-tuple-element.217, bf16[1024,2048]{1,0:T(8,128)(2,1)} %constant_dynamic-update-slice_fusion), kind=kOutput, calls=%fused_computation.4 | convolution fusion | flops 2954231808 | bytes 8519680 | tf_op jit(solution)/shard_map/dot_general | solution.py:29
  323.0 4.0 add_convert_fusion.5
  328.9 4.0 collective-permute-start.28
  332.9 4.5 convolution_convert_fusion
  337.4 5.7 collective-permute-done.27.refs_1_
  345.5 3.9 second_norm_back.1
  351.7 4.3 convolution_convert_fusion.3.do_ref
  358.2 5.3 all-to-all-start.3
  363.5 7.6 %fusion.40 = (bf16[1024,2048]{1,0:T(8,128)(2,1)S(1)}, f32[1024,2048]{1,0:T(8,128)}) fusion(bf16[1024,704]{0,1:T(8,128)(2,1)S(1)} %copy-done.27, bf16[2048,704]{0,1:T(8,128)(2,1)} %all-gather.8.cloned.1.call-done), kind=kOutput, calls=%fused_computation.140 | convolution fusion | flops 2954887168 | bytes 16908288 | tf_op jit(solution)/shard_map/dot_general | solution.py:23
  372.5 9.5 %slot_backward.1 = (f32[256,1024]{1,0:T(8,128)}, f32[256,1024]{1,0:T(8,128)}, f32[256,1024]{1,0:T(8,128)}, f32[256,128]{1,0:T(8,128)}) custom-call(s32[1,3]{1,0:T(1,128)} %starts_ref.3, bf16[256,1024]{1,0:T(8,128)(2,1)} %get-tuple-element.239.q_ref, bf16[256,1024]{1,0:T(8,128)(2,1)} %get-tuple-element.241.k_ref, bf16[256,1024]{1,0:T(8,128)(2,1)} %get-tuple-element.243.v_ref, ...), custom_call_target="tpu_custom_call" | custom-call | flops 12000000000 | bytes 8000000 | tf_op jit(solution)/shard_map/slot_backward/pallas_call | solution.py:369
  392.7 3.4 collective-permute-start.34
  406.1 3.6 all-to-all-start.4
  417.9 8.4 %collective-permute-done.45 = bf16[128,2048]{1,0:T(8,128)(2,1)} collective-permute-done((bf16[128,2048]{1,0:T(8,128)(2,1)}, bf16[128,2048]{1,0:T(8,128)(2,1)}, u32[]{:S(2)}, u32[]{:S(2)}) %collective-permute-start.45) | collective-permute-done | bytes 524320 | tf_op jit(solution)/shard_map/ppermute | solution.py:612
  428.1 16.0 %collective-permute-done.46 = bf16[128,2048]{1,0:T(8,128)(2,1)S(1)} collective-permute-done((bf16[128,2048]{1,0:T(8,128)(2,1)S(1)}, bf16[128,2048]{1,0:T(8,128)(2,1)S(1)}, u32[]{:S(2)}, u32[]{:S(2)}) %collective-permute-start.46) | collective-permute-done | bytes 524320 | tf_op jit(solution)/shard_map/ppermute | solution.py:612
  450.5 4.0 collective-permute-start.37
  455.8 3.9 reshape.153
  459.6 3.4 constant_dynamic-slice_fusion
  467.3 3.5 fusion.46
  470.8 3.6 add_convert_fusion
  481.8 3.8 fusion.10
  495.6 5.5 all-to-all-start.7
  501.2 3.9 convolution_add_fusion.7
  507.9 3.9 first_norm_back.1
  515.1 21.8 %all-to-all-done.7 = bf16[4,128,704]{1,2,0:T(8,128)(2,1)} async-done(((bf16[4,128,704]{1,2,0:T(8,128)(2,1)}), bf16[4,128,704]{1,2,0:T(8,128)(2,1)}, u32[]{:S(2)}, u32[]{:S(2)}) %all-to-all-start.7) | async-done | bytes 720928 | tf_op jit(solution)/shard_map/all_to_all | solution.py:557
  536.9 9.1 %all-to-all-start.5 = ((f32[16,2,128]{2,1,0:T(2,128)}), f32[16,2,128]{2,1,0:T(2,128)S(1)}, u32[]{:S(2)}, u32[]{:S(2)}) async-start(f32[16,2,128]{2,1,0:T(2,128)} %add_bitcast_fusion), calls=%async_computation.7 | async-start | bytes 32768 | tf_op jit(solution)/shard_map/all_to_all | solution.py:792
  547.0 6.9 %all-to-all-done.5 = f32[16,2,128]{2,1,0:T(2,128)S(1)} async-done(((f32[16,2,128]{2,1,0:T(2,128)}), f32[16,2,128]{2,1,0:T(2,128)S(1)}, u32[]{:S(2)}, u32[]{:S(2)}) %all-to-all-start.5) | async-done | bytes 16416 | tf_op jit(solution)/shard_map/all_to_all | solution.py:792
  553.9 4.8 all-to-all-start.8
  558.7 4.4 add_convert_fusion.1
  563.1 3.4 collective-permute-start.38
  577.1 22.5 %collective-permute-done.38.refs_1_ = bf16[128,2048]{1,0:T(8,128)(2,1)S(1)} collective-permute-done((bf16[128,2048]{1,0:T(8,128)(2,1)}, bf16[128,2048]{1,0:T(8,128)(2,1)S(1)}, u32[]{:S(2)}, u32[]{:S(2)}) %collective-permute-start.38) | collective-permute-done | bytes 524320 | tf_op jit(solution)/shard_map/ppermute | solution.py:599
  607.9 3.6 all-to-all-start.6
  617.2 9.1 %all-to-all-done.6 = bf16[4,128,1056]{1,2,0:T(8,128)(2,1)S(1)} async-done(((bf16[4,128,1056]{1,2,0:T(8,128)(2,1)}), bf16[4,128,1056]{1,2,0:T(8,128)(2,1)S(1)}, u32[]{:S(2)}, u32[]{:S(2)}) %all-to-all-start.6) | async-done | bytes 1081376 | tf_op jit(solution)/shard_map/all_to_all | solution.py:557
  (301 shorter events, 215.2 us)
Async XLA Ops:
  11.4 36.2 %all-to-all-start = ((bf16[128,4,1408]{0,2,1:T(8,128)(2,1)}), bf16[128,4,1408]{0,2,1:T(8,128)(2,1)}, u32[]{:S(2)}, u32[]{:S(2)}) async-start(bf16[128,4,1408]{0,2,1:T(8,128)(2,1)} %pad_maximum_fusion.4), calls=%async_computation | async-start | bytes 2883584 | tf_op jit(solution)/shard_map/all_to_all | solution.py:557
  16.7 166.5 %all-gather.4.cloned.1.call-start = ((), (), s32[]{:S(2)}) async-start(), calls=%async_computation.13 | async-start | bytes 3932160 | tf_op jit(solution)/shard_map/all_gather | solution.py:641
  55.8 20.6 %collective-permute-start.7 = (bf16[128,2048]{1,0:T(8,128)(2,1)}, bf16[128,2048]{1,0:T(8,128)(2,1)S(1)}, u32[]{:S(2)}, u32[]{:S(2)}) collective-permute-start(bf16[128,2048]{1,0:T(8,128)(2,1)} %get-tuple-element.201), channel_id=1, source_target_pairs={{0,2},{2,0},{4,6},{6,4},{8,10},{10,8},{12,14},{14,12},{16,18},{18,... | collective-permute-start | bytes 1572872 | tf_op jit(solution)/shard_map/ppermute | solution.py:612
  57.3 24.3 %collective-permute-start.8 = (bf16[128,2048]{1,0:T(8,128)(2,1)}, bf16[128,2048]{1,0:T(8,128)(2,1)S(1)}, u32[]{:S(2)}, u32[]{:S(2)}) collective-permute-start(bf16[128,2048]{1,0:T(8,128)(2,1)} %get-tuple-element.201), channel_id=1, source_target_pairs={{0,4},{2,6},{4,0},{6,2},{8,12},{10,14},{12,8},{14,10},{16,20},{18,... | collective-permute-start | bytes 1572872 | tf_op jit(solution)/shard_map/ppermute | solution.py:612
  58.9 38.9 %collective-permute-start.9 = (bf16[128,2048]{1,0:T(8,128)(2,1)}, bf16[128,2048]{1,0:T(8,128)(2,1)}, u32[]{:S(2)}, u32[]{:S(2)}) collective-permute-start(bf16[128,2048]{1,0:T(8,128)(2,1)} %get-tuple-element.201), channel_id=1, source_target_pairs={{0,6},{2,4},{4,2},{6,0},{8,14},{10,12},{12,10},{14,8},{16,22},{18,... | collective-permute-start | bytes 1572872 | tf_op jit(solution)/shard_map/ppermute | solution.py:612
  87.2 38.0 %collective-permute-start = (f32[128,2048]{1,0:T(8,128)}, f32[128,2048]{1,0:T(8,128)S(1)}, u32[]{:S(2)}, u32[]{:S(2)}) collective-permute-start(f32[128,2048]{1,0:T(8,128)} %fusion.17), channel_id=1, source_target_pairs={{0,1},{1,0},{2,3},{3,2},{4,5},{5,4},{6,7},{7,6},{8,9},{9,8},{10,11... | collective-permute-start | bytes 3145736 | tf_op jit(solution)/shard_map/ppermute | solution.py:436
  99.6 55.0 %collective-permute-start.10 = (bf16[512,2048]{1,0:T(8,128)(2,1)}, bf16[512,2048]{1,0:T(8,128)(2,1)}, u32[]{:S(2)}, u32[]{:S(2)}) collective-permute-start(bf16[512,2048]{1,0:T(8,128)(2,1)} %bitcast.12), channel_id=1, source_target_pairs={{0,1},{1,0},{2,3},{3,2},{4,5},{5,4},{6,7},{7,6},{8,9},{9,8},{10,11... | collective-permute-start | bytes 6291464 | tf_op jit(solution)/shard_map/ppermute | solution.py:436
  100.7 36.4 %all-to-all-start.1 = ((bf16[128,4,704]{0,2,1:T(8,128)(2,1)}), bf16[128,4,704]{0,2,1:T(8,128)(2,1)S(1)}, u32[]{:S(2)}, u32[]{:S(2)}) async-start(bf16[128,4,704]{0,2,1:T(8,128)(2,1)} %bitcast.6), calls=%async_computation.1 | async-start | bytes 1441792 | tf_op jit(solution)/shard_map/all_to_all | solution.py:557
  110.8 103.9 %all-gather.6.cloned.1.call-start = ((), (), s32[]{:S(2)}) async-start(), calls=%async_computation.14 | async-start | bytes 3932160 | tf_op jit(solution)/shard_map/all_gather | solution.py:641
  120.5 126.1 %all-gather.8.cloned.1.call-start = ((), (), s32[]{:S(2)}) async-start(), calls=%async_computation.15 | async-start | bytes 3604480 | tf_op jit(solution)/shard_map/all_gather | solution.py:641
  129.2 16.3 %collective-permute-start.1 = (bf16[128,2048]{1,0:T(8,128)(2,1)}, bf16[128,2048]{1,0:T(8,128)(2,1)S(1)}, u32[]{:S(2)}, u32[]{:S(2)}) collective-permute-start(bf16[128,2048]{1,0:T(8,128)(2,1)} %get-tuple-element.85), channel_id=1, source_target_pairs={{0,8},{2,10},{4,12},{6,14},{8,16},{10,18},{12,20},{14,22},{16,24},... | collective-permute-start | bytes 1572872 | tf_op jit(solution)/shard_map/ppermute | solution.py:569
  132.7 16.0 %collective-permute-start.2 = (bf16[128,2048]{1,0:T(8,128)(2,1)}, bf16[128,2048]{1,0:T(8,128)(2,1)}, u32[]{:S(2)}, u32[]{:S(2)}) collective-permute-start(bf16[128,2048]{1,0:T(8,128)(2,1)} %get-tuple-element.85), channel_id=1, source_target_pairs={{8,0},{10,2},{12,4},{14,6},{16,8},{18,10},{20,12},{22,14},{24,16},... | collective-permute-start | bytes 1572872 | tf_op jit(solution)/shard_map/ppermute | solution.py:570
  148.7 14.8 %collective-permute-start.5 = (bf16[128,2048]{1,0:T(8,128)(2,1)S(1)}, bf16[128,2048]{1,0:T(8,128)(2,1)S(1)}, u32[]{:S(2)}, u32[]{:S(2)}) collective-permute-start(bf16[128,2048]{1,0:T(8,128)(2,1)S(1)} %collective-permute-done.1), channel_id=1, source_target_pairs={{0,8},{2,10},{4,12},{6,14},{8,16},{10,18},{12,20},{14,22},{16,24},... | collective-permute-start | bytes 1572872 | tf_op jit(solution)/shard_map/ppermute | solution.py:569
  152.1 14.9 %collective-permute-start.6 = (bf16[128,2048]{1,0:T(8,128)(2,1)}, bf16[128,2048]{1,0:T(8,128)(2,1)}, u32[]{:S(2)}, u32[]{:S(2)}) collective-permute-start(bf16[128,2048]{1,0:T(8,128)(2,1)} %collective-permute-done.2), channel_id=1, source_target_pairs={{8,0},{10,2},{12,4},{14,6},{16,8},{18,10},{20,12},{22,14},{24,16},... | collective-permute-start | bytes 1572872 | tf_op jit(solution)/shard_map/ppermute | solution.py:570
  167.0 13.8 %collective-permute-start.11 = (bf16[128,2048]{1,0:T(8,128)(2,1)S(1)}, bf16[128,2048]{1,0:T(8,128)(2,1)}, u32[]{:S(2)}, u32[]{:S(2)}) collective-permute-start(bf16[128,2048]{1,0:T(8,128)(2,1)S(1)} %collective-permute-done.5), channel_id=1, source_target_pairs={{0,8},{2,10},{4,12},{6,14},{8,16},{10,18},{12,20},{14,22},{16,24},... | collective-permute-start | bytes 1572872 | tf_op jit(solution)/shard_map/ppermute | solution.py:569
  169.2 14.0 %collective-permute-start.12 = (bf16[128,2048]{1,0:T(8,128)(2,1)}, bf16[128,2048]{1,0:T(8,128)(2,1)}, u32[]{:S(2)}, u32[]{:S(2)}) collective-permute-start(bf16[128,2048]{1,0:T(8,128)(2,1)} %collective-permute-done.6), channel_id=1, source_target_pairs={{8,0},{10,2},{12,4},{14,6},{16,8},{18,10},{20,12},{22,14},{24,16},... | collective-permute-start | bytes 1572872 | tf_op jit(solution)/shard_map/ppermute | solution.py:570
  191.8 10.9 %collective-permute-start.13 = (bf16[512,2048]{1,0:T(8,128)(2,1)}, bf16[512,2048]{1,0:T(8,128)(2,1)}, u32[]{:S(2)}, u32[]{:S(2)}) collective-permute-start(bf16[512,2048]{1,0:T(8,128)(2,1)} %pad_maximum_fusion.1), channel_id=1, source_target_pairs={{0,1},{1,0},{2,3},{3,2},{4,5},{5,4},{6,7},{7,6},{8,9},{9,8},{10,11... | collective-permute-start | bytes 6291464 | tf_op jit(solution)/shard_map/ppermute | solution.py:436
  192.7 27.9 %all-to-all-start.2 = ((bf16[256,4,256]{2,0,1:T(8,128)(2,1)}), bf16[256,4,256]{2,0,1:T(8,128)(2,1)S(1)}, u32[]{:S(2)}, u32[]{:S(2)}) async-start(bf16[256,4,256]{2,0,1:T(8,128)(2,1)} %bitcast.149), calls=%async_computation.2 | async-start | bytes 1048576 | tf_op jit(solution)/shard_map/all_to_all | solution.py:557
  196.6 159.4 %reduce-scatter.5.cloned.1.call-start = ((), (), s32[]{:S(2)}) async-start(), calls=%async_computation.16 | async-start | bytes 3604480 | tf_op jit(solution)/shard_map/reduce_scatter | solution.py:719
  196.6 16.4 %collective-permute-start.3 = (bf16[128,2048]{1,0:T(8,128)(2,1)S(1)}, bf16[128,2048]{1,0:T(8,128)(2,1)S(1)}, u32[]{:S(2)}, u32[]{:S(2)}) collective-permute-start(bf16[128,2048]{1,0:T(8,128)(2,1)S(1)} %copy-done.12), channel_id=1, source_target_pairs={{0,8},{2,10},{4,12},{6,14},{8,16},{10,18},{12,20},{14,22},{16,24},... | collective-permute-start | bytes 1572872 | tf_op jit(solution)/shard_map/ppermute | solution.py:569
  198.8 15.9 %collective-permute-start.4 = (bf16[128,2048]{1,0:T(8,128)(2,1)S(1)}, bf16[128,2048]{1,0:T(8,128)(2,1)S(1)}, u32[]{:S(2)}, u32[]{:S(2)}) collective-permute-start(bf16[128,2048]{1,0:T(8,128)(2,1)S(1)} %copy-done.12), channel_id=1, source_target_pairs={{8,0},{10,2},{12,4},{14,6},{16,8},{18,10},{20,12},{22,14},{24,16},... | collective-permute-start | bytes 1572872 | tf_op jit(solution)/shard_map/ppermute | solution.py:570
  214.7 15.2 %collective-permute-start.14 = (bf16[128,2048]{1,0:T(8,128)(2,1)S(1)}, bf16[128,2048]{1,0:T(8,128)(2,1)S(1)}, u32[]{:S(2)}, u32[]{:S(2)}) collective-permute-start(bf16[128,2048]{1,0:T(8,128)(2,1)S(1)} %collective-permute-done.3), channel_id=1, source_target_pairs={{0,8},{2,10},{4,12},{6,14},{8,16},{10,18},{12,20},{14,22},{16,24},... | collective-permute-start | bytes 1572872 | tf_op jit(solution)/shard_map/ppermute | solution.py:569
  216.6 15.3 %collective-permute-start.15 = (bf16[128,2048]{1,0:T(8,128)(2,1)S(1)}, bf16[128,2048]{1,0:T(8,128)(2,1)}, u32[]{:S(2)}, u32[]{:S(2)}) collective-permute-start(bf16[128,2048]{1,0:T(8,128)(2,1)S(1)} %collective-permute-done.4), channel_id=1, source_target_pairs={{8,0},{10,2},{12,4},{14,6},{16,8},{18,10},{20,12},{22,14},{24,16},... | collective-permute-start | bytes 1572872 | tf_op jit(solution)/shard_map/ppermute | solution.py:570
  231.9 14.7 %collective-permute-start.16 = (bf16[128,2048]{1,0:T(8,128)(2,1)S(1)}, bf16[128,2048]{1,0:T(8,128)(2,1)}, u32[]{:S(2)}, u32[]{:S(2)}) collective-permute-start(bf16[128,2048]{1,0:T(8,128)(2,1)S(1)} %collective-permute-done.14), channel_id=1, source_target_pairs={{0,8},{2,10},{4,12},{6,14},{8,16},{10,18},{12,20},{14,22},{16,24},... | collective-permute-start | bytes 1572872 | tf_op jit(solution)/shard_map/ppermute | solution.py:569
  233.8 14.7 %collective-permute-start.17 = (bf16[128,2048]{1,0:T(8,128)(2,1)}, bf16[128,2048]{1,0:T(8,128)(2,1)S(1)}, u32[]{:S(2)}, u32[]{:S(2)}) collective-permute-start(bf16[128,2048]{1,0:T(8,128)(2,1)} %collective-permute-done.15), channel_id=1, source_target_pairs={{8,0},{10,2},{12,4},{14,6},{16,8},{18,10},{20,12},{22,14},{24,16},... | collective-permute-start | bytes 1572872 | tf_op jit(solution)/shard_map/ppermute | solution.py:570
  252.8 4.2 collective-permute-start.18
  275.1 1.9 collective-permute-start.20
  275.2 2.5 collective-permute-start.22
  279.1 16.3 %collective-permute-start.23 = (bf16[128,2048]{1,0:T(8,128)(2,1)}, bf16[128,2048]{1,0:T(8,128)(2,1)}, u32[]{:S(2)}, u32[]{:S(2)}) collective-permute-start(bf16[128,2048]{1,0:T(8,128)(2,1)} %get-tuple-element.215), channel_id=1, source_target_pairs={{0,8},{2,10},{4,12},{6,14},{8,16},{10,18},{12,20},{14,22},{16,24},... | collective-permute-start | bytes 1572872 | tf_op jit(solution)/shard_map/ppermute | solution.py:599
  281.2 16.2 %collective-permute-start.24 = (bf16[128,2048]{1,0:T(8,128)(2,1)}, bf16[128,2048]{1,0:T(8,128)(2,1)}, u32[]{:S(2)}, u32[]{:S(2)}) collective-permute-start(bf16[128,2048]{1,0:T(8,128)(2,1)} %get-tuple-element.214), channel_id=1, source_target_pairs={{8,0},{10,2},{12,4},{14,6},{16,8},{18,10},{20,12},{22,14},{24,16},... | collective-permute-start | bytes 1572872 | tf_op jit(solution)/shard_map/ppermute | solution.py:600
  297.4 103.1 %reduce-scatter.7.cloned.1.call-start = ((), (), s32[]{:S(2)}) async-start(), calls=%async_computation.17 | async-start | bytes 3604480 | tf_op jit(solution)/shard_map/reduce_scatter | solution.py:719
  297.5 2.2 collective-permute-start.21
  302.5 16.3 %collective-permute-start.25 = (bf16[128,2048]{1,0:T(8,128)(2,1)}, bf16[128,2048]{1,0:T(8,128)(2,1)}, u32[]{:S(2)}, u32[]{:S(2)}) collective-permute-start(bf16[128,2048]{1,0:T(8,128)(2,1)} %get-tuple-element.205), channel_id=1, source_target_pairs={{0,8},{2,10},{4,12},{6,14},{8,16},{10,18},{12,20},{14,22},{16,24},... | collective-permute-start | bytes 1572872 | tf_op jit(solution)/shard_map/ppermute | solution.py:599
  304.4 16.3 %collective-permute-start.26 = (bf16[128,2048]{1,0:T(8,128)(2,1)}, bf16[128,2048]{1,0:T(8,128)(2,1)}, u32[]{:S(2)}, u32[]{:S(2)}) collective-permute-start(bf16[128,2048]{1,0:T(8,128)(2,1)} %get-tuple-element.204), channel_id=1, source_target_pairs={{8,0},{10,2},{12,4},{14,6},{16,8},{18,10},{20,12},{22,14},{24,16},... | collective-permute-start | bytes 1572872 | tf_op jit(solution)/shard_map/ppermute | solution.py:600
  320.8 160.9 %reduce-scatter.9.cloned.1.call-start = ((), (), s32[]{:S(2)}) async-start(), calls=%async_computation.18 | async-start | bytes 3604480 | tf_op jit(solution)/shard_map/reduce_scatter | solution.py:719
  321.0 2.0 collective-permute-start.19
  327.0 16.1 %collective-permute-start.27 = (bf16[128,2048]{1,0:T(8,128)(2,1)}, bf16[128,2048]{1,0:T(8,128)(2,1)S(1)}, u32[]{:S(2)}, u32[]{:S(2)}) collective-permute-start(bf16[128,2048]{1,0:T(8,128)(2,1)} %get-tuple-element.212), channel_id=1, source_target_pairs={{0,8},{2,10},{4,12},{6,14},{8,16},{10,18},{12,20},{14,22},{16,24},... | collective-permute-start | bytes 1572872 | tf_op jit(solution)/shard_map/ppermute | solution.py:599
  328.9 15.8 %collective-permute-start.28 = (bf16[128,2048]{1,0:T(8,128)(2,1)S(1)}, bf16[128,2048]{1,0:T(8,128)(2,1)S(1)}, u32[]{:S(2)}, u32[]{:S(2)}) collective-permute-start(bf16[128,2048]{1,0:T(8,128)(2,1)S(1)} %get-tuple-element.211), channel_id=1, source_target_pairs={{8,0},{10,2},{12,4},{14,6},{16,8},{18,10},{20,12},{22,14},{24,16},... | collective-permute-start | bytes 1572872 | tf_op jit(solution)/shard_map/ppermute | solution.py:600
  349.5 2.1 collective-permute-start.29
  358.2 41.2 %all-to-all-start.3 = ((bf16[4,128,704]{1,2,0:T(8,128)(2,1)}), bf16[4,128,704]{1,2,0:T(8,128)(2,1)S(1)}, u32[]{:S(2)}, u32[]{:S(2)}) async-start(bf16[4,128,704]{1,2,0:T(8,128)(2,1)} %copy_bitcast_fusion.6), calls=%async_computation.5 | async-start | bytes 1441792 | tf_op jit(solution)/shard_map/all_to_all | solution.py:557
  386.6 2.8 collective-permute-start.31
  386.6 2.9 collective-permute-start.33
  387.2 57.7 %collective-permute-start.32 = (bf16[128,2048]{1,0:T(8,128)(2,1)}, bf16[128,2048]{1,0:T(8,128)(2,1)}, u32[]{:S(2)}, u32[]{:S(2)}) collective-permute-start(bf16[128,2048]{1,0:T(8,128)(2,1)} %get-tuple-element.219), channel_id=1, source_target_pairs={{0,1},{1,0},{2,3},{3,2},{4,5},{5,4},{6,7},{7,6},{8,9},{9,8},{10,11... | collective-permute-start | bytes 1572872 | tf_op jit(solution)/shard_map/ppermute | solution.py:436
  392.7 20.4 %collective-permute-start.34 = (bf16[128,2048]{1,0:T(8,128)(2,1)}, bf16[128,2048]{1,0:T(8,128)(2,1)}, u32[]{:S(2)}, u32[]{:S(2)}) collective-permute-start(bf16[128,2048]{1,0:T(8,128)(2,1)} %get-tuple-element.210), channel_id=1, source_target_pairs={{0,8},{2,10},{4,12},{6,14},{8,16},{10,18},{12,20},{14,22},{16,24},... | collective-permute-start | bytes 1572872 | tf_op jit(solution)/shard_map/ppermute | solution.py:599
  396.1 19.9 %collective-permute-start.35 = (bf16[128,2048]{1,0:T(8,128)(2,1)}, bf16[128,2048]{1,0:T(8,128)(2,1)}, u32[]{:S(2)}, u32[]{:S(2)}) collective-permute-start(bf16[128,2048]{1,0:T(8,128)(2,1)} %get-tuple-element.209), channel_id=1, source_target_pairs={{8,0},{10,2},{12,4},{14,6},{16,8},{18,10},{20,12},{22,14},{24,16},... | collective-permute-start | bytes 1572872 | tf_op jit(solution)/shard_map/ppermute | solution.py:600
  400.6 15.4 %collective-permute-start.44 = (bf16[128,2048]{1,0:T(8,128)(2,1)}, bf16[128,2048]{1,0:T(8,128)(2,1)}, u32[]{:S(2)}, u32[]{:S(2)}) collective-permute-start(bf16[128,2048]{1,0:T(8,128)(2,1)} %get-tuple-element.144), channel_id=1, source_target_pairs={{0,2},{2,0},{4,6},{6,4},{8,10},{10,8},{12,14},{14,12},{16,18},{18,... | collective-permute-start | bytes 1572872 | tf_op jit(solution)/shard_map/ppermute | solution.py:612
  402.4 23.9 %collective-permute-start.45 = (bf16[128,2048]{1,0:T(8,128)(2,1)}, bf16[128,2048]{1,0:T(8,128)(2,1)}, u32[]{:S(2)}, u32[]{:S(2)}) collective-permute-start(bf16[128,2048]{1,0:T(8,128)(2,1)} %get-tuple-element.144), channel_id=1, source_target_pairs={{0,4},{2,6},{4,0},{6,2},{8,12},{10,14},{12,8},{14,10},{16,20},{18,... | collective-permute-start | bytes 1572872 | tf_op jit(solution)/shard_map/ppermute | solution.py:612
  406.1 48.5 %all-to-all-start.4 = ((bf16[256,4,800]{0,2,1:T(8,128)(2,1)}), bf16[256,4,800]{0,2,1:T(8,128)(2,1)S(1)}, u32[]{:S(2)}, u32[]{:S(2)}) async-start(bf16[256,4,800]{0,2,1:T(8,128)(2,1)} %pad_maximum_fusion.3), calls=%async_computation.6 | async-start | bytes 3276800 | tf_op jit(solution)/shard_map/all_to_all | solution.py:557
  409.6 195.0 %reduce-scatter.11.cloned.1.call-start = ((), (), s32[]{:S(2)}) async-start(), calls=%async_computation.19 | async-start | bytes 5406720 | tf_op jit(solution)/shard_map/reduce_scatter | solution.py:687
  413.2 30.9 %collective-permute-start.46 = (bf16[128,2048]{1,0:T(8,128)(2,1)S(1)}, bf16[128,2048]{1,0:T(8,128)(2,1)S(1)}, u32[]{:S(2)}, u32[]{:S(2)}) collective-permute-start(bf16[128,2048]{1,0:T(8,128)(2,1)S(1)} %copy-done.24), channel_id=1, source_target_pairs={{0,6},{2,4},{4,2},{6,0},{8,14},{10,12},{12,10},{14,8},{16,22},{18,... | collective-permute-start | bytes 1572872 | tf_op jit(solution)/shard_map/ppermute | solution.py:612
  444.9 29.4 %collective-permute-start.47 = (bf16[512,2048]{1,0:T(8,128)(2,1)}, bf16[512,2048]{1,0:T(8,128)(2,1)}, u32[]{:S(2)}, u32[]{:S(2)}) collective-permute-start(bf16[512,2048]{1,0:T(8,128)(2,1)} %bitcast.34), channel_id=1, source_target_pairs={{0,1},{1,0},{2,3},{3,2},{4,5},{5,4},{6,7},{7,6},{8,9},{9,8},{10,11... | collective-permute-start | bytes 6291464 | tf_op jit(solution)/shard_map/ppermute | solution.py:436
  447.9 17.5 %collective-permute-start.36 = (bf16[128,2048]{1,0:T(8,128)(2,1)}, bf16[128,2048]{1,0:T(8,128)(2,1)}, u32[]{:S(2)}, u32[]{:S(2)}) collective-permute-start(bf16[128,2048]{1,0:T(8,128)(2,1)} %get-tuple-element.203), channel_id=1, source_target_pairs={{0,8},{2,10},{4,12},{6,14},{8,16},{10,18},{12,20},{14,22},{16,24},... | collective-permute-start | bytes 1572872 | tf_op jit(solution)/shard_map/ppermute | solution.py:599
  450.5 16.8 %collective-permute-start.37 = (bf16[128,2048]{1,0:T(8,128)(2,1)}, bf16[128,2048]{1,0:T(8,128)(2,1)}, u32[]{:S(2)}, u32[]{:S(2)}) collective-permute-start(bf16[128,2048]{1,0:T(8,128)(2,1)} %get-tuple-element.202), channel_id=1, source_target_pairs={{8,0},{10,2},{12,4},{14,6},{16,8},{18,10},{20,12},{22,14},{24,16},... | collective-permute-start | bytes 1572872 | tf_op jit(solution)/shard_map/ppermute | solution.py:600
  481.8 76.9 %collective-permute-start.30 = (bf16[128,2048]{1,0:T(8,128)(2,1)}, bf16[128,2048]{1,0:T(8,128)(2,1)}, u32[]{:S(2)}, u32[]{:S(2)}) collective-permute-start(bf16[128,2048]{1,0:T(8,128)(2,1)} %get-tuple-element.222), channel_id=1, source_target_pairs={{0,1},{1,0},{2,3},{3,2},{4,5},{5,4},{6,7},{7,6},{8,9},{9,8},{10,11... | collective-permute-start | bytes 1572872 | tf_op jit(solution)/shard_map/ppermute | solution.py:436
  493.5 14.4 %collective-permute-start.41 = (f32[128,2048]{1,0:T(8,128)}, f32[128,2048]{1,0:T(8,128)}, u32[]{:S(2)}, u32[]{:S(2)}) collective-permute-start(f32[128,2048]{1,0:T(8,128)} %convolution_add_fusion.2), channel_id=1, source_target_pairs={{0,1},{1,0},{2,3},{3,2},{4,5},{5,4},{6,7},{7,6},{8,9},{9,8},{10,11... | collective-permute-start | bytes 3145736 | tf_op jit(solution)/shard_map/ppermute | solution.py:436
  495.6 41.2 %all-to-all-start.7 = ((bf16[4,128,704]{1,2,0:T(8,128)(2,1)}), bf16[4,128,704]{1,2,0:T(8,128)(2,1)}, u32[]{:S(2)}, u32[]{:S(2)}) async-start(bf16[4,128,704]{1,2,0:T(8,128)(2,1)} %copy_bitcast_fusion.5), calls=%async_computation.11 | async-start | bytes 1441792 | tf_op jit(solution)/shard_map/all_to_all | solution.py:557
  512.5 1.2 collective-permute-start.43
  536.9 17.0 %all-to-all-start.5 = ((f32[16,2,128]{2,1,0:T(2,128)}), f32[16,2,128]{2,1,0:T(2,128)S(1)}, u32[]{:S(2)}, u32[]{:S(2)}) async-start(f32[16,2,128]{2,1,0:T(2,128)} %add_bitcast_fusion), calls=%async_computation.7 | async-start | bytes 32768 | tf_op jit(solution)/shard_map/all_to_all | solution.py:792
  553.9 53.2 %all-to-all-start.8 = ((bf16[4,128,704]{1,2,0:T(8,128)(2,1)}), bf16[4,128,704]{1,2,0:T(8,128)(2,1)S(1)}, u32[]{:S(2)}, u32[]{:S(2)}) async-start(bf16[4,128,704]{1,2,0:T(8,128)(2,1)} %copy_bitcast_fusion.4), calls=%async_computation.12 | async-start | bytes 1441792 | tf_op jit(solution)/shard_map/all_to_all | solution.py:557
  563.1 36.6 %collective-permute-start.38 = (bf16[128,2048]{1,0:T(8,128)(2,1)}, bf16[128,2048]{1,0:T(8,128)(2,1)S(1)}, u32[]{:S(2)}, u32[]{:S(2)}) collective-permute-start(bf16[128,2048]{1,0:T(8,128)(2,1)} %get-tuple-element.207), channel_id=1, source_target_pairs={{0,8},{2,10},{4,12},{6,14},{8,16},{10,18},{12,20},{14,22},{16,24},... | collective-permute-start | bytes 1572872 | tf_op jit(solution)/shard_map/ppermute | solution.py:599
  566.5 35.2 %collective-permute-start.39 = (bf16[128,2048]{1,0:T(8,128)(2,1)}, bf16[128,2048]{1,0:T(8,128)(2,1)}, u32[]{:S(2)}, u32[]{:S(2)}) collective-permute-start(bf16[128,2048]{1,0:T(8,128)(2,1)} %get-tuple-element.206), channel_id=1, source_target_pairs={{8,0},{10,2},{12,4},{14,6},{16,8},{18,10},{20,12},{22,14},{24,16},... | collective-permute-start | bytes 1572872 | tf_op jit(solution)/shard_map/ppermute | solution.py:600
  570.5 41.8 %collective-permute-start.42 = (f32[128,2048]{1,0:T(8,128)}, f32[128,2048]{1,0:T(8,128)}, u32[]{:S(2)}, u32[]{:S(2)}) collective-permute-start(f32[128,2048]{1,0:T(8,128)} %get-tuple-element.137), channel_id=1, source_target_pairs={{0,1},{1,0},{2,3},{3,2},{4,5},{5,4},{6,7},{7,6},{8,9},{9,8},{10,11... | collective-permute-start | bytes 3145736 | tf_op jit(solution)/shard_map/ppermute | solution.py:436
  604.6 10.0 %collective-permute-start.40 = (bf16[128,2048]{1,0:T(8,128)(2,1)}, bf16[128,2048]{1,0:T(8,128)(2,1)S(1)}, u32[]{:S(2)}, u32[]{:S(2)}) collective-permute-start(bf16[128,2048]{1,0:T(8,128)(2,1)} %block_result.1), channel_id=1, source_target_pairs={{0,1},{1,0},{2,3},{3,2},{4,5},{5,4},{6,7},{7,6},{8,9},{9,8},{10,11... | collective-permute-start | bytes 1572872 | tf_op jit(solution)/shard_map/ppermute | solution.py:436
  607.9 18.4 %all-to-all-start.6 = ((bf16[4,128,1056]{1,2,0:T(8,128)(2,1)}), bf16[4,128,1056]{1,2,0:T(8,128)(2,1)S(1)}, u32[]{:S(2)}, u32[]{:S(2)}) async-start(bf16[4,128,1056]{1,2,0:T(8,128)(2,1)} %copy_bitcast_fusion), calls=%async_computation.10 | async-start | bytes 2162688 | tf_op jit(solution)/shard_map/all_to_all | solution.py:557
  (53 other events, 400.5 us)
Sparse Core Ops, SparseCore 0:
  53.2 53.4 all-gather.3
  120.6 37.1 all-gather.5
  192.0 36.9 all-gather.7
  297.6 32.1 reduce-scatter.4
  331.9 32.3 reduce-scatter.6
  366.5 32.3 reduce-scatter.8
  481.9 112.7 reduce-scatter.10

commit v5 on v4

--- a/solution.py
+++ b/solution.py
@@ -569,6 +569,7 @@
         below = lax.ppermute(below, "dp", grid.up)
         above = lax.ppermute(above, "dp", grid.down)
         extra = beside[k] if k < len(beside) else ()
+        extra = extra(*done) if callable(extra) else extra
         below, above, *extra = tie(below, above, *extra)
         from_below.append(below)
         from_above.append(above)
@@ -583,14 +584,15 @@
     return jnp.concatenate([own, swap(own)], axis=0)
 
 
-def scatter_tokens(x, grid, beside=()):
+def add_other_core(x, grid):
     n = grid.outer
     size = x.shape[0] // (2 * n)
     block = [x[k * size : (k + 1) * size] for k in range(2 * n)]
-    order = [k for s in range(1, n) for k in (n - s, s)]
-    order = list(dict.fromkeys(order)) + [0]
-    swapped = {k: swap(block[n + k].astype(bf16)) for k in order}
-    own = {k: block[k] + swapped[k].astype(f32) for k in order}
+    return [block[k] + swap(block[n + k].astype(bf16)).astype(f32) for k in range(n)]
+
+
+def scatter_along(own, grid, beside=()):
+    n = grid.outer
     up = down = None
     done = []
     for k in range(n - 1):
@@ -599,6 +601,7 @@
         up = lax.ppermute(up.astype(bf16), "dp", grid.up)
         down = lax.ppermute(down.astype(bf16), "dp", grid.down)
         extra = beside[k] if k < len(beside) else ()
+        extra = extra(*done) if callable(extra) else extra
         up, down, *extra = tie(up, down, *extra)
         done += extra
     return (own[0], up, down), done
@@ -611,7 +614,7 @@
         if k:
             y = lax.ppermute(x, "dp", [(d, d ^ k) for d in range(grid.dp)])
         out = lax.dynamic_update_slice_in_dim(out, y[None], inner ^ k, 0)
-    return out.reshape(INNER * x.shape[0], x.shape[1])
+    return out
 
 
 def on_device(
@@ -658,30 +661,32 @@
     value = jax.nn.silu(value_pre).astype(bf16)
     log_keep = jax.nn.log_sigmoid(forget_pre) * tau_inv
     mixed, *saved = attend_forward(query, key, value, log_keep, doc_starts)
-    mixed, gate_piece, up_piece, down_later = tie(mixed, gate_piece, up_piece, w_down)
+    normed_own = lax.all_gather(
+        half_of(normed, core), "dp", axis=0, tiled=True, axis_index_groups=grid.rows
+    )
+    mixed, gate_piece, up_piece, down_later, normed_own = tie(
+        mixed, gate_piece, up_piece, w_down, normed_own
+    )
     full_gate, full_up = gather_rows(gate_piece), gather_rows(up_piece)
     down_piece = columns(down_later)
 
     branch_other = swap(nt(half_of(mixed, 1 - core), w_output))
     branch_mine = nt(half_of(mixed, core), w_output)
     hidden, normed_two = second_norm(block_in, branch_mine, branch_other, mlp_gain, core, grid)
-    def plane_tokens(half):
-        own = plane_gather(half, grid, inner)
-        return own, swap(own)
+    def plane_tokens(own):
+        own = own.reshape(INNER, 1, -1, own.shape[-1])
+        out = jnp.zeros((INNER, 2) + own.shape[2:], own.dtype)
+        out = lax.dynamic_update_slice_in_dim(out, own, core, 1)
+        out = lax.dynamic_update_slice_in_dim(out, swap(own), 1 - core, 1)
+        return out.reshape(-1, own.shape[-1])
 
     def plane_columns(parts):
         rows = parts[0].shape[0]
         x = jnp.concatenate([p.reshape(rows, INNER, -1) for p in parts], axis=2)
-        size = x.shape[2]
-        x = exchange(x.reshape(rows, INNER * size), 1, 0, grid.rows)
-        x = x.reshape(INNER, 2, rows // 2, size)
-        return tuple(
-            lax.dynamic_index_in_dim(x, c, 1, keepdims=False).reshape(-1, size)
-            for c in (core, 1 - core)
-        )
+        return exchange(x.reshape(rows, -1), 1, 0, grid.rows)
 
     def plane_product(left, right):
-        return (tn(left[0], right[0]) + tn(left[1], right[1])).astype(bf16)
+        return tn(left, right).astype(bf16)
 
     def plane_sum(g):
         return lax.psum_scatter(
@@ -693,26 +698,24 @@
         return exchange(g, 0, 1, grid.rows).reshape(-1, INNER, size).astype(f32)
 
     cot_rows = cotangent_rows(out_grad, core, grid)
-    own, (cot_rows, down_piece, normed_own, normed_rest, full_gate) = gather_along(
+    own, (cot_rows, down_piece, normed_plane, full_gate) = gather_along(
         normed_two,
         grid,
         place,
-        ((cot_rows, down_piece), plane_tokens(half_of(normed, core)), (full_gate,)),
-    )
-    normed_plane = (normed_own, normed_rest)
+        ((cot_rows, down_piece), (plane_tokens(normed_own),), (full_gate,)),
+    )
     full_down = gather_rows(down_piece)
     tokens = with_other_core(own)
-    own, (gate_act, full_up, mixed_own, mixed_rest, up_act, full_down) = gather_along(
+    own, (gate_act, full_up, mixed_plane, up_act, full_down) = gather_along(
         cot_rows,
         grid,
         place,
         (
             (nn(tokens, full_gate), full_up),
-            plane_columns([mixed]),
+            (plane_columns([mixed]),),
             (nn(tokens, full_up), full_down),
         ),
     )
-    mixed_plane = (mixed_own, mixed_rest)
     cot_all = with_other_core(own)
 
     def scatter_rows(g):
@@ -727,12 +730,12 @@
     gate_grad = (inner_grad * up_act * silu_slope(gate_act)).astype(bf16)
     up_grad = (inner_grad * jax.nn.silu(gate_act)).astype(bf16)
     inner_act = (jax.nn.silu(gate_act) * up_act).astype(bf16)
-    back_parts, (down_rows, gate_rows, up_rows) = scatter_tokens(
-        nt(gate_grad, full_gate) + nt(up_grad, full_up),
+    back_parts, (down_rows, *out_own, gate_rows, up_rows) = scatter_along(
+        add_other_core(nt(gate_grad, full_gate) + nt(up_grad, full_up), grid),
         grid,
         (
             (tn(cot_all, inner_act).astype(bf16),),
-            (tn(tokens, gate_grad).astype(bf16),),
+            (*add_other_core(nt(inner_act, full_down), grid), tn(tokens, gate_grad).astype(bf16)),
             (tn(tokens, up_grad).astype(bf16),),
         ),
     )
@@ -742,7 +745,7 @@
     )
     branch_grad = join(low_half, swap(low_half), core)
     mixed_grad = nn(branch_grad, w_output).astype(bf16)
-    mixed_grad, down_rows, later_act = tie(mixed_grad, down_rows, inner_act)
+    mixed_grad, down_rows = tie(mixed_grad, down_rows)
     saved_grads = attend_backward(query, key, value, log_keep, doc_starts, saved, mixed_grad)
     query_grad, key_grad, value_grad, log_grad = saved_grads
     query_pre_grad = (query_grad * silu_slope(query_pre)).astype(bf16)
@@ -751,28 +754,26 @@
     forget_pre_grad = (log_grad * tau_inv * jax.nn.sigmoid(-forget_pre)).astype(bf16)
     pre_grads = (query_pre_grad, key_pre_grad, value_pre_grad, forget_pre_grad)
 
-    down_sum = to_columns(down_rows)
-    query_pre_grad, gate_rows, down_sum, low_half = tie(
-        query_pre_grad, gate_rows, down_sum, low_half
-    )
+    query_pre_grad, *out_own = tie(query_pre_grad, *out_own)
     pre_grads = (query_pre_grad,) + pre_grads[1:]
-    out_parts, (query_pre_grad, *grad_columns) = scatter_tokens(
-        nt(later_act, full_down), grid, ((query_pre_grad,), tuple(plane_columns(pre_grads)))
-    )
-    pre_grads = (query_pre_grad,) + pre_grads[1:]
-    output_grad = plane_product(plane_tokens(low_half), mixed_plane)
-    pre_grad = plane_product(normed_plane, grad_columns)
-    pre_grad, up_rows = tie(jnp.concatenate([pre_grad, output_grad], axis=1), up_rows)
-    sums = plane_sum(pre_grad)
-
+    grad_columns = plane_columns(pre_grads)
+    out_parts, (grad_columns, pre_grad, low_half) = scatter_along(
+        out_own,
+        grid,
+        ((grad_columns,), lambda columns: (plane_product(normed_plane, columns), low_half)),
+    )
+    low_plane = plane_tokens(plane_gather(low_half, grid, inner))
+    sums, output_grad = tie(plane_sum(pre_grad), plane_product(low_plane, mixed_plane))
+    output_sum = plane_sum(output_grad)
     result = block_result(block_in, hidden, out_parts, core, grid)
     result = join(result, swap(result), core)
 
     sums = from_plane(sums)
+    output_sum = from_plane(output_sum).reshape(sums.shape[0], -1)
     ends = [0]
-    for g in (*pre_grads, mixed):
+    for g in pre_grads:
         ends.append(ends[-1] + g.shape[1] // INNER)
-    query_sum, key_sum, value_sum, forget_sum, output_sum = (
+    query_sum, key_sum, value_sum, forget_sum = (
         sums[:, :, a:b].reshape(sums.shape[0], -1) for a, b in zip(ends, ends[1:])
     )
 
@@ -803,7 +804,7 @@
         output_sum,
         to_columns(gate_rows),
         to_columns(up_rows),
-        down_sum,
+        to_columns(down_rows),
     )
 
 

time: 646 us -> 576 us (0.89)
  the two profiles are of different devices: /device:TPU:8 before, /device:TPU:18 now
where the time goes in v5:
time: 576 us; the launch traced here: 565 us
  waiting for transfers between devices  157 us (27%)
  starting transfers between devices  137 us (24%)
  matrix products  103 us (18%)
  local copies, waits for them, and re-layouts  72.6 us (13%)
  other arithmetic  49.4 us (9%)
  Pallas kernels  31.3 us (5%)
  between operations  15.2 us (3%)
    all_to_all x9, starting transfers between devices, exchange(): lax.all_to_all(x, 'dp', split, concat, tiled=True, axis_index_groups=groups)  48.6 us
    dot_general x13, matrix products, nt(): lax.dot_general(a.astype(bf16), b.astype(bf16), (((1,), (1,)), ((), ())),...  46 us
    ppermute x6, waiting for transfers between devices, scatter_along(): up = lax.ppermute(up.astype(bf16), 'dp', grid.up)  40.7 us
    all_to_all x9, waiting for transfers between devices, exchange(): lax.all_to_all(x, 'dp', split, concat, tiled=True, axis_index_groups=groups)  39.1 us
    dot_general x8, matrix products, nn(): return jnp.dot(a.astype(bf16), b.astype(bf16), preferred_element_type=f32)  33.6 us
    dot_general x5, matrix products, tn(): lax.dot_general(a.astype(bf16), b.astype(bf16), (((0,), (0,)), ((), ())),...  23 us
    ppermute x6, starting transfers between devices, gather_along(): above = lax.ppermute(above, 'dp', grid.down)  22.2 us
    ppermute x6, starting transfers between devices, scatter_along(): down = lax.ppermute(down.astype(bf16), 'dp', grid.down)  22.1 us
  transfers between devices with their start and end apart: 64, of which 34 were waited for; matrix products, arithmetic and copies ran while one was open for 34% of the time, Pallas kernels for 6%

profile of v5, /device:TPU:18, one launch (start us, length us, event | category | flops | bytes accessed | tf_op | source)
XLA Modules:
  0.0 565.1 jit_solution(12471856994606693499)
XLA Ops:
  14.3 5.2 all-to-all-start
  20.7 4.8 multiply_convert_fusion.8
  30.4 6.4 %slot_forward.1 = (bf16[256,1024]{1,0:T(8,128)(2,1)}, f32[256,128]{1,0:T(8,128)}, f32[4,256,128]{2,1,0:T(8,128)}, bf16[2,256,256]{2,1,0:T(8,128)(2,1)}, bf16[2,256,16]{2,1,0:T(8,128)(2,1)}) custom-call(s32[1,3]{1,0:T(1,128)} %starts_ref.3, bf16[256,1024]{1,0:T(8,128)(2,1)} %get-tuple-element.225.q_ref, bf16[256,1024]{1,0:T(8,128)(2,1)} %get-tuple-element.227.k_ref, ...), custom_call_target="tpu_custom_call" | custom-call | flops 4000000000 | bytes 4000000 | tf_op jit(solution)/shard_map/slot_forward/pallas_call | solution.py:348
  36.8 13.6 %all-to-all-done = bf16[128,4,1408]{0,2,1:T(8,128)(2,1)S(1)} async-done(((bf16[128,4,1408]{0,2,1:T(8,128)(2,1)}), bf16[128,4,1408]{0,2,1:T(8,128)(2,1)S(1)}, u32[]{:S(2)}, u32[]{:S(2)}) %all-to-all-start) | async-done | bytes 1441824 | tf_op jit(solution)/shard_map/all_to_all | solution.py:557
  52.9 4.7 fusion.14
  59.3 6.8 %all-to-all-start.1 = ((bf16[128,4,704]{0,2,1:T(8,128)(2,1)}), bf16[128,4,704]{0,2,1:T(8,128)(2,1)S(1)}, u32[]{:S(2)}, u32[]{:S(2)}) async-start(bf16[128,4,704]{0,2,1:T(8,128)(2,1)} %bitcast.6), calls=%async_computation.1 | async-start | bytes 1441792 | tf_op jit(solution)/shard_map/all_to_all | solution.py:557
  68.8 4.7 fusion.16.mine_ref
  74.5 3.1 second_norm.1
  77.6 3.5 collective-permute-start.1
  88.6 5.6 collective-permute-done.1
  98.5 3.9 collective-permute-start.6
  102.4 3.2 bitcast_dynamic-update-slice_fusion
  105.6 5.4 collective-permute-done.5
  114.9 3.9 collective-permute-start.9
  119.7 6.9 %collective-permute-done.8 = bf16[128,2048]{1,0:T(8,128)(2,1)} collective-permute-done((bf16[128,2048]{1,0:T(8,128)(2,1)S(1)}, bf16[128,2048]{1,0:T(8,128)(2,1)}, u32[]{:S(2)}, u32[]{:S(2)}) %collective-permute-start.8) | collective-permute-done | bytes 524320 | tf_op jit(solution)/shard_map/ppermute | solution.py:569
  136.5 4.7 collective-permute-start.4
  141.2 3.2 constant_dynamic-update-slice_fusion
  144.4 7.3 %fusion.38 = f32[1024,704]{0,1:T(8,128)} fusion(bf16[1024,2048]{1,0:T(8,128)(2,1)} %constant_dynamic-update-slice_fusion, bf16[2048,704]{1,0:T(8,128)(2,1)S(1)} %copy-done.15), kind=kOutput, calls=%fused_computation.132 | convolution fusion | flops 2952790016 | bytes 9961472 | tf_op jit(solution)/shard_map/dot_general | solution.py:19
  154.9 4.6 collective-permute-start.12
  160.4 4.3 all-to-all-start.2
  165.5 11.5 %all-to-all-done.2 = bf16[256,4,256]{2,0,1:T(8,128)(2,1)S(1)} async-done(((bf16[256,4,256]{2,0,1:T(8,128)(2,1)}), bf16[256,4,256]{2,0,1:T(8,128)(2,1)S(1)}, u32[]{:S(2)}, u32[]{:S(2)}) %all-to-all-start.2) | async-done | bytes 524320 | tf_op jit(solution)/shard_map/all_to_all | solution.py:557
  177.9 3.3 collective-permute-start.13
  183.7 7.9 %fusion.39 = f32[1024,704]{0,1:T(8,128)} fusion(bf16[1024,2048]{1,0:T(8,128)(2,1)} %constant_dynamic-update-slice_fusion, bf16[2048,704]{1,0:T(8,128)(2,1)} %all-gather.9.cloned.1.call-done), kind=kOutput, calls=%fused_computation.133 | convolution fusion | flops 2952790016 | bytes 9961472 | tf_op jit(solution)/shard_map/dot_general | solution.py:19
  198.6 4.1 collective-permute-done.15
  203.0 3.2 fusion.40
  207.2 3.2 multiply_convert_fusion
  210.4 3.5 fusion.41
  213.9 5.5 fusion.36
  227.7 3.9 collective-permute-start.21
  231.6 4.5 convolution_convert_fusion.3
  236.1 6.0 %collective-permute-done.20 = bf16[128,2048]{1,0:T(8,128)(2,1)} collective-permute-done((bf16[128,2048]{1,0:T(8,128)(2,1)}, bf16[128,2048]{1,0:T(8,128)(2,1)}, u32[]{:S(2)}, u32[]{:S(2)}) %collective-permute-start.20) | collective-permute-done | bytes 524320 | tf_op jit(solution)/shard_map/ppermute | solution.py:601
  244.0 9.1 %fusion.37 = (bf16[1024,2048]{1,0:T(8,128)(2,1)S(1)}, f32[1024,2048]{1,0:T(8,128)}) fusion(bf16[1024,704]{0,1:T(8,128)(2,1)} %get-tuple-element.205, bf16[2048,704]{0,1:T(8,128)(2,1)} %all-gather.11.cloned.1.call-done), kind=kOutput, calls=%fused_computation.131 | convolution fusion | flops 2954887168 | bytes 16908288 | tf_op jit(solution)/shard_map/dot_general | solution.py:23
  256.1 4.5 convolution_convert_fusion.2
  264.5 4.2 collective-permute-start.23
  268.8 4.9 slice_add_fusion
  273.6 5.2 collective-permute-done.22
  283.4 4.0 add_convert_fusion.4
  289.3 4.3 collective-permute-start.29
  293.6 4.5 convolution_convert_fusion.1
  298.1 5.8 %collective-permute-done.28.refs_1_ = bf16[128,2048]{1,0:T(8,128)(2,1)S(1)} collective-permute-done((bf16[128,2048]{1,0:T(8,128)(2,1)}, bf16[128,2048]{1,0:T(8,128)(2,1)S(1)}, u32[]{:S(2)}, u32[]{:S(2)}) %collective-permute-start.28) | collective-permute-done | bytes 524320 | tf_op jit(solution)/shard_map/ppermute | solution.py:601
  305.5 3.9 second_norm_back.1
  311.6 4.4 convolution_convert_fusion.5.do_ref
  315.9 9.2 %slot_backward.1 = (f32[256,1024]{1,0:T(8,128)}, f32[256,1024]{1,0:T(8,128)}, f32[256,1024]{1,0:T(8,128)}, f32[256,128]{1,0:T(8,128)}) custom-call(s32[1,3]{1,0:T(1,128)} %starts_ref.3, bf16[256,1024]{1,0:T(8,128)(2,1)} %get-tuple-element.225.q_ref, bf16[256,1024]{1,0:T(8,128)(2,1)} %get-tuple-element.227.k_ref, bf16[256,1024]{1,0:T(8,128)(2,1)} %get-tuple-element.229.v_ref, ...), custom_call_target="tpu_custom_call" | custom-call | flops 12000000000 | bytes 8000000 | tf_op jit(solution)/shard_map/slot_backward/pallas_call | solution.py:369
  325.2 3.8 multiply_convert_fusion.3
  337.9 5.0 all-to-all-start.3
  346.7 4.5 collective-permute-start.32
  351.3 3.7 fusion.8
  357.5 7.5 %all-to-all-done.3 = bf16[256,4,800]{0,2,1:T(8,128)(2,1)} async-done(((bf16[256,4,800]{0,2,1:T(8,128)(2,1)}), bf16[256,4,800]{0,2,1:T(8,128)(2,1)}, u32[]{:S(2)}, u32[]{:S(2)}) %all-to-all-start.3) | async-done | bytes 1638432 | tf_op jit(solution)/shard_map/all_to_all | solution.py:557
  369.2 3.4 collective-permute-start.33
  375.1 7.1 %convolution_convert_fusion = bf16[2048,800]{0,1:T(8,128)(2,1)} fusion(bf16[1024,800]{0,1:T(8,128)(2,1)S(1)} %bitcast.150, bf16[1024,2048]{1,0:T(8,128)(2,1)} %bitcast.11), kind=kOutput, calls=%fused_computation.1 | convolution fusion | flops 3357081600 | bytes 9109504 | tf_op jit(solution)/shard_map/dot_general | solution.py:29
  385.1 3.1 collective-permute-done.34
  388.3 4.2 convolution_add_fusion.2
  400.4 4.3 all-to-all-start.9
  415.8 13.3 %collective-permute-done.42 = bf16[128,2048]{1,0:T(8,128)(2,1)S(1)} collective-permute-done((bf16[128,2048]{1,0:T(8,128)(2,1)}, bf16[128,2048]{1,0:T(8,128)(2,1)S(1)}, u32[]{:S(2)}, u32[]{:S(2)}) %collective-permute-start.42) | collective-permute-done | bytes 524320 | tf_op jit(solution)/shard_map/ppermute | solution.py:615
  433.7 3.9 first_norm_back.1
  442.3 7.0 %all-to-all-start.4 = ((f32[16,2,128]{2,1,0:T(2,128)}), f32[16,2,128]{2,1,0:T(2,128)S(1)}, u32[]{:S(2)}, u32[]{:S(2)}) async-start(f32[16,2,128]{2,1,0:T(2,128)} %add_bitcast_fusion), calls=%async_computation.5 | async-start | bytes 32768 | tf_op jit(solution)/shard_map/all_to_all | solution.py:793
  453.9 7.4 %all-to-all-start.7 = ((bf16[4,128,704]{1,2,0:T(8,128)(2,1)}), bf16[4,128,704]{1,2,0:T(8,128)(2,1)}, u32[]{:S(2)}, u32[]{:S(2)}) async-start(bf16[4,128,704]{1,2,0:T(8,128)(2,1)} %copy_bitcast_fusion.4), calls=%async_computation.11 | async-start | bytes 1441792 | tf_op jit(solution)/shard_map/all_to_all | solution.py:557
  473.9 4.0 all-to-all-done.7
  478.0 7.6 %all-to-all-start.8 = ((bf16[4,128,704]{1,2,0:T(8,128)(2,1)}), bf16[4,128,704]{1,2,0:T(8,128)(2,1)}, u32[]{:S(2)}, u32[]{:S(2)}) async-start(bf16[4,128,704]{1,2,0:T(8,128)(2,1)} %copy_bitcast_fusion.3), calls=%async_computation.13 | async-start | bytes 1441792 | tf_op jit(solution)/shard_map/all_to_all | solution.py:557
  487.5 3.4 collective-permute-start.35
  497.4 9.8 %collective-permute-done.36.refs_2_ = bf16[128,2048]{1,0:T(8,128)(2,1)} collective-permute-done((bf16[128,2048]{1,0:T(8,128)(2,1)}, bf16[128,2048]{1,0:T(8,128)(2,1)}, u32[]{:S(2)}, u32[]{:S(2)}) %collective-permute-start.36) | collective-permute-done | bytes 524320 | tf_op jit(solution)/shard_map/ppermute | solution.py:602
  507.2 20.7 %collective-permute-done.35.refs_1_ = bf16[128,2048]{1,0:T(8,128)(2,1)} collective-permute-done((bf16[128,2048]{1,0:T(8,128)(2,1)}, bf16[128,2048]{1,0:T(8,128)(2,1)}, u32[]{:S(2)}, u32[]{:S(2)}) %collective-permute-start.35) | collective-permute-done | bytes 524320 | tf_op jit(solution)/shard_map/ppermute | solution.py:601
  531.9 4.2 all-to-all-start.5
  547.6 4.0 all-to-all-start.6
  (292 shorter events, 191.7 us)
Async XLA Ops:
  7.2 45.6 %all-gather.5.cloned.1.call-start = ((), (), s32[]{:S(2)}) async-start(), calls=%async_computation.15 | async-start | bytes 2621440 | tf_op jit(solution)/shard_map/all_gather | solution.py:664
  14.3 36.1 %all-to-all-start = ((bf16[128,4,1408]{0,2,1:T(8,128)(2,1)}), bf16[128,4,1408]{0,2,1:T(8,128)(2,1)S(1)}, u32[]{:S(2)}, u32[]{:S(2)}) async-start(bf16[128,4,1408]{0,2,1:T(8,128)(2,1)} %pad_maximum_fusion.3), calls=%async_computation | async-start | bytes 2883584 | tf_op jit(solution)/shard_map/all_to_all | solution.py:557
  19.5 109.3 %all-gather.7.cloned.1.call-start = ((), (), s32[]{:S(2)}) async-start(), calls=%async_computation.16 | async-start | bytes 3932160 | tf_op jit(solution)/shard_map/all_gather | solution.py:644
  52.8 49.6 %collective-permute-start.7 = (bf16[4,1,128,2048]{3,2,0,1:T(8,128)(2,1)}, bf16[4,1,128,2048]{3,2,0,1:T(8,128)(2,1)}, u32[]{:S(2)}, u32[]{:S(2)}) collective-permute-start(bf16[4,1,128,2048]{3,2,0,1:T(8,128)(2,1)} %bitcast.145), channel_id=1, source_target_pairs={{0,1},{1,0},{2,3},{3,2},{4,5},{5,4},{6,7},{7,6},{8,9},{9,8},{10,11... | collective-permute-start | bytes 6291464 | tf_op jit(solution)/shard_map/ppermute | solution.py:436
  57.7 15.9 %collective-permute-start = (f32[128,2048]{1,0:T(8,128)}, f32[128,2048]{1,0:T(8,128)S(1)}, u32[]{:S(2)}, u32[]{:S(2)}) collective-permute-start(f32[128,2048]{1,0:T(8,128)} %fusion.14), channel_id=1, source_target_pairs={{0,1},{1,0},{2,3},{3,2},{4,5},{5,4},{6,7},{7,6},{8,9},{9,8},{10,11... | collective-permute-start | bytes 3145736 | tf_op jit(solution)/shard_map/ppermute | solution.py:436
  59.3 28.4 %all-to-all-start.1 = ((bf16[128,4,704]{0,2,1:T(8,128)(2,1)}), bf16[128,4,704]{0,2,1:T(8,128)(2,1)S(1)}, u32[]{:S(2)}, u32[]{:S(2)}) async-start(bf16[128,4,704]{0,2,1:T(8,128)(2,1)} %bitcast.6), calls=%async_computation.1 | async-start | bytes 1441792 | tf_op jit(solution)/shard_map/all_to_all | solution.py:557
  66.0 87.0 %all-gather.9.cloned.1.call-start = ((), (), s32[]{:S(2)}) async-start(), calls=%async_computation.17 | async-start | bytes 3932160 | tf_op jit(solution)/shard_map/all_gather | solution.py:644
  66.7 124.9 %all-gather.11.cloned.1.call-start = ((), (), s32[]{:S(2)}) async-start(), calls=%async_computation.18 | async-start | bytes 3604480 | tf_op jit(solution)/shard_map/all_gather | solution.py:644
  77.6 16.6 %collective-permute-start.1 = (bf16[128,2048]{1,0:T(8,128)(2,1)}, bf16[128,2048]{1,0:T(8,128)(2,1)S(1)}, u32[]{:S(2)}, u32[]{:S(2)}) collective-permute-start(bf16[128,2048]{1,0:T(8,128)(2,1)} %get-tuple-element.92), channel_id=1, source_target_pairs={{0,8},{2,10},{4,12},{6,14},{8,16},{10,18},{12,20},{14,22},{16,24},... | collective-permute-start | bytes 1572872 | tf_op jit(solution)/shard_map/ppermute | solution.py:569
  81.1 15.5 %collective-permute-start.2 = (bf16[128,2048]{1,0:T(8,128)(2,1)}, bf16[128,2048]{1,0:T(8,128)(2,1)S(1)}, u32[]{:S(2)}, u32[]{:S(2)}) collective-permute-start(bf16[128,2048]{1,0:T(8,128)(2,1)} %get-tuple-element.92), channel_id=1, source_target_pairs={{8,0},{10,2},{12,4},{14,6},{16,8},{18,10},{20,12},{22,14},{24,16},... | collective-permute-start | bytes 1572872 | tf_op jit(solution)/shard_map/ppermute | solution.py:570
  96.6 14.4 %collective-permute-start.5 = (bf16[128,2048]{1,0:T(8,128)(2,1)S(1)}, bf16[128,2048]{1,0:T(8,128)(2,1)S(1)}, u32[]{:S(2)}, u32[]{:S(2)}) collective-permute-start(bf16[128,2048]{1,0:T(8,128)(2,1)S(1)} %collective-permute-done.1), channel_id=1, source_target_pairs={{0,8},{2,10},{4,12},{6,14},{8,16},{10,18},{12,20},{14,22},{16,24},... | collective-permute-start | bytes 1572872 | tf_op jit(solution)/shard_map/ppermute | solution.py:569
  98.5 14.5 %collective-permute-start.6 = (bf16[128,2048]{1,0:T(8,128)(2,1)S(1)}, bf16[128,2048]{1,0:T(8,128)(2,1)}, u32[]{:S(2)}, u32[]{:S(2)}) collective-permute-start(bf16[128,2048]{1,0:T(8,128)(2,1)S(1)} %collective-permute-done.2), channel_id=1, source_target_pairs={{8,0},{10,2},{12,4},{14,6},{16,8},{18,10},{20,12},{22,14},{24,16},... | collective-permute-start | bytes 1572872 | tf_op jit(solution)/shard_map/ppermute | solution.py:570
  113.0 13.6 %collective-permute-start.8 = (bf16[128,2048]{1,0:T(8,128)(2,1)S(1)}, bf16[128,2048]{1,0:T(8,128)(2,1)}, u32[]{:S(2)}, u32[]{:S(2)}) collective-permute-start(bf16[128,2048]{1,0:T(8,128)(2,1)S(1)} %collective-permute-done.5), channel_id=1, source_target_pairs={{0,8},{2,10},{4,12},{6,14},{8,16},{10,18},{12,20},{14,22},{16,24},... | collective-permute-start | bytes 1572872 | tf_op jit(solution)/shard_map/ppermute | solution.py:569
  114.9 13.9 %collective-permute-start.9 = (bf16[128,2048]{1,0:T(8,128)(2,1)}, bf16[128,2048]{1,0:T(8,128)(2,1)}, u32[]{:S(2)}, u32[]{:S(2)}) collective-permute-start(bf16[128,2048]{1,0:T(8,128)(2,1)} %collective-permute-done.6), channel_id=1, source_target_pairs={{8,0},{10,2},{12,4},{14,6},{16,8},{18,10},{20,12},{22,14},{24,16},... | collective-permute-start | bytes 1572872 | tf_op jit(solution)/shard_map/ppermute | solution.py:570
  134.2 6.9 %collective-permute-start.10 = (bf16[512,2048]{1,0:T(8,128)(2,1)}, bf16[512,2048]{1,0:T(8,128)(2,1)}, u32[]{:S(2)}, u32[]{:S(2)}) collective-permute-start(bf16[512,2048]{1,0:T(8,128)(2,1)} %pad_maximum_fusion), channel_id=1, source_target_pairs={{0,1},{1,0},{2,3},{3,2},{4,5},{5,4},{6,7},{7,6},{8,9},{9,8},{10,11... | collective-permute-start | bytes 6291464 | tf_op jit(solution)/shard_map/ppermute | solution.py:436
  134.3 17.5 %collective-permute-start.3 = (bf16[128,2048]{1,0:T(8,128)(2,1)S(1)}, bf16[128,2048]{1,0:T(8,128)(2,1)S(1)}, u32[]{:S(2)}, u32[]{:S(2)}) collective-permute-start(bf16[128,2048]{1,0:T(8,128)(2,1)S(1)} %copy-done.8), channel_id=1, source_target_pairs={{0,8},{2,10},{4,12},{6,14},{8,16},{10,18},{12,20},{14,22},{16,24},... | collective-permute-start | bytes 1572872 | tf_op jit(solution)/shard_map/ppermute | solution.py:569
  136.5 16.5 %collective-permute-start.4 = (bf16[128,2048]{1,0:T(8,128)(2,1)S(1)}, bf16[128,2048]{1,0:T(8,128)(2,1)S(1)}, u32[]{:S(2)}, u32[]{:S(2)}) collective-permute-start(bf16[128,2048]{1,0:T(8,128)(2,1)S(1)} %copy-done.8), channel_id=1, source_target_pairs={{8,0},{10,2},{12,4},{14,6},{16,8},{18,10},{20,12},{22,14},{24,16},... | collective-permute-start | bytes 1572872 | tf_op jit(solution)/shard_map/ppermute | solution.py:570
  153.0 24.1 %collective-permute-start.11 = (bf16[128,2048]{1,0:T(8,128)(2,1)S(1)}, bf16[128,2048]{1,0:T(8,128)(2,1)S(1)}, u32[]{:S(2)}, u32[]{:S(2)}) collective-permute-start(bf16[128,2048]{1,0:T(8,128)(2,1)S(1)} %collective-permute-done.3), channel_id=1, source_target_pairs={{0,8},{2,10},{4,12},{6,14},{8,16},{10,18},{12,20},{14,22},{16,24},... | collective-permute-start | bytes 1572872 | tf_op jit(solution)/shard_map/ppermute | solution.py:569
  154.9 22.2 %collective-permute-start.12 = (bf16[128,2048]{1,0:T(8,128)(2,1)S(1)}, bf16[128,2048]{1,0:T(8,128)(2,1)}, u32[]{:S(2)}, u32[]{:S(2)}) collective-permute-start(bf16[128,2048]{1,0:T(8,128)(2,1)S(1)} %collective-permute-done.4), channel_id=1, source_target_pairs={{8,0},{10,2},{12,4},{14,6},{16,8},{18,10},{20,12},{22,14},{24,16},... | collective-permute-start | bytes 1572872 | tf_op jit(solution)/shard_map/ppermute | solution.py:570
  160.4 16.7 %all-to-all-start.2 = ((bf16[256,4,256]{2,0,1:T(8,128)(2,1)}), bf16[256,4,256]{2,0,1:T(8,128)(2,1)S(1)}, u32[]{:S(2)}, u32[]{:S(2)}) async-start(bf16[256,4,256]{2,0,1:T(8,128)(2,1)} %bitcast.132), calls=%async_computation.2 | async-start | bytes 1048576 | tf_op jit(solution)/shard_map/all_to_all | solution.py:557
  164.7 151.2 %reduce-scatter.6.cloned.1.call-start = ((), (), s32[]{:S(2)}) async-start(), calls=%async_computation.19 | async-start | bytes 3604480 | tf_op jit(solution)/shard_map/reduce_scatter | solution.py:722
  177.9 15.3 %collective-permute-start.13 = (bf16[128,2048]{1,0:T(8,128)(2,1)S(1)}, bf16[128,2048]{1,0:T(8,128)(2,1)}, u32[]{:S(2)}, u32[]{:S(2)}) collective-permute-start(bf16[128,2048]{1,0:T(8,128)(2,1)S(1)} %collective-permute-done.11), channel_id=1, source_target_pairs={{0,8},{2,10},{4,12},{6,14},{8,16},{10,18},{12,20},{14,22},{16,24},... | collective-permute-start | bytes 1572872 | tf_op jit(solution)/shard_map/ppermute | solution.py:569
  181.1 14.2 %collective-permute-start.14 = (bf16[128,2048]{1,0:T(8,128)(2,1)}, bf16[128,2048]{1,0:T(8,128)(2,1)S(1)}, u32[]{:S(2)}, u32[]{:S(2)}) collective-permute-start(bf16[128,2048]{1,0:T(8,128)(2,1)} %collective-permute-done.12), channel_id=1, source_target_pairs={{8,0},{10,2},{12,4},{14,6},{16,8},{18,10},{20,12},{22,14},{24,16},... | collective-permute-start | bytes 1572872 | tf_op jit(solution)/shard_map/ppermute | solution.py:570
  198.5 4.2 collective-permute-start.15
  220.6 1.9 collective-permute-start.17
  220.8 2.5 collective-permute-start.19
  224.9 17.2 %collective-permute-start.20 = (bf16[128,2048]{1,0:T(8,128)(2,1)}, bf16[128,2048]{1,0:T(8,128)(2,1)}, u32[]{:S(2)}, u32[]{:S(2)}) collective-permute-start(bf16[128,2048]{1,0:T(8,128)(2,1)} %get-tuple-element.204), channel_id=1, source_target_pairs={{0,8},{2,10},{4,12},{6,14},{8,16},{10,18},{12,20},{14,22},{16,24},... | collective-permute-start | bytes 1572872 | tf_op jit(solution)/shard_map/ppermute | solution.py:601
  227.7 15.9 %collective-permute-start.21 = (bf16[128,2048]{1,0:T(8,128)(2,1)}, bf16[128,2048]{1,0:T(8,128)(2,1)}, u32[]{:S(2)}, u32[]{:S(2)}) collective-permute-start(bf16[128,2048]{1,0:T(8,128)(2,1)} %get-tuple-element.203), channel_id=1, source_target_pairs={{8,0},{10,2},{12,4},{14,6},{16,8},{18,10},{20,12},{22,14},{24,16},... | collective-permute-start | bytes 1572872 | tf_op jit(solution)/shard_map/ppermute | solution.py:602
  243.6 195.2 %reduce-scatter.12.cloned.1.call-start = ((), (), s32[]{:S(2)}) async-start(), calls=%async_computation.22 | async-start | bytes 3604480 | tf_op jit(solution)/shard_map/reduce_scatter | solution.py:722
  254.5 10.0 %collective-permute-start.24 = (bf16[128,2048]{1,0:T(8,128)(2,1)}, bf16[128,2048]{1,0:T(8,128)(2,1)}, u32[]{:S(2)}, u32[]{:S(2)}) collective-permute-start(bf16[128,2048]{1,0:T(8,128)(2,1)} %get-tuple-element.211), channel_id=1, source_target_pairs={{0,1},{1,0},{2,3},{3,2},{4,5},{5,4},{6,7},{7,6},{8,9},{9,8},{10,11... | collective-permute-start | bytes 1572872 | tf_op jit(solution)/shard_map/ppermute | solution.py:436
  254.5 14.2 %collective-permute-start.25 = (bf16[128,2048]{1,0:T(8,128)(2,1)}, bf16[128,2048]{1,0:T(8,128)(2,1)}, u32[]{:S(2)}, u32[]{:S(2)}) collective-permute-start(bf16[128,2048]{1,0:T(8,128)(2,1)} %get-tuple-element.210), channel_id=1, source_target_pairs={{0,1},{1,0},{2,3},{3,2},{4,5},{5,4},{6,7},{7,6},{8,9},{9,8},{10,11... | collective-permute-start | bytes 1572872 | tf_op jit(solution)/shard_map/ppermute | solution.py:436
  255.0 13.7 %collective-permute-start.26 = (bf16[128,2048]{1,0:T(8,128)(2,1)}, bf16[128,2048]{1,0:T(8,128)(2,1)}, u32[]{:S(2)}, u32[]{:S(2)}) collective-permute-start(bf16[128,2048]{1,0:T(8,128)(2,1)} %get-tuple-element.209), channel_id=1, source_target_pairs={{0,1},{1,0},{2,3},{3,2},{4,5},{5,4},{6,7},{7,6},{8,9},{9,8},{10,11... | collective-permute-start | bytes 1572872 | tf_op jit(solution)/shard_map/ppermute | solution.py:436
  255.0 13.7 %collective-permute-start.27 = (bf16[128,2048]{1,0:T(8,128)(2,1)}, bf16[128,2048]{1,0:T(8,128)(2,1)}, u32[]{:S(2)}, u32[]{:S(2)}) collective-permute-start(bf16[128,2048]{1,0:T(8,128)(2,1)} %get-tuple-element.208), channel_id=1, source_target_pairs={{0,1},{1,0},{2,3},{3,2},{4,5},{5,4},{6,7},{7,6},{8,9},{9,8},{10,11... | collective-permute-start | bytes 1572872 | tf_op jit(solution)/shard_map/ppermute | solution.py:436
  255.5 5.0 collective-permute-start.18
  262.6 16.3 %collective-permute-start.22 = (bf16[128,2048]{1,0:T(8,128)(2,1)S(1)}, bf16[128,2048]{1,0:T(8,128)(2,1)S(1)}, u32[]{:S(2)}, u32[]{:S(2)}) collective-permute-start(bf16[128,2048]{1,0:T(8,128)(2,1)S(1)} %get-tuple-element.195), channel_id=1, source_target_pairs={{0,8},{2,10},{4,12},{6,14},{8,16},{10,18},{12,20},{14,22},{16,24},... | collective-permute-start | bytes 1572872 | tf_op jit(solution)/shard_map/ppermute | solution.py:601
  264.5 15.8 %collective-permute-start.23 = (bf16[128,2048]{1,0:T(8,128)(2,1)S(1)}, bf16[128,2048]{1,0:T(8,128)(2,1)S(1)}, u32[]{:S(2)}, u32[]{:S(2)}) collective-permute-start(bf16[128,2048]{1,0:T(8,128)(2,1)S(1)} %get-tuple-element.194), channel_id=1, source_target_pairs={{8,0},{10,2},{12,4},{14,6},{16,8},{18,10},{20,12},{22,14},{24,16},... | collective-permute-start | bytes 1572872 | tf_op jit(solution)/shard_map/ppermute | solution.py:602
  281.1 168.2 %reduce-scatter.14.cloned.1.call-start = ((), (), s32[]{:S(2)}) async-start(), calls=%async_computation.23 | async-start | bytes 3604480 | tf_op jit(solution)/shard_map/reduce_scatter | solution.py:722
  281.2 2.2 collective-permute-start.16
  287.4 16.6 %collective-permute-start.28 = (bf16[128,2048]{1,0:T(8,128)(2,1)}, bf16[128,2048]{1,0:T(8,128)(2,1)S(1)}, u32[]{:S(2)}, u32[]{:S(2)}) collective-permute-start(bf16[128,2048]{1,0:T(8,128)(2,1)} %get-tuple-element.197), channel_id=1, source_target_pairs={{0,8},{2,10},{4,12},{6,14},{8,16},{10,18},{12,20},{14,22},{16,24},... | collective-permute-start | bytes 1572872 | tf_op jit(solution)/shard_map/ppermute | solution.py:601
  289.3 16.2 %collective-permute-start.29 = (bf16[128,2048]{1,0:T(8,128)(2,1)}, bf16[128,2048]{1,0:T(8,128)(2,1)}, u32[]{:S(2)}, u32[]{:S(2)}) collective-permute-start(bf16[128,2048]{1,0:T(8,128)(2,1)} %get-tuple-element.196), channel_id=1, source_target_pairs={{8,0},{10,2},{12,4},{14,6},{16,8},{18,10},{20,12},{22,14},{24,16},... | collective-permute-start | bytes 1572872 | tf_op jit(solution)/shard_map/ppermute | solution.py:602
  309.4 2.1 collective-permute-start.30
  337.9 27.1 %all-to-all-start.3 = ((bf16[256,4,800]{0,2,1:T(8,128)(2,1)}), bf16[256,4,800]{0,2,1:T(8,128)(2,1)}, u32[]{:S(2)}, u32[]{:S(2)}) async-start(bf16[256,4,800]{0,2,1:T(8,128)(2,1)} %pad_maximum_fusion.2), calls=%async_computation.4 | async-start | bytes 3276800 | tf_op jit(solution)/shard_map/all_to_all | solution.py:557
  342.9 131.0 %reduce-scatter.8.cloned.1.call-start = ((), (), s32[]{:S(2)}) async-start(), calls=%async_computation.20 | async-start | bytes 4096000 | tf_op jit(solution)/shard_map/reduce_scatter | solution.py:692
  343.7 23.0 %collective-permute-start.31 = (bf16[128,2048]{1,0:T(8,128)(2,1)}, bf16[128,2048]{1,0:T(8,128)(2,1)}, u32[]{:S(2)}, u32[]{:S(2)}) collective-permute-start(bf16[128,2048]{1,0:T(8,128)(2,1)} %convert_element_type.220), channel_id=1, source_target_pairs={{0,8},{2,10},{4,12},{6,14},{8,16},{10,18},{12,20},{14,22},{16,24},... | collective-permute-start | bytes 1572872 | tf_op jit(solution)/shard_map/ppermute | solution.py:601
  346.7 20.0 %collective-permute-start.32 = (bf16[128,2048]{1,0:T(8,128)(2,1)}, bf16[128,2048]{1,0:T(8,128)(2,1)}, u32[]{:S(2)}, u32[]{:S(2)}) collective-permute-start(bf16[128,2048]{1,0:T(8,128)(2,1)} %convert_element_type.221), channel_id=1, source_target_pairs={{8,0},{10,2},{12,4},{14,6},{16,8},{18,10},{20,12},{22,14},{24,16},... | collective-permute-start | bytes 1572872 | tf_op jit(solution)/shard_map/ppermute | solution.py:602
  369.2 15.9 %collective-permute-start.33 = (bf16[128,2048]{1,0:T(8,128)(2,1)}, bf16[128,2048]{1,0:T(8,128)(2,1)}, u32[]{:S(2)}, u32[]{:S(2)}) collective-permute-start(bf16[128,2048]{1,0:T(8,128)(2,1)} %get-tuple-element.222), channel_id=1, source_target_pairs={{0,8},{2,10},{4,12},{6,14},{8,16},{10,18},{12,20},{14,22},{16,24},... | collective-permute-start | bytes 1572872 | tf_op jit(solution)/shard_map/ppermute | solution.py:601
  372.6 15.6 %collective-permute-start.34 = (bf16[128,2048]{1,0:T(8,128)(2,1)}, bf16[128,2048]{1,0:T(8,128)(2,1)}, u32[]{:S(2)}, u32[]{:S(2)}) collective-permute-start(bf16[128,2048]{1,0:T(8,128)(2,1)} %get-tuple-element.221), channel_id=1, source_target_pairs={{8,0},{10,2},{12,4},{14,6},{16,8},{18,10},{20,12},{22,14},{24,16},... | collective-permute-start | bytes 1572872 | tf_op jit(solution)/shard_map/ppermute | solution.py:602
  393.8 39.8 %collective-permute-start.38 = (f32[128,2048]{1,0:T(8,128)}, f32[128,2048]{1,0:T(8,128)}, u32[]{:S(2)}, u32[]{:S(2)}) collective-permute-start(f32[128,2048]{1,0:T(8,128)} %convolution_add_fusion.1), channel_id=1, source_target_pairs={{0,1},{1,0},{2,3},{3,2},{4,5},{5,4},{6,7},{7,6},{8,9},{9,8},{10,11... | collective-permute-start | bytes 3145736 | tf_op jit(solution)/shard_map/ppermute | solution.py:436
  398.8 15.1 %collective-permute-start.41 = (bf16[128,2048]{1,0:T(8,128)(2,1)}, bf16[128,2048]{1,0:T(8,128)(2,1)}, u32[]{:S(2)}, u32[]{:S(2)}) collective-permute-start(bf16[128,2048]{1,0:T(8,128)(2,1)} %get-tuple-element.151), channel_id=1, source_target_pairs={{0,2},{2,0},{4,6},{6,4},{8,10},{10,8},{12,14},{14,12},{16,18},{18,... | collective-permute-start | bytes 1572872 | tf_op jit(solution)/shard_map/ppermute | solution.py:615
  400.4 41.9 %all-to-all-start.9 = ((bf16[4,128,704]{1,2,0:T(8,128)(2,1)}), bf16[4,128,704]{1,2,0:T(8,128)(2,1)S(1)}, u32[]{:S(2)}, u32[]{:S(2)}) async-start(bf16[4,128,704]{1,2,0:T(8,128)(2,1)} %copy_bitcast_fusion.2), calls=%async_computation.14 | async-start | bytes 1441792 | tf_op jit(solution)/shard_map/all_to_all | solution.py:557
  404.6 24.5 %collective-permute-start.42 = (bf16[128,2048]{1,0:T(8,128)(2,1)}, bf16[128,2048]{1,0:T(8,128)(2,1)S(1)}, u32[]{:S(2)}, u32[]{:S(2)}) collective-permute-start(bf16[128,2048]{1,0:T(8,128)(2,1)} %get-tuple-element.151), channel_id=1, source_target_pairs={{0,4},{2,6},{4,0},{6,2},{8,12},{10,14},{12,8},{14,10},{16,20},{18,... | collective-permute-start | bytes 1572872 | tf_op jit(solution)/shard_map/ppermute | solution.py:615
  406.2 23.8 %collective-permute-start.43 = (bf16[128,2048]{1,0:T(8,128)(2,1)}, bf16[128,2048]{1,0:T(8,128)(2,1)S(1)}, u32[]{:S(2)}, u32[]{:S(2)}) collective-permute-start(bf16[128,2048]{1,0:T(8,128)(2,1)} %get-tuple-element.151), channel_id=1, source_target_pairs={{0,6},{2,4},{4,2},{6,0},{8,14},{10,12},{12,10},{14,8},{16,22},{18,... | collective-permute-start | bytes 1572872 | tf_op jit(solution)/shard_map/ppermute | solution.py:615
  430.8 37.5 %collective-permute-start.44 = (bf16[4,1,128,2048]{3,2,1,0:T(8,128)(2,1)}, bf16[4,1,128,2048]{3,2,1,0:T(8,128)(2,1)}, u32[]{:S(2)}, u32[]{:S(2)}) collective-permute-start(bf16[4,1,128,2048]{3,2,1,0:T(8,128)(2,1)} %bitcast_dynamic-update-slice_fusion.1), channel_id=1, source_target_pairs={{0,1},{1,0},{2,3},{3,2},{4,5},{5,4},{6,7},{7,6},{8,9},{9,8},{10,11... | collective-permute-start | bytes 6291464 | tf_op jit(solution)/shard_map/ppermute | solution.py:436
  438.3 2.7 collective-permute-start.40
  440.9 95.2 %collective-permute-start.39 = (f32[128,2048]{1,0:T(8,128)}, f32[128,2048]{1,0:T(8,128)}, u32[]{:S(2)}, u32[]{:S(2)}) collective-permute-start(f32[128,2048]{1,0:T(8,128)} %get-tuple-element.147), channel_id=1, source_target_pairs={{0,1},{1,0},{2,3},{3,2},{4,5},{5,4},{6,7},{7,6},{8,9},{9,8},{10,11... | collective-permute-start | bytes 3145736 | tf_op jit(solution)/shard_map/ppermute | solution.py:436
  442.3 11.6 %all-to-all-start.4 = ((f32[16,2,128]{2,1,0:T(2,128)}), f32[16,2,128]{2,1,0:T(2,128)S(1)}, u32[]{:S(2)}, u32[]{:S(2)}) async-start(f32[16,2,128]{2,1,0:T(2,128)} %add_bitcast_fusion), calls=%async_computation.5 | async-start | bytes 32768 | tf_op jit(solution)/shard_map/all_to_all | solution.py:793
  453.9 24.1 %all-to-all-start.7 = ((bf16[4,128,704]{1,2,0:T(8,128)(2,1)}), bf16[4,128,704]{1,2,0:T(8,128)(2,1)}, u32[]{:S(2)}, u32[]{:S(2)}) async-start(bf16[4,128,704]{1,2,0:T(8,128)(2,1)} %copy_bitcast_fusion.4), calls=%async_computation.11 | async-start | bytes 1441792 | tf_op jit(solution)/shard_map/all_to_all | solution.py:557
  461.2 86.4 %reduce-scatter.10.cloned.1.call-start = ((), (), s32[]{:S(2)}) async-start(), calls=%async_computation.21 | async-start | bytes 1310720 | tf_op jit(solution)/shard_map/reduce_scatter | solution.py:692
  463.2 44.0 %collective-permute-start.36 = (bf16[128,2048]{1,0:T(8,128)(2,1)}, bf16[128,2048]{1,0:T(8,128)(2,1)}, u32[]{:S(2)}, u32[]{:S(2)}) collective-permute-start(bf16[128,2048]{1,0:T(8,128)(2,1)} %add_convert_fusion), channel_id=1, source_target_pairs={{8,0},{10,2},{12,4},{14,6},{16,8},{18,10},{20,12},{22,14},{24,16},... | collective-permute-start | bytes 1572872 | tf_op jit(solution)/shard_map/ppermute | solution.py:602
  478.0 53.9 %all-to-all-start.8 = ((bf16[4,128,704]{1,2,0:T(8,128)(2,1)}), bf16[4,128,704]{1,2,0:T(8,128)(2,1)}, u32[]{:S(2)}, u32[]{:S(2)}) async-start(bf16[4,128,704]{1,2,0:T(8,128)(2,1)} %copy_bitcast_fusion.3), calls=%async_computation.13 | async-start | bytes 1441792 | tf_op jit(solution)/shard_map/all_to_all | solution.py:557
  487.5 40.4 %collective-permute-start.35 = (bf16[128,2048]{1,0:T(8,128)(2,1)}, bf16[128,2048]{1,0:T(8,128)(2,1)}, u32[]{:S(2)}, u32[]{:S(2)}) collective-permute-start(bf16[128,2048]{1,0:T(8,128)(2,1)} %add_convert_fusion.1), channel_id=1, source_target_pairs={{0,8},{2,10},{4,12},{6,14},{8,16},{10,18},{12,20},{14,22},{16,24},... | collective-permute-start | bytes 1572872 | tf_op jit(solution)/shard_map/ppermute | solution.py:601
  530.8 12.3 %collective-permute-start.37 = (bf16[128,2048]{1,0:T(8,128)(2,1)}, bf16[128,2048]{1,0:T(8,128)(2,1)}, u32[]{:S(2)}, u32[]{:S(2)}) collective-permute-start(bf16[128,2048]{1,0:T(8,128)(2,1)} %block_result.1), channel_id=1, source_target_pairs={{0,1},{1,0},{2,3},{3,2},{4,5},{5,4},{6,7},{7,6},{8,9},{9,8},{10,11... | collective-permute-start | bytes 1572872 | tf_op jit(solution)/shard_map/ppermute | solution.py:436
  531.9 15.6 %all-to-all-start.5 = ((bf16[4,128,800]{1,2,0:T(8,128)(2,1)}), bf16[4,128,800]{1,2,0:T(8,128)(2,1)S(1)}, u32[]{:S(2)}, u32[]{:S(2)}) async-start(bf16[4,128,800]{1,2,0:T(8,128)(2,1)} %copy_bitcast_fusion), calls=%async_computation.7 | async-start | bytes 1638400 | tf_op jit(solution)/shard_map/all_to_all | solution.py:557
  547.6 9.6 %all-to-all-start.6 = ((bf16[4,128,256]{2,1,0:T(8,128)(2,1)}), bf16[4,128,256]{2,1,0:T(8,128)(2,1)S(1)}, u32[]{:S(2)}, u32[]{:S(2)}) async-start(bf16[4,128,256]{2,1,0:T(8,128)(2,1)} %bitcast.154), calls=%async_computation.9 | async-start | bytes 524288 | tf_op jit(solution)/shard_map/all_to_all | solution.py:557
  (49 other events, 398.9 us)
Sparse Core Ops, SparseCore 0:
  11.4 36.2 all-gather.4
  53.0 38.0 all-gather.6
  92.6 36.1 all-gather.8
  134.4 42.9 all-gather.10
  243.7 33.2 reduce-scatter.5
  281.2 32.6 reduce-scatter.11
  316.2 34.4 reduce-scatter.13
  388.4 85.4 reduce-scatter.7
  476.2 41.8 reduce-scatter.9

commit v6 on v5

--- a/solution.py
+++ b/solution.py
@@ -313,9 +313,43 @@
         mixc_ref[i] = mixc[i].astype(bf16)
 
 
+tau_inv = 0.125
+
+
+def silu_slope(values):
+    sigmoid_val = jax.nn.sigmoid(values)
+    return sigmoid_val * (1.0 + values * (1.0 - sigmoid_val))
+
+
+def through_silu(grads, z):
+    width = grads[0].shape[1]
+    return [g * silu_slope(z[:, i * width : (i + 1) * width]) for i, g in enumerate(grads)]
+
+
+def through_gate(dla, zf):
+    return dla * tau_inv * jax.nn.sigmoid(-zf)
+
+
+INNER = 4
+
+
+def share_columns(wide_parts, dzf, shares_ref):
+    lanes = dzf.shape[1]
+    size = lanes // INNER
+    lane = lax.broadcasted_iota(jnp.int32, dzf.shape, 1)
+    for n in range(INNER):
+        at = 0
+        for x in wide_parts:
+            width = x.shape[1] // INNER
+            shares_ref[n, :, at : at + width] = x[:, n * width : (n + 1) * width]
+            at += width
+        turned = pltpu.roll(dzf, (lanes - n * size) % lanes, 1) if n else dzf
+        shares_ref[n, :, at : at + lanes] = jnp.where(lane < size, turned, 0.0).astype(bf16)
+
+
 def backward_kernel(
     starts_ref, q_ref, k_ref, v_ref, la_ref, p_ref, parts_ref, mix_ref, mixc_ref, do_ref,
-    dq_ref, dk_ref, dv_ref, dla_ref,
+    zq_ref, zk_ref, zv_ref, zf_ref, dzq_ref, dzk_ref, dzv_ref, dzf_ref, shares_ref,
 ):
     starts = [starts_ref[0, n] for n in range(starts_ref.shape[1])]
     heads = mix_ref.shape[0]
@@ -331,10 +365,11 @@
         [mixc_ref[i] for i in range(heads)],
         do_ref[...],
     )
-    head_split(dq, dq_ref, DK)
-    head_split(dk, dk_ref, DK)
-    head_split(dv, dv_ref, DV)
-    dla_ref[...] = dla
+    for grads, z_ref, dz_ref in ((dq, zq_ref, dzq_ref), (dk, zk_ref, dzk_ref), (dv, zv_ref, dzv_ref)):
+        head_split(through_silu(grads, z_ref[...]), dz_ref, grads[0].shape[1])
+    dzf = through_gate(dla, zf_ref[...])
+    dzf_ref[...] = dzf.astype(bf16)
+    share_columns([dzq_ref[...], dzk_ref[...], dzv_ref[...]], dzf, shares_ref)
 
 
 SMEM = pl.BlockSpec(memory_space=pltpu.SMEM)
@@ -363,29 +398,27 @@
     )(starts, q, k, v, la)
 
 
-def attend_backward(q, k, v, la, starts, saved, dout):
-    length, lanes = la.shape
+def attend_backward(q, k, v, la, starts, saved, dout, pres):
     sds = jax.ShapeDtypeStruct
     return pl.pallas_call(
         backward_kernel,
         out_shape=(
-            sds(q.shape, f32),
-            sds(k.shape, f32),
-            sds(v.shape, f32),
-            sds((length, lanes), f32),
+            sds(q.shape, bf16),
+            sds(k.shape, bf16),
+            sds(v.shape, bf16),
+            sds(la.shape, bf16),
+            sds((INNER, q.shape[0], (2 * DK + DV) * (q.shape[1] // DK) // INNER + la.shape[1]), bf16),
         ),
-        in_specs=[SMEM] + [VMEM] * 9,
-        out_specs=(VMEM,) * 4,
+        in_specs=[SMEM] + [VMEM] * 13,
+        out_specs=(VMEM,) * 5,
         cost_estimate=pl.CostEstimate(
             flops=12 * 10**9, transcendentals=10**6, bytes_accessed=8 * 10**6
         ),
         name="slot_backward",
-    )(starts, q, k, v, la, *saved, dout)
+    )(starts, q, k, v, la, *saved, dout, *pres)
 
 
 eps = 1e-06
-tau_inv = 0.125
-INNER = 4
 LAP = (0, 1, 3, 2)
 
 
@@ -400,11 +433,6 @@
         weighted * values, axis=-1, keepdims=True
     )
     return (gain_grad, input_grad)
-
-
-def silu_slope(values):
-    sigmoid_val = jax.nn.sigmoid(values)
-    return sigmoid_val * (1.0 + values * (1.0 - sigmoid_val))
 
 
 class Grid:
@@ -565,30 +593,32 @@
     n = grid.outer
     above = below = x
     from_below, from_above, done = [], [], []
+    other = swap(x)
     for k in range(n - 1):
         below = lax.ppermute(below, "dp", grid.up)
         above = lax.ppermute(above, "dp", grid.down)
         extra = beside[k] if k < len(beside) else ()
         extra = extra(*done) if callable(extra) else extra
         below, above, *extra = tie(below, above, *extra)
-        from_below.append(below)
-        from_above.append(above)
+        from_below.append((below, swap(below)))
+        from_above.append((above, swap(above)))
         done += extra
     blocks = [x]
-    for k in range(1, n):
-        blocks.append(jnp.where(place + k < n, from_above[k - 1], from_below[n - 1 - k]))
+    for c in range(2):
+        blocks += [other] if c else []
+        for k in range(1, n):
+            blocks.append(
+                jnp.where(place + k < n, from_above[k - 1][c], from_below[n - 1 - k][c])
+            )
     return jnp.concatenate(blocks, axis=0), done
-
-
-def with_other_core(own):
-    return jnp.concatenate([own, swap(own)], axis=0)
 
 
 def add_other_core(x, grid):
     n = grid.outer
     size = x.shape[0] // (2 * n)
     block = [x[k * size : (k + 1) * size] for k in range(2 * n)]
-    return [block[k] + swap(block[n + k].astype(bf16)).astype(f32) for k in range(n)]
+    other = tie(*[swap(block[n + k].astype(bf16)) for k in range(n)])
+    return [block[k] + other[k].astype(f32) for k in range(n)]
 
 
 def scatter_along(own, grid, beside=()):
@@ -664,14 +694,14 @@
     normed_own = lax.all_gather(
         half_of(normed, core), "dp", axis=0, tiled=True, axis_index_groups=grid.rows
     )
-    mixed, gate_piece, up_piece, down_later, normed_own = tie(
-        mixed, gate_piece, up_piece, w_down, normed_own
+    branch_other = swap(nt(half_of(mixed, 1 - core), w_output))
+    branch_mine = nt(half_of(mixed, core), w_output)
+    branch_mine, gate_piece, up_piece, down_later, normed_own = tie(
+        branch_mine, gate_piece, up_piece, w_down, normed_own
     )
     full_gate, full_up = gather_rows(gate_piece), gather_rows(up_piece)
     down_piece = columns(down_later)
 
-    branch_other = swap(nt(half_of(mixed, 1 - core), w_output))
-    branch_mine = nt(half_of(mixed, core), w_output)
     hidden, normed_two = second_norm(block_in, branch_mine, branch_other, mlp_gain, core, grid)
     def plane_tokens(own):
         own = own.reshape(INNER, 1, -1, own.shape[-1])
@@ -680,10 +710,8 @@
         out = lax.dynamic_update_slice_in_dim(out, swap(own), 1 - core, 1)
         return out.reshape(-1, own.shape[-1])
 
-    def plane_columns(parts):
-        rows = parts[0].shape[0]
-        x = jnp.concatenate([p.reshape(rows, INNER, -1) for p in parts], axis=2)
-        return exchange(x.reshape(rows, -1), 1, 0, grid.rows)
+    def plane_columns(shares):
+        return exchange(shares.reshape(-1, shares.shape[2]), 0, 0, grid.rows)
 
     def plane_product(left, right):
         return tn(left, right).astype(bf16)
@@ -698,25 +726,23 @@
         return exchange(g, 0, 1, grid.rows).reshape(-1, INNER, size).astype(f32)
 
     cot_rows = cotangent_rows(out_grad, core, grid)
-    own, (cot_rows, down_piece, normed_plane, full_gate) = gather_along(
+    tokens, (cot_rows, down_piece, normed_plane, full_gate) = gather_along(
         normed_two,
         grid,
         place,
         ((cot_rows, down_piece), (plane_tokens(normed_own),), (full_gate,)),
     )
     full_down = gather_rows(down_piece)
-    tokens = with_other_core(own)
-    own, (gate_act, full_up, mixed_plane, up_act, full_down) = gather_along(
+    cot_all, (gate_act, full_up, up_act, full_down) = gather_along(
         cot_rows,
         grid,
         place,
         (
             (nn(tokens, full_gate), full_up),
-            (plane_columns([mixed]),),
+            (),
             (nn(tokens, full_up), full_down),
         ),
     )
-    cot_all = with_other_core(own)
 
     def scatter_rows(g):
         return lax.psum_scatter(
@@ -730,42 +756,44 @@
     gate_grad = (inner_grad * up_act * silu_slope(gate_act)).astype(bf16)
     up_grad = (inner_grad * jax.nn.silu(gate_act)).astype(bf16)
     inner_act = (jax.nn.silu(gate_act) * up_act).astype(bf16)
-    back_parts, (down_rows, *out_own, gate_rows, up_rows) = scatter_along(
+    back_parts, (down_rows, gate_rows, *out_own, up_rows) = scatter_along(
         add_other_core(nt(gate_grad, full_gate) + nt(up_grad, full_up), grid),
         grid,
         (
-            (tn(cot_all, inner_act).astype(bf16),),
-            (*add_other_core(nt(inner_act, full_down), grid), tn(tokens, gate_grad).astype(bf16)),
+            (tn(cot_all, inner_act).astype(bf16), tn(tokens, gate_grad).astype(bf16)),
+            add_other_core(nt(inner_act, full_down), grid),
             (tn(tokens, up_grad).astype(bf16),),
         ),
     )
-    down_rows, gate_rows, up_rows = (scatter_rows(g) for g in (down_rows, gate_rows, up_rows))
+    down_rows, gate_rows = scatter_rows(down_rows), scatter_rows(gate_rows)
+    out_blocks = jnp.zeros((grid.outer,) + out_own[0].shape, bf16)
+    for k, x in enumerate(out_own):
+        at = (place + k) % grid.outer
+        out_blocks = lax.dynamic_update_slice_in_dim(out_blocks, x.astype(bf16)[None], at, 0)
+    out_blocks = out_blocks.reshape(-1, out_blocks.shape[2])
+    out_sum = lax.psum_scatter(
+        out_blocks, "dp", scatter_dimension=0, tiled=True, axis_index_groups=grid.cols
+    )
+    up_rows = scatter_rows(up_rows)
     hidden_grad, low_half, mlp_gain_part = second_norm_back(
         out_grad, hidden, mlp_gain, back_parts, core, grid
     )
     branch_grad = join(low_half, swap(low_half), core)
     mixed_grad = nn(branch_grad, w_output).astype(bf16)
     mixed_grad, down_rows = tie(mixed_grad, down_rows)
-    saved_grads = attend_backward(query, key, value, log_keep, doc_starts, saved, mixed_grad)
-    query_grad, key_grad, value_grad, log_grad = saved_grads
-    query_pre_grad = (query_grad * silu_slope(query_pre)).astype(bf16)
-    key_pre_grad = (key_grad * silu_slope(key_pre)).astype(bf16)
-    value_pre_grad = (value_grad * silu_slope(value_pre)).astype(bf16)
-    forget_pre_grad = (log_grad * tau_inv * jax.nn.sigmoid(-forget_pre)).astype(bf16)
-    pre_grads = (query_pre_grad, key_pre_grad, value_pre_grad, forget_pre_grad)
-
-    query_pre_grad, *out_own = tie(query_pre_grad, *out_own)
-    pre_grads = (query_pre_grad,) + pre_grads[1:]
-    grad_columns = plane_columns(pre_grads)
-    out_parts, (grad_columns, pre_grad, low_half) = scatter_along(
-        out_own,
-        grid,
-        ((grad_columns,), lambda columns: (plane_product(normed_plane, columns), low_half)),
-    )
+    *pre_grads, shares = attend_backward(
+        query, key, value, log_keep, doc_starts, saved, mixed_grad,
+        (query_pre, key_pre, value_pre, forget_pre),
+    )
+    down_sum = to_columns(down_rows)
+    down_sum, shares, *pre_grads = tie(down_sum, shares, *pre_grads)
+    pre_grad = plane_product(normed_plane, plane_columns(shares))
+    _, low_half, mixed = tie(pre_grad, low_half, mixed)
+    mixed_plane = plane_columns(jnp.stack(jnp.split(mixed, INNER, axis=1)))
     low_plane = plane_tokens(plane_gather(low_half, grid, inner))
     sums, output_grad = tie(plane_sum(pre_grad), plane_product(low_plane, mixed_plane))
     output_sum = plane_sum(output_grad)
-    result = block_result(block_in, hidden, out_parts, core, grid)
+    result = block_result(block_in, hidden, [out_sum], core, grid)
     result = join(result, swap(result), core)
 
     sums = from_plane(sums)
@@ -804,7 +832,7 @@
         output_sum,
         to_columns(gate_rows),
         to_columns(up_rows),
-        to_columns(down_rows),
+        down_sum,
     )
 
 

time: 576 us -> 593 us (1.030)
  the two profiles are of different devices: /device:TPU:18 before, /device:TPU:0 now
where the time goes in v6:
time: 593 us; the launch traced here: 583 us
  waiting for transfers between devices  182 us (31%)
  matrix products  104 us (18%)
  starting transfers between devices  97.5 us (16%)
  local copies, waits for them, and re-layouts  65.5 us (11%)
  other arithmetic  45.8 us (8%)
  blocking collectives  39.1 us (7%)
  Pallas kernels  33.2 us (6%)
  between operations  15.7 us (3%)
    dot_general x13, matrix products, nt(): lax.dot_general(a.astype(bf16), b.astype(bf16), (((1,), (1,)), ((), ())),...  41.1 us
    all_to_all x1, blocking collectives, exchange(): lax.all_to_all(x, 'dp', split, concat, tiled=True, axis_index_groups=groups)  39.1 us
    all_to_all x8, waiting for transfers between devices, exchange(): lax.all_to_all(x, 'dp', split, concat, tiled=True, axis_index_groups=groups)  34.7 us
    all_to_all x8, starting transfers between devices, exchange(): lax.all_to_all(x, 'dp', split, concat, tiled=True, axis_index_groups=groups)  34.3 us
    dot_general x8, matrix products, nn(): return jnp.dot(a.astype(bf16), b.astype(bf16), preferred_element_type=f32)  33.9 us
    dot_general x5, matrix products, tn(): lax.dot_general(a.astype(bf16), b.astype(bf16), (((0,), (0,)), ((), ())),...  28.6 us
    ppermute x3, waiting for transfers between devices, scatter_along(): up = lax.ppermute(up.astype(bf16), 'dp', grid.up)  28.1 us
    ppermute x6, waiting for transfers between devices, gather_along(): above = lax.ppermute(above, 'dp', grid.down)  27.7 us
  transfers between devices with their start and end apart: 70, of which 31 were waited for; matrix products, arithmetic and copies ran while one was open for 31% of the time, Pallas kernels for 6%

profile of v6, /device:TPU:0, one launch (start us, length us, event | category | flops | bytes accessed | tf_op | source)
XLA Modules:
  0.0 582.9 jit_solution(5324674176284925954)
XLA Ops:
  14.3 6.3 %all-to-all-start = ((bf16[128,4,1408]{0,2,1:T(8,128)(2,1)}), bf16[128,4,1408]{0,2,1:T(8,128)(2,1)S(1)}, u32[]{:S(2)}, u32[]{:S(2)}) async-start(bf16[128,4,1408]{0,2,1:T(8,128)(2,1)} %pad_maximum_fusion), calls=%async_computation | async-start | bytes 2883584 | tf_op jit(solution)/shard_map/all_to_all | solution.py:585
  20.7 5.0 multiply_convert_fusion.5
  31.8 6.4 %slot_forward.1 = (bf16[256,1024]{1,0:T(8,128)(2,1)}, f32[256,128]{1,0:T(8,128)}, f32[4,256,128]{2,1,0:T(8,128)}, bf16[2,256,256]{2,1,0:T(8,128)(2,1)}, bf16[2,256,16]{2,1,0:T(8,128)(2,1)}) custom-call(s32[1,3]{1,0:T(1,128)} %starts_ref.3, bf16[256,1024]{1,0:T(8,128)(2,1)} %get-tuple-element.219.q_ref, bf16[256,1024]{1,0:T(8,128)(2,1)} %get-tuple-element.221.k_ref, ...), custom_call_target="tpu_custom_call" | custom-call | flops 4000000000 | bytes 4000000 | tf_op jit(solution)/shard_map/slot_forward/pallas_call | solution.py:383
  38.2 4.8 fusion.16.mine_ref
  42.9 11.9 %all-to-all-done = bf16[128,4,1408]{0,2,1:T(8,128)(2,1)S(1)} async-done(((bf16[128,4,1408]{0,2,1:T(8,128)(2,1)}), bf16[128,4,1408]{0,2,1:T(8,128)(2,1)S(1)}, u32[]{:S(2)}, u32[]{:S(2)}) %all-to-all-start) | async-done | bytes 1441824 | tf_op jit(solution)/shard_map/all_to_all | solution.py:585
  58.1 4.7 fusion.14
  64.4 3.5 all-to-all-start.1
  70.0 3.1 second_norm.1
  73.1 4.6 collective-permute-start.1
  79.0 2.5 broadcast.41.clone
  83.0 5.0 all-to-all-done.1
  91.5 4.5 collective-permute-done.2
  96.0 4.9 collective-permute-start.5
  102.2 3.3 bitcast_dynamic-update-slice_fusion
  105.5 6.2 %collective-permute-done.5 = bf16[128,2048]{1,0:T(8,128)(2,1)S(1)} collective-permute-done((bf16[128,2048]{1,0:T(8,128)(2,1)}, bf16[128,2048]{1,0:T(8,128)(2,1)S(1)}, u32[]{:S(2)}, u32[]{:S(2)}) %collective-permute-start.5) | collective-permute-done | bytes 524320 | tf_op jit(solution)/shard_map/ppermute | solution.py:598
  111.7 4.0 collective-permute-done.6
  121.0 6.6 %collective-permute-done.8 = bf16[128,2048]{1,0:T(8,128)(2,1)S(1)} collective-permute-done((bf16[128,2048]{1,0:T(8,128)(2,1)S(1)}, bf16[128,2048]{1,0:T(8,128)(2,1)S(1)}, u32[]{:S(2)}, u32[]{:S(2)}) %collective-permute-start.8) | collective-permute-done | bytes 524320 | tf_op jit(solution)/shard_map/ppermute | solution.py:598
  127.6 4.1 collective-permute-done.9
  138.0 4.5 collective-permute-start.3
  148.7 5.1 fusion.38
  153.8 7.2 %collective-permute-done.4 = bf16[128,2048]{1,0:T(8,128)(2,1)} collective-permute-done((bf16[128,2048]{1,0:T(8,128)(2,1)}, bf16[128,2048]{1,0:T(8,128)(2,1)}, u32[]{:S(2)}, u32[]{:S(2)}) %collective-permute-start.4) | collective-permute-done | bytes 524320 | tf_op jit(solution)/shard_map/ppermute | solution.py:599
  166.3 7.6 %collective-permute-done.17 = bf16[128,2048]{1,0:T(8,128)(2,1)S(1)} collective-permute-done((bf16[128,2048]{1,0:T(8,128)(2,1)}, bf16[128,2048]{1,0:T(8,128)(2,1)S(1)}, u32[]{:S(2)}, u32[]{:S(2)}) %collective-permute-start.17) | collective-permute-done | bytes 524320 | tf_op jit(solution)/shard_map/ppermute | solution.py:598
  173.9 4.1 collective-permute-done.18
  181.4 7.9 %fusion.39 = f32[1024,704]{0,1:T(8,128)} fusion(bf16[1024,2048]{1,0:T(8,128)(2,1)} %select_dynamic-update-slice_fusion.6, bf16[2048,704]{1,0:T(8,128)(2,1)} %all-gather.9.cloned.1.call-done), kind=kOutput, calls=%fused_computation.126 | convolution fusion | flops 2952790016 | bytes 9961472 | tf_op jit(solution)/shard_map/dot_general | solution.py:19
  190.9 3.7 collective-permute-done.20
  208.0 5.6 fusion.40
  213.6 2.9 multiply_convert_fusion
  216.5 3.5 fusion.41
  220.1 5.7 fusion.36
  228.8 4.5 convolution_convert_fusion.2
  233.3 3.0 fusion.5
  236.3 4.0 collective-permute-start.32
  241.7 6.6 %convolution_convert_fusion.3 = bf16[2048,704]{0,1:T(8,128)(2,1)} fusion(bf16[1024,704]{0,1:T(8,128)(2,1)S(1)} %copy-done.19, bf16[1024,2048]{1,0:T(8,128)(2,1)} %select_dynamic-update-slice_fusion), kind=kOutput, calls=%fused_computation.4 | convolution fusion | flops 2954231808 | bytes 8519680 | tf_op jit(solution)/shard_map/dot_general | solution.py:29
  248.3 3.4 collective-permute-done.32
  251.7 4.9 collective-permute-done.33
  256.7 7.7 %fusion.37 = (bf16[1024,2048]{1,0:T(8,128)(2,1)S(1)}, f32[1024,2048]{1,0:T(8,128)}) fusion(bf16[1024,704]{0,1:T(8,128)(2,1)S(1)} %copy-done.19, bf16[2048,704]{0,1:T(8,128)(2,1)} %all-gather.11.cloned.1.call-done), kind=kOutput, calls=%fused_computation.124 | convolution fusion | flops 2954887168 | bytes 16908288 | tf_op jit(solution)/shard_map/dot_general | solution.py:23
  274.9 2.9 slice_add_fusion.1
  277.9 7.3 %collective-permute-done.34 = bf16[128,2048]{1,0:T(8,128)(2,1)S(1)} collective-permute-done((bf16[128,2048]{1,0:T(8,128)(2,1)S(1)}, bf16[128,2048]{1,0:T(8,128)(2,1)S(1)}, u32[]{:S(2)}, u32[]{:S(2)}) %collective-permute-start.34) | collective-permute-done | bytes 524320 | tf_op jit(solution)/shard_map/ppermute | solution.py:631
  285.1 4.1 collective-permute-done.35
  292.3 4.3 add_convert_fusion
  299.9 4.5 convolution_convert_fusion.1
  304.5 17.4 %collective-permute-done.41.refs_1_ = bf16[128,2048]{1,0:T(8,128)(2,1)S(1)} collective-permute-done((bf16[128,2048]{1,0:T(8,128)(2,1)}, bf16[128,2048]{1,0:T(8,128)(2,1)S(1)}, u32[]{:S(2)}, u32[]{:S(2)}) %collective-permute-start.41) | collective-permute-done | bytes 524320 | tf_op jit(solution)/shard_map/ppermute | solution.py:631
  321.9 16.7 %collective-permute-done.42.refs_2_ = bf16[128,2048]{1,0:T(8,128)(2,1)S(1)} collective-permute-done((bf16[128,2048]{1,0:T(8,128)(2,1)}, bf16[128,2048]{1,0:T(8,128)(2,1)S(1)}, u32[]{:S(2)}, u32[]{:S(2)}) %collective-permute-start.42) | collective-permute-done | bytes 524320 | tf_op jit(solution)/shard_map/ppermute | solution.py:632
  339.5 3.9 second_norm_back.1
  345.6 4.3 convolution_convert_fusion.5.do_ref
  351.9 3.5 all-to-all-start.2
  355.7 11.3 %slot_backward.1 = (bf16[256,1024]{1,0:T(8,128)(2,1)}, bf16[256,1024]{1,0:T(8,128)(2,1)}, bf16[256,1024]{1,0:T(8,128)(2,1)}, bf16[256,128]{1,0:T(8,128)(2,1)}, bf16[4,256,896]{2,1,0:T(8,128)(2,1)}) custom-call(s32[1,3]{1,0:T(1,128)} %starts_ref.3, bf16[256,1024]{1,0:T(8,128)(2,1)} %get-tuple-element.219.q_ref, bf16[256,1024]{1,0:T(8,128)(2,1)} %get-tuple-element.221.k_ref, ...), custom_call_target="tpu_custom_call" | custom-call | flops 12000000000 | bytes 8000000 | tf_op jit(solution)/shard_map/slot_backward/pallas_call | solution.py:403
  367.0 7.7 %all-to-all-done.2 = bf16[4,128,704]{1,2,0:T(8,128)(2,1)S(1)} async-done(((bf16[4,128,704]{1,2,0:T(8,128)(2,1)}), bf16[4,128,704]{1,2,0:T(8,128)(2,1)S(1)}, u32[]{:S(2)}, u32[]{:S(2)}) %all-to-all-start.2) | async-done | bytes 720928 | tf_op jit(solution)/shard_map/all_to_all | solution.py:585
  375.9 39.1 %all_to_all.123 = bf16[4,256,896]{2,1,0:T(8,128)(2,1)S(1)} all-to-all(bf16[4,256,896]{2,1,0:T(8,128)(2,1)} %get-tuple-element.154), channel_id=1, replica_groups={{0,2,4,6},{8,10,12,14},{16,18,20,22},{24,26,28,30},{1,3,5,7},{9,11,13,1..., dimensions={0} | all-to-all | bytes 3670016 | tf_op jit(solution)/shard_map/all_to_all | solution.py:585
  415.0 8.3 %convolution_convert_fusion = bf16[2048,896]{1,0:T(8,128)(2,1)} fusion(bf16[1024,2048]{1,0:T(8,128)(2,1)} %bitcast.11, bf16[1024,896]{1,0:T(8,128)(2,1)S(1)} %bitcast.147), kind=kOutput, calls=%fused_computation.1 | convolution fusion | flops 3759931392 | bytes 9699328 | tf_op jit(solution)/shard_map/dot_general | solution.py:29
  427.9 3.9 all-to-all-start.8
  434.3 3.7 fusion.8
  444.5 8.6 %collective-permute-done.47 = bf16[128,2048]{1,0:T(8,128)(2,1)S(1)} collective-permute-done((bf16[128,2048]{1,0:T(8,128)(2,1)}, bf16[128,2048]{1,0:T(8,128)(2,1)S(1)}, u32[]{:S(2)}, u32[]{:S(2)}) %collective-permute-start.47) | collective-permute-done | bytes 524320 | tf_op jit(solution)/shard_map/ppermute | solution.py:645
  453.1 13.5 %collective-permute-done.48 = bf16[128,2048]{1,0:T(8,128)(2,1)S(1)} collective-permute-done((bf16[128,2048]{1,0:T(8,128)(2,1)}, bf16[128,2048]{1,0:T(8,128)(2,1)S(1)}, u32[]{:S(2)}, u32[]{:S(2)}) %collective-permute-start.48) | collective-permute-done | bytes 524320 | tf_op jit(solution)/shard_map/ppermute | solution.py:645
  476.6 4.2 all-to-all-start.5
  484.8 3.2 constant_dynamic-update-slice_fusion.4
  489.3 4.7 all-to-all-start.9
  494.1 4.7 convolution_convert_fusion.4
  498.8 14.6 %reduce-scatter.11.cloned.1.call-done = bf16[512,896]{1,0:T(8,128)(2,1)} async-done(((bf16[2048,896]{1,0:T(8,128)(2,1)}), bf16[512,896]{1,0:T(8,128)(2,1)}) %reduce-scatter.11.cloned.1.call-update) | async-done | bytes 917520 | tf_op jit(solution)/shard_map/reduce_scatter | solution.py:720
  514.8 4.0 first_norm_back.1
  524.9 13.7 %all-to-all-start.3 = ((f32[16,2,128]{2,1,0:T(2,128)}), f32[16,2,128]{2,1,0:T(2,128)S(1)}, u32[]{:S(2)}, u32[]{:S(2)}) async-start(f32[16,2,128]{2,1,0:T(2,128)} %add_bitcast_fusion), calls=%async_computation.5 | async-start | bytes 32768 | tf_op jit(solution)/shard_map/all_to_all | solution.py:821
  547.7 4.2 all-to-all-start.6
  557.4 6.5 %all-to-all-done.6 = bf16[4,128,896]{1,2,0:T(8,128)(2,1)S(1)} async-done(((bf16[4,128,896]{1,2,0:T(8,128)(2,1)}), bf16[4,128,896]{1,2,0:T(8,128)(2,1)S(1)}, u32[]{:S(2)}, u32[]{:S(2)}) %all-to-all-start.6) | async-done | bytes 917536 | tf_op jit(solution)/shard_map/all_to_all | solution.py:585
  564.0 4.1 all-to-all-start.7
  (292 shorter events, 154.9 us)
Async XLA Ops:
  7.2 50.0 %all-gather.5.cloned.1.call-start = ((), (), s32[]{:S(2)}) async-start(), calls=%async_computation.16 | async-start | bytes 2621440 | tf_op jit(solution)/shard_map/all_gather | solution.py:694
  14.3 40.5 %all-to-all-start = ((bf16[128,4,1408]{0,2,1:T(8,128)(2,1)}), bf16[128,4,1408]{0,2,1:T(8,128)(2,1)S(1)}, u32[]{:S(2)}, u32[]{:S(2)}) async-start(bf16[128,4,1408]{0,2,1:T(8,128)(2,1)} %pad_maximum_fusion), calls=%async_computation | async-start | bytes 2883584 | tf_op jit(solution)/shard_map/all_to_all | solution.py:585
  20.7 111.1 %all-gather.7.cloned.1.call-start = ((), (), s32[]{:S(2)}) async-start(), calls=%async_computation.17 | async-start | bytes 3932160 | tf_op jit(solution)/shard_map/all_gather | solution.py:674
  57.2 103.8 %all-gather.9.cloned.1.call-start = ((), (), s32[]{:S(2)}) async-start(), calls=%async_computation.18 | async-start | bytes 3932160 | tf_op jit(solution)/shard_map/all_gather | solution.py:674
  58.0 44.2 %collective-permute-start.7 = (bf16[4,1,128,2048]{3,2,0,1:T(8,128)(2,1)}, bf16[4,1,128,2048]{3,2,0,1:T(8,128)(2,1)}, u32[]{:S(2)}, u32[]{:S(2)}) collective-permute-start(bf16[4,1,128,2048]{3,2,0,1:T(8,128)(2,1)} %bitcast.142), channel_id=1, source_target_pairs={{0,1},{1,0},{2,3},{3,2},{4,5},{5,4},{6,7},{7,6},{8,9},{9,8},{10,11... | collective-permute-start | bytes 6291464 | tf_op jit(solution)/shard_map/ppermute | solution.py:464
  62.7 7.2 %collective-permute-start = (f32[128,2048]{1,0:T(8,128)}, f32[128,2048]{1,0:T(8,128)}, u32[]{:S(2)}, u32[]{:S(2)}) collective-permute-start(f32[128,2048]{1,0:T(8,128)} %fusion.14), channel_id=1, source_target_pairs={{0,1},{1,0},{2,3},{3,2},{4,5},{5,4},{6,7},{7,6},{8,9},{9,8},{10,11... | collective-permute-start | bytes 3145736 | tf_op jit(solution)/shard_map/ppermute | solution.py:464
  64.4 23.6 %all-to-all-start.1 = ((bf16[128,4,704]{0,2,1:T(8,128)(2,1)}), bf16[128,4,704]{0,2,1:T(8,128)(2,1)S(1)}, u32[]{:S(2)}, u32[]{:S(2)}) async-start(bf16[128,4,704]{0,2,1:T(8,128)(2,1)} %bitcast.6), calls=%async_computation.1 | async-start | bytes 1441792 | tf_op jit(solution)/shard_map/all_to_all | solution.py:585
  67.9 123.1 %all-gather.11.cloned.1.call-start = ((), (), s32[]{:S(2)}) async-start(), calls=%async_computation.19 | async-start | bytes 3604480 | tf_op jit(solution)/shard_map/all_gather | solution.py:674
  73.1 18.4 %collective-permute-start.1 = (bf16[128,2048]{1,0:T(8,128)(2,1)}, bf16[128,2048]{1,0:T(8,128)(2,1)}, u32[]{:S(2)}, u32[]{:S(2)}) collective-permute-start(bf16[128,2048]{1,0:T(8,128)(2,1)} %get-tuple-element.90), channel_id=1, source_target_pairs={{0,8},{2,10},{4,12},{6,14},{8,16},{10,18},{12,20},{14,22},{16,24},... | collective-permute-start | bytes 1572872 | tf_op jit(solution)/shard_map/ppermute | solution.py:598
  77.7 18.3 %collective-permute-start.2 = (bf16[128,2048]{1,0:T(8,128)(2,1)}, bf16[128,2048]{1,0:T(8,128)(2,1)}, u32[]{:S(2)}, u32[]{:S(2)}) collective-permute-start(bf16[128,2048]{1,0:T(8,128)(2,1)} %get-tuple-element.90), channel_id=1, source_target_pairs={{8,0},{10,2},{12,4},{14,6},{16,8},{18,10},{20,12},{22,14},{24,16},... | collective-permute-start | bytes 1572872 | tf_op jit(solution)/shard_map/ppermute | solution.py:599
  96.0 15.7 %collective-permute-start.5 = (bf16[128,2048]{1,0:T(8,128)(2,1)}, bf16[128,2048]{1,0:T(8,128)(2,1)S(1)}, u32[]{:S(2)}, u32[]{:S(2)}) collective-permute-start(bf16[128,2048]{1,0:T(8,128)(2,1)} %collective-permute-done.1), channel_id=1, source_target_pairs={{0,8},{2,10},{4,12},{6,14},{8,16},{10,18},{12,20},{14,22},{16,24},... | collective-permute-start | bytes 1572872 | tf_op jit(solution)/shard_map/ppermute | solution.py:598
  100.9 14.8 %collective-permute-start.6 = (bf16[128,2048]{1,0:T(8,128)(2,1)}, bf16[128,2048]{1,0:T(8,128)(2,1)S(1)}, u32[]{:S(2)}, u32[]{:S(2)}) collective-permute-start(bf16[128,2048]{1,0:T(8,128)(2,1)} %collective-permute-done.2), channel_id=1, source_target_pairs={{8,0},{10,2},{12,4},{14,6},{16,8},{18,10},{20,12},{22,14},{24,16},... | collective-permute-start | bytes 1572872 | tf_op jit(solution)/shard_map/ppermute | solution.py:599
  115.7 11.9 %collective-permute-start.8 = (bf16[128,2048]{1,0:T(8,128)(2,1)S(1)}, bf16[128,2048]{1,0:T(8,128)(2,1)S(1)}, u32[]{:S(2)}, u32[]{:S(2)}) collective-permute-start(bf16[128,2048]{1,0:T(8,128)(2,1)S(1)} %collective-permute-done.5), channel_id=1, source_target_pairs={{0,8},{2,10},{4,12},{6,14},{8,16},{10,18},{12,20},{14,22},{16,24},... | collective-permute-start | bytes 1572872 | tf_op jit(solution)/shard_map/ppermute | solution.py:598
  118.2 13.6 %collective-permute-start.9 = (bf16[128,2048]{1,0:T(8,128)(2,1)S(1)}, bf16[128,2048]{1,0:T(8,128)(2,1)S(1)}, u32[]{:S(2)}, u32[]{:S(2)}) collective-permute-start(bf16[128,2048]{1,0:T(8,128)(2,1)S(1)} %collective-permute-done.6), channel_id=1, source_target_pairs={{8,0},{10,2},{12,4},{14,6},{16,8},{18,10},{20,12},{22,14},{24,16},... | collective-permute-start | bytes 1572872 | tf_op jit(solution)/shard_map/ppermute | solution.py:599
  119.5 16.1 %collective-permute-start.10 = (bf16[128,2048]{1,0:T(8,128)(2,1)S(1)}, bf16[128,2048]{1,0:T(8,128)(2,1)}, u32[]{:S(2)}, u32[]{:S(2)}) collective-permute-start(bf16[128,2048]{1,0:T(8,128)(2,1)S(1)} %copy-done.29), channel_id=1, source_target_pairs={{0,1},{1,0},{2,3},{3,2},{4,5},{5,4},{6,7},{7,6},{8,9},{9,8},{10,11... | collective-permute-start | bytes 1572872 | tf_op jit(solution)/shard_map/ppermute | solution.py:464
  120.5 17.5 %collective-permute-start.11 = (bf16[128,2048]{1,0:T(8,128)(2,1)}, bf16[128,2048]{1,0:T(8,128)(2,1)}, u32[]{:S(2)}, u32[]{:S(2)}) collective-permute-start(bf16[128,2048]{1,0:T(8,128)(2,1)} %collective-permute-done.2), channel_id=1, source_target_pairs={{0,1},{1,0},{2,3},{3,2},{4,5},{5,4},{6,7},{7,6},{8,9},{9,8},{10,11... | collective-permute-start | bytes 1572872 | tf_op jit(solution)/shard_map/ppermute | solution.py:464
  121.0 26.8 %collective-permute-start.16 = (bf16[128,2048]{1,0:T(8,128)(2,1)}, bf16[128,2048]{1,0:T(8,128)(2,1)}, u32[]{:S(2)}, u32[]{:S(2)}) collective-permute-start(bf16[128,2048]{1,0:T(8,128)(2,1)} %collective-permute-done.1), channel_id=1, source_target_pairs={{0,1},{1,0},{2,3},{3,2},{4,5},{5,4},{6,7},{7,6},{8,9},{9,8},{10,11... | collective-permute-start | bytes 1572872 | tf_op jit(solution)/shard_map/ppermute | solution.py:464
  121.0 228.9 %reduce-scatter.9.cloned.1.call-start = ((), (), s32[]{:S(2)}) async-start(), calls=%async_computation.21 | async-start | bytes 3604480 | tf_op jit(solution)/shard_map/reduce_scatter | solution.py:748
  127.6 16.8 %collective-permute-start.13 = (bf16[128,2048]{1,0:T(8,128)(2,1)S(1)}, bf16[128,2048]{1,0:T(8,128)(2,1)}, u32[]{:S(2)}, u32[]{:S(2)}) collective-permute-start(bf16[128,2048]{1,0:T(8,128)(2,1)S(1)} %collective-permute-done.6), channel_id=1, source_target_pairs={{0,1},{1,0},{2,3},{3,2},{4,5},{5,4},{6,7},{7,6},{8,9},{9,8},{10,11... | collective-permute-start | bytes 1572872 | tf_op jit(solution)/shard_map/ppermute | solution.py:464
  131.8 10.7 %collective-permute-start.12 = (bf16[128,2048]{1,0:T(8,128)(2,1)S(1)}, bf16[128,2048]{1,0:T(8,128)(2,1)S(1)}, u32[]{:S(2)}, u32[]{:S(2)}) collective-permute-start(bf16[128,2048]{1,0:T(8,128)(2,1)S(1)} %collective-permute-done.8), channel_id=1, source_target_pairs={{0,1},{1,0},{2,3},{3,2},{4,5},{5,4},{6,7},{7,6},{8,9},{9,8},{10,11... | collective-permute-start | bytes 1572872 | tf_op jit(solution)/shard_map/ppermute | solution.py:464
  135.6 10.1 %collective-permute-start.14 = (bf16[128,2048]{1,0:T(8,128)(2,1)S(1)}, bf16[128,2048]{1,0:T(8,128)(2,1)S(1)}, u32[]{:S(2)}, u32[]{:S(2)}) collective-permute-start(bf16[128,2048]{1,0:T(8,128)(2,1)S(1)} %collective-permute-done.5), channel_id=1, source_target_pairs={{0,1},{1,0},{2,3},{3,2},{4,5},{5,4},{6,7},{7,6},{8,9},{9,8},{10,11... | collective-permute-start | bytes 1572872 | tf_op jit(solution)/shard_map/ppermute | solution.py:464
  138.0 15.8 %collective-permute-start.3 = (bf16[128,2048]{1,0:T(8,128)(2,1)}, bf16[128,2048]{1,0:T(8,128)(2,1)}, u32[]{:S(2)}, u32[]{:S(2)}) collective-permute-start(bf16[128,2048]{1,0:T(8,128)(2,1)} %cotangent_rows.1), channel_id=1, source_target_pairs={{0,8},{2,10},{4,12},{6,14},{8,16},{10,18},{12,20},{14,22},{16,24},... | collective-permute-start | bytes 1572872 | tf_op jit(solution)/shard_map/ppermute | solution.py:598
  142.5 5.3 collective-permute-start.15
  144.5 16.5 %collective-permute-start.4 = (bf16[128,2048]{1,0:T(8,128)(2,1)}, bf16[128,2048]{1,0:T(8,128)(2,1)}, u32[]{:S(2)}, u32[]{:S(2)}) collective-permute-start(bf16[128,2048]{1,0:T(8,128)(2,1)} %cotangent_rows.1), channel_id=1, source_target_pairs={{8,0},{10,2},{12,4},{14,6},{16,8},{18,10},{20,12},{22,14},{24,16},... | collective-permute-start | bytes 1572872 | tf_op jit(solution)/shard_map/ppermute | solution.py:599
  161.0 12.9 %collective-permute-start.17 = (bf16[128,2048]{1,0:T(8,128)(2,1)}, bf16[128,2048]{1,0:T(8,128)(2,1)S(1)}, u32[]{:S(2)}, u32[]{:S(2)}) collective-permute-start(bf16[128,2048]{1,0:T(8,128)(2,1)} %collective-permute-done.3), channel_id=1, source_target_pairs={{0,8},{2,10},{4,12},{6,14},{8,16},{10,18},{12,20},{14,22},{16,24},... | collective-permute-start | bytes 1572872 | tf_op jit(solution)/shard_map/ppermute | solution.py:598
  162.5 15.5 %collective-permute-start.18 = (bf16[128,2048]{1,0:T(8,128)(2,1)}, bf16[128,2048]{1,0:T(8,128)(2,1)}, u32[]{:S(2)}, u32[]{:S(2)}) collective-permute-start(bf16[128,2048]{1,0:T(8,128)(2,1)} %collective-permute-done.4), channel_id=1, source_target_pairs={{8,0},{10,2},{12,4},{14,6},{16,8},{18,10},{20,12},{22,14},{24,16},... | collective-permute-start | bytes 1572872 | tf_op jit(solution)/shard_map/ppermute | solution.py:599
  163.8 36.9 %collective-permute-start.21 = (bf16[128,2048]{1,0:T(8,128)(2,1)}, bf16[128,2048]{1,0:T(8,128)(2,1)}, u32[]{:S(2)}, u32[]{:S(2)}) collective-permute-start(bf16[128,2048]{1,0:T(8,128)(2,1)} %cotangent_rows.1), channel_id=1, source_target_pairs={{0,1},{1,0},{2,3},{3,2},{4,5},{5,4},{6,7},{7,6},{8,9},{9,8},{10,11... | collective-permute-start | bytes 1572872 | tf_op jit(solution)/shard_map/ppermute | solution.py:464
  165.8 37.3 %collective-permute-start.22 = (bf16[128,2048]{1,0:T(8,128)(2,1)}, bf16[128,2048]{1,0:T(8,128)(2,1)}, u32[]{:S(2)}, u32[]{:S(2)}) collective-permute-start(bf16[128,2048]{1,0:T(8,128)(2,1)} %collective-permute-done.4), channel_id=1, source_target_pairs={{0,1},{1,0},{2,3},{3,2},{4,5},{5,4},{6,7},{7,6},{8,9},{9,8},{10,11... | collective-permute-start | bytes 1572872 | tf_op jit(solution)/shard_map/ppermute | solution.py:464
  166.3 40.8 %collective-permute-start.27 = (bf16[128,2048]{1,0:T(8,128)(2,1)}, bf16[128,2048]{1,0:T(8,128)(2,1)}, u32[]{:S(2)}, u32[]{:S(2)}) collective-permute-start(bf16[128,2048]{1,0:T(8,128)(2,1)} %collective-permute-done.3), channel_id=1, source_target_pairs={{0,1},{1,0},{2,3},{3,2},{4,5},{5,4},{6,7},{7,6},{8,9},{9,8},{10,11... | collective-permute-start | bytes 1572872 | tf_op jit(solution)/shard_map/ppermute | solution.py:464
  178.0 12.1 %collective-permute-start.19 = (bf16[128,2048]{1,0:T(8,128)(2,1)S(1)}, bf16[128,2048]{1,0:T(8,128)(2,1)S(1)}, u32[]{:S(2)}, u32[]{:S(2)}) collective-permute-start(bf16[128,2048]{1,0:T(8,128)(2,1)S(1)} %collective-permute-done.17), channel_id=1, source_target_pairs={{0,8},{2,10},{4,12},{6,14},{8,16},{10,18},{12,20},{14,22},{16,24},... | collective-permute-start | bytes 1572872 | tf_op jit(solution)/shard_map/ppermute | solution.py:598
  180.1 14.5 %collective-permute-start.20 = (bf16[128,2048]{1,0:T(8,128)(2,1)}, bf16[128,2048]{1,0:T(8,128)(2,1)}, u32[]{:S(2)}, u32[]{:S(2)}) collective-permute-start(bf16[128,2048]{1,0:T(8,128)(2,1)} %collective-permute-done.18), channel_id=1, source_target_pairs={{8,0},{10,2},{12,4},{14,6},{16,8},{18,10},{20,12},{22,14},{24,16},... | collective-permute-start | bytes 1572872 | tf_op jit(solution)/shard_map/ppermute | solution.py:599
  190.9 14.2 %collective-permute-start.24 = (bf16[128,2048]{1,0:T(8,128)(2,1)}, bf16[128,2048]{1,0:T(8,128)(2,1)}, u32[]{:S(2)}, u32[]{:S(2)}) collective-permute-start(bf16[128,2048]{1,0:T(8,128)(2,1)} %collective-permute-done.18), channel_id=1, source_target_pairs={{0,1},{1,0},{2,3},{3,2},{4,5},{5,4},{6,7},{7,6},{8,9},{9,8},{10,11... | collective-permute-start | bytes 1572872 | tf_op jit(solution)/shard_map/ppermute | solution.py:464
  194.6 8.5 %collective-permute-start.23 = (bf16[128,2048]{1,0:T(8,128)(2,1)}, bf16[128,2048]{1,0:T(8,128)(2,1)S(1)}, u32[]{:S(2)}, u32[]{:S(2)}) collective-permute-start(bf16[128,2048]{1,0:T(8,128)(2,1)} %copy-done.32), channel_id=1, source_target_pairs={{0,1},{1,0},{2,3},{3,2},{4,5},{5,4},{6,7},{7,6},{8,9},{9,8},{10,11... | collective-permute-start | bytes 1572872 | tf_op jit(solution)/shard_map/ppermute | solution.py:464
  200.7 4.4 collective-permute-start.25
  203.1 4.0 collective-permute-start.26
  227.2 6.1 %collective-permute-start.28 = (bf16[128,2048]{1,0:T(8,128)(2,1)}, bf16[128,2048]{1,0:T(8,128)(2,1)}, u32[]{:S(2)}, u32[]{:S(2)}) collective-permute-start(bf16[128,2048]{1,0:T(8,128)(2,1)} %get-tuple-element.207), channel_id=1, source_target_pairs={{0,1},{1,0},{2,3},{3,2},{4,5},{5,4},{6,7},{7,6},{8,9},{9,8},{10,11... | collective-permute-start | bytes 1572872 | tf_op jit(solution)/shard_map/ppermute | solution.py:464
  227.7 5.6 collective-permute-start.29
  227.7 5.6 collective-permute-start.30
  228.2 5.1 collective-permute-start.31
  236.3 15.4 %collective-permute-start.32 = (bf16[128,2048]{1,0:T(8,128)(2,1)}, bf16[128,2048]{1,0:T(8,128)(2,1)}, u32[]{:S(2)}, u32[]{:S(2)}) collective-permute-start(bf16[128,2048]{1,0:T(8,128)(2,1)} %get-tuple-element.196), channel_id=1, source_target_pairs={{0,8},{2,10},{4,12},{6,14},{8,16},{10,18},{12,20},{14,22},{16,24},... | collective-permute-start | bytes 1572872 | tf_op jit(solution)/shard_map/ppermute | solution.py:631
  240.4 16.2 %collective-permute-start.33 = (bf16[128,2048]{1,0:T(8,128)(2,1)}, bf16[128,2048]{1,0:T(8,128)(2,1)}, u32[]{:S(2)}, u32[]{:S(2)}) collective-permute-start(bf16[128,2048]{1,0:T(8,128)(2,1)} %get-tuple-element.195), channel_id=1, source_target_pairs={{8,0},{10,2},{12,4},{14,6},{16,8},{18,10},{20,12},{22,14},{24,16},... | collective-permute-start | bytes 1572872 | tf_op jit(solution)/shard_map/ppermute | solution.py:632
  256.6 166.7 %reduce-scatter.7.cloned.1.call-start = ((), (), s32[]{:S(2)}) async-start(), calls=%async_computation.20 | async-start | bytes 2621440 | tf_op jit(solution)/shard_map/reduce_scatter | solution.py:774
  272.1 13.0 %collective-permute-start.34 = (bf16[128,2048]{1,0:T(8,128)(2,1)S(1)}, bf16[128,2048]{1,0:T(8,128)(2,1)S(1)}, u32[]{:S(2)}, u32[]{:S(2)}) collective-permute-start(bf16[128,2048]{1,0:T(8,128)(2,1)S(1)} %get-tuple-element.187), channel_id=1, source_target_pairs={{0,8},{2,10},{4,12},{6,14},{8,16},{10,18},{12,20},{14,22},{16,24},... | collective-permute-start | bytes 1572872 | tf_op jit(solution)/shard_map/ppermute | solution.py:631
  273.6 15.7 %collective-permute-start.35 = (bf16[128,2048]{1,0:T(8,128)(2,1)S(1)}, bf16[128,2048]{1,0:T(8,128)(2,1)S(1)}, u32[]{:S(2)}, u32[]{:S(2)}) collective-permute-start(bf16[128,2048]{1,0:T(8,128)(2,1)S(1)} %get-tuple-element.186), channel_id=1, source_target_pairs={{8,0},{10,2},{12,4},{14,6},{16,8},{18,10},{20,12},{22,14},{24,16},... | collective-permute-start | bytes 1572872 | tf_op jit(solution)/shard_map/ppermute | solution.py:632
  291.4 134.4 %reduce-scatter.15.cloned.1.call-start = ((), (), s32[]{:S(2)}) async-start(), calls=%async_computation.24 | async-start | bytes 3604480 | tf_op jit(solution)/shard_map/reduce_scatter | solution.py:748
  292.2 139.6 %reduce-scatter.17.cloned.1.call-start = ((), (), s32[]{:S(2)}) async-start(), calls=%async_computation.25 | async-start | bytes 3604480 | tf_op jit(solution)/shard_map/reduce_scatter | solution.py:748
  296.6 25.4 %collective-permute-start.41 = (bf16[128,2048]{1,0:T(8,128)(2,1)}, bf16[128,2048]{1,0:T(8,128)(2,1)S(1)}, u32[]{:S(2)}, u32[]{:S(2)}) collective-permute-start(bf16[128,2048]{1,0:T(8,128)(2,1)} %get-tuple-element.189), channel_id=1, source_target_pairs={{0,8},{2,10},{4,12},{6,14},{8,16},{10,18},{12,20},{14,22},{16,24},... | collective-permute-start | bytes 1572872 | tf_op jit(solution)/shard_map/ppermute | solution.py:631
  298.6 40.0 %collective-permute-start.42 = (bf16[128,2048]{1,0:T(8,128)(2,1)}, bf16[128,2048]{1,0:T(8,128)(2,1)S(1)}, u32[]{:S(2)}, u32[]{:S(2)}) collective-permute-start(bf16[128,2048]{1,0:T(8,128)(2,1)} %get-tuple-element.188), channel_id=1, source_target_pairs={{8,0},{10,2},{12,4},{14,6},{16,8},{18,10},{20,12},{22,14},{24,16},... | collective-permute-start | bytes 1572872 | tf_op jit(solution)/shard_map/ppermute | solution.py:632
  351.9 22.7 %all-to-all-start.2 = ((bf16[4,128,704]{1,2,0:T(8,128)(2,1)}), bf16[4,128,704]{1,2,0:T(8,128)(2,1)S(1)}, u32[]{:S(2)}, u32[]{:S(2)}) async-start(bf16[4,128,704]{1,2,0:T(8,128)(2,1)} %copy_bitcast_fusion.3), calls=%async_computation.4 | async-start | bytes 1441792 | tf_op jit(solution)/shard_map/all_to_all | solution.py:585
  355.4 158.0 %reduce-scatter.11.cloned.1.call-start = ((), (), s32[]{:S(2)}) async-start(), calls=%async_computation.22 | async-start | bytes 4587520 | tf_op jit(solution)/shard_map/reduce_scatter | solution.py:720
  425.8 112.8 %collective-permute-start.40 = (bf16[128,2048]{1,0:T(8,128)(2,1)}, bf16[128,2048]{1,0:T(8,128)(2,1)}, u32[]{:S(2)}, u32[]{:S(2)}) collective-permute-start(bf16[128,2048]{1,0:T(8,128)(2,1)} %block_result.1), channel_id=1, source_target_pairs={{0,1},{1,0},{2,3},{3,2},{4,5},{5,4},{6,7},{7,6},{8,9},{9,8},{10,11... | collective-permute-start | bytes 1572872 | tf_op jit(solution)/shard_map/ppermute | solution.py:464
  427.9 48.7 %all-to-all-start.8 = ((bf16[4,128,704]{1,2,0:T(8,128)(2,1)}), bf16[4,128,704]{1,2,0:T(8,128)(2,1)S(1)}, u32[]{:S(2)}, u32[]{:S(2)}) async-start(bf16[4,128,704]{1,2,0:T(8,128)(2,1)} %copy_bitcast_fusion.2), calls=%async_computation.13 | async-start | bytes 1441792 | tf_op jit(solution)/shard_map/all_to_all | solution.py:585
  438.0 15.1 %collective-permute-start.47 = (bf16[128,2048]{1,0:T(8,128)(2,1)}, bf16[128,2048]{1,0:T(8,128)(2,1)S(1)}, u32[]{:S(2)}, u32[]{:S(2)}) collective-permute-start(bf16[128,2048]{1,0:T(8,128)(2,1)} %get-tuple-element.155), channel_id=1, source_target_pairs={{0,2},{2,0},{4,6},{6,4},{8,10},{10,8},{12,14},{14,12},{16,18},{18,... | collective-permute-start | bytes 1572872 | tf_op jit(solution)/shard_map/ppermute | solution.py:645
  441.1 25.5 %collective-permute-start.48 = (bf16[128,2048]{1,0:T(8,128)(2,1)}, bf16[128,2048]{1,0:T(8,128)(2,1)S(1)}, u32[]{:S(2)}, u32[]{:S(2)}) collective-permute-start(bf16[128,2048]{1,0:T(8,128)(2,1)} %get-tuple-element.155), channel_id=1, source_target_pairs={{0,4},{2,6},{4,0},{6,2},{8,12},{10,14},{12,8},{14,10},{16,20},{18,... | collective-permute-start | bytes 1572872 | tf_op jit(solution)/shard_map/ppermute | solution.py:645
  441.2 25.5 %collective-permute-start.49 = (bf16[128,2048]{1,0:T(8,128)(2,1)}, bf16[128,2048]{1,0:T(8,128)(2,1)S(1)}, u32[]{:S(2)}, u32[]{:S(2)}) collective-permute-start(bf16[128,2048]{1,0:T(8,128)(2,1)} %get-tuple-element.155), channel_id=1, source_target_pairs={{0,6},{2,4},{4,2},{6,0},{8,14},{10,12},{12,10},{14,8},{16,22},{18,... | collective-permute-start | bytes 1572872 | tf_op jit(solution)/shard_map/ppermute | solution.py:645
  466.8 18.1 %collective-permute-start.50 = (bf16[4,1,128,2048]{3,2,1,0:T(8,128)(2,1)S(1)}, bf16[4,1,128,2048]{3,2,1,0:T(8,128)(2,1)}, u32[]{:S(2)}, u32[]{:S(2)}) collective-permute-start(bf16[4,1,128,2048]{3,2,1,0:T(8,128)(2,1)S(1)} %bitcast_dynamic-update-slice_fusion.1), channel_id=1, source_target_pairs={{0,1},{1,0},{2,3},{3,2},{4,5},{5,4},{6,7},{7,6},{8,9},{9,8},{10,11... | collective-permute-start | bytes 6291464 | tf_op jit(solution)/shard_map/ppermute | solution.py:464
  469.7 45.1 %collective-permute-start.44 = (f32[128,2048]{1,0:T(8,128)}, f32[128,2048]{1,0:T(8,128)}, u32[]{:S(2)}, u32[]{:S(2)}) collective-permute-start(f32[128,2048]{1,0:T(8,128)} %convolution_add_fusion.1), channel_id=1, source_target_pairs={{0,1},{1,0},{2,3},{3,2},{4,5},{5,4},{6,7},{7,6},{8,9},{9,8},{10,11... | collective-permute-start | bytes 3145736 | tf_op jit(solution)/shard_map/ppermute | solution.py:464
  476.6 12.7 %all-to-all-start.5 = ((bf16[4,256,256]{2,1,0:T(8,128)(2,1)}), bf16[4,256,256]{2,1,0:T(8,128)(2,1)}, u32[]{:S(2)}, u32[]{:S(2)}) async-start(bf16[4,256,256]{2,1,0:T(8,128)(2,1)} %pad_maximum_fusion.1), calls=%async_computation.8 | async-start | bytes 1048576 | tf_op jit(solution)/shard_map/all_to_all | solution.py:585
  489.3 35.6 %all-to-all-start.9 = ((bf16[4,128,704]{1,2,0:T(8,128)(2,1)}), bf16[4,128,704]{1,2,0:T(8,128)(2,1)}, u32[]{:S(2)}, u32[]{:S(2)}) async-start(bf16[4,128,704]{1,2,0:T(8,128)(2,1)} %copy_bitcast_fusion.1), calls=%async_computation.15 | async-start | bytes 1441792 | tf_op jit(solution)/shard_map/all_to_all | solution.py:585
  494.1 69.9 %reduce-scatter.13.cloned.1.call-start = ((), (), s32[]{:S(2)}) async-start(), calls=%async_computation.23 | async-start | bytes 1310720 | tf_op jit(solution)/shard_map/reduce_scatter | solution.py:720
  519.6 35.5 %collective-permute-start.45 = (f32[128,2048]{1,0:T(8,128)}, f32[128,2048]{1,0:T(8,128)}, u32[]{:S(2)}, u32[]{:S(2)}) collective-permute-start(f32[128,2048]{1,0:T(8,128)} %get-tuple-element.150), channel_id=1, source_target_pairs={{0,1},{1,0},{2,3},{3,2},{4,5},{5,4},{6,7},{7,6},{8,9},{9,8},{10,11... | collective-permute-start | bytes 3145736 | tf_op jit(solution)/shard_map/ppermute | solution.py:464
  524.9 22.8 %all-to-all-start.3 = ((f32[16,2,128]{2,1,0:T(2,128)}), f32[16,2,128]{2,1,0:T(2,128)S(1)}, u32[]{:S(2)}, u32[]{:S(2)}) async-start(f32[16,2,128]{2,1,0:T(2,128)} %add_bitcast_fusion), calls=%async_computation.5 | async-start | bytes 32768 | tf_op jit(solution)/shard_map/all_to_all | solution.py:821
  547.7 16.1 %all-to-all-start.6 = ((bf16[4,128,896]{1,2,0:T(8,128)(2,1)}), bf16[4,128,896]{1,2,0:T(8,128)(2,1)S(1)}, u32[]{:S(2)}, u32[]{:S(2)}) async-start(bf16[4,128,896]{1,2,0:T(8,128)(2,1)} %copy.63), calls=%async_computation.9 | async-start | bytes 1835008 | tf_op jit(solution)/shard_map/all_to_all | solution.py:585
  564.0 9.7 %all-to-all-start.7 = ((bf16[4,128,256]{2,1,0:T(8,128)(2,1)}), bf16[4,128,256]{2,1,0:T(8,128)(2,1)}, u32[]{:S(2)}, u32[]{:S(2)}) async-start(bf16[4,128,256]{2,1,0:T(8,128)(2,1)} %bitcast.150), calls=%async_computation.11 | async-start | bytes 524288 | tf_op jit(solution)/shard_map/all_to_all | solution.py:585
  (50 other events, 433.7 us)
Sparse Core Ops, SparseCore 0:
  11.4 37.8 all-gather.4
  57.4 35.2 all-gather.6
  94.8 36.1 all-gather.8
  133.0 33.9 all-gather.10
  256.8 30.7 reduce-scatter.8
  291.6 53.5 reduce-scatter.6
  347.4 31.5 reduce-scatter.14
  381.3 44.2 reduce-scatter.16
  427.9 85.4 reduce-scatter.10
  515.6 37.6 reduce-scatter.12

commit v7 on v6

--- a/solution.py
+++ b/solution.py
@@ -613,12 +613,15 @@
     return jnp.concatenate(blocks, axis=0), done
 
 
-def add_other_core(x, grid):
+def by_core(x):
+    size = x.shape[0] // 2
+    return x[:size], x[size:].astype(bf16)
+
+
+def add_other_core(mine, other, grid):
     n = grid.outer
-    size = x.shape[0] // (2 * n)
-    block = [x[k * size : (k + 1) * size] for k in range(2 * n)]
-    other = tie(*[swap(block[n + k].astype(bf16)) for k in range(n)])
-    return [block[k] + other[k].astype(f32) for k in range(n)]
+    other = tie(*[swap(y) for y in jnp.split(other, n)])
+    return [x + y.astype(f32) for x, y in zip(jnp.split(mine, n), other)]
 
 
 def scatter_along(own, grid, beside=()):
@@ -733,15 +736,27 @@
         ((cot_rows, down_piece), (plane_tokens(normed_own),), (full_gate,)),
     )
     full_down = gather_rows(down_piece)
-    cot_all, (gate_act, full_up, up_act, full_down) = gather_along(
+    def gated(gate, up):
+        return (jax.nn.silu(gate) * up).astype(bf16)
+
+    cot_all, (gate_act, full_up, up_act, full_down, out_mine, out_other) = gather_along(
         cot_rows,
         grid,
         place,
         (
             (nn(tokens, full_gate), full_up),
-            (),
-            (nn(tokens, full_up), full_down),
+            lambda gate, w_up_all: (nn(tokens, w_up_all), full_down),
+            lambda gate, _, up, w_down_all: by_core(nt(gated(gate, up), w_down_all)),
         ),
+    )
+    out_own = add_other_core(out_mine, out_other, grid)
+    out_blocks = jnp.zeros((grid.outer,) + out_own[0].shape, bf16)
+    for k, x in enumerate(out_own):
+        at = (place + k) % grid.outer
+        out_blocks = lax.dynamic_update_slice_in_dim(out_blocks, x.astype(bf16)[None], at, 0)
+    out_blocks, cot_all = tie(out_blocks.reshape(-1, out_blocks.shape[2]), cot_all)
+    out_sum = lax.psum_scatter(
+        out_blocks, "dp", scatter_dimension=0, tiled=True, axis_index_groups=grid.cols
     )
 
     def scatter_rows(g):
@@ -755,26 +770,17 @@
     inner_grad = nn(cot_all, full_down)
     gate_grad = (inner_grad * up_act * silu_slope(gate_act)).astype(bf16)
     up_grad = (inner_grad * jax.nn.silu(gate_act)).astype(bf16)
-    inner_act = (jax.nn.silu(gate_act) * up_act).astype(bf16)
-    back_parts, (down_rows, gate_rows, *out_own, up_rows) = scatter_along(
-        add_other_core(nt(gate_grad, full_gate) + nt(up_grad, full_up), grid),
+    inner_act = gated(gate_act, up_act)
+    back_parts, (down_rows, out_sum, gate_rows, up_rows) = scatter_along(
+        add_other_core(*by_core(nt(gate_grad, full_gate) + nt(up_grad, full_up)), grid),
         grid,
         (
-            (tn(cot_all, inner_act).astype(bf16), tn(tokens, gate_grad).astype(bf16)),
-            add_other_core(nt(inner_act, full_down), grid),
+            (tn(cot_all, inner_act).astype(bf16), out_sum),
+            (tn(tokens, gate_grad).astype(bf16),),
             (tn(tokens, up_grad).astype(bf16),),
         ),
     )
-    down_rows, gate_rows = scatter_rows(down_rows), scatter_rows(gate_rows)
-    out_blocks = jnp.zeros((grid.outer,) + out_own[0].shape, bf16)
-    for k, x in enumerate(out_own):
-        at = (place + k) % grid.outer
-        out_blocks = lax.dynamic_update_slice_in_dim(out_blocks, x.astype(bf16)[None], at, 0)
-    out_blocks = out_blocks.reshape(-1, out_blocks.shape[2])
-    out_sum = lax.psum_scatter(
-        out_blocks, "dp", scatter_dimension=0, tiled=True, axis_index_groups=grid.cols
-    )
-    up_rows = scatter_rows(up_rows)
+    down_rows, gate_rows, up_rows = (scatter_rows(g) for g in (down_rows, gate_rows, up_rows))
     hidden_grad, low_half, mlp_gain_part = second_norm_back(
         out_grad, hidden, mlp_gain, back_parts, core, grid
     )

time: 593 us -> 558 us (0.941)
  waiting for transfers between devices: 182 us -> 154 us
  other arithmetic: 45.8 us -> 34.3 us
    ppermute x3, waiting for transfers between devices: 25.8 us -> 10.5 us  [scatter_along(): down = lax.ppermute(down.astype(bf16), 'dp', grid.down)]
    ppermute x6, waiting for transfers between devices: 23.7 us -> 15.3 us  [gather_along(): below = lax.ppermute(below, 'dp', grid.up)]
    unnamed x11, other arithmetic: 18.8 us -> 11.6 us
    unnamed x101 -> x105, local copies, waits for them, and re-layouts: 22.6 us -> 23.5 us
  transfers between devices with their start and end apart: 70 -> 70, of which waited for: 31 -> 37; matrix products, arithmetic and copies ran while one was open for 31% -> 35% of each run, Pallas kernels for 6% -> 6%
where the time goes in v7:
time: 558 us; the launch traced here: 548 us
  waiting for transfers between devices  154 us (28%)
  matrix products  103 us (18%)
  starting transfers between devices  101 us (18%)
  local copies, waits for them, and re-layouts  64.7 us (12%)
  blocking collectives  42.3 us (8%)
  other arithmetic  34.3 us (6%)
  Pallas kernels  33.2 us (6%)
  between operations  15.6 us (3%)
    all_to_all x1, blocking collectives, exchange(): lax.all_to_all(x, 'dp', split, concat, tiled=True, axis_index_groups=groups)  42.3 us
    dot_general x8, matrix products, nn(): return jnp.dot(a.astype(bf16), b.astype(bf16), preferred_element_type=f32)  37.6 us
    dot_general x13, matrix products, nt(): lax.dot_general(a.astype(bf16), b.astype(bf16), (((1,), (1,)), ((), ())),...  35.8 us
    all_to_all x8, starting transfers between devices, exchange(): lax.all_to_all(x, 'dp', split, concat, tiled=True, axis_index_groups=groups)  35.4 us
    all_to_all x8, waiting for transfers between devices, exchange(): lax.all_to_all(x, 'dp', split, concat, tiled=True, axis_index_groups=groups)  34.9 us
    dot_general x5, matrix products, tn(): lax.dot_general(a.astype(bf16), b.astype(bf16), (((0,), (0,)), ((), ())),...  29.2 us
    ppermute x6, waiting for transfers between devices, gather_along(): above = lax.ppermute(above, 'dp', grid.down)  29.2 us
    unnamed x105, local copies, waits for them, and re-layouts  23.5 us
  transfers between devices with their start and end apart: 70, of which 37 were waited for; matrix products, arithmetic and copies ran while one was open for 35% of the time, Pallas kernels for 6%

profile of v7, /device:TPU:0, one launch (start us, length us, event | category | flops | bytes accessed | tf_op | source)
XLA Modules:
  0.0 547.8 jit_solution(15835175210786159028)
XLA Ops:
  14.3 6.3 %all-to-all-start = ((bf16[128,4,1408]{0,2,1:T(8,128)(2,1)}), bf16[128,4,1408]{0,2,1:T(8,128)(2,1)S(1)}, u32[]{:S(2)}, u32[]{:S(2)}) async-start(bf16[128,4,1408]{0,2,1:T(8,128)(2,1)} %pad_maximum_fusion), calls=%async_computation | async-start | bytes 2883584 | tf_op jit(solution)/shard_map/all_to_all | solution.py:585
  20.7 5.0 multiply_convert_fusion.5
  31.8 6.4 %slot_forward.1 = (bf16[256,1024]{1,0:T(8,128)(2,1)}, f32[256,128]{1,0:T(8,128)}, f32[4,256,128]{2,1,0:T(8,128)}, bf16[2,256,256]{2,1,0:T(8,128)(2,1)}, bf16[2,256,16]{2,1,0:T(8,128)(2,1)}) custom-call(s32[1,3]{1,0:T(1,128)} %starts_ref.3, bf16[256,1024]{1,0:T(8,128)(2,1)} %get-tuple-element.216.q_ref, bf16[256,1024]{1,0:T(8,128)(2,1)} %get-tuple-element.218.k_ref, ...), custom_call_target="tpu_custom_call" | custom-call | flops 4000000000 | bytes 4000000 | tf_op jit(solution)/shard_map/slot_forward/pallas_call | solution.py:383
  38.1 4.8 fusion.24.mine_ref
  42.9 11.9 %all-to-all-done = bf16[128,4,1408]{0,2,1:T(8,128)(2,1)S(1)} async-done(((bf16[128,4,1408]{0,2,1:T(8,128)(2,1)}), bf16[128,4,1408]{0,2,1:T(8,128)(2,1)S(1)}, u32[]{:S(2)}, u32[]{:S(2)}) %all-to-all-start) | async-done | bytes 1441824 | tf_op jit(solution)/shard_map/all_to_all | solution.py:585
  58.1 3.7 fusion.22
  63.5 3.5 all-to-all-start.1
  69.8 3.3 second_norm.1
  73.1 4.6 collective-permute-start.1
  79.0 2.5 broadcast.40.clone
  83.0 4.0 all-to-all-done.1
  90.6 5.5 collective-permute-done.2
  96.0 4.0 collective-permute-start.5
  101.3 3.4 bitcast_dynamic-update-slice_fusion
  104.7 6.1 %collective-permute-done.5 = bf16[128,2048]{1,0:T(8,128)(2,1)S(1)} collective-permute-done((bf16[128,2048]{1,0:T(8,128)(2,1)}, bf16[128,2048]{1,0:T(8,128)(2,1)S(1)}, u32[]{:S(2)}, u32[]{:S(2)}) %collective-permute-start.5) | collective-permute-done | bytes 524320 | tf_op jit(solution)/shard_map/ppermute | solution.py:598
  110.8 4.0 collective-permute-done.6
  122.1 4.7 collective-permute-done.8
  126.8 4.1 collective-permute-done.9
  137.5 4.3 collective-permute-start.3
  148.5 5.1 fusion.45
  153.6 6.6 %collective-permute-done.4 = bf16[128,2048]{1,0:T(8,128)(2,1)} collective-permute-done((bf16[128,2048]{1,0:T(8,128)(2,1)}, bf16[128,2048]{1,0:T(8,128)(2,1)}, u32[]{:S(2)}, u32[]{:S(2)}) %collective-permute-start.4) | collective-permute-done | bytes 524320 | tf_op jit(solution)/shard_map/ppermute | solution.py:599
  163.8 7.9 %fusion.46 = f32[1024,704]{0,1:T(8,128)} fusion(bf16[1024,2048]{1,0:T(8,128)(2,1)} %select_dynamic-update-slice_fusion.6, bf16[2048,704]{1,0:T(8,128)(2,1)} %all-gather.9.cloned.1.call-done), kind=kOutput, calls=%fused_computation.130 | convolution fusion | flops 2952790016 | bytes 9961472 | tf_op jit(solution)/shard_map/dot_general | solution.py:19
  173.1 4.9 collective-permute-done.18
  181.5 2.7 multiply_convert_fusion.2
  185.3 3.5 fusion.47
  190.1 4.0 collective-permute-done.20
  202.1 2.6 collective-permute-done.27
  208.3 9.2 %multiply_convert_fusion.1 = (bf16[1024,704]{0,1:T(8,128)(2,1)S(1)}, bf16[1024,704]{0,1:T(8,128)(2,1)S(1)}) fusion(f32[1024,704]{0,1:T(8,128)} %copy-done.11, f32[1024,704]{0,1:T(8,128)} %fusion.46, bf16[1024,2048]{1,0:T(8,128)(2,1)} %copy-done.38, bf16[2048,704]{0,1:T(8,128)(2,1)} %all-gather.11.cloned.1.call-done), kind=kOutput, calls=%fused_computation.7 | convolution fusion | flops 2962161664 | bytes 15728640 | tf_op jit(solution)/shard_map/dot_general | solution.py:19
  217.6 3.5 fusion.48
  221.1 5.5 %fusion.44 = (bf16[1024,2048]{1,0:T(8,128)(2,1)S(1)}, f32[1024,2048]{1,0:T(8,128)S(1)}) fusion(f32[1024,2048]{1,0:T(8,128)S(1)} %fusion.48, bf16[1024,704]{0,1:T(8,128)(2,1)S(1)} %get-tuple-element.195, bf16[2048,704]{1,0:T(8,128)(2,1)} %all-gather.7.cloned.1.call-done), kind=kOutput, calls=%fused_computation.128 | convolution fusion | flops 2956984320 | bytes 25296896 | tf_op jit(solution)/shard_map/dot_general | solution.py:23
  236.4 4.6 convolution_convert_fusion.3
  241.0 16.5 %collective-permute-done.36 = bf16[128,2048]{1,0:T(8,128)(2,1)} collective-permute-done((bf16[128,2048]{1,0:T(8,128)(2,1)}, bf16[128,2048]{1,0:T(8,128)(2,1)}, u32[]{:S(2)}, u32[]{:S(2)}) %collective-permute-start.36) | collective-permute-done | bytes 524320 | tf_op jit(solution)/shard_map/ppermute | solution.py:634
  260.3 3.0 add_convert_fusion.2
  263.3 3.2 collective-permute-start.39
  267.8 7.2 %convolution_convert_fusion.2 = bf16[2048,704]{0,1:T(8,128)(2,1)} fusion(bf16[1024,704]{0,1:T(8,128)(2,1)S(1)} %get-tuple-element.195, bf16[1024,2048]{1,0:T(8,128)(2,1)} %select_dynamic-update-slice_fusion.6), kind=kOutput, calls=%fused_computation.4 | convolution fusion | flops 2954231808 | bytes 8519680 | tf_op jit(solution)/shard_map/dot_general | solution.py:29
  277.4 4.9 collective-permute-done.40
  282.4 4.1 add_convert_fusion
  286.5 3.3 collective-permute-start.41
  291.1 4.6 convolution_convert_fusion.1
  295.7 4.1 collective-permute-done.41.refs_1_
  299.9 3.8 collective-permute-done.42.refs_2_
  304.5 3.9 second_norm_back.1
  310.6 4.3 convolution_convert_fusion.5.do_ref
  317.0 3.5 all-to-all-start.2
  320.9 11.3 %slot_backward.1 = (bf16[256,1024]{1,0:T(8,128)(2,1)}, bf16[256,1024]{1,0:T(8,128)(2,1)}, bf16[256,1024]{1,0:T(8,128)(2,1)}, bf16[256,128]{1,0:T(8,128)(2,1)}, bf16[4,256,896]{2,1,0:T(8,128)(2,1)}) custom-call(s32[1,3]{1,0:T(1,128)} %starts_ref.3, bf16[256,1024]{1,0:T(8,128)(2,1)} %get-tuple-element.216.q_ref, bf16[256,1024]{1,0:T(8,128)(2,1)} %get-tuple-element.218.k_ref, ...), custom_call_target="tpu_custom_call" | custom-call | flops 12000000000 | bytes 8000000 | tf_op jit(solution)/shard_map/slot_backward/pallas_call | solution.py:403
  332.2 7.6 %all-to-all-done.2 = bf16[4,128,704]{1,2,0:T(8,128)(2,1)S(1)} async-done(((bf16[4,128,704]{1,2,0:T(8,128)(2,1)}), bf16[4,128,704]{1,2,0:T(8,128)(2,1)S(1)}, u32[]{:S(2)}, u32[]{:S(2)}) %all-to-all-start.2) | async-done | bytes 720928 | tf_op jit(solution)/shard_map/all_to_all | solution.py:585
  341.0 42.3 %all_to_all.123 = bf16[4,256,896]{2,1,0:T(8,128)(2,1)S(1)} all-to-all(bf16[4,256,896]{2,1,0:T(8,128)(2,1)S(1)} %copy-done.16), channel_id=1, replica_groups={{0,2,4,6},{8,10,12,14},{16,18,20,22},{24,26,28,30},{1,3,5,7},{9,11,13,1..., dimensions={0} | all-to-all | bytes 3670016 | tf_op jit(solution)/shard_map/all_to_all | solution.py:585
  383.3 8.2 %convolution_convert_fusion = bf16[2048,896]{1,0:T(8,128)(2,1)} fusion(bf16[1024,2048]{1,0:T(8,128)(2,1)} %bitcast.11, bf16[1024,896]{1,0:T(8,128)(2,1)S(1)} %bitcast.155), kind=kOutput, calls=%fused_computation.2 | convolution fusion | flops 3759931392 | bytes 9699328 | tf_op jit(solution)/shard_map/dot_general | solution.py:29
  396.1 4.8 all-to-all-start.8
  403.2 3.7 fusion.16
  413.4 8.6 %collective-permute-done.47 = bf16[128,2048]{1,0:T(8,128)(2,1)S(1)} collective-permute-done((bf16[128,2048]{1,0:T(8,128)(2,1)}, bf16[128,2048]{1,0:T(8,128)(2,1)S(1)}, u32[]{:S(2)}, u32[]{:S(2)}) %collective-permute-start.47) | collective-permute-done | bytes 524320 | tf_op jit(solution)/shard_map/ppermute | solution.py:648
  422.0 12.8 %collective-permute-done.48 = bf16[128,2048]{1,0:T(8,128)(2,1)S(1)} collective-permute-done((bf16[128,2048]{1,0:T(8,128)(2,1)}, bf16[128,2048]{1,0:T(8,128)(2,1)S(1)}, u32[]{:S(2)}, u32[]{:S(2)}) %collective-permute-start.48) | collective-permute-done | bytes 524320 | tf_op jit(solution)/shard_map/ppermute | solution.py:648
  444.8 4.1 all-to-all-start.5
  448.9 2.5 broadcast.40
  452.9 3.2 constant_dynamic-update-slice_fusion.4
  457.5 4.9 all-to-all-start.9
  462.3 4.7 convolution_convert_fusion.4
  467.0 10.3 %reduce-scatter.11.cloned.1.call-done = bf16[512,896]{1,0:T(8,128)(2,1)} async-done(((bf16[2048,896]{1,0:T(8,128)(2,1)}), bf16[512,896]{1,0:T(8,128)(2,1)}) %reduce-scatter.11.cloned.1.call-update) | async-done | bytes 917520 | tf_op jit(solution)/shard_map/reduce_scatter | solution.py:723
  478.6 4.0 first_norm_back.1
  486.4 3.6 all-to-all-done.9
  490.0 13.7 %all-to-all-start.3 = ((f32[16,2,128]{2,1,0:T(2,128)}), f32[16,2,128]{2,1,0:T(2,128)S(1)}, u32[]{:S(2)}, u32[]{:S(2)}) async-start(f32[16,2,128]{2,1,0:T(2,128)} %add_bitcast_fusion), calls=%async_computation.5 | async-start | bytes 32768 | tf_op jit(solution)/shard_map/all_to_all | solution.py:827
  512.9 4.2 all-to-all-start.6
  522.6 6.5 %all-to-all-done.6 = bf16[4,128,896]{1,2,0:T(8,128)(2,1)S(1)} async-done(((bf16[4,128,896]{1,2,0:T(8,128)(2,1)}), bf16[4,128,896]{1,2,0:T(8,128)(2,1)S(1)}, u32[]{:S(2)}, u32[]{:S(2)}) %all-to-all-start.6) | async-done | bytes 917536 | tf_op jit(solution)/shard_map/all_to_all | solution.py:585
  529.2 4.1 all-to-all-start.7
  (297 shorter events, 148.6 us)
Async XLA Ops:
  7.2 50.0 %all-gather.5.cloned.1.call-start = ((), (), s32[]{:S(2)}) async-start(), calls=%async_computation.16 | async-start | bytes 2621440 | tf_op jit(solution)/shard_map/all_gather | solution.py:697
  14.3 40.5 %all-to-all-start = ((bf16[128,4,1408]{0,2,1:T(8,128)(2,1)}), bf16[128,4,1408]{0,2,1:T(8,128)(2,1)S(1)}, u32[]{:S(2)}, u32[]{:S(2)}) async-start(bf16[128,4,1408]{0,2,1:T(8,128)(2,1)} %pad_maximum_fusion), calls=%async_computation | async-start | bytes 2883584 | tf_op jit(solution)/shard_map/all_to_all | solution.py:585
  20.6 110.3 %all-gather.7.cloned.1.call-start = ((), (), s32[]{:S(2)}) async-start(), calls=%async_computation.17 | async-start | bytes 3932160 | tf_op jit(solution)/shard_map/all_gather | solution.py:677
  57.2 103.0 %all-gather.9.cloned.1.call-start = ((), (), s32[]{:S(2)}) async-start(), calls=%async_computation.18 | async-start | bytes 3932160 | tf_op jit(solution)/shard_map/all_gather | solution.py:677
  58.0 43.3 %collective-permute-start.7 = (bf16[4,1,128,2048]{3,2,0,1:T(8,128)(2,1)}, bf16[4,1,128,2048]{3,2,0,1:T(8,128)(2,1)}, u32[]{:S(2)}, u32[]{:S(2)}) collective-permute-start(bf16[4,1,128,2048]{3,2,0,1:T(8,128)(2,1)} %bitcast.150), channel_id=1, source_target_pairs={{0,1},{1,0},{2,3},{3,2},{4,5},{5,4},{6,7},{7,6},{8,9},{9,8},{10,11... | collective-permute-start | bytes 6291464 | tf_op jit(solution)/shard_map/ppermute | solution.py:464
  61.8 7.1 %collective-permute-start = (f32[128,2048]{1,0:T(8,128)S(1)}, f32[128,2048]{1,0:T(8,128)S(1)}, u32[]{:S(2)}, u32[]{:S(2)}) collective-permute-start(f32[128,2048]{1,0:T(8,128)S(1)} %fusion.22), channel_id=1, source_target_pairs={{0,1},{1,0},{2,3},{3,2},{4,5},{5,4},{6,7},{7,6},{8,9},{9,8},{10,11... | collective-permute-start | bytes 3145736 | tf_op jit(solution)/shard_map/ppermute | solution.py:464
  63.5 23.6 %all-to-all-start.1 = ((bf16[128,4,704]{0,2,1:T(8,128)(2,1)}), bf16[128,4,704]{0,2,1:T(8,128)(2,1)S(1)}, u32[]{:S(2)}, u32[]{:S(2)}) async-start(bf16[128,4,704]{0,2,1:T(8,128)(2,1)} %bitcast.6), calls=%async_computation.1 | async-start | bytes 1441792 | tf_op jit(solution)/shard_map/all_to_all | solution.py:585
  67.0 111.0 %all-gather.11.cloned.1.call-start = ((), (), s32[]{:S(2)}) async-start(), calls=%async_computation.19 | async-start | bytes 3604480 | tf_op jit(solution)/shard_map/all_gather | solution.py:677
  73.1 17.5 %collective-permute-start.1 = (bf16[128,2048]{1,0:T(8,128)(2,1)}, bf16[128,2048]{1,0:T(8,128)(2,1)}, u32[]{:S(2)}, u32[]{:S(2)}) collective-permute-start(bf16[128,2048]{1,0:T(8,128)(2,1)} %get-tuple-element.91), channel_id=1, source_target_pairs={{0,8},{2,10},{4,12},{6,14},{8,16},{10,18},{12,20},{14,22},{16,24},... | collective-permute-start | bytes 1572872 | tf_op jit(solution)/shard_map/ppermute | solution.py:598
  77.7 18.3 %collective-permute-start.2 = (bf16[128,2048]{1,0:T(8,128)(2,1)}, bf16[128,2048]{1,0:T(8,128)(2,1)}, u32[]{:S(2)}, u32[]{:S(2)}) collective-permute-start(bf16[128,2048]{1,0:T(8,128)(2,1)} %get-tuple-element.91), channel_id=1, source_target_pairs={{8,0},{10,2},{12,4},{14,6},{16,8},{18,10},{20,12},{22,14},{24,16},... | collective-permute-start | bytes 1572872 | tf_op jit(solution)/shard_map/ppermute | solution.py:599
  96.0 14.8 %collective-permute-start.5 = (bf16[128,2048]{1,0:T(8,128)(2,1)}, bf16[128,2048]{1,0:T(8,128)(2,1)S(1)}, u32[]{:S(2)}, u32[]{:S(2)}) collective-permute-start(bf16[128,2048]{1,0:T(8,128)(2,1)} %collective-permute-done.1), channel_id=1, source_target_pairs={{0,8},{2,10},{4,12},{6,14},{8,16},{10,18},{12,20},{14,22},{16,24},... | collective-permute-start | bytes 1572872 | tf_op jit(solution)/shard_map/ppermute | solution.py:598
  100.0 14.9 %collective-permute-start.6 = (bf16[128,2048]{1,0:T(8,128)(2,1)}, bf16[128,2048]{1,0:T(8,128)(2,1)S(1)}, u32[]{:S(2)}, u32[]{:S(2)}) collective-permute-start(bf16[128,2048]{1,0:T(8,128)(2,1)} %collective-permute-done.2), channel_id=1, source_target_pairs={{8,0},{10,2},{12,4},{14,6},{16,8},{18,10},{20,12},{22,14},{24,16},... | collective-permute-start | bytes 1572872 | tf_op jit(solution)/shard_map/ppermute | solution.py:599
  114.9 11.9 %collective-permute-start.8 = (bf16[128,2048]{1,0:T(8,128)(2,1)S(1)}, bf16[128,2048]{1,0:T(8,128)(2,1)S(1)}, u32[]{:S(2)}, u32[]{:S(2)}) collective-permute-start(bf16[128,2048]{1,0:T(8,128)(2,1)S(1)} %collective-permute-done.5), channel_id=1, source_target_pairs={{0,8},{2,10},{4,12},{6,14},{8,16},{10,18},{12,20},{14,22},{16,24},... | collective-permute-start | bytes 1572872 | tf_op jit(solution)/shard_map/ppermute | solution.py:598
  117.3 13.6 %collective-permute-start.9 = (bf16[128,2048]{1,0:T(8,128)(2,1)S(1)}, bf16[128,2048]{1,0:T(8,128)(2,1)S(1)}, u32[]{:S(2)}, u32[]{:S(2)}) collective-permute-start(bf16[128,2048]{1,0:T(8,128)(2,1)S(1)} %collective-permute-done.6), channel_id=1, source_target_pairs={{8,0},{10,2},{12,4},{14,6},{16,8},{18,10},{20,12},{22,14},{24,16},... | collective-permute-start | bytes 1572872 | tf_op jit(solution)/shard_map/ppermute | solution.py:599
  118.7 16.1 %collective-permute-start.10 = (bf16[128,2048]{1,0:T(8,128)(2,1)S(1)}, bf16[128,2048]{1,0:T(8,128)(2,1)}, u32[]{:S(2)}, u32[]{:S(2)}) collective-permute-start(bf16[128,2048]{1,0:T(8,128)(2,1)S(1)} %copy-done.30), channel_id=1, source_target_pairs={{0,1},{1,0},{2,3},{3,2},{4,5},{5,4},{6,7},{7,6},{8,9},{9,8},{10,11... | collective-permute-start | bytes 1572872 | tf_op jit(solution)/shard_map/ppermute | solution.py:464
  119.6 17.8 %collective-permute-start.11 = (bf16[128,2048]{1,0:T(8,128)(2,1)}, bf16[128,2048]{1,0:T(8,128)(2,1)}, u32[]{:S(2)}, u32[]{:S(2)}) collective-permute-start(bf16[128,2048]{1,0:T(8,128)(2,1)} %collective-permute-done.2), channel_id=1, source_target_pairs={{0,1},{1,0},{2,3},{3,2},{4,5},{5,4},{6,7},{7,6},{8,9},{9,8},{10,11... | collective-permute-start | bytes 1572872 | tf_op jit(solution)/shard_map/ppermute | solution.py:464
  120.1 27.5 %collective-permute-start.16 = (bf16[128,2048]{1,0:T(8,128)(2,1)}, bf16[128,2048]{1,0:T(8,128)(2,1)}, u32[]{:S(2)}, u32[]{:S(2)}) collective-permute-start(bf16[128,2048]{1,0:T(8,128)(2,1)} %collective-permute-done.1), channel_id=1, source_target_pairs={{0,1},{1,0},{2,3},{3,2},{4,5},{5,4},{6,7},{7,6},{8,9},{9,8},{10,11... | collective-permute-start | bytes 1572872 | tf_op jit(solution)/shard_map/ppermute | solution.py:464
  120.2 140.1 %reduce-scatter.7.cloned.1.call-start = ((), (), s32[]{:S(2)}) async-start(), calls=%async_computation.20 | async-start | bytes 2621440 | tf_op jit(solution)/shard_map/reduce_scatter | solution.py:758
  126.8 16.9 %collective-permute-start.13 = (bf16[128,2048]{1,0:T(8,128)(2,1)S(1)}, bf16[128,2048]{1,0:T(8,128)(2,1)}, u32[]{:S(2)}, u32[]{:S(2)}) collective-permute-start(bf16[128,2048]{1,0:T(8,128)(2,1)S(1)} %collective-permute-done.6), channel_id=1, source_target_pairs={{0,1},{1,0},{2,3},{3,2},{4,5},{5,4},{6,7},{7,6},{8,9},{9,8},{10,11... | collective-permute-start | bytes 1572872 | tf_op jit(solution)/shard_map/ppermute | solution.py:464
  130.9 10.8 %collective-permute-start.12 = (bf16[128,2048]{1,0:T(8,128)(2,1)S(1)}, bf16[128,2048]{1,0:T(8,128)(2,1)S(1)}, u32[]{:S(2)}, u32[]{:S(2)}) collective-permute-start(bf16[128,2048]{1,0:T(8,128)(2,1)S(1)} %collective-permute-done.8), channel_id=1, source_target_pairs={{0,1},{1,0},{2,3},{3,2},{4,5},{5,4},{6,7},{7,6},{8,9},{9,8},{10,11... | collective-permute-start | bytes 1572872 | tf_op jit(solution)/shard_map/ppermute | solution.py:464
  134.8 10.2 %collective-permute-start.14 = (bf16[128,2048]{1,0:T(8,128)(2,1)S(1)}, bf16[128,2048]{1,0:T(8,128)(2,1)S(1)}, u32[]{:S(2)}, u32[]{:S(2)}) collective-permute-start(bf16[128,2048]{1,0:T(8,128)(2,1)S(1)} %collective-permute-done.5), channel_id=1, source_target_pairs={{0,1},{1,0},{2,3},{3,2},{4,5},{5,4},{6,7},{7,6},{8,9},{9,8},{10,11... | collective-permute-start | bytes 1572872 | tf_op jit(solution)/shard_map/ppermute | solution.py:464
  137.5 16.1 %collective-permute-start.3 = (bf16[128,2048]{1,0:T(8,128)(2,1)}, bf16[128,2048]{1,0:T(8,128)(2,1)}, u32[]{:S(2)}, u32[]{:S(2)}) collective-permute-start(bf16[128,2048]{1,0:T(8,128)(2,1)} %cotangent_rows.1), channel_id=1, source_target_pairs={{0,8},{2,10},{4,12},{6,14},{8,16},{10,18},{12,20},{14,22},{16,24},... | collective-permute-start | bytes 1572872 | tf_op jit(solution)/shard_map/ppermute | solution.py:598
  141.8 5.8 %collective-permute-start.15 = (bf16[128,2048]{1,0:T(8,128)(2,1)S(1)}, bf16[128,2048]{1,0:T(8,128)(2,1)S(1)}, u32[]{:S(2)}, u32[]{:S(2)}) collective-permute-start(bf16[128,2048]{1,0:T(8,128)(2,1)S(1)} %collective-permute-done.9), channel_id=1, source_target_pairs={{0,1},{1,0},{2,3},{3,2},{4,5},{5,4},{6,7},{7,6},{8,9},{9,8},{10,11... | collective-permute-start | bytes 1572872 | tf_op jit(solution)/shard_map/ppermute | solution.py:464
  143.7 16.5 %collective-permute-start.4 = (bf16[128,2048]{1,0:T(8,128)(2,1)}, bf16[128,2048]{1,0:T(8,128)(2,1)}, u32[]{:S(2)}, u32[]{:S(2)}) collective-permute-start(bf16[128,2048]{1,0:T(8,128)(2,1)} %cotangent_rows.1), channel_id=1, source_target_pairs={{8,0},{10,2},{12,4},{14,6},{16,8},{18,10},{20,12},{22,14},{24,16},... | collective-permute-start | bytes 1572872 | tf_op jit(solution)/shard_map/ppermute | solution.py:599
  145.0 53.0 %collective-permute-start.25 = (bf16[128,2048]{1,0:T(8,128)(2,1)}, bf16[128,2048]{1,0:T(8,128)(2,1)}, u32[]{:S(2)}, u32[]{:S(2)}) collective-permute-start(bf16[128,2048]{1,0:T(8,128)(2,1)} %cotangent_rows.1), channel_id=1, source_target_pairs={{0,1},{1,0},{2,3},{3,2},{4,5},{5,4},{6,7},{7,6},{8,9},{9,8},{10,11... | collective-permute-start | bytes 1572872 | tf_op jit(solution)/shard_map/ppermute | solution.py:464
  160.3 12.9 %collective-permute-start.17 = (bf16[128,2048]{1,0:T(8,128)(2,1)}, bf16[128,2048]{1,0:T(8,128)(2,1)}, u32[]{:S(2)}, u32[]{:S(2)}) collective-permute-start(bf16[128,2048]{1,0:T(8,128)(2,1)} %collective-permute-done.3), channel_id=1, source_target_pairs={{0,8},{2,10},{4,12},{6,14},{8,16},{10,18},{12,20},{14,22},{16,24},... | collective-permute-start | bytes 1572872 | tf_op jit(solution)/shard_map/ppermute | solution.py:598
  162.5 15.5 %collective-permute-start.18 = (bf16[128,2048]{1,0:T(8,128)(2,1)}, bf16[128,2048]{1,0:T(8,128)(2,1)}, u32[]{:S(2)}, u32[]{:S(2)}) collective-permute-start(bf16[128,2048]{1,0:T(8,128)(2,1)} %collective-permute-done.4), channel_id=1, source_target_pairs={{8,0},{10,2},{12,4},{14,6},{16,8},{18,10},{20,12},{22,14},{24,16},... | collective-permute-start | bytes 1572872 | tf_op jit(solution)/shard_map/ppermute | solution.py:599
  178.0 12.1 %collective-permute-start.19 = (bf16[128,2048]{1,0:T(8,128)(2,1)}, bf16[128,2048]{1,0:T(8,128)(2,1)S(1)}, u32[]{:S(2)}, u32[]{:S(2)}) collective-permute-start(bf16[128,2048]{1,0:T(8,128)(2,1)} %collective-permute-done.17), channel_id=1, source_target_pairs={{0,8},{2,10},{4,12},{6,14},{8,16},{10,18},{12,20},{14,22},{16,24},... | collective-permute-start | bytes 1572872 | tf_op jit(solution)/shard_map/ppermute | solution.py:598
  179.8 14.4 %collective-permute-start.20 = (bf16[128,2048]{1,0:T(8,128)(2,1)}, bf16[128,2048]{1,0:T(8,128)(2,1)S(1)}, u32[]{:S(2)}, u32[]{:S(2)}) collective-permute-start(bf16[128,2048]{1,0:T(8,128)(2,1)} %collective-permute-done.18), channel_id=1, source_target_pairs={{8,0},{10,2},{12,4},{14,6},{16,8},{18,10},{20,12},{22,14},{24,16},... | collective-permute-start | bytes 1572872 | tf_op jit(solution)/shard_map/ppermute | solution.py:599
  197.3 2.9 collective-permute-start.23
  197.4 3.6 collective-permute-start.24
  198.0 3.7 collective-permute-start.26
  199.2 6.1 %collective-permute-start.31 = (bf16[128,2048]{1,0:T(8,128)(2,1)}, bf16[128,2048]{1,0:T(8,128)(2,1)S(1)}, u32[]{:S(2)}, u32[]{:S(2)}) collective-permute-start(bf16[128,2048]{1,0:T(8,128)(2,1)} %collective-permute-done.3), channel_id=1, source_target_pairs={{0,1},{1,0},{2,3},{3,2},{4,5},{5,4},{6,7},{7,6},{8,9},{9,8},{10,11... | collective-permute-start | bytes 1572872 | tf_op jit(solution)/shard_map/ppermute | solution.py:464
  199.7 5.3 collective-permute-start.28
  200.2 4.8 collective-permute-start.29
  201.0 3.7 collective-permute-start.27
  201.7 3.7 collective-permute-start.30
  208.1 106.8 %reduce-scatter.9.cloned.1.call-start = ((), (), s32[]{:S(2)}) async-start(), calls=%async_computation.21 | async-start | bytes 3604480 | tf_op jit(solution)/shard_map/reduce_scatter | solution.py:763
  227.5 2.9 collective-permute-start.34
  227.6 3.6 collective-permute-start.35
  232.5 25.0 %collective-permute-start.36 = (bf16[128,2048]{1,0:T(8,128)(2,1)}, bf16[128,2048]{1,0:T(8,128)(2,1)}, u32[]{:S(2)}, u32[]{:S(2)}) collective-permute-start(bf16[128,2048]{1,0:T(8,128)(2,1)} %get-tuple-element.194), channel_id=1, source_target_pairs={{0,8},{2,10},{4,12},{6,14},{8,16},{10,18},{12,20},{14,22},{16,24},... | collective-permute-start | bytes 1572872 | tf_op jit(solution)/shard_map/ppermute | solution.py:634
  234.9 24.4 %collective-permute-start.37 = (bf16[128,2048]{1,0:T(8,128)(2,1)}, bf16[128,2048]{1,0:T(8,128)(2,1)}, u32[]{:S(2)}, u32[]{:S(2)}) collective-permute-start(bf16[128,2048]{1,0:T(8,128)(2,1)} %get-tuple-element.193), channel_id=1, source_target_pairs={{8,0},{10,2},{12,4},{14,6},{16,8},{18,10},{20,12},{22,14},{24,16},... | collective-permute-start | bytes 1572872 | tf_op jit(solution)/shard_map/ppermute | solution.py:635
  260.3 133.7 %reduce-scatter.15.cloned.1.call-start = ((), (), s32[]{:S(2)}) async-start(), calls=%async_computation.24 | async-start | bytes 3604480 | tf_op jit(solution)/shard_map/reduce_scatter | solution.py:763
  263.3 14.0 %collective-permute-start.39 = (bf16[128,2048]{1,0:T(8,128)(2,1)}, bf16[128,2048]{1,0:T(8,128)(2,1)}, u32[]{:S(2)}, u32[]{:S(2)}) collective-permute-start(bf16[128,2048]{1,0:T(8,128)(2,1)} %get-tuple-element.189), channel_id=1, source_target_pairs={{0,8},{2,10},{4,12},{6,14},{8,16},{10,18},{12,20},{14,22},{16,24},... | collective-permute-start | bytes 1572872 | tf_op jit(solution)/shard_map/ppermute | solution.py:634
  266.5 15.7 %collective-permute-start.40 = (bf16[128,2048]{1,0:T(8,128)(2,1)}, bf16[128,2048]{1,0:T(8,128)(2,1)}, u32[]{:S(2)}, u32[]{:S(2)}) collective-permute-start(bf16[128,2048]{1,0:T(8,128)(2,1)} %get-tuple-element.188), channel_id=1, source_target_pairs={{8,0},{10,2},{12,4},{14,6},{16,8},{18,10},{20,12},{22,14},{24,16},... | collective-permute-start | bytes 1572872 | tf_op jit(solution)/shard_map/ppermute | solution.py:635
  282.3 118.6 %reduce-scatter.17.cloned.1.call-start = ((), (), s32[]{:S(2)}) async-start(), calls=%async_computation.25 | async-start | bytes 3604480 | tf_op jit(solution)/shard_map/reduce_scatter | solution.py:763
  286.5 13.3 %collective-permute-start.41 = (bf16[128,2048]{1,0:T(8,128)(2,1)}, bf16[128,2048]{1,0:T(8,128)(2,1)S(1)}, u32[]{:S(2)}, u32[]{:S(2)}) collective-permute-start(bf16[128,2048]{1,0:T(8,128)(2,1)} %get-tuple-element.191), channel_id=1, source_target_pairs={{0,8},{2,10},{4,12},{6,14},{8,16},{10,18},{12,20},{14,22},{16,24},... | collective-permute-start | bytes 1572872 | tf_op jit(solution)/shard_map/ppermute | solution.py:634
  289.8 13.9 %collective-permute-start.42 = (bf16[128,2048]{1,0:T(8,128)(2,1)S(1)}, bf16[128,2048]{1,0:T(8,128)(2,1)S(1)}, u32[]{:S(2)}, u32[]{:S(2)}) collective-permute-start(bf16[128,2048]{1,0:T(8,128)(2,1)S(1)} %get-tuple-element.190), channel_id=1, source_target_pairs={{8,0},{10,2},{12,4},{14,6},{16,8},{18,10},{20,12},{22,14},{24,16},... | collective-permute-start | bytes 1572872 | tf_op jit(solution)/shard_map/ppermute | solution.py:635
  317.0 22.8 %all-to-all-start.2 = ((bf16[4,128,704]{1,2,0:T(8,128)(2,1)}), bf16[4,128,704]{1,2,0:T(8,128)(2,1)S(1)}, u32[]{:S(2)}, u32[]{:S(2)}) async-start(bf16[4,128,704]{1,2,0:T(8,128)(2,1)} %copy_bitcast_fusion.3), calls=%async_computation.4 | async-start | bytes 1441792 | tf_op jit(solution)/shard_map/all_to_all | solution.py:585
  320.5 156.8 %reduce-scatter.11.cloned.1.call-start = ((), (), s32[]{:S(2)}) async-start(), calls=%async_computation.22 | async-start | bytes 4587520 | tf_op jit(solution)/shard_map/reduce_scatter | solution.py:723
  394.0 109.7 %collective-permute-start.38 = (bf16[128,2048]{1,0:T(8,128)(2,1)}, bf16[128,2048]{1,0:T(8,128)(2,1)}, u32[]{:S(2)}, u32[]{:S(2)}) collective-permute-start(bf16[128,2048]{1,0:T(8,128)(2,1)} %block_result.1), channel_id=1, source_target_pairs={{0,1},{1,0},{2,3},{3,2},{4,5},{5,4},{6,7},{7,6},{8,9},{9,8},{10,11... | collective-permute-start | bytes 1572872 | tf_op jit(solution)/shard_map/ppermute | solution.py:464
  396.1 48.7 %all-to-all-start.8 = ((bf16[4,128,704]{1,2,0:T(8,128)(2,1)}), bf16[4,128,704]{1,2,0:T(8,128)(2,1)S(1)}, u32[]{:S(2)}, u32[]{:S(2)}) async-start(bf16[4,128,704]{1,2,0:T(8,128)(2,1)} %copy_bitcast_fusion.2), calls=%async_computation.13 | async-start | bytes 1441792 | tf_op jit(solution)/shard_map/all_to_all | solution.py:585
  406.8 15.1 %collective-permute-start.47 = (bf16[128,2048]{1,0:T(8,128)(2,1)}, bf16[128,2048]{1,0:T(8,128)(2,1)S(1)}, u32[]{:S(2)}, u32[]{:S(2)}) collective-permute-start(bf16[128,2048]{1,0:T(8,128)(2,1)} %get-tuple-element.157), channel_id=1, source_target_pairs={{0,2},{2,0},{4,6},{6,4},{8,10},{10,8},{12,14},{14,12},{16,18},{18,... | collective-permute-start | bytes 1572872 | tf_op jit(solution)/shard_map/ppermute | solution.py:648
  409.4 25.3 %collective-permute-start.48 = (bf16[128,2048]{1,0:T(8,128)(2,1)}, bf16[128,2048]{1,0:T(8,128)(2,1)S(1)}, u32[]{:S(2)}, u32[]{:S(2)}) collective-permute-start(bf16[128,2048]{1,0:T(8,128)(2,1)} %get-tuple-element.157), channel_id=1, source_target_pairs={{0,4},{2,6},{4,0},{6,2},{8,12},{10,14},{12,8},{14,10},{16,20},{18,... | collective-permute-start | bytes 1572872 | tf_op jit(solution)/shard_map/ppermute | solution.py:648
  410.0 24.7 %collective-permute-start.49 = (bf16[128,2048]{1,0:T(8,128)(2,1)}, bf16[128,2048]{1,0:T(8,128)(2,1)S(1)}, u32[]{:S(2)}, u32[]{:S(2)}) collective-permute-start(bf16[128,2048]{1,0:T(8,128)(2,1)} %get-tuple-element.157), channel_id=1, source_target_pairs={{0,6},{2,4},{4,2},{6,0},{8,14},{10,12},{12,10},{14,8},{16,22},{18,... | collective-permute-start | bytes 1572872 | tf_op jit(solution)/shard_map/ppermute | solution.py:648
  434.9 18.1 %collective-permute-start.50 = (bf16[4,1,128,2048]{3,2,1,0:T(8,128)(2,1)S(1)}, bf16[4,1,128,2048]{3,2,1,0:T(8,128)(2,1)}, u32[]{:S(2)}, u32[]{:S(2)}) collective-permute-start(bf16[4,1,128,2048]{3,2,1,0:T(8,128)(2,1)S(1)} %bitcast_dynamic-update-slice_fusion.1), channel_id=1, source_target_pairs={{0,1},{1,0},{2,3},{3,2},{4,5},{5,4},{6,7},{7,6},{8,9},{9,8},{10,11... | collective-permute-start | bytes 6291464 | tf_op jit(solution)/shard_map/ppermute | solution.py:464
  437.8 40.8 %collective-permute-start.44 = (f32[128,2048]{1,0:T(8,128)}, f32[128,2048]{1,0:T(8,128)}, u32[]{:S(2)}, u32[]{:S(2)}) collective-permute-start(f32[128,2048]{1,0:T(8,128)} %convolution_add_fusion.1), channel_id=1, source_target_pairs={{0,1},{1,0},{2,3},{3,2},{4,5},{5,4},{6,7},{7,6},{8,9},{9,8},{10,11... | collective-permute-start | bytes 3145736 | tf_op jit(solution)/shard_map/ppermute | solution.py:464
  444.8 12.7 %all-to-all-start.5 = ((bf16[4,256,256]{2,1,0:T(8,128)(2,1)}), bf16[4,256,256]{2,1,0:T(8,128)(2,1)}, u32[]{:S(2)}, u32[]{:S(2)}) async-start(bf16[4,256,256]{2,1,0:T(8,128)(2,1)} %pad_maximum_fusion.1), calls=%async_computation.8 | async-start | bytes 1048576 | tf_op jit(solution)/shard_map/all_to_all | solution.py:585
  457.5 32.6 %all-to-all-start.9 = ((bf16[4,128,704]{1,2,0:T(8,128)(2,1)}), bf16[4,128,704]{1,2,0:T(8,128)(2,1)}, u32[]{:S(2)}, u32[]{:S(2)}) async-start(bf16[4,128,704]{1,2,0:T(8,128)(2,1)} %copy_bitcast_fusion.1), calls=%async_computation.15 | async-start | bytes 1441792 | tf_op jit(solution)/shard_map/all_to_all | solution.py:585
  462.3 66.8 %reduce-scatter.13.cloned.1.call-start = ((), (), s32[]{:S(2)}) async-start(), calls=%async_computation.23 | async-start | bytes 1310720 | tf_op jit(solution)/shard_map/reduce_scatter | solution.py:723
  483.4 36.8 %collective-permute-start.45 = (f32[128,2048]{1,0:T(8,128)}, f32[128,2048]{1,0:T(8,128)}, u32[]{:S(2)}, u32[]{:S(2)}) collective-permute-start(f32[128,2048]{1,0:T(8,128)} %get-tuple-element.152), channel_id=1, source_target_pairs={{0,1},{1,0},{2,3},{3,2},{4,5},{5,4},{6,7},{7,6},{8,9},{9,8},{10,11... | collective-permute-start | bytes 3145736 | tf_op jit(solution)/shard_map/ppermute | solution.py:464
  490.0 22.9 %all-to-all-start.3 = ((f32[16,2,128]{2,1,0:T(2,128)}), f32[16,2,128]{2,1,0:T(2,128)S(1)}, u32[]{:S(2)}, u32[]{:S(2)}) async-start(f32[16,2,128]{2,1,0:T(2,128)} %add_bitcast_fusion), calls=%async_computation.5 | async-start | bytes 32768 | tf_op jit(solution)/shard_map/all_to_all | solution.py:827
  512.9 16.1 %all-to-all-start.6 = ((bf16[4,128,896]{1,2,0:T(8,128)(2,1)}), bf16[4,128,896]{1,2,0:T(8,128)(2,1)S(1)}, u32[]{:S(2)}, u32[]{:S(2)}) async-start(bf16[4,128,896]{1,2,0:T(8,128)(2,1)} %copy.63), calls=%async_computation.9 | async-start | bytes 1835008 | tf_op jit(solution)/shard_map/all_to_all | solution.py:585
  529.2 9.7 %all-to-all-start.7 = ((bf16[4,128,256]{2,1,0:T(8,128)(2,1)}), bf16[4,128,256]{2,1,0:T(8,128)(2,1)}, u32[]{:S(2)}, u32[]{:S(2)}) async-start(bf16[4,128,256]{2,1,0:T(8,128)(2,1)} %bitcast.158), calls=%async_computation.11 | async-start | bytes 524288 | tf_op jit(solution)/shard_map/all_to_all | solution.py:585
  (52 other events, 398.2 us)
Sparse Core Ops, SparseCore 0:
  11.4 37.9 all-gather.4
  57.3 35.2 all-gather.6
  94.8 36.1 all-gather.8
  133.0 33.9 all-gather.10
  208.2 51.9 reduce-scatter.6
  262.4 32.4 reduce-scatter.8
  297.2 32.3 reduce-scatter.14
  331.9 51.6 reduce-scatter.16
  391.6 85.6 reduce-scatter.10
  479.4 38.9 reduce-scatter.12

commit v8 on v7

--- a/solution.py
+++ b/solution.py
@@ -755,9 +755,7 @@
         at = (place + k) % grid.outer
         out_blocks = lax.dynamic_update_slice_in_dim(out_blocks, x.astype(bf16)[None], at, 0)
     out_blocks, cot_all = tie(out_blocks.reshape(-1, out_blocks.shape[2]), cot_all)
-    out_sum = lax.psum_scatter(
-        out_blocks, "dp", scatter_dimension=0, tiled=True, axis_index_groups=grid.cols
-    )
+
 
     def scatter_rows(g):
         return lax.psum_scatter(
@@ -771,11 +769,11 @@
     gate_grad = (inner_grad * up_act * silu_slope(gate_act)).astype(bf16)
     up_grad = (inner_grad * jax.nn.silu(gate_act)).astype(bf16)
     inner_act = gated(gate_act, up_act)
-    back_parts, (down_rows, out_sum, gate_rows, up_rows) = scatter_along(
+    back_parts, (down_rows, gate_rows, up_rows) = scatter_along(
         add_other_core(*by_core(nt(gate_grad, full_gate) + nt(up_grad, full_up)), grid),
         grid,
         (
-            (tn(cot_all, inner_act).astype(bf16), out_sum),
+            (tn(cot_all, inner_act).astype(bf16),),
             (tn(tokens, gate_grad).astype(bf16),),
             (tn(tokens, up_grad).astype(bf16),),
         ),
@@ -793,8 +791,24 @@
     )
     down_sum = to_columns(down_rows)
     down_sum, shares, *pre_grads = tie(down_sum, shares, *pre_grads)
-    pre_grad = plane_product(normed_plane, plane_columns(shares))
-    _, low_half, mixed = tie(pre_grad, low_half, mixed)
+
+    def normed_part(which):
+        q, k, v, f = (half_of(g, which) for g in pre_grads)
+        return nt(q, w_query) + nt(k, w_key) + nt(v, w_value) + nt(f, w_forget)
+
+    columns_here, part_other, part_mine, out_blocks, gate_rows, up_rows = tie(
+        plane_columns(shares),
+        normed_part(1 - core),
+        normed_part(core),
+        out_blocks,
+        gate_rows,
+        up_rows,
+    )
+    out_sum = lax.psum_scatter(
+        out_blocks, "dp", scatter_dimension=0, tiled=True, axis_index_groups=grid.cols
+    )
+    pre_grad = plane_product(normed_plane, columns_here)
+    _, low_half, mixed, out_sum = tie(pre_grad, low_half, mixed, out_sum)
     mixed_plane = plane_columns(jnp.stack(jnp.split(mixed, INNER, axis=1)))
     low_plane = plane_tokens(plane_gather(low_half, grid, inner))
     sums, output_grad = tie(plane_sum(pre_grad), plane_product(low_plane, mixed_plane))
@@ -811,13 +825,8 @@
         sums[:, :, a:b].reshape(sums.shape[0], -1) for a, b in zip(ends, ends[1:])
     )
 
-    def normed_part(which):
-        q, k, v, f = (half_of(g, which) for g in pre_grads)
-        return nt(q, w_query) + nt(k, w_key) + nt(v, w_value) + nt(f, w_forget)
-
-    part_other = swap(normed_part(1 - core))
     input_grad, attn_gain_part = first_norm_back(
-        block_in, hidden_grad, attn_gain, normed_part(core), part_other, core
+        block_in, hidden_grad, attn_gain, part_mine, swap(part_other), core
     )
     input_grad = join(input_grad, swap(input_grad), core)
 

time: 558 us -> 586 us (1.050)
  waiting for transfers between devices: 154 us -> 235 us
  blocking collectives: 42.3 us -> 0 us
  starting transfers between devices: 101 us -> 90.2 us
    all_to_all x1 -> x0, blocking collectives: 42.3 us -> none  [exchange(): lax.all_to_all(x, 'dp', split, concat, tiled=True, axis_index_groups=groups)]
    all_to_all x8 -> x9, waiting for transfers between devices: 34.9 us -> 73.7 us  [exchange(): lax.all_to_all(x, 'dp', split, concat, tiled=True, axis_index_groups=groups)]
    reduce_scatter x1, waiting for transfers between devices: 0.97 us -> 38.2 us  [on_device(): lax.psum_scatter(out_blocks, 'dp', scatter_dimension=0, tiled=True, axis_...]
    reduce_scatter x3, waiting for transfers between devices: 0.02 us -> 22.5 us  [scatter_rows(): lax.psum_scatter(g, 'dp', scatter_dimension=0, tiled=True, axis_index_gro...]
    ppermute x3, waiting for transfers between devices: 23 us -> 11.8 us  [scatter_along(): up = lax.ppermute(up.astype(bf16), 'dp', grid.up)]
    reduce_scatter x2, waiting for transfers between devices: 10.3 us -> 0.02 us  [plane_sum(): lax.psum_scatter(g, 'dp', scatter_dimension=0, tiled=True, axis_index_gro...]
    all_to_all x1, starting transfers between devices: 13.7 us -> 4.44 us  [on_device(): gains = jnp.sum(lax.all_to_all(gains, 'dp', 0, 0, tiled=True), axis=0)]
    unnamed x105 -> x101, local copies, waits for them, and re-layouts: 23.5 us -> 26 us
  transfers between devices with their start and end apart: 70 -> 71, of which waited for: 37 -> 40; matrix products, arithmetic and copies ran while one was open for 35% -> 29% of each run, Pallas kernels for 6% -> 6%
where the time goes in v8:
time: 586 us; the launch traced here: 576 us
  waiting for transfers between devices  235 us (40%)
  matrix products  102 us (17%)
  starting transfers between devices  90.2 us (15%)
  local copies, waits for them, and re-layouts  65.1 us (11%)
  other arithmetic  34.2 us (6%)
  Pallas kernels  33.2 us (6%)
  between operations  15.8 us (3%)
    all_to_all x9, waiting for transfers between devices, exchange(): lax.all_to_all(x, 'dp', split, concat, tiled=True, axis_index_groups=groups)  73.7 us
    dot_general x8, matrix products, nn(): return jnp.dot(a.astype(bf16), b.astype(bf16), preferred_element_type=f32)  38.3 us
    reduce_scatter x1, waiting for transfers between devices, on_device(): lax.psum_scatter(out_blocks, 'dp', scatter_dimension=0, tiled=True, axis_...  38.2 us
    all_to_all x9, starting transfers between devices, exchange(): lax.all_to_all(x, 'dp', split, concat, tiled=True, axis_index_groups=groups)  36.5 us
    dot_general x13, matrix products, nt(): lax.dot_general(a.astype(bf16), b.astype(bf16), (((1,), (1,)), ((), ())),...  35.4 us
    ppermute x6, waiting for transfers between devices, gather_along(): above = lax.ppermute(above, 'dp', grid.down)  29.3 us
    dot_general x5, matrix products, tn(): lax.dot_general(a.astype(bf16), b.astype(bf16), (((0,), (0,)), ((), ())),...  28.7 us
    unnamed x101, local copies, waits for them, and re-layouts  26 us
  transfers between devices with their start and end apart: 71, of which 40 were waited for; matrix products, arithmetic and copies ran while one was open for 29% of the time, Pallas kernels for 6%

profile of v8, /device:TPU:0, one launch (start us, length us, event | category | flops | bytes accessed | tf_op | source)
XLA Modules:
  0.0 575.5 jit_solution(10182419615987057532)
XLA Ops:
  14.3 6.3 %all-to-all-start = ((bf16[128,4,1408]{0,2,1:T(8,128)(2,1)}), bf16[128,4,1408]{0,2,1:T(8,128)(2,1)S(1)}, u32[]{:S(2)}, u32[]{:S(2)}) async-start(bf16[128,4,1408]{0,2,1:T(8,128)(2,1)} %pad_maximum_fusion), calls=%async_computation | async-start | bytes 2883584 | tf_op jit(solution)/shard_map/all_to_all | solution.py:585
  20.6 5.0 multiply_convert_fusion.5
  31.7 6.4 %slot_forward.1 = (bf16[256,1024]{1,0:T(8,128)(2,1)}, f32[256,128]{1,0:T(8,128)}, f32[4,256,128]{2,1,0:T(8,128)}, bf16[2,256,256]{2,1,0:T(8,128)(2,1)}, bf16[2,256,16]{2,1,0:T(8,128)(2,1)}) custom-call(s32[1,3]{1,0:T(1,128)} %starts_ref.3, bf16[256,1024]{1,0:T(8,128)(2,1)} %get-tuple-element.228.q_ref, bf16[256,1024]{1,0:T(8,128)(2,1)} %get-tuple-element.230.k_ref, ...), custom_call_target="tpu_custom_call" | custom-call | flops 4000000000 | bytes 4000000 | tf_op jit(solution)/shard_map/slot_forward/pallas_call | solution.py:383
  38.1 4.8 fusion.24.mine_ref
  42.9 11.9 %all-to-all-done = bf16[128,4,1408]{0,2,1:T(8,128)(2,1)S(1)} async-done(((bf16[128,4,1408]{0,2,1:T(8,128)(2,1)}), bf16[128,4,1408]{0,2,1:T(8,128)(2,1)S(1)}, u32[]{:S(2)}, u32[]{:S(2)}) %all-to-all-start) | async-done | bytes 1441824 | tf_op jit(solution)/shard_map/all_to_all | solution.py:585
  58.1 3.7 fusion.22
  63.4 3.5 all-to-all-start.1
  69.8 3.3 second_norm.1
  73.1 4.6 collective-permute-start.1
  83.1 4.0 all-to-all-done.1
  88.0 2.6 collective-permute-done.1
  90.5 5.5 collective-permute-done.2
  96.1 3.9 collective-permute-start.3
  101.3 3.4 bitcast_dynamic-update-slice_fusion
  104.7 6.1 %collective-permute-done.3 = bf16[128,2048]{1,0:T(8,128)(2,1)S(1)} collective-permute-done((bf16[128,2048]{1,0:T(8,128)(2,1)}, bf16[128,2048]{1,0:T(8,128)(2,1)S(1)}, u32[]{:S(2)}, u32[]{:S(2)}) %collective-permute-start.3) | collective-permute-done | bytes 524320 | tf_op jit(solution)/shard_map/ppermute | solution.py:598
  110.8 4.0 collective-permute-done.4
  122.1 4.7 collective-permute-done.8
  126.8 4.1 collective-permute-done.9
  137.5 4.3 collective-permute-start.6
  148.5 5.1 fusion.45
  153.6 6.6 %collective-permute-done.7 = bf16[128,2048]{1,0:T(8,128)(2,1)} collective-permute-done((bf16[128,2048]{1,0:T(8,128)(2,1)}, bf16[128,2048]{1,0:T(8,128)(2,1)}, u32[]{:S(2)}, u32[]{:S(2)}) %collective-permute-start.7) | collective-permute-done | bytes 524320 | tf_op jit(solution)/shard_map/ppermute | solution.py:599
  163.8 7.9 %fusion.46 = f32[1024,704]{0,1:T(8,128)} fusion(bf16[1024,2048]{1,0:T(8,128)(2,1)} %select_dynamic-update-slice_fusion.6, bf16[2048,704]{1,0:T(8,128)(2,1)} %all-gather.9.cloned.1.call-done), kind=kOutput, calls=%fused_computation.130 | convolution fusion | flops 2952790016 | bytes 9961472 | tf_op jit(solution)/shard_map/dot_general | solution.py:19
  173.1 4.9 collective-permute-done.18
  181.3 2.7 multiply_convert_fusion.2
  185.1 3.5 fusion.47
  190.1 4.0 collective-permute-done.20
  202.1 2.6 collective-permute-done.27
  207.9 10.0 %multiply_convert_fusion.1 = (bf16[1024,704]{0,1:T(8,128)(2,1)}, bf16[1024,704]{0,1:T(8,128)(2,1)S(1)}) fusion(f32[1024,704]{0,1:T(8,128)} %copy-done.11, f32[1024,704]{0,1:T(8,128)} %fusion.46, bf16[1024,2048]{1,0:T(8,128)(2,1)} %copy-done.36, bf16[2048,704]{0,1:T(8,128)(2,1)} %all-gather.11.cloned.1.call-done), kind=kOutput, calls=%fused_computation.7 | convolution fusion | flops 2962161664 | bytes 15728640 | tf_op jit(solution)/shard_map/dot_general | solution.py:19
  217.9 4.0 fusion.48
  221.9 5.5 fusion.44
  233.1 2.8 collective-permute-start.36
  237.3 4.6 convolution_convert_fusion.3
  241.9 5.3 collective-permute-done.36
  247.2 4.9 collective-permute-done.37
  252.2 3.0 add_convert_fusion.2
  258.7 6.8 %convolution_convert_fusion.2 = bf16[2048,704]{0,1:T(8,128)(2,1)} fusion(bf16[1024,704]{0,1:T(8,128)(2,1)S(1)} %copy-done.9, bf16[1024,2048]{1,0:T(8,128)(2,1)} %select_dynamic-update-slice_fusion.6), kind=kOutput, calls=%fused_computation.4 | convolution fusion | flops 2954231808 | bytes 8519680 | tf_op jit(solution)/shard_map/dot_general | solution.py:29
  267.7 4.9 collective-permute-done.39
  272.7 4.1 add_convert_fusion
  279.8 4.5 convolution_convert_fusion.1
  284.4 4.2 collective-permute-done.40.refs_1_
  288.5 3.8 collective-permute-done.41.refs_2_
  293.2 3.9 second_norm_back.1
  299.3 4.3 convolution_convert_fusion.5.do_ref
  305.7 3.5 all-to-all-start.2
  309.2 11.3 %slot_backward.1 = (bf16[256,1024]{1,0:T(8,128)(2,1)}, bf16[256,1024]{1,0:T(8,128)(2,1)}, bf16[256,1024]{1,0:T(8,128)(2,1)}, bf16[256,128]{1,0:T(8,128)(2,1)}, bf16[4,256,896]{2,1,0:T(8,128)(2,1)}) custom-call(s32[1,3]{1,0:T(1,128)} %starts_ref.3, bf16[256,1024]{1,0:T(8,128)(2,1)} %get-tuple-element.228.q_ref, bf16[256,1024]{1,0:T(8,128)(2,1)} %get-tuple-element.230.k_ref, ...), custom_call_target="tpu_custom_call" | custom-call | flops 12000000000 | bytes 8000000 | tf_op jit(solution)/shard_map/slot_backward/pallas_call | solution.py:403
  320.6 7.8 %all-to-all-done.2 = bf16[4,128,704]{1,2,0:T(8,128)(2,1)S(1)} async-done(((bf16[4,128,704]{1,2,0:T(8,128)(2,1)}), bf16[4,128,704]{1,2,0:T(8,128)(2,1)S(1)}, u32[]{:S(2)}, u32[]{:S(2)}) %all-to-all-start.2) | async-done | bytes 720928 | tf_op jit(solution)/shard_map/all_to_all | solution.py:585
  329.6 3.6 all-to-all-start.3
  333.5 3.9 fusion.16
  349.1 22.5 %reduce-scatter.11.cloned.1.call-done = bf16[512,704]{0,1:T(8,128)(2,1)} async-done(((bf16[2048,704]{0,1:T(8,128)(2,1)}), bf16[512,704]{0,1:T(8,128)(2,1)}) %reduce-scatter.11.cloned.1.call-update) | async-done | bytes 720912 | tf_op jit(solution)/shard_map/reduce_scatter | solution.py:761
  371.7 8.2 %convolution_convert_fusion = bf16[2048,896]{1,0:T(8,128)(2,1)} fusion(bf16[1024,2048]{1,0:T(8,128)(2,1)} %bitcast.11, bf16[1024,896]{1,0:T(8,128)(2,1)S(1)} %bitcast.155), kind=kOutput, calls=%fused_computation.2 | convolution fusion | flops 3759931392 | bytes 9699328 | tf_op jit(solution)/shard_map/dot_general | solution.py:29
  379.9 38.2 %reduce-scatter.13.cloned.1.call-done.refs_0_ = bf16[128,2048]{1,0:T(8,128)(2,1)} async-done(((bf16[512,2048]{1,0:T(8,128)(2,1)}), bf16[128,2048]{1,0:T(8,128)(2,1)}) %reduce-scatter.13.cloned.1.call-update) | async-done | bytes 524304 | tf_op jit(solution)/shard_map/reduce_scatter | solution.py:807
  422.0 11.1 %collective-permute-done.47 = bf16[128,2048]{1,0:T(8,128)(2,1)} collective-permute-done((bf16[128,2048]{1,0:T(8,128)(2,1)S(1)}, bf16[128,2048]{1,0:T(8,128)(2,1)}, u32[]{:S(2)}, u32[]{:S(2)}) %collective-permute-start.47) | collective-permute-done | bytes 524320 | tf_op jit(solution)/shard_map/ppermute | solution.py:648
  434.1 9.7 %collective-permute-done.48 = bf16[128,2048]{1,0:T(8,128)(2,1)S(1)} collective-permute-done((bf16[128,2048]{1,0:T(8,128)(2,1)S(1)}, bf16[128,2048]{1,0:T(8,128)(2,1)S(1)}, u32[]{:S(2)}, u32[]{:S(2)}) %collective-permute-start.48) | collective-permute-done | bytes 524320 | tf_op jit(solution)/shard_map/ppermute | solution.py:648
  445.1 3.5 all-to-all-start.8
  451.1 37.4 %all-to-all-done.8 = bf16[4,128,704]{1,2,0:T(8,128)(2,1)S(1)} async-done(((bf16[4,128,704]{1,2,0:T(8,128)(2,1)}), bf16[4,128,704]{1,2,0:T(8,128)(2,1)S(1)}, u32[]{:S(2)}, u32[]{:S(2)}) %all-to-all-start.8) | async-done | bytes 720928 | tf_op jit(solution)/shard_map/all_to_all | solution.py:585
  488.5 4.1 all-to-all-start.5
  500.8 4.2 all-to-all-start.9
  505.3 3.2 constant_dynamic-update-slice_fusion.4
  508.5 4.6 convolution_convert_fusion.4
  513.2 4.0 first_norm_back.1
  523.6 4.4 all-to-all-start.4
  539.9 3.7 all-to-all-start.6
  548.1 8.4 %all-to-all-done.6 = bf16[4,128,896]{1,2,0:T(8,128)(2,1)S(1)} async-done(((bf16[4,128,896]{1,2,0:T(8,128)(2,1)}), bf16[4,128,896]{1,2,0:T(8,128)(2,1)S(1)}, u32[]{:S(2)}, u32[]{:S(2)}) %all-to-all-start.6) | async-done | bytes 917536 | tf_op jit(solution)/shard_map/all_to_all | solution.py:585
  556.7 4.1 all-to-all-start.7
  (294 shorter events, 152.1 us)
Async XLA Ops:
  7.2 50.0 %all-gather.5.cloned.1.call-start = ((), (), s32[]{:S(2)}) async-start(), calls=%async_computation.16 | async-start | bytes 2621440 | tf_op jit(solution)/shard_map/all_gather | solution.py:697
  14.3 40.5 %all-to-all-start = ((bf16[128,4,1408]{0,2,1:T(8,128)(2,1)}), bf16[128,4,1408]{0,2,1:T(8,128)(2,1)S(1)}, u32[]{:S(2)}, u32[]{:S(2)}) async-start(bf16[128,4,1408]{0,2,1:T(8,128)(2,1)} %pad_maximum_fusion), calls=%async_computation | async-start | bytes 2883584 | tf_op jit(solution)/shard_map/all_to_all | solution.py:585
  20.6 110.3 %all-gather.7.cloned.1.call-start = ((), (), s32[]{:S(2)}) async-start(), calls=%async_computation.17 | async-start | bytes 3932160 | tf_op jit(solution)/shard_map/all_gather | solution.py:677
  57.2 103.0 %all-gather.9.cloned.1.call-start = ((), (), s32[]{:S(2)}) async-start(), calls=%async_computation.18 | async-start | bytes 3932160 | tf_op jit(solution)/shard_map/all_gather | solution.py:677
  58.0 43.3 %collective-permute-start.5 = (bf16[4,1,128,2048]{3,2,0,1:T(8,128)(2,1)}, bf16[4,1,128,2048]{3,2,0,1:T(8,128)(2,1)}, u32[]{:S(2)}, u32[]{:S(2)}) collective-permute-start(bf16[4,1,128,2048]{3,2,0,1:T(8,128)(2,1)} %bitcast.150), channel_id=1, source_target_pairs={{0,1},{1,0},{2,3},{3,2},{4,5},{5,4},{6,7},{7,6},{8,9},{9,8},{10,11... | collective-permute-start | bytes 6291464 | tf_op jit(solution)/shard_map/ppermute | solution.py:464
  61.8 7.1 %collective-permute-start = (f32[128,2048]{1,0:T(8,128)S(1)}, f32[128,2048]{1,0:T(8,128)S(1)}, u32[]{:S(2)}, u32[]{:S(2)}) collective-permute-start(f32[128,2048]{1,0:T(8,128)S(1)} %fusion.22), channel_id=1, source_target_pairs={{0,1},{1,0},{2,3},{3,2},{4,5},{5,4},{6,7},{7,6},{8,9},{9,8},{10,11... | collective-permute-start | bytes 3145736 | tf_op jit(solution)/shard_map/ppermute | solution.py:464
  63.4 23.6 %all-to-all-start.1 = ((bf16[128,4,704]{0,2,1:T(8,128)(2,1)}), bf16[128,4,704]{0,2,1:T(8,128)(2,1)S(1)}, u32[]{:S(2)}, u32[]{:S(2)}) async-start(bf16[128,4,704]{0,2,1:T(8,128)(2,1)} %bitcast.6), calls=%async_computation.1 | async-start | bytes 1441792 | tf_op jit(solution)/shard_map/all_to_all | solution.py:585
  66.9 111.1 %all-gather.11.cloned.1.call-start = ((), (), s32[]{:S(2)}) async-start(), calls=%async_computation.19 | async-start | bytes 3604480 | tf_op jit(solution)/shard_map/all_gather | solution.py:677
  73.1 17.4 %collective-permute-start.1 = (bf16[128,2048]{1,0:T(8,128)(2,1)}, bf16[128,2048]{1,0:T(8,128)(2,1)}, u32[]{:S(2)}, u32[]{:S(2)}) collective-permute-start(bf16[128,2048]{1,0:T(8,128)(2,1)} %get-tuple-element.97), channel_id=1, source_target_pairs={{0,8},{2,10},{4,12},{6,14},{8,16},{10,18},{12,20},{14,22},{16,24},... | collective-permute-start | bytes 1572872 | tf_op jit(solution)/shard_map/ppermute | solution.py:598
  77.7 18.3 %collective-permute-start.2 = (bf16[128,2048]{1,0:T(8,128)(2,1)}, bf16[128,2048]{1,0:T(8,128)(2,1)}, u32[]{:S(2)}, u32[]{:S(2)}) collective-permute-start(bf16[128,2048]{1,0:T(8,128)(2,1)} %get-tuple-element.97), channel_id=1, source_target_pairs={{8,0},{10,2},{12,4},{14,6},{16,8},{18,10},{20,12},{22,14},{24,16},... | collective-permute-start | bytes 1572872 | tf_op jit(solution)/shard_map/ppermute | solution.py:599
  96.1 14.8 %collective-permute-start.3 = (bf16[128,2048]{1,0:T(8,128)(2,1)}, bf16[128,2048]{1,0:T(8,128)(2,1)S(1)}, u32[]{:S(2)}, u32[]{:S(2)}) collective-permute-start(bf16[128,2048]{1,0:T(8,128)(2,1)} %collective-permute-done.1), channel_id=1, source_target_pairs={{0,8},{2,10},{4,12},{6,14},{8,16},{10,18},{12,20},{14,22},{16,24},... | collective-permute-start | bytes 1572872 | tf_op jit(solution)/shard_map/ppermute | solution.py:598
  100.0 14.9 %collective-permute-start.4 = (bf16[128,2048]{1,0:T(8,128)(2,1)}, bf16[128,2048]{1,0:T(8,128)(2,1)S(1)}, u32[]{:S(2)}, u32[]{:S(2)}) collective-permute-start(bf16[128,2048]{1,0:T(8,128)(2,1)} %collective-permute-done.2), channel_id=1, source_target_pairs={{8,0},{10,2},{12,4},{14,6},{16,8},{18,10},{20,12},{22,14},{24,16},... | collective-permute-start | bytes 1572872 | tf_op jit(solution)/shard_map/ppermute | solution.py:599
  114.9 11.9 %collective-permute-start.8 = (bf16[128,2048]{1,0:T(8,128)(2,1)S(1)}, bf16[128,2048]{1,0:T(8,128)(2,1)S(1)}, u32[]{:S(2)}, u32[]{:S(2)}) collective-permute-start(bf16[128,2048]{1,0:T(8,128)(2,1)S(1)} %collective-permute-done.3), channel_id=1, source_target_pairs={{0,8},{2,10},{4,12},{6,14},{8,16},{10,18},{12,20},{14,22},{16,24},... | collective-permute-start | bytes 1572872 | tf_op jit(solution)/shard_map/ppermute | solution.py:598
  117.3 13.6 %collective-permute-start.9 = (bf16[128,2048]{1,0:T(8,128)(2,1)S(1)}, bf16[128,2048]{1,0:T(8,128)(2,1)S(1)}, u32[]{:S(2)}, u32[]{:S(2)}) collective-permute-start(bf16[128,2048]{1,0:T(8,128)(2,1)S(1)} %collective-permute-done.4), channel_id=1, source_target_pairs={{8,0},{10,2},{12,4},{14,6},{16,8},{18,10},{20,12},{22,14},{24,16},... | collective-permute-start | bytes 1572872 | tf_op jit(solution)/shard_map/ppermute | solution.py:599
  118.7 16.1 %collective-permute-start.10 = (bf16[128,2048]{1,0:T(8,128)(2,1)S(1)}, bf16[128,2048]{1,0:T(8,128)(2,1)}, u32[]{:S(2)}, u32[]{:S(2)}) collective-permute-start(bf16[128,2048]{1,0:T(8,128)(2,1)S(1)} %copy-done.29), channel_id=1, source_target_pairs={{0,1},{1,0},{2,3},{3,2},{4,5},{5,4},{6,7},{7,6},{8,9},{9,8},{10,11... | collective-permute-start | bytes 1572872 | tf_op jit(solution)/shard_map/ppermute | solution.py:464
  119.6 17.8 %collective-permute-start.11 = (bf16[128,2048]{1,0:T(8,128)(2,1)}, bf16[128,2048]{1,0:T(8,128)(2,1)}, u32[]{:S(2)}, u32[]{:S(2)}) collective-permute-start(bf16[128,2048]{1,0:T(8,128)(2,1)} %collective-permute-done.2), channel_id=1, source_target_pairs={{0,1},{1,0},{2,3},{3,2},{4,5},{5,4},{6,7},{7,6},{8,9},{9,8},{10,11... | collective-permute-start | bytes 1572872 | tf_op jit(solution)/shard_map/ppermute | solution.py:464
  120.1 27.5 %collective-permute-start.16 = (bf16[128,2048]{1,0:T(8,128)(2,1)}, bf16[128,2048]{1,0:T(8,128)(2,1)}, u32[]{:S(2)}, u32[]{:S(2)}) collective-permute-start(bf16[128,2048]{1,0:T(8,128)(2,1)} %collective-permute-done.1), channel_id=1, source_target_pairs={{0,1},{1,0},{2,3},{3,2},{4,5},{5,4},{6,7},{7,6},{8,9},{9,8},{10,11... | collective-permute-start | bytes 1572872 | tf_op jit(solution)/shard_map/ppermute | solution.py:464
  120.2 183.4 %reduce-scatter.7.cloned.1.call-start = ((), (), s32[]{:S(2)}) async-start(), calls=%async_computation.20 | async-start | bytes 3604480 | tf_op jit(solution)/shard_map/reduce_scatter | solution.py:761
  126.8 16.9 %collective-permute-start.13 = (bf16[128,2048]{1,0:T(8,128)(2,1)S(1)}, bf16[128,2048]{1,0:T(8,128)(2,1)}, u32[]{:S(2)}, u32[]{:S(2)}) collective-permute-start(bf16[128,2048]{1,0:T(8,128)(2,1)S(1)} %collective-permute-done.4), channel_id=1, source_target_pairs={{0,1},{1,0},{2,3},{3,2},{4,5},{5,4},{6,7},{7,6},{8,9},{9,8},{10,11... | collective-permute-start | bytes 1572872 | tf_op jit(solution)/shard_map/ppermute | solution.py:464
  130.9 10.8 %collective-permute-start.12 = (bf16[128,2048]{1,0:T(8,128)(2,1)S(1)}, bf16[128,2048]{1,0:T(8,128)(2,1)S(1)}, u32[]{:S(2)}, u32[]{:S(2)}) collective-permute-start(bf16[128,2048]{1,0:T(8,128)(2,1)S(1)} %collective-permute-done.8), channel_id=1, source_target_pairs={{0,1},{1,0},{2,3},{3,2},{4,5},{5,4},{6,7},{7,6},{8,9},{9,8},{10,11... | collective-permute-start | bytes 1572872 | tf_op jit(solution)/shard_map/ppermute | solution.py:464
  134.8 10.2 %collective-permute-start.14 = (bf16[128,2048]{1,0:T(8,128)(2,1)S(1)}, bf16[128,2048]{1,0:T(8,128)(2,1)S(1)}, u32[]{:S(2)}, u32[]{:S(2)}) collective-permute-start(bf16[128,2048]{1,0:T(8,128)(2,1)S(1)} %collective-permute-done.3), channel_id=1, source_target_pairs={{0,1},{1,0},{2,3},{3,2},{4,5},{5,4},{6,7},{7,6},{8,9},{9,8},{10,11... | collective-permute-start | bytes 1572872 | tf_op jit(solution)/shard_map/ppermute | solution.py:464
  137.5 16.1 %collective-permute-start.6 = (bf16[128,2048]{1,0:T(8,128)(2,1)}, bf16[128,2048]{1,0:T(8,128)(2,1)}, u32[]{:S(2)}, u32[]{:S(2)}) collective-permute-start(bf16[128,2048]{1,0:T(8,128)(2,1)} %cotangent_rows.1), channel_id=1, source_target_pairs={{0,8},{2,10},{4,12},{6,14},{8,16},{10,18},{12,20},{14,22},{16,24},... | collective-permute-start | bytes 1572872 | tf_op jit(solution)/shard_map/ppermute | solution.py:598
  141.8 5.8 %collective-permute-start.15 = (bf16[128,2048]{1,0:T(8,128)(2,1)S(1)}, bf16[128,2048]{1,0:T(8,128)(2,1)S(1)}, u32[]{:S(2)}, u32[]{:S(2)}) collective-permute-start(bf16[128,2048]{1,0:T(8,128)(2,1)S(1)} %collective-permute-done.9), channel_id=1, source_target_pairs={{0,1},{1,0},{2,3},{3,2},{4,5},{5,4},{6,7},{7,6},{8,9},{9,8},{10,11... | collective-permute-start | bytes 1572872 | tf_op jit(solution)/shard_map/ppermute | solution.py:464
  143.7 16.5 %collective-permute-start.7 = (bf16[128,2048]{1,0:T(8,128)(2,1)}, bf16[128,2048]{1,0:T(8,128)(2,1)}, u32[]{:S(2)}, u32[]{:S(2)}) collective-permute-start(bf16[128,2048]{1,0:T(8,128)(2,1)} %cotangent_rows.1), channel_id=1, source_target_pairs={{8,0},{10,2},{12,4},{14,6},{16,8},{18,10},{20,12},{22,14},{24,16},... | collective-permute-start | bytes 1572872 | tf_op jit(solution)/shard_map/ppermute | solution.py:599
  145.0 53.0 %collective-permute-start.25 = (bf16[128,2048]{1,0:T(8,128)(2,1)}, bf16[128,2048]{1,0:T(8,128)(2,1)}, u32[]{:S(2)}, u32[]{:S(2)}) collective-permute-start(bf16[128,2048]{1,0:T(8,128)(2,1)} %cotangent_rows.1), channel_id=1, source_target_pairs={{0,1},{1,0},{2,3},{3,2},{4,5},{5,4},{6,7},{7,6},{8,9},{9,8},{10,11... | collective-permute-start | bytes 1572872 | tf_op jit(solution)/shard_map/ppermute | solution.py:464
  160.3 12.9 %collective-permute-start.17 = (bf16[128,2048]{1,0:T(8,128)(2,1)}, bf16[128,2048]{1,0:T(8,128)(2,1)}, u32[]{:S(2)}, u32[]{:S(2)}) collective-permute-start(bf16[128,2048]{1,0:T(8,128)(2,1)} %collective-permute-done.6), channel_id=1, source_target_pairs={{0,8},{2,10},{4,12},{6,14},{8,16},{10,18},{12,20},{14,22},{16,24},... | collective-permute-start | bytes 1572872 | tf_op jit(solution)/shard_map/ppermute | solution.py:598
  162.6 15.5 %collective-permute-start.18 = (bf16[128,2048]{1,0:T(8,128)(2,1)}, bf16[128,2048]{1,0:T(8,128)(2,1)}, u32[]{:S(2)}, u32[]{:S(2)}) collective-permute-start(bf16[128,2048]{1,0:T(8,128)(2,1)} %collective-permute-done.7), channel_id=1, source_target_pairs={{8,0},{10,2},{12,4},{14,6},{16,8},{18,10},{20,12},{22,14},{24,16},... | collective-permute-start | bytes 1572872 | tf_op jit(solution)/shard_map/ppermute | solution.py:599
  178.0 12.1 %collective-permute-start.19 = (bf16[128,2048]{1,0:T(8,128)(2,1)}, bf16[128,2048]{1,0:T(8,128)(2,1)S(1)}, u32[]{:S(2)}, u32[]{:S(2)}) collective-permute-start(bf16[128,2048]{1,0:T(8,128)(2,1)} %collective-permute-done.17), channel_id=1, source_target_pairs={{0,8},{2,10},{4,12},{6,14},{8,16},{10,18},{12,20},{14,22},{16,24},... | collective-permute-start | bytes 1572872 | tf_op jit(solution)/shard_map/ppermute | solution.py:598
  179.8 14.4 %collective-permute-start.20 = (bf16[128,2048]{1,0:T(8,128)(2,1)}, bf16[128,2048]{1,0:T(8,128)(2,1)S(1)}, u32[]{:S(2)}, u32[]{:S(2)}) collective-permute-start(bf16[128,2048]{1,0:T(8,128)(2,1)} %collective-permute-done.18), channel_id=1, source_target_pairs={{8,0},{10,2},{12,4},{14,6},{16,8},{18,10},{20,12},{22,14},{24,16},... | collective-permute-start | bytes 1572872 | tf_op jit(solution)/shard_map/ppermute | solution.py:599
  197.4 2.9 collective-permute-start.23
  197.4 3.6 collective-permute-start.24
  198.0 3.7 collective-permute-start.26
  199.2 6.1 %collective-permute-start.31 = (bf16[128,2048]{1,0:T(8,128)(2,1)}, bf16[128,2048]{1,0:T(8,128)(2,1)S(1)}, u32[]{:S(2)}, u32[]{:S(2)}) collective-permute-start(bf16[128,2048]{1,0:T(8,128)(2,1)} %collective-permute-done.6), channel_id=1, source_target_pairs={{0,1},{1,0},{2,3},{3,2},{4,5},{5,4},{6,7},{7,6},{8,9},{9,8},{10,11... | collective-permute-start | bytes 1572872 | tf_op jit(solution)/shard_map/ppermute | solution.py:464
  199.7 5.3 collective-permute-start.28
  200.3 4.8 collective-permute-start.29
  201.0 3.7 collective-permute-start.27
  201.8 3.7 collective-permute-start.30
  228.3 3.5 collective-permute-start.35
  233.1 14.1 %collective-permute-start.36 = (bf16[128,2048]{1,0:T(8,128)(2,1)}, bf16[128,2048]{1,0:T(8,128)(2,1)}, u32[]{:S(2)}, u32[]{:S(2)}) collective-permute-start(bf16[128,2048]{1,0:T(8,128)(2,1)} %get-tuple-element.206), channel_id=1, source_target_pairs={{0,8},{2,10},{4,12},{6,14},{8,16},{10,18},{12,20},{14,22},{16,24},... | collective-permute-start | bytes 1572872 | tf_op jit(solution)/shard_map/ppermute | solution.py:634
  236.0 16.1 %collective-permute-start.37 = (bf16[128,2048]{1,0:T(8,128)(2,1)}, bf16[128,2048]{1,0:T(8,128)(2,1)}, u32[]{:S(2)}, u32[]{:S(2)}) collective-permute-start(bf16[128,2048]{1,0:T(8,128)(2,1)} %get-tuple-element.205), channel_id=1, source_target_pairs={{8,0},{10,2},{12,4},{14,6},{16,8},{18,10},{20,12},{22,14},{24,16},... | collective-permute-start | bytes 1572872 | tf_op jit(solution)/shard_map/ppermute | solution.py:635
  252.1 97.0 %reduce-scatter.9.cloned.1.call-start = ((), (), s32[]{:S(2)}) async-start(), calls=%async_computation.21 | async-start | bytes 3604480 | tf_op jit(solution)/shard_map/reduce_scatter | solution.py:761
  255.2 12.6 %collective-permute-start.38 = (bf16[128,2048]{1,0:T(8,128)(2,1)}, bf16[128,2048]{1,0:T(8,128)(2,1)}, u32[]{:S(2)}, u32[]{:S(2)}) collective-permute-start(bf16[128,2048]{1,0:T(8,128)(2,1)} %get-tuple-element.201), channel_id=1, source_target_pairs={{0,8},{2,10},{4,12},{6,14},{8,16},{10,18},{12,20},{14,22},{16,24},... | collective-permute-start | bytes 1572872 | tf_op jit(solution)/shard_map/ppermute | solution.py:634
  257.4 15.2 %collective-permute-start.39 = (bf16[128,2048]{1,0:T(8,128)(2,1)}, bf16[128,2048]{1,0:T(8,128)(2,1)}, u32[]{:S(2)}, u32[]{:S(2)}) collective-permute-start(bf16[128,2048]{1,0:T(8,128)(2,1)} %get-tuple-element.200), channel_id=1, source_target_pairs={{8,0},{10,2},{12,4},{14,6},{16,8},{18,10},{20,12},{22,14},{24,16},... | collective-permute-start | bytes 1572872 | tf_op jit(solution)/shard_map/ppermute | solution.py:635
  272.7 99.0 %reduce-scatter.11.cloned.1.call-start = ((), (), s32[]{:S(2)}) async-start(), calls=%async_computation.22 | async-start | bytes 3604480 | tf_op jit(solution)/shard_map/reduce_scatter | solution.py:761
  276.9 11.7 %collective-permute-start.40 = (bf16[128,2048]{1,0:T(8,128)(2,1)}, bf16[128,2048]{1,0:T(8,128)(2,1)S(1)}, u32[]{:S(2)}, u32[]{:S(2)}) collective-permute-start(bf16[128,2048]{1,0:T(8,128)(2,1)} %get-tuple-element.203), channel_id=1, source_target_pairs={{0,8},{2,10},{4,12},{6,14},{8,16},{10,18},{12,20},{14,22},{16,24},... | collective-permute-start | bytes 1572872 | tf_op jit(solution)/shard_map/ppermute | solution.py:634
  278.3 14.0 %collective-permute-start.41 = (bf16[128,2048]{1,0:T(8,128)(2,1)S(1)}, bf16[128,2048]{1,0:T(8,128)(2,1)S(1)}, u32[]{:S(2)}, u32[]{:S(2)}) collective-permute-start(bf16[128,2048]{1,0:T(8,128)(2,1)S(1)} %get-tuple-element.202), channel_id=1, source_target_pairs={{8,0},{10,2},{12,4},{14,6},{16,8},{18,10},{20,12},{22,14},{24,16},... | collective-permute-start | bytes 1572872 | tf_op jit(solution)/shard_map/ppermute | solution.py:635
  305.7 22.7 %all-to-all-start.2 = ((bf16[4,128,704]{1,2,0:T(8,128)(2,1)}), bf16[4,128,704]{1,2,0:T(8,128)(2,1)S(1)}, u32[]{:S(2)}, u32[]{:S(2)}) async-start(bf16[4,128,704]{1,2,0:T(8,128)(2,1)} %copy_bitcast_fusion.3), calls=%async_computation.3 | async-start | bytes 1441792 | tf_op jit(solution)/shard_map/all_to_all | solution.py:585
  329.6 42.0 %all-to-all-start.3 = ((bf16[4,256,896]{2,1,0:T(8,128)(2,1)}), bf16[4,256,896]{2,1,0:T(8,128)(2,1)S(1)}, u32[]{:S(2)}, u32[]{:S(2)}) async-start(bf16[4,256,896]{2,1,0:T(8,128)(2,1)} %get-tuple-element.152), calls=%async_computation.4 | async-start | bytes 3670016 | tf_op jit(solution)/shard_map/all_to_all | solution.py:585
  333.2 85.0 %reduce-scatter.13.cloned.1.call-start = ((), (), s32[]{:S(2)}) async-start(), calls=%async_computation.23 | async-start | bytes 2621440 | tf_op jit(solution)/shard_map/reduce_scatter | solution.py:807
  371.7 141.5 %reduce-scatter.15.cloned.1.call-start = ((), (), s32[]{:S(2)}) async-start(), calls=%async_computation.24 | async-start | bytes 4587520 | tf_op jit(solution)/shard_map/reduce_scatter | solution.py:723
  418.2 14.9 %collective-permute-start.47 = (bf16[128,2048]{1,0:T(8,128)(2,1)S(1)}, bf16[128,2048]{1,0:T(8,128)(2,1)}, u32[]{:S(2)}, u32[]{:S(2)}) collective-permute-start(bf16[128,2048]{1,0:T(8,128)(2,1)S(1)} %copy-done.15), channel_id=1, source_target_pairs={{0,2},{2,0},{4,6},{6,4},{8,10},{10,8},{12,14},{14,12},{16,18},{18,... | collective-permute-start | bytes 1572872 | tf_op jit(solution)/shard_map/ppermute | solution.py:648
  419.6 24.2 %collective-permute-start.48 = (bf16[128,2048]{1,0:T(8,128)(2,1)S(1)}, bf16[128,2048]{1,0:T(8,128)(2,1)S(1)}, u32[]{:S(2)}, u32[]{:S(2)}) collective-permute-start(bf16[128,2048]{1,0:T(8,128)(2,1)S(1)} %copy-done.15), channel_id=1, source_target_pairs={{0,4},{2,6},{4,0},{6,2},{8,12},{10,14},{12,8},{14,10},{16,20},{18,... | collective-permute-start | bytes 1572872 | tf_op jit(solution)/shard_map/ppermute | solution.py:648
  421.1 22.8 %collective-permute-start.49 = (bf16[128,2048]{1,0:T(8,128)(2,1)S(1)}, bf16[128,2048]{1,0:T(8,128)(2,1)S(1)}, u32[]{:S(2)}, u32[]{:S(2)}) collective-permute-start(bf16[128,2048]{1,0:T(8,128)(2,1)S(1)} %copy-done.15), channel_id=1, source_target_pairs={{0,6},{2,4},{4,2},{6,0},{8,14},{10,12},{12,10},{14,8},{16,22},{18,... | collective-permute-start | bytes 1572872 | tf_op jit(solution)/shard_map/ppermute | solution.py:648
  444.0 61.3 %collective-permute-start.50 = (bf16[4,1,128,2048]{3,2,1,0:T(8,128)(2,1)S(1)}, bf16[4,1,128,2048]{3,2,1,0:T(8,128)(2,1)}, u32[]{:S(2)}, u32[]{:S(2)}) collective-permute-start(bf16[4,1,128,2048]{3,2,1,0:T(8,128)(2,1)S(1)} %bitcast_dynamic-update-slice_fusion.1), channel_id=1, source_target_pairs={{0,1},{1,0},{2,3},{3,2},{4,5},{5,4},{6,7},{7,6},{8,9},{9,8},{10,11... | collective-permute-start | bytes 6291464 | tf_op jit(solution)/shard_map/ppermute | solution.py:464
  445.1 43.5 %all-to-all-start.8 = ((bf16[4,128,704]{1,2,0:T(8,128)(2,1)}), bf16[4,128,704]{1,2,0:T(8,128)(2,1)S(1)}, u32[]{:S(2)}, u32[]{:S(2)}) async-start(bf16[4,128,704]{1,2,0:T(8,128)(2,1)} %copy_bitcast_fusion.2), calls=%async_computation.14 | async-start | bytes 1441792 | tf_op jit(solution)/shard_map/all_to_all | solution.py:585
  448.6 64.6 %collective-permute-start.44 = (f32[128,2048]{1,0:T(8,128)}, f32[128,2048]{1,0:T(8,128)}, u32[]{:S(2)}, u32[]{:S(2)}) collective-permute-start(f32[128,2048]{1,0:T(8,128)} %convolution_add_fusion.4), channel_id=1, source_target_pairs={{0,1},{1,0},{2,3},{3,2},{4,5},{5,4},{6,7},{7,6},{8,9},{9,8},{10,11... | collective-permute-start | bytes 3145736 | tf_op jit(solution)/shard_map/ppermute | solution.py:464
  488.5 12.3 %all-to-all-start.5 = ((bf16[4,256,256]{2,1,0:T(8,128)(2,1)}), bf16[4,256,256]{2,1,0:T(8,128)(2,1)}, u32[]{:S(2)}, u32[]{:S(2)}) async-start(bf16[4,256,256]{2,1,0:T(8,128)(2,1)} %pad_maximum_fusion.1), calls=%async_computation.10 | async-start | bytes 1048576 | tf_op jit(solution)/shard_map/all_to_all | solution.py:585
  500.8 22.7 %all-to-all-start.9 = ((bf16[4,128,704]{1,2,0:T(8,128)(2,1)}), bf16[4,128,704]{1,2,0:T(8,128)(2,1)}, u32[]{:S(2)}, u32[]{:S(2)}) async-start(bf16[4,128,704]{1,2,0:T(8,128)(2,1)} %copy_bitcast_fusion.1), calls=%async_computation.15 | async-start | bytes 1441792 | tf_op jit(solution)/shard_map/all_to_all | solution.py:585
  505.0 51.7 %reduce-scatter.17.cloned.1.call-start = ((), (), s32[]{:S(2)}) async-start(), calls=%async_computation.25 | async-start | bytes 1310720 | tf_op jit(solution)/shard_map/reduce_scatter | solution.py:723
  517.2 26.4 %collective-permute-start.45 = (f32[128,2048]{1,0:T(8,128)}, f32[128,2048]{1,0:T(8,128)}, u32[]{:S(2)}, u32[]{:S(2)}) collective-permute-start(f32[128,2048]{1,0:T(8,128)} %get-tuple-element.166), channel_id=1, source_target_pairs={{0,1},{1,0},{2,3},{3,2},{4,5},{5,4},{6,7},{7,6},{8,9},{9,8},{10,11... | collective-permute-start | bytes 3145736 | tf_op jit(solution)/shard_map/ppermute | solution.py:464
  523.6 12.0 %all-to-all-start.4 = ((f32[16,2,128]{2,1,0:T(2,128)}), f32[16,2,128]{2,1,0:T(2,128)S(1)}, u32[]{:S(2)}, u32[]{:S(2)}) async-start(f32[16,2,128]{2,1,0:T(2,128)} %add_bitcast_fusion), calls=%async_computation.8 | async-start | bytes 32768 | tf_op jit(solution)/shard_map/all_to_all | solution.py:836
  538.0 8.0 %collective-permute-start.43 = (bf16[128,2048]{1,0:T(8,128)(2,1)}, bf16[128,2048]{1,0:T(8,128)(2,1)}, u32[]{:S(2)}, u32[]{:S(2)}) collective-permute-start(bf16[128,2048]{1,0:T(8,128)(2,1)} %block_result.1), channel_id=1, source_target_pairs={{0,1},{1,0},{2,3},{3,2},{4,5},{5,4},{6,7},{7,6},{8,9},{9,8},{10,11... | collective-permute-start | bytes 1572872 | tf_op jit(solution)/shard_map/ppermute | solution.py:464
  539.9 16.7 %all-to-all-start.6 = ((bf16[4,128,896]{1,2,0:T(8,128)(2,1)}), bf16[4,128,896]{1,2,0:T(8,128)(2,1)S(1)}, u32[]{:S(2)}, u32[]{:S(2)}) async-start(bf16[4,128,896]{1,2,0:T(8,128)(2,1)} %copy.63), calls=%async_computation.11 | async-start | bytes 1835008 | tf_op jit(solution)/shard_map/all_to_all | solution.py:585
  556.7 9.7 %all-to-all-start.7 = ((bf16[4,128,256]{2,1,0:T(8,128)(2,1)}), bf16[4,128,256]{2,1,0:T(8,128)(2,1)}, u32[]{:S(2)}, u32[]{:S(2)}) async-start(bf16[4,128,256]{2,1,0:T(8,128)(2,1)} %bitcast.158), calls=%async_computation.13 | async-start | bytes 524288 | tf_op jit(solution)/shard_map/all_to_all | solution.py:585
  (51 other events, 367.5 us)
Sparse Core Ops, SparseCore 0:
  11.4 37.8 all-gather.4
  57.3 35.2 all-gather.6
  94.8 36.1 all-gather.8
  133.0 33.9 all-gather.10
  252.2 30.4 reduce-scatter.6
  284.9 32.3 reduce-scatter.8
  319.6 51.9 reduce-scatter.10
  374.5 43.6 reduce-scatter.12
  420.5 79.1 reduce-scatter.14
  513.3 27.9 reduce-scatter.16

commit v9 on v8

--- a/solution.py
+++ b/solution.py
@@ -755,7 +755,9 @@
         at = (place + k) % grid.outer
         out_blocks = lax.dynamic_update_slice_in_dim(out_blocks, x.astype(bf16)[None], at, 0)
     out_blocks, cot_all = tie(out_blocks.reshape(-1, out_blocks.shape[2]), cot_all)
-
+    out_sum = lax.psum_scatter(
+        out_blocks, "dp", scatter_dimension=0, tiled=True, axis_index_groups=grid.cols
+    )
 
     def scatter_rows(g):
         return lax.psum_scatter(
@@ -769,16 +771,19 @@
     gate_grad = (inner_grad * up_act * silu_slope(gate_act)).astype(bf16)
     up_grad = (inner_grad * jax.nn.silu(gate_act)).astype(bf16)
     inner_act = gated(gate_act, up_act)
-    back_parts, (down_rows, gate_rows, up_rows) = scatter_along(
+    back_parts, (down_rows, out_sum, mixed_plane, gate_rows) = scatter_along(
         add_other_core(*by_core(nt(gate_grad, full_gate) + nt(up_grad, full_up)), grid),
         grid,
         (
-            (tn(cot_all, inner_act).astype(bf16),),
+            (
+                tn(cot_all, inner_act).astype(bf16),
+                out_sum,
+                plane_columns(jnp.stack(jnp.split(mixed, INNER, axis=1))),
+            ),
             (tn(tokens, gate_grad).astype(bf16),),
-            (tn(tokens, up_grad).astype(bf16),),
         ),
     )
-    down_rows, gate_rows, up_rows = (scatter_rows(g) for g in (down_rows, gate_rows, up_rows))
+    down_rows, gate_rows = scatter_rows(down_rows), scatter_rows(gate_rows)
     hidden_grad, low_half, mlp_gain_part = second_norm_back(
         out_grad, hidden, mlp_gain, back_parts, core, grid
     )
@@ -796,20 +801,19 @@
         q, k, v, f = (half_of(g, which) for g in pre_grads)
         return nt(q, w_query) + nt(k, w_key) + nt(v, w_value) + nt(f, w_forget)
 
-    columns_here, part_other, part_mine, out_blocks, gate_rows, up_rows = tie(
+    up_later, _ = tie(up_grad, shares)
+    columns_here, part_other, part_mine, up_rows = tie(
         plane_columns(shares),
         normed_part(1 - core),
         normed_part(core),
-        out_blocks,
-        gate_rows,
-        up_rows,
-    )
-    out_sum = lax.psum_scatter(
-        out_blocks, "dp", scatter_dimension=0, tiled=True, axis_index_groups=grid.cols
+        tn(tokens, up_later).astype(bf16),
     )
     pre_grad = plane_product(normed_plane, columns_here)
-    _, low_half, mixed, out_sum = tie(pre_grad, low_half, mixed, out_sum)
-    mixed_plane = plane_columns(jnp.stack(jnp.split(mixed, INNER, axis=1)))
+    up_rows = scatter_rows(up_rows)
+    input_grad, attn_gain_part = first_norm_back(
+        block_in, hidden_grad, attn_gain, part_mine, swap(part_other), core
+    )
+    _, low_half, attn_gain_part = tie(pre_grad, low_half, attn_gain_part)
     low_plane = plane_tokens(plane_gather(low_half, grid, inner))
     sums, output_grad = tie(plane_sum(pre_grad), plane_product(low_plane, mixed_plane))
     output_sum = plane_sum(output_grad)
@@ -825,9 +829,6 @@
         sums[:, :, a:b].reshape(sums.shape[0], -1) for a, b in zip(ends, ends[1:])
     )
 
-    input_grad, attn_gain_part = first_norm_back(
-        block_in, hidden_grad, attn_gain, part_mine, swap(part_other), core
-    )
     input_grad = join(input_grad, swap(input_grad), core)
 
     gains = jnp.concatenate([attn_gain_part, mlp_gain_part], axis=0)

time: 586 us -> 576 us (0.983)
  waiting for transfers between devices: 235 us -> 217 us
    reduce_scatter x1, waiting for transfers between devices: 38.2 us -> 0.01 us  [on_device(): lax.psum_scatter(out_blocks, 'dp', scatter_dimension=0, tiled=True, axis_...]
    reduce_scatter x2, waiting for transfers between devices: 0.02 us -> 34 us  [plane_sum(): lax.psum_scatter(g, 'dp', scatter_dimension=0, tiled=True, axis_index_gro...]
    reduce_scatter x3, waiting for transfers between devices: 22.5 us -> 0.04 us  [scatter_rows(): lax.psum_scatter(g, 'dp', scatter_dimension=0, tiled=True, axis_index_gro...]
    all_to_all x9, waiting for transfers between devices: 73.7 us -> 60.9 us  [exchange(): lax.all_to_all(x, 'dp', split, concat, tiled=True, axis_index_groups=groups)]
    ppermute x3, waiting for transfers between devices: 11.8 us -> 21.9 us  [scatter_along(): up = lax.ppermute(up.astype(bf16), 'dp', grid.up)]
    ppermute x3, waiting for transfers between devices: 20.8 us -> 30.5 us  [plane_gather(): y = lax.ppermute(x, 'dp', [(d, d ^ k) for d in range(grid.dp)])]
    unnamed x101 -> x93, local copies, waits for them, and re-layouts: 26 us -> 26.3 us
  transfers between devices with their start and end apart: 71 -> 71, of which waited for: 40 -> 36; matrix products, arithmetic and copies ran while one was open for 29% -> 34% of each run, Pallas kernels for 6% -> 6%
where the time goes in v9:
time: 576 us; the launch traced here: 565 us
  waiting for transfers between devices  217 us (38%)
  matrix products  104 us (18%)
  starting transfers between devices  92.5 us (16%)
  local copies, waits for them, and re-layouts  69 us (12%)
  other arithmetic  34 us (6%)
  Pallas kernels  33.2 us (6%)
  between operations  15.7 us (3%)
    all_to_all x9, waiting for transfers between devices, exchange(): lax.all_to_all(x, 'dp', split, concat, tiled=True, axis_index_groups=groups)  60.9 us
    dot_general x8, matrix products, nn(): return jnp.dot(a.astype(bf16), b.astype(bf16), preferred_element_type=f32)  37.6 us
    all_to_all x9, starting transfers between devices, exchange(): lax.all_to_all(x, 'dp', split, concat, tiled=True, axis_index_groups=groups)  37.5 us
    dot_general x13, matrix products, nt(): lax.dot_general(a.astype(bf16), b.astype(bf16), (((1,), (1,)), ((), ())),...  35.7 us
    reduce_scatter x2, waiting for transfers between devices, plane_sum(): lax.psum_scatter(g, 'dp', scatter_dimension=0, tiled=True, axis_index_gro...  34 us
    dot_general x5, matrix products, tn(): lax.dot_general(a.astype(bf16), b.astype(bf16), (((0,), (0,)), ((), ())),...  30.7 us
    ppermute x3, waiting for transfers between devices, plane_gather(): y = lax.ppermute(x, 'dp', [(d, d ^ k) for d in range(grid.dp)])  30.5 us
    ppermute x6, waiting for transfers between devices, gather_along(): above = lax.ppermute(above, 'dp', grid.down)  29.2 us
  transfers between devices with their start and end apart: 71, of which 36 were waited for; matrix products, arithmetic and copies ran while one was open for 34% of the time, Pallas kernels for 6%

profile of v9, /device:TPU:0, one launch (start us, length us, event | category | flops | bytes accessed | tf_op | source)
XLA Modules:
  0.0 565.2 jit_solution(1498462103700349985)
XLA Ops:
  14.3 6.3 %all-to-all-start = ((bf16[128,4,1408]{0,2,1:T(8,128)(2,1)}), bf16[128,4,1408]{0,2,1:T(8,128)(2,1)S(1)}, u32[]{:S(2)}, u32[]{:S(2)}) async-start(bf16[128,4,1408]{0,2,1:T(8,128)(2,1)} %pad_maximum_fusion), calls=%async_computation | async-start | bytes 2883584 | tf_op jit(solution)/shard_map/all_to_all | solution.py:585
  20.7 5.0 multiply_convert_fusion.5
  31.7 6.4 %slot_forward.1 = (bf16[256,1024]{1,0:T(8,128)(2,1)}, f32[256,128]{1,0:T(8,128)}, f32[4,256,128]{2,1,0:T(8,128)}, bf16[2,256,256]{2,1,0:T(8,128)(2,1)}, bf16[2,256,16]{2,1,0:T(8,128)(2,1)}) custom-call(s32[1,3]{1,0:T(1,128)} %starts_ref.3, bf16[256,1024]{1,0:T(8,128)(2,1)} %get-tuple-element.226.q_ref, bf16[256,1024]{1,0:T(8,128)(2,1)} %get-tuple-element.228.k_ref, ...), custom_call_target="tpu_custom_call" | custom-call | flops 4000000000 | bytes 4000000 | tf_op jit(solution)/shard_map/slot_forward/pallas_call | solution.py:383
  38.1 4.8 fusion.24.mine_ref
  42.9 11.9 %all-to-all-done = bf16[128,4,1408]{0,2,1:T(8,128)(2,1)S(1)} async-done(((bf16[128,4,1408]{0,2,1:T(8,128)(2,1)}), bf16[128,4,1408]{0,2,1:T(8,128)(2,1)S(1)}, u32[]{:S(2)}, u32[]{:S(2)}) %all-to-all-start) | async-done | bytes 1441824 | tf_op jit(solution)/shard_map/all_to_all | solution.py:585
  58.1 3.7 fusion.22
  63.5 3.5 all-to-all-start.1
  69.9 3.3 second_norm.1
  73.1 4.6 collective-permute-start.1
  83.1 4.0 all-to-all-done.1
  90.6 5.5 collective-permute-done.2
  96.1 3.9 collective-permute-start.5
  101.3 3.3 bitcast_dynamic-update-slice_fusion
  104.7 6.2 %collective-permute-done.5 = bf16[128,2048]{1,0:T(8,128)(2,1)S(1)} collective-permute-done((bf16[128,2048]{1,0:T(8,128)(2,1)}, bf16[128,2048]{1,0:T(8,128)(2,1)S(1)}, u32[]{:S(2)}, u32[]{:S(2)}) %collective-permute-start.5) | collective-permute-done | bytes 524320 | tf_op jit(solution)/shard_map/ppermute | solution.py:598
  110.8 4.0 collective-permute-done.6
  122.1 4.7 collective-permute-done.8
  126.8 4.1 collective-permute-done.9
  137.4 4.3 collective-permute-start.3
  148.5 5.1 fusion.45
  153.6 6.6 %collective-permute-done.4 = bf16[128,2048]{1,0:T(8,128)(2,1)} collective-permute-done((bf16[128,2048]{1,0:T(8,128)(2,1)}, bf16[128,2048]{1,0:T(8,128)(2,1)}, u32[]{:S(2)}, u32[]{:S(2)}) %collective-permute-start.4) | collective-permute-done | bytes 524320 | tf_op jit(solution)/shard_map/ppermute | solution.py:599
  163.8 7.9 %fusion.46 = f32[1024,704]{0,1:T(8,128)} fusion(bf16[1024,2048]{1,0:T(8,128)(2,1)} %select_dynamic-update-slice_fusion.6, bf16[2048,704]{1,0:T(8,128)(2,1)} %all-gather.9.cloned.1.call-done), kind=kOutput, calls=%fused_computation.130 | convolution fusion | flops 2952790016 | bytes 9961472 | tf_op jit(solution)/shard_map/dot_general | solution.py:19
  173.1 4.9 collective-permute-done.18
  185.1 3.5 fusion.47
  190.1 4.0 collective-permute-done.20
  208.1 9.2 %multiply_convert_fusion.1 = (bf16[1024,704]{0,1:T(8,128)(2,1)S(1)}, bf16[1024,704]{0,1:T(8,128)(2,1)S(1)}) fusion(f32[1024,704]{0,1:T(8,128)} %copy-done.10, f32[1024,704]{0,1:T(8,128)} %fusion.46, bf16[1024,2048]{1,0:T(8,128)(2,1)} %copy-done.32, bf16[2048,704]{0,1:T(8,128)(2,1)} %all-gather.11.cloned.1.call-done), kind=kOutput, calls=%fused_computation.7 | convolution fusion | flops 2962161664 | bytes 15728640 | tf_op jit(solution)/shard_map/dot_general | solution.py:19
  217.4 4.0 fusion.48
  221.4 5.8 %fusion.44 = (bf16[1024,2048]{1,0:T(8,128)(2,1)S(1)}, f32[1024,2048]{1,0:T(8,128)}) fusion(f32[1024,2048]{1,0:T(8,128)S(1)} %fusion.48, bf16[1024,704]{0,1:T(8,128)(2,1)S(1)} %get-tuple-element.205, bf16[2048,704]{1,0:T(8,128)(2,1)S(1)} %copy-done.9), kind=kOutput, calls=%fused_computation.128 | convolution fusion | flops 2956984320 | bytes 25296896 | tf_op jit(solution)/shard_map/dot_general | solution.py:23
  230.4 4.1 all-to-all-start.2
  234.7 2.9 fusion.5
  241.3 6.7 %convolution_convert_fusion.3 = bf16[2048,704]{0,1:T(8,128)(2,1)} fusion(bf16[1024,704]{0,1:T(8,128)(2,1)S(1)} %copy-done.16, bf16[1024,2048]{1,0:T(8,128)(2,1)} %copy-done.32), kind=kOutput, calls=%fused_computation.5 | convolution fusion | flops 2954231808 | bytes 8519680 | tf_op jit(solution)/shard_map/dot_general | solution.py:29
  248.0 9.5 %collective-permute-done.36 = bf16[128,2048]{1,0:T(8,128)(2,1)} collective-permute-done((bf16[128,2048]{1,0:T(8,128)(2,1)}, bf16[128,2048]{1,0:T(8,128)(2,1)}, u32[]{:S(2)}, u32[]{:S(2)}) %collective-permute-start.36) | collective-permute-done | bytes 524320 | tf_op jit(solution)/shard_map/ppermute | solution.py:634
  259.4 2.8 add_convert_fusion.2
  262.2 3.4 collective-permute-start.39
  266.9 6.6 %convolution_convert_fusion.2 = bf16[2048,704]{0,1:T(8,128)(2,1)} fusion(bf16[1024,704]{0,1:T(8,128)(2,1)S(1)} %get-tuple-element.205, bf16[1024,2048]{1,0:T(8,128)(2,1)} %select_dynamic-update-slice_fusion.6), kind=kOutput, calls=%fused_computation.4 | convolution fusion | flops 2954231808 | bytes 8519680 | tf_op jit(solution)/shard_map/dot_general | solution.py:29
  273.6 3.7 collective-permute-done.39
  277.2 4.1 collective-permute-done.40
  281.4 3.8 add_convert_fusion
  285.1 3.4 collective-permute-start.41
  289.9 8.8 %collective-permute-done.41.refs_1_ = bf16[128,2048]{1,0:T(8,128)(2,1)S(1)} collective-permute-done((bf16[128,2048]{1,0:T(8,128)(2,1)S(1)}, bf16[128,2048]{1,0:T(8,128)(2,1)S(1)}, u32[]{:S(2)}, u32[]{:S(2)}) %collective-permute-start.41) | collective-permute-done | bytes 524320 | tf_op jit(solution)/shard_map/ppermute | solution.py:634
  298.6 4.1 collective-permute-done.42.refs_2_
  303.6 3.9 second_norm_back.1
  309.7 4.3 convolution_convert_fusion.5.do_ref
  316.1 3.7 all-to-all-start.3
  319.7 11.4 %slot_backward.1 = (bf16[256,1024]{1,0:T(8,128)(2,1)}, bf16[256,1024]{1,0:T(8,128)(2,1)}, bf16[256,1024]{1,0:T(8,128)(2,1)}, bf16[256,128]{1,0:T(8,128)(2,1)}, bf16[4,256,896]{2,1,0:T(8,128)(2,1)}) custom-call(s32[1,3]{1,0:T(1,128)} %starts_ref.3, bf16[256,1024]{1,0:T(8,128)(2,1)} %get-tuple-element.226.q_ref, bf16[256,1024]{1,0:T(8,128)(2,1)} %get-tuple-element.228.k_ref, ...), custom_call_target="tpu_custom_call" | custom-call | flops 12000000000 | bytes 8000000 | tf_op jit(solution)/shard_map/slot_backward/pallas_call | solution.py:403
  331.1 7.9 %all-to-all-done.3 = bf16[4,128,704]{1,2,0:T(8,128)(2,1)S(1)} async-done(((bf16[4,128,704]{1,2,0:T(8,128)(2,1)}), bf16[4,128,704]{1,2,0:T(8,128)(2,1)S(1)}, u32[]{:S(2)}, u32[]{:S(2)}) %all-to-all-start.3) | async-done | bytes 720928 | tf_op jit(solution)/shard_map/all_to_all | solution.py:585
  340.2 3.6 all-to-all-start.4
  344.0 3.9 fusion.16
  359.0 4.5 convolution_convert_fusion.1
  365.8 8.2 %convolution_convert_fusion = bf16[2048,896]{1,0:T(8,128)(2,1)} fusion(bf16[1024,2048]{1,0:T(8,128)(2,1)} %bitcast.11, bf16[1024,896]{1,0:T(8,128)(2,1)S(1)} %bitcast.155), kind=kOutput, calls=%fused_computation.2 | convolution fusion | flops 3759931392 | bytes 9699328 | tf_op jit(solution)/shard_map/dot_general | solution.py:29
  378.9 3.9 first_norm_back.1
  386.6 19.8 %collective-permute-done.47 = bf16[128,2048]{1,0:T(8,128)(2,1)} collective-permute-done((bf16[128,2048]{1,0:T(8,128)(2,1)S(1)}, bf16[128,2048]{1,0:T(8,128)(2,1)}, u32[]{:S(2)}, u32[]{:S(2)}) %collective-permute-start.47) | collective-permute-done | bytes 524320 | tf_op jit(solution)/shard_map/ppermute | solution.py:648
  407.6 10.7 %collective-permute-done.49 = bf16[128,2048]{1,0:T(8,128)(2,1)S(1)} collective-permute-done((bf16[128,2048]{1,0:T(8,128)(2,1)S(1)}, bf16[128,2048]{1,0:T(8,128)(2,1)S(1)}, u32[]{:S(2)}, u32[]{:S(2)}) %collective-permute-start.49) | collective-permute-done | bytes 524320 | tf_op jit(solution)/shard_map/ppermute | solution.py:648
  420.5 4.6 all-to-all-start.8
  430.9 3.1 constant_dynamic-update-slice_fusion.4
  434.1 30.7 %all-to-all-done.8 = bf16[4,128,704]{1,2,0:T(8,128)(2,1)S(1)} async-done(((bf16[4,128,704]{1,2,0:T(8,128)(2,1)}), bf16[4,128,704]{1,2,0:T(8,128)(2,1)S(1)}, u32[]{:S(2)}, u32[]{:S(2)}) %all-to-all-start.8) | async-done | bytes 720928 | tf_op jit(solution)/shard_map/all_to_all | solution.py:585
  464.8 3.5 all-to-all-start.5
  470.4 5.4 all-to-all-done.5
  475.8 4.2 all-to-all-start.9
  480.1 4.6 convolution_convert_fusion.4
  484.7 26.9 %reduce-scatter.11.cloned.1.call-done = bf16[512,896]{1,0:T(8,128)(2,1)} async-done(((bf16[2048,896]{1,0:T(8,128)(2,1)}), bf16[512,896]{1,0:T(8,128)(2,1)}) %reduce-scatter.11.cloned.1.call-update) | async-done | bytes 917520 | tf_op jit(solution)/shard_map/reduce_scatter | solution.py:723
  523.0 3.5 all-to-all-start.6
  534.7 4.5 all-to-all-done.6
  539.3 7.1 %reduce-scatter.13.cloned.1.call-done = bf16[512,256]{1,0:T(8,128)(2,1)} async-done(((bf16[2048,256]{1,0:T(8,128)(2,1)}), bf16[512,256]{1,0:T(8,128)(2,1)}) %reduce-scatter.13.cloned.1.call-update) | async-done | bytes 262160 | tf_op jit(solution)/shard_map/reduce_scatter | solution.py:723
  546.4 4.0 all-to-all-start.7
  (286 shorter events, 157.0 us)
Async XLA Ops:
  7.2 50.0 %all-gather.5.cloned.1.call-start = ((), (), s32[]{:S(2)}) async-start(), calls=%async_computation.16 | async-start | bytes 2621440 | tf_op jit(solution)/shard_map/all_gather | solution.py:697
  14.3 40.5 %all-to-all-start = ((bf16[128,4,1408]{0,2,1:T(8,128)(2,1)}), bf16[128,4,1408]{0,2,1:T(8,128)(2,1)S(1)}, u32[]{:S(2)}, u32[]{:S(2)}) async-start(bf16[128,4,1408]{0,2,1:T(8,128)(2,1)} %pad_maximum_fusion), calls=%async_computation | async-start | bytes 2883584 | tf_op jit(solution)/shard_map/all_to_all | solution.py:585
  20.7 110.3 %all-gather.7.cloned.1.call-start = ((), (), s32[]{:S(2)}) async-start(), calls=%async_computation.17 | async-start | bytes 3932160 | tf_op jit(solution)/shard_map/all_gather | solution.py:677
  57.2 103.0 %all-gather.9.cloned.1.call-start = ((), (), s32[]{:S(2)}) async-start(), calls=%async_computation.18 | async-start | bytes 3932160 | tf_op jit(solution)/shard_map/all_gather | solution.py:677
  58.0 43.3 %collective-permute-start.7 = (bf16[4,1,128,2048]{3,2,0,1:T(8,128)(2,1)}, bf16[4,1,128,2048]{3,2,0,1:T(8,128)(2,1)}, u32[]{:S(2)}, u32[]{:S(2)}) collective-permute-start(bf16[4,1,128,2048]{3,2,0,1:T(8,128)(2,1)} %bitcast.150), channel_id=1, source_target_pairs={{0,1},{1,0},{2,3},{3,2},{4,5},{5,4},{6,7},{7,6},{8,9},{9,8},{10,11... | collective-permute-start | bytes 6291464 | tf_op jit(solution)/shard_map/ppermute | solution.py:464
  61.8 7.1 %collective-permute-start = (f32[128,2048]{1,0:T(8,128)S(1)}, f32[128,2048]{1,0:T(8,128)S(1)}, u32[]{:S(2)}, u32[]{:S(2)}) collective-permute-start(f32[128,2048]{1,0:T(8,128)S(1)} %fusion.22), channel_id=1, source_target_pairs={{0,1},{1,0},{2,3},{3,2},{4,5},{5,4},{6,7},{7,6},{8,9},{9,8},{10,11... | collective-permute-start | bytes 3145736 | tf_op jit(solution)/shard_map/ppermute | solution.py:464
  63.5 23.6 %all-to-all-start.1 = ((bf16[128,4,704]{0,2,1:T(8,128)(2,1)}), bf16[128,4,704]{0,2,1:T(8,128)(2,1)S(1)}, u32[]{:S(2)}, u32[]{:S(2)}) async-start(bf16[128,4,704]{0,2,1:T(8,128)(2,1)} %bitcast.6), calls=%async_computation.1 | async-start | bytes 1441792 | tf_op jit(solution)/shard_map/all_to_all | solution.py:585
  67.0 111.0 %all-gather.11.cloned.1.call-start = ((), (), s32[]{:S(2)}) async-start(), calls=%async_computation.19 | async-start | bytes 3604480 | tf_op jit(solution)/shard_map/all_gather | solution.py:677
  73.1 17.4 %collective-permute-start.1 = (bf16[128,2048]{1,0:T(8,128)(2,1)}, bf16[128,2048]{1,0:T(8,128)(2,1)}, u32[]{:S(2)}, u32[]{:S(2)}) collective-permute-start(bf16[128,2048]{1,0:T(8,128)(2,1)} %get-tuple-element.96), channel_id=1, source_target_pairs={{0,8},{2,10},{4,12},{6,14},{8,16},{10,18},{12,20},{14,22},{16,24},... | collective-permute-start | bytes 1572872 | tf_op jit(solution)/shard_map/ppermute | solution.py:598
  77.7 18.3 %collective-permute-start.2 = (bf16[128,2048]{1,0:T(8,128)(2,1)}, bf16[128,2048]{1,0:T(8,128)(2,1)}, u32[]{:S(2)}, u32[]{:S(2)}) collective-permute-start(bf16[128,2048]{1,0:T(8,128)(2,1)} %get-tuple-element.96), channel_id=1, source_target_pairs={{8,0},{10,2},{12,4},{14,6},{16,8},{18,10},{20,12},{22,14},{24,16},... | collective-permute-start | bytes 1572872 | tf_op jit(solution)/shard_map/ppermute | solution.py:599
  96.1 14.8 %collective-permute-start.5 = (bf16[128,2048]{1,0:T(8,128)(2,1)}, bf16[128,2048]{1,0:T(8,128)(2,1)S(1)}, u32[]{:S(2)}, u32[]{:S(2)}) collective-permute-start(bf16[128,2048]{1,0:T(8,128)(2,1)} %collective-permute-done.1), channel_id=1, source_target_pairs={{0,8},{2,10},{4,12},{6,14},{8,16},{10,18},{12,20},{14,22},{16,24},... | collective-permute-start | bytes 1572872 | tf_op jit(solution)/shard_map/ppermute | solution.py:598
  100.0 14.9 %collective-permute-start.6 = (bf16[128,2048]{1,0:T(8,128)(2,1)}, bf16[128,2048]{1,0:T(8,128)(2,1)S(1)}, u32[]{:S(2)}, u32[]{:S(2)}) collective-permute-start(bf16[128,2048]{1,0:T(8,128)(2,1)} %collective-permute-done.2), channel_id=1, source_target_pairs={{8,0},{10,2},{12,4},{14,6},{16,8},{18,10},{20,12},{22,14},{24,16},... | collective-permute-start | bytes 1572872 | tf_op jit(solution)/shard_map/ppermute | solution.py:599
  114.9 11.9 %collective-permute-start.8 = (bf16[128,2048]{1,0:T(8,128)(2,1)S(1)}, bf16[128,2048]{1,0:T(8,128)(2,1)S(1)}, u32[]{:S(2)}, u32[]{:S(2)}) collective-permute-start(bf16[128,2048]{1,0:T(8,128)(2,1)S(1)} %collective-permute-done.5), channel_id=1, source_target_pairs={{0,8},{2,10},{4,12},{6,14},{8,16},{10,18},{12,20},{14,22},{16,24},... | collective-permute-start | bytes 1572872 | tf_op jit(solution)/shard_map/ppermute | solution.py:598
  117.3 13.6 %collective-permute-start.9 = (bf16[128,2048]{1,0:T(8,128)(2,1)S(1)}, bf16[128,2048]{1,0:T(8,128)(2,1)S(1)}, u32[]{:S(2)}, u32[]{:S(2)}) collective-permute-start(bf16[128,2048]{1,0:T(8,128)(2,1)S(1)} %collective-permute-done.6), channel_id=1, source_target_pairs={{8,0},{10,2},{12,4},{14,6},{16,8},{18,10},{20,12},{22,14},{24,16},... | collective-permute-start | bytes 1572872 | tf_op jit(solution)/shard_map/ppermute | solution.py:599
  118.8 16.1 %collective-permute-start.10 = (bf16[128,2048]{1,0:T(8,128)(2,1)S(1)}, bf16[128,2048]{1,0:T(8,128)(2,1)}, u32[]{:S(2)}, u32[]{:S(2)}) collective-permute-start(bf16[128,2048]{1,0:T(8,128)(2,1)S(1)} %copy-done.27), channel_id=1, source_target_pairs={{0,1},{1,0},{2,3},{3,2},{4,5},{5,4},{6,7},{7,6},{8,9},{9,8},{10,11... | collective-permute-start | bytes 1572872 | tf_op jit(solution)/shard_map/ppermute | solution.py:464
  119.7 17.8 %collective-permute-start.11 = (bf16[128,2048]{1,0:T(8,128)(2,1)}, bf16[128,2048]{1,0:T(8,128)(2,1)}, u32[]{:S(2)}, u32[]{:S(2)}) collective-permute-start(bf16[128,2048]{1,0:T(8,128)(2,1)} %collective-permute-done.2), channel_id=1, source_target_pairs={{0,1},{1,0},{2,3},{3,2},{4,5},{5,4},{6,7},{7,6},{8,9},{9,8},{10,11... | collective-permute-start | bytes 1572872 | tf_op jit(solution)/shard_map/ppermute | solution.py:464
  120.2 27.4 %collective-permute-start.16 = (bf16[128,2048]{1,0:T(8,128)(2,1)}, bf16[128,2048]{1,0:T(8,128)(2,1)}, u32[]{:S(2)}, u32[]{:S(2)}) collective-permute-start(bf16[128,2048]{1,0:T(8,128)(2,1)} %collective-permute-done.1), channel_id=1, source_target_pairs={{0,1},{1,0},{2,3},{3,2},{4,5},{5,4},{6,7},{7,6},{8,9},{9,8},{10,11... | collective-permute-start | bytes 1572872 | tf_op jit(solution)/shard_map/ppermute | solution.py:464
  120.2 139.1 %reduce-scatter.7.cloned.1.call-start = ((), (), s32[]{:S(2)}) async-start(), calls=%async_computation.20 | async-start | bytes 2621440 | tf_op jit(solution)/shard_map/reduce_scatter | solution.py:758
  126.8 16.9 %collective-permute-start.13 = (bf16[128,2048]{1,0:T(8,128)(2,1)S(1)}, bf16[128,2048]{1,0:T(8,128)(2,1)}, u32[]{:S(2)}, u32[]{:S(2)}) collective-permute-start(bf16[128,2048]{1,0:T(8,128)(2,1)S(1)} %collective-permute-done.6), channel_id=1, source_target_pairs={{0,1},{1,0},{2,3},{3,2},{4,5},{5,4},{6,7},{7,6},{8,9},{9,8},{10,11... | collective-permute-start | bytes 1572872 | tf_op jit(solution)/shard_map/ppermute | solution.py:464
  131.0 10.8 %collective-permute-start.12 = (bf16[128,2048]{1,0:T(8,128)(2,1)S(1)}, bf16[128,2048]{1,0:T(8,128)(2,1)S(1)}, u32[]{:S(2)}, u32[]{:S(2)}) collective-permute-start(bf16[128,2048]{1,0:T(8,128)(2,1)S(1)} %collective-permute-done.8), channel_id=1, source_target_pairs={{0,1},{1,0},{2,3},{3,2},{4,5},{5,4},{6,7},{7,6},{8,9},{9,8},{10,11... | collective-permute-start | bytes 1572872 | tf_op jit(solution)/shard_map/ppermute | solution.py:464
  134.8 10.2 %collective-permute-start.14 = (bf16[128,2048]{1,0:T(8,128)(2,1)S(1)}, bf16[128,2048]{1,0:T(8,128)(2,1)S(1)}, u32[]{:S(2)}, u32[]{:S(2)}) collective-permute-start(bf16[128,2048]{1,0:T(8,128)(2,1)S(1)} %collective-permute-done.5), channel_id=1, source_target_pairs={{0,1},{1,0},{2,3},{3,2},{4,5},{5,4},{6,7},{7,6},{8,9},{9,8},{10,11... | collective-permute-start | bytes 1572872 | tf_op jit(solution)/shard_map/ppermute | solution.py:464
  137.4 16.2 %collective-permute-start.3 = (bf16[128,2048]{1,0:T(8,128)(2,1)}, bf16[128,2048]{1,0:T(8,128)(2,1)}, u32[]{:S(2)}, u32[]{:S(2)}) collective-permute-start(bf16[128,2048]{1,0:T(8,128)(2,1)} %cotangent_rows.1), channel_id=1, source_target_pairs={{0,8},{2,10},{4,12},{6,14},{8,16},{10,18},{12,20},{14,22},{16,24},... | collective-permute-start | bytes 1572872 | tf_op jit(solution)/shard_map/ppermute | solution.py:598
  141.7 5.9 %collective-permute-start.15 = (bf16[128,2048]{1,0:T(8,128)(2,1)S(1)}, bf16[128,2048]{1,0:T(8,128)(2,1)S(1)}, u32[]{:S(2)}, u32[]{:S(2)}) collective-permute-start(bf16[128,2048]{1,0:T(8,128)(2,1)S(1)} %collective-permute-done.9), channel_id=1, source_target_pairs={{0,1},{1,0},{2,3},{3,2},{4,5},{5,4},{6,7},{7,6},{8,9},{9,8},{10,11... | collective-permute-start | bytes 1572872 | tf_op jit(solution)/shard_map/ppermute | solution.py:464
  143.7 16.5 %collective-permute-start.4 = (bf16[128,2048]{1,0:T(8,128)(2,1)}, bf16[128,2048]{1,0:T(8,128)(2,1)}, u32[]{:S(2)}, u32[]{:S(2)}) collective-permute-start(bf16[128,2048]{1,0:T(8,128)(2,1)} %cotangent_rows.1), channel_id=1, source_target_pairs={{8,0},{10,2},{12,4},{14,6},{16,8},{18,10},{20,12},{22,14},{24,16},... | collective-permute-start | bytes 1572872 | tf_op jit(solution)/shard_map/ppermute | solution.py:599
  145.0 53.0 %collective-permute-start.25 = (bf16[128,2048]{1,0:T(8,128)(2,1)}, bf16[128,2048]{1,0:T(8,128)(2,1)}, u32[]{:S(2)}, u32[]{:S(2)}) collective-permute-start(bf16[128,2048]{1,0:T(8,128)(2,1)} %cotangent_rows.1), channel_id=1, source_target_pairs={{0,1},{1,0},{2,3},{3,2},{4,5},{5,4},{6,7},{7,6},{8,9},{9,8},{10,11... | collective-permute-start | bytes 1572872 | tf_op jit(solution)/shard_map/ppermute | solution.py:464
  160.2 12.9 %collective-permute-start.17 = (bf16[128,2048]{1,0:T(8,128)(2,1)}, bf16[128,2048]{1,0:T(8,128)(2,1)}, u32[]{:S(2)}, u32[]{:S(2)}) collective-permute-start(bf16[128,2048]{1,0:T(8,128)(2,1)} %collective-permute-done.3), channel_id=1, source_target_pairs={{0,8},{2,10},{4,12},{6,14},{8,16},{10,18},{12,20},{14,22},{16,24},... | collective-permute-start | bytes 1572872 | tf_op jit(solution)/shard_map/ppermute | solution.py:598
  162.6 15.4 %collective-permute-start.18 = (bf16[128,2048]{1,0:T(8,128)(2,1)}, bf16[128,2048]{1,0:T(8,128)(2,1)}, u32[]{:S(2)}, u32[]{:S(2)}) collective-permute-start(bf16[128,2048]{1,0:T(8,128)(2,1)} %collective-permute-done.4), channel_id=1, source_target_pairs={{8,0},{10,2},{12,4},{14,6},{16,8},{18,10},{20,12},{22,14},{24,16},... | collective-permute-start | bytes 1572872 | tf_op jit(solution)/shard_map/ppermute | solution.py:599
  178.0 12.1 %collective-permute-start.19 = (bf16[128,2048]{1,0:T(8,128)(2,1)}, bf16[128,2048]{1,0:T(8,128)(2,1)S(1)}, u32[]{:S(2)}, u32[]{:S(2)}) collective-permute-start(bf16[128,2048]{1,0:T(8,128)(2,1)} %collective-permute-done.17), channel_id=1, source_target_pairs={{0,8},{2,10},{4,12},{6,14},{8,16},{10,18},{12,20},{14,22},{16,24},... | collective-permute-start | bytes 1572872 | tf_op jit(solution)/shard_map/ppermute | solution.py:598
  179.8 14.4 %collective-permute-start.20 = (bf16[128,2048]{1,0:T(8,128)(2,1)}, bf16[128,2048]{1,0:T(8,128)(2,1)S(1)}, u32[]{:S(2)}, u32[]{:S(2)}) collective-permute-start(bf16[128,2048]{1,0:T(8,128)(2,1)} %collective-permute-done.18), channel_id=1, source_target_pairs={{8,0},{10,2},{12,4},{14,6},{16,8},{18,10},{20,12},{22,14},{24,16},... | collective-permute-start | bytes 1572872 | tf_op jit(solution)/shard_map/ppermute | solution.py:599
  197.4 3.6 collective-permute-start.24
  198.0 3.7 collective-permute-start.26
  199.2 6.2 %collective-permute-start.31 = (bf16[128,2048]{1,0:T(8,128)(2,1)}, bf16[128,2048]{1,0:T(8,128)(2,1)S(1)}, u32[]{:S(2)}, u32[]{:S(2)}) collective-permute-start(bf16[128,2048]{1,0:T(8,128)(2,1)} %collective-permute-done.3), channel_id=1, source_target_pairs={{0,1},{1,0},{2,3},{3,2},{4,5},{5,4},{6,7},{7,6},{8,9},{9,8},{10,11... | collective-permute-start | bytes 1572872 | tf_op jit(solution)/shard_map/ppermute | solution.py:464
  199.7 5.3 collective-permute-start.28
  200.3 4.8 collective-permute-start.29
  201.0 3.7 collective-permute-start.27
  201.8 3.7 collective-permute-start.30
  228.5 6.1 %collective-permute-start.32 = (bf16[128,2048]{1,0:T(8,128)(2,1)}, bf16[128,2048]{1,0:T(8,128)(2,1)}, u32[]{:S(2)}, u32[]{:S(2)}) collective-permute-start(bf16[128,2048]{1,0:T(8,128)(2,1)} %get-tuple-element.210), channel_id=1, source_target_pairs={{0,1},{1,0},{2,3},{3,2},{4,5},{5,4},{6,7},{7,6},{8,9},{9,8},{10,11... | collective-permute-start | bytes 1572872 | tf_op jit(solution)/shard_map/ppermute | solution.py:464
  228.6 6.0 %collective-permute-start.33 = (bf16[128,2048]{1,0:T(8,128)(2,1)}, bf16[128,2048]{1,0:T(8,128)(2,1)S(1)}, u32[]{:S(2)}, u32[]{:S(2)}) collective-permute-start(bf16[128,2048]{1,0:T(8,128)(2,1)} %get-tuple-element.209), channel_id=1, source_target_pairs={{0,1},{1,0},{2,3},{3,2},{4,5},{5,4},{6,7},{7,6},{8,9},{9,8},{10,11... | collective-permute-start | bytes 1572872 | tf_op jit(solution)/shard_map/ppermute | solution.py:464
  229.0 5.6 collective-permute-start.34
  229.2 5.5 collective-permute-start.35
  230.4 17.6 %all-to-all-start.2 = ((bf16[4,256,256]{2,1,0:T(8,128)(2,1)}), bf16[4,256,256]{2,1,0:T(8,128)(2,1)}, u32[]{:S(2)}, u32[]{:S(2)}) async-start(bf16[4,256,256]{2,1,0:T(8,128)(2,1)} %pad_maximum_fusion.1), calls=%async_computation.3 | async-start | bytes 1048576 | tf_op jit(solution)/shard_map/all_to_all | solution.py:585
  234.6 79.4 %reduce-scatter.9.cloned.1.call-start = ((), (), s32[]{:S(2)}) async-start(), calls=%async_computation.21 | async-start | bytes 3604480 | tf_op jit(solution)/shard_map/reduce_scatter | solution.py:763
  237.6 20.0 %collective-permute-start.36 = (bf16[128,2048]{1,0:T(8,128)(2,1)}, bf16[128,2048]{1,0:T(8,128)(2,1)}, u32[]{:S(2)}, u32[]{:S(2)}) collective-permute-start(bf16[128,2048]{1,0:T(8,128)(2,1)} %get-tuple-element.204), channel_id=1, source_target_pairs={{0,8},{2,10},{4,12},{6,14},{8,16},{10,18},{12,20},{14,22},{16,24},... | collective-permute-start | bytes 1572872 | tf_op jit(solution)/shard_map/ppermute | solution.py:634
  240.0 19.3 %collective-permute-start.37 = (bf16[128,2048]{1,0:T(8,128)(2,1)}, bf16[128,2048]{1,0:T(8,128)(2,1)}, u32[]{:S(2)}, u32[]{:S(2)}) collective-permute-start(bf16[128,2048]{1,0:T(8,128)(2,1)} %get-tuple-element.203), channel_id=1, source_target_pairs={{8,0},{10,2},{12,4},{14,6},{16,8},{18,10},{20,12},{22,14},{24,16},... | collective-permute-start | bytes 1572872 | tf_op jit(solution)/shard_map/ppermute | solution.py:635
  259.3 159.1 %reduce-scatter.15.cloned.1.call-start = ((), (), s32[]{:S(2)}) async-start(), calls=%async_computation.24 | async-start | bytes 3604480 | tf_op jit(solution)/shard_map/reduce_scatter | solution.py:763
  262.2 15.0 %collective-permute-start.39 = (bf16[128,2048]{1,0:T(8,128)(2,1)}, bf16[128,2048]{1,0:T(8,128)(2,1)S(1)}, u32[]{:S(2)}, u32[]{:S(2)}) collective-permute-start(bf16[128,2048]{1,0:T(8,128)(2,1)} %get-tuple-element.199), channel_id=1, source_target_pairs={{0,8},{2,10},{4,12},{6,14},{8,16},{10,18},{12,20},{14,22},{16,24},... | collective-permute-start | bytes 1572872 | tf_op jit(solution)/shard_map/ppermute | solution.py:634
  265.6 15.7 %collective-permute-start.40 = (bf16[128,2048]{1,0:T(8,128)(2,1)}, bf16[128,2048]{1,0:T(8,128)(2,1)}, u32[]{:S(2)}, u32[]{:S(2)}) collective-permute-start(bf16[128,2048]{1,0:T(8,128)(2,1)} %get-tuple-element.198), channel_id=1, source_target_pairs={{8,0},{10,2},{12,4},{14,6},{16,8},{18,10},{20,12},{22,14},{24,16},... | collective-permute-start | bytes 1572872 | tf_op jit(solution)/shard_map/ppermute | solution.py:635
  285.1 13.5 %collective-permute-start.41 = (bf16[128,2048]{1,0:T(8,128)(2,1)S(1)}, bf16[128,2048]{1,0:T(8,128)(2,1)S(1)}, u32[]{:S(2)}, u32[]{:S(2)}) collective-permute-start(bf16[128,2048]{1,0:T(8,128)(2,1)S(1)} %get-tuple-element.201), channel_id=1, source_target_pairs={{0,8},{2,10},{4,12},{6,14},{8,16},{10,18},{12,20},{14,22},{16,24},... | collective-permute-start | bytes 1572872 | tf_op jit(solution)/shard_map/ppermute | solution.py:634
  288.6 14.2 %collective-permute-start.42 = (bf16[128,2048]{1,0:T(8,128)(2,1)S(1)}, bf16[128,2048]{1,0:T(8,128)(2,1)S(1)}, u32[]{:S(2)}, u32[]{:S(2)}) collective-permute-start(bf16[128,2048]{1,0:T(8,128)(2,1)S(1)} %get-tuple-element.200), channel_id=1, source_target_pairs={{8,0},{10,2},{12,4},{14,6},{16,8},{18,10},{20,12},{22,14},{24,16},... | collective-permute-start | bytes 1572872 | tf_op jit(solution)/shard_map/ppermute | solution.py:635
  316.1 22.9 %all-to-all-start.3 = ((bf16[4,128,704]{1,2,0:T(8,128)(2,1)}), bf16[4,128,704]{1,2,0:T(8,128)(2,1)S(1)}, u32[]{:S(2)}, u32[]{:S(2)}) async-start(bf16[4,128,704]{1,2,0:T(8,128)(2,1)} %copy_bitcast_fusion.3), calls=%async_computation.5 | async-start | bytes 1441792 | tf_op jit(solution)/shard_map/all_to_all | solution.py:585
  340.2 25.3 %all-to-all-start.4 = ((bf16[4,256,896]{2,1,0:T(8,128)(2,1)}), bf16[4,256,896]{2,1,0:T(8,128)(2,1)S(1)}, u32[]{:S(2)}, u32[]{:S(2)}) async-start(bf16[4,256,896]{2,1,0:T(8,128)(2,1)} %get-tuple-element.153), calls=%async_computation.6 | async-start | bytes 3670016 | tf_op jit(solution)/shard_map/all_to_all | solution.py:585
  343.7 124.5 %reduce-scatter.17.cloned.1.call-start = ((), (), s32[]{:S(2)}) async-start(), calls=%async_computation.25 | async-start | bytes 3604480 | tf_op jit(solution)/shard_map/reduce_scatter | solution.py:763
  365.5 146.1 %reduce-scatter.11.cloned.1.call-start = ((), (), s32[]{:S(2)}) async-start(), calls=%async_computation.22 | async-start | bytes 4587520 | tf_op jit(solution)/shard_map/reduce_scatter | solution.py:723
  382.8 23.6 %collective-permute-start.47 = (bf16[128,2048]{1,0:T(8,128)(2,1)S(1)}, bf16[128,2048]{1,0:T(8,128)(2,1)}, u32[]{:S(2)}, u32[]{:S(2)}) collective-permute-start(bf16[128,2048]{1,0:T(8,128)(2,1)S(1)} %copy-done.14), channel_id=1, source_target_pairs={{0,2},{2,0},{4,6},{6,4},{8,10},{10,8},{12,14},{14,12},{16,18},{18,... | collective-permute-start | bytes 1572872 | tf_op jit(solution)/shard_map/ppermute | solution.py:648
  384.2 23.3 %collective-permute-start.48 = (bf16[128,2048]{1,0:T(8,128)(2,1)S(1)}, bf16[128,2048]{1,0:T(8,128)(2,1)S(1)}, u32[]{:S(2)}, u32[]{:S(2)}) collective-permute-start(bf16[128,2048]{1,0:T(8,128)(2,1)S(1)} %copy-done.14), channel_id=1, source_target_pairs={{0,4},{2,6},{4,0},{6,2},{8,12},{10,14},{12,8},{14,10},{16,20},{18,... | collective-permute-start | bytes 1572872 | tf_op jit(solution)/shard_map/ppermute | solution.py:648
  384.8 33.5 %collective-permute-start.49 = (bf16[128,2048]{1,0:T(8,128)(2,1)S(1)}, bf16[128,2048]{1,0:T(8,128)(2,1)S(1)}, u32[]{:S(2)}, u32[]{:S(2)}) collective-permute-start(bf16[128,2048]{1,0:T(8,128)(2,1)S(1)} %copy-done.14), channel_id=1, source_target_pairs={{0,6},{2,4},{4,2},{6,0},{8,14},{10,12},{12,10},{14,8},{16,22},{18,... | collective-permute-start | bytes 1572872 | tf_op jit(solution)/shard_map/ppermute | solution.py:648
  418.3 12.6 %collective-permute-start.50 = (bf16[4,1,128,2048]{3,2,1,0:T(8,128)(2,1)S(1)}, bf16[4,1,128,2048]{3,2,1,0:T(8,128)(2,1)}, u32[]{:S(2)}, u32[]{:S(2)}) collective-permute-start(bf16[4,1,128,2048]{3,2,1,0:T(8,128)(2,1)S(1)} %bitcast_dynamic-update-slice_fusion.1), channel_id=1, source_target_pairs={{0,1},{1,0},{2,3},{3,2},{4,5},{5,4},{6,7},{7,6},{8,9},{9,8},{10,11... | collective-permute-start | bytes 6291464 | tf_op jit(solution)/shard_map/ppermute | solution.py:464
  420.5 44.2 %all-to-all-start.8 = ((bf16[4,128,704]{1,2,0:T(8,128)(2,1)}), bf16[4,128,704]{1,2,0:T(8,128)(2,1)S(1)}, u32[]{:S(2)}, u32[]{:S(2)}) async-start(bf16[4,128,704]{1,2,0:T(8,128)(2,1)} %copy_bitcast_fusion.2), calls=%async_computation.13 | async-start | bytes 1441792 | tf_op jit(solution)/shard_map/all_to_all | solution.py:585
  464.8 11.1 %all-to-all-start.5 = ((f32[16,2,128]{2,1,0:T(2,128)}), f32[16,2,128]{2,1,0:T(2,128)S(1)}, u32[]{:S(2)}, u32[]{:S(2)}) async-start(f32[16,2,128]{2,1,0:T(2,128)} %add_bitcast_fusion), calls=%async_computation.7 | async-start | bytes 32768 | tf_op jit(solution)/shard_map/all_to_all | solution.py:837
  475.8 47.1 %all-to-all-start.9 = ((bf16[4,128,704]{1,2,0:T(8,128)(2,1)}), bf16[4,128,704]{1,2,0:T(8,128)(2,1)}, u32[]{:S(2)}, u32[]{:S(2)}) async-start(bf16[4,128,704]{1,2,0:T(8,128)(2,1)} %copy_bitcast_fusion.1), calls=%async_computation.15 | async-start | bytes 1441792 | tf_op jit(solution)/shard_map/all_to_all | solution.py:585
  480.0 66.4 %reduce-scatter.13.cloned.1.call-start = ((), (), s32[]{:S(2)}) async-start(), calls=%async_computation.23 | async-start | bytes 1310720 | tf_op jit(solution)/shard_map/reduce_scatter | solution.py:723
  514.2 15.5 %collective-permute-start.45 = (f32[128,2048]{1,0:T(8,128)}, f32[128,2048]{1,0:T(8,128)}, u32[]{:S(2)}, u32[]{:S(2)}) collective-permute-start(f32[128,2048]{1,0:T(8,128)} %get-tuple-element.161), channel_id=1, source_target_pairs={{0,1},{1,0},{2,3},{3,2},{4,5},{5,4},{6,7},{7,6},{8,9},{9,8},{10,11... | collective-permute-start | bytes 3145736 | tf_op jit(solution)/shard_map/ppermute | solution.py:464
  523.0 16.2 %all-to-all-start.6 = ((bf16[4,128,896]{1,2,0:T(8,128)(2,1)}), bf16[4,128,896]{1,2,0:T(8,128)(2,1)S(1)}, u32[]{:S(2)}, u32[]{:S(2)}) async-start(bf16[4,128,896]{1,2,0:T(8,128)(2,1)} %copy.63), calls=%async_computation.9 | async-start | bytes 1835008 | tf_op jit(solution)/shard_map/all_to_all | solution.py:585
  546.4 9.7 %all-to-all-start.7 = ((bf16[4,128,256]{2,1,0:T(8,128)(2,1)}), bf16[4,128,256]{2,1,0:T(8,128)(2,1)}, u32[]{:S(2)}, u32[]{:S(2)}) async-start(bf16[4,128,256]{2,1,0:T(8,128)(2,1)} %bitcast.158), calls=%async_computation.11 | async-start | bytes 524288 | tf_op jit(solution)/shard_map/all_to_all | solution.py:585
  (47 other events, 316.0 us)
Sparse Core Ops, SparseCore 0:
  11.4 37.8 all-gather.4
  57.4 35.2 all-gather.6
  94.8 36.1 all-gather.8
  133.0 33.9 all-gather.10
  208.2 46.8 reduce-scatter.6
  259.5 32.4 reduce-scatter.8
  307.7 30.6 reduce-scatter.14
  365.6 39.7 reduce-scatter.16
  407.7 103.8 reduce-scatter.10
  513.7 32.6 reduce-scatter.12

commit v10 on v9

--- a/solution.py
+++ b/solution.py
@@ -767,11 +767,25 @@
     def to_columns(g):
         return exchange(g, 0, 1, grid.cols).astype(f32)
 
+    def to_columns_beside(g):
+        n = grid.outer
+        if n & (n - 1) or n > 4:
+            return to_columns(g)
+        blocks = g.reshape(n, -1, g.shape[1])
+        out = jnp.zeros_like(blocks)
+        for s in range(n):
+            piece = lax.dynamic_slice_in_dim(blocks, place ^ s, 1, 0)
+            if s:
+                pairs = [(d, (d // INNER ^ s) * INNER + d % INNER) for d in range(grid.dp)]
+                piece = lax.ppermute(piece, "dp", pairs)
+            out = lax.dynamic_update_slice_in_dim(out, piece, place ^ s, 0)
+        return jnp.swapaxes(out, 0, 1).reshape(blocks.shape[1], -1).astype(f32)
+
     inner_grad = nn(cot_all, full_down)
     gate_grad = (inner_grad * up_act * silu_slope(gate_act)).astype(bf16)
     up_grad = (inner_grad * jax.nn.silu(gate_act)).astype(bf16)
     inner_act = gated(gate_act, up_act)
-    back_parts, (down_rows, out_sum, mixed_plane, gate_rows) = scatter_along(
+    back_parts, (down_rows, out_sum, mixed_plane, gate_rows, up_rows) = scatter_along(
         add_other_core(*by_core(nt(gate_grad, full_gate) + nt(up_grad, full_up)), grid),
         grid,
         (
@@ -781,9 +795,10 @@
                 plane_columns(jnp.stack(jnp.split(mixed, INNER, axis=1))),
             ),
             (tn(tokens, gate_grad).astype(bf16),),
+            (tn(tokens, up_grad).astype(bf16),),
         ),
     )
-    down_rows, gate_rows = scatter_rows(down_rows), scatter_rows(gate_rows)
+    down_rows, gate_rows, up_rows = (scatter_rows(g) for g in (down_rows, gate_rows, up_rows))
     hidden_grad, low_half, mlp_gain_part = second_norm_back(
         out_grad, hidden, mlp_gain, back_parts, core, grid
     )
@@ -794,22 +809,19 @@
         query, key, value, log_keep, doc_starts, saved, mixed_grad,
         (query_pre, key_pre, value_pre, forget_pre),
     )
-    down_sum = to_columns(down_rows)
-    down_sum, shares, *pre_grads = tie(down_sum, shares, *pre_grads)
 
     def normed_part(which):
         q, k, v, f = (half_of(g, which) for g in pre_grads)
         return nt(q, w_query) + nt(k, w_key) + nt(v, w_value) + nt(f, w_forget)
 
-    up_later, _ = tie(up_grad, shares)
-    columns_here, part_other, part_mine, up_rows = tie(
+    columns_here, part_other, part_mine, down_sum, gate_sum = tie(
         plane_columns(shares),
         normed_part(1 - core),
         normed_part(core),
-        tn(tokens, up_later).astype(bf16),
+        to_columns_beside(down_rows),
+        to_columns_beside(gate_rows),
     )
     pre_grad = plane_product(normed_plane, columns_here)
-    up_rows = scatter_rows(up_rows)
     input_grad, attn_gain_part = first_norm_back(
         block_in, hidden_grad, attn_gain, part_mine, swap(part_other), core
     )
@@ -846,7 +858,7 @@
         value_sum,
         forget_sum,
         output_sum,
-        to_columns(gate_rows),
+        gate_sum,
         to_columns(up_rows),
         down_sum,
     )

time: 576 us -> 546 us (0.948)
  waiting for transfers between devices: 217 us -> 180 us
  starting transfers between devices: 92.5 us -> 99.8 us
    all_to_all x9 -> x7, waiting for transfers between devices: 60.9 us -> 22.7 us  [exchange(): lax.all_to_all(x, 'dp', split, concat, tiled=True, axis_index_groups=groups)]
    ppermute x0 -> x6, waiting for transfers between devices: none -> 23.5 us  [to_columns_beside(): piece = lax.ppermute(piece, 'dp', pairs)]
    ppermute x3, waiting for transfers between devices: 30.5 us -> 21.6 us  [plane_gather(): y = lax.ppermute(x, 'dp', [(d, d ^ k) for d in range(grid.dp)])]
    ppermute x0 -> x6, starting transfers between devices: none -> 7.43 us  [to_columns_beside(): piece = lax.ppermute(piece, 'dp', pairs)]
    all_to_all x9 -> x7, starting transfers between devices: 37.5 us -> 32 us  [exchange(): lax.all_to_all(x, 'dp', split, concat, tiled=True, axis_index_groups=groups)]
    unnamed x93 -> x103, local copies, waits for them, and re-layouts: 26.3 us -> 26.6 us
  transfers between devices with their start and end apart: 71 -> 75, of which waited for: 36 -> 33; matrix products, arithmetic and copies ran while one was open for 34% -> 36% of each run, Pallas kernels for 6% -> 6%
where the time goes in v10:
time: 546 us; the launch traced here: 535 us
  waiting for transfers between devices  180 us (33%)
  matrix products  104 us (19%)
  starting transfers between devices  99.8 us (18%)
  local copies, waits for them, and re-layouts  67.4 us (12%)
  other arithmetic  35.5 us (7%)
  Pallas kernels  33.2 us (6%)
  between operations  15.7 us (3%)
    dot_general x8, matrix products, nn(): return jnp.dot(a.astype(bf16), b.astype(bf16), preferred_element_type=f32)  37.7 us
    dot_general x13, matrix products, nt(): lax.dot_general(a.astype(bf16), b.astype(bf16), (((1,), (1,)), ((), ())),...  35.5 us
    reduce_scatter x2, waiting for transfers between devices, plane_sum(): lax.psum_scatter(g, 'dp', scatter_dimension=0, tiled=True, axis_index_gro...  32.2 us
    all_to_all x7, starting transfers between devices, exchange(): lax.all_to_all(x, 'dp', split, concat, tiled=True, axis_index_groups=groups)  32 us
    dot_general x5, matrix products, tn(): lax.dot_general(a.astype(bf16), b.astype(bf16), (((0,), (0,)), ((), ())),...  30.4 us
    ppermute x6, waiting for transfers between devices, gather_along(): above = lax.ppermute(above, 'dp', grid.down)  29.2 us
    unnamed x103, local copies, waits for them, and re-layouts  26.6 us
    ppermute x6, waiting for transfers between devices, to_columns_beside(): piece = lax.ppermute(piece, 'dp', pairs)  23.5 us
  transfers between devices with their start and end apart: 75, of which 33 were waited for; matrix products, arithmetic and copies ran while one was open for 36% of the time, Pallas kernels for 6%

profile of v10, /device:TPU:0, one launch (start us, length us, event | category | flops | bytes accessed | tf_op | source)
XLA Modules:
  0.0 535.3 jit_solution(12307128178806119023)
XLA Ops:
  14.3 6.3 %all-to-all-start = ((bf16[128,4,1408]{0,2,1:T(8,128)(2,1)}), bf16[128,4,1408]{0,2,1:T(8,128)(2,1)S(1)}, u32[]{:S(2)}, u32[]{:S(2)}) async-start(bf16[128,4,1408]{0,2,1:T(8,128)(2,1)} %pad_maximum_fusion), calls=%async_computation | async-start | bytes 2883584 | tf_op jit(solution)/shard_map/all_to_all | solution.py:585
  20.7 5.0 multiply_convert_fusion.5
  31.8 6.4 %slot_forward.1 = (bf16[256,1024]{1,0:T(8,128)(2,1)}, f32[256,128]{1,0:T(8,128)}, f32[4,256,128]{2,1,0:T(8,128)}, bf16[2,256,256]{2,1,0:T(8,128)(2,1)}, bf16[2,256,16]{2,1,0:T(8,128)(2,1)}) custom-call(s32[1,3]{1,0:T(1,128)} %starts_ref.3, bf16[256,1024]{1,0:T(8,128)(2,1)} %get-tuple-element.224.q_ref, bf16[256,1024]{1,0:T(8,128)(2,1)} %get-tuple-element.226.k_ref, ...), custom_call_target="tpu_custom_call" | custom-call | flops 4000000000 | bytes 4000000 | tf_op jit(solution)/shard_map/slot_forward/pallas_call | solution.py:383
  38.1 4.8 fusion.24.mine_ref
  42.9 11.9 %all-to-all-done = bf16[128,4,1408]{0,2,1:T(8,128)(2,1)S(1)} async-done(((bf16[128,4,1408]{0,2,1:T(8,128)(2,1)}), bf16[128,4,1408]{0,2,1:T(8,128)(2,1)S(1)}, u32[]{:S(2)}, u32[]{:S(2)}) %all-to-all-start) | async-done | bytes 1441824 | tf_op jit(solution)/shard_map/all_to_all | solution.py:585
  58.1 3.7 fusion.22
  63.5 3.5 all-to-all-start.1
  69.9 3.3 second_norm.1
  73.1 4.6 collective-permute-start.1
  83.1 4.0 all-to-all-done.1
  90.6 5.5 %collective-permute-done.2 = bf16[128,2048]{1,0:T(8,128)(2,1)} collective-permute-done((bf16[128,2048]{1,0:T(8,128)(2,1)}, bf16[128,2048]{1,0:T(8,128)(2,1)}, u32[]{:S(2)}, u32[]{:S(2)}) %collective-permute-start.2) | collective-permute-done | bytes 524320 | tf_op jit(solution)/shard_map/ppermute | solution.py:599
  96.1 4.0 collective-permute-start.5
  101.3 3.4 bitcast_dynamic-update-slice_fusion
  104.7 6.1 %collective-permute-done.5 = bf16[128,2048]{1,0:T(8,128)(2,1)S(1)} collective-permute-done((bf16[128,2048]{1,0:T(8,128)(2,1)}, bf16[128,2048]{1,0:T(8,128)(2,1)S(1)}, u32[]{:S(2)}, u32[]{:S(2)}) %collective-permute-start.5) | collective-permute-done | bytes 524320 | tf_op jit(solution)/shard_map/ppermute | solution.py:598
  110.8 4.0 collective-permute-done.6
  122.1 4.7 collective-permute-done.8
  126.8 4.1 collective-permute-done.9
  137.5 4.3 collective-permute-start.3
  148.6 5.1 fusion.45
  153.7 6.6 %collective-permute-done.4 = bf16[128,2048]{1,0:T(8,128)(2,1)} collective-permute-done((bf16[128,2048]{1,0:T(8,128)(2,1)}, bf16[128,2048]{1,0:T(8,128)(2,1)}, u32[]{:S(2)}, u32[]{:S(2)}) %collective-permute-start.4) | collective-permute-done | bytes 524320 | tf_op jit(solution)/shard_map/ppermute | solution.py:599
  163.9 7.9 %fusion.46 = f32[1024,704]{0,1:T(8,128)} fusion(bf16[1024,2048]{1,0:T(8,128)(2,1)} %select_dynamic-update-slice_fusion.6, bf16[2048,704]{1,0:T(8,128)(2,1)} %all-gather.9.cloned.1.call-done), kind=kOutput, calls=%fused_computation.144 | convolution fusion | flops 2952790016 | bytes 9961472 | tf_op jit(solution)/shard_map/dot_general | solution.py:19
  173.2 4.9 collective-permute-done.18
  181.6 2.7 multiply_convert_fusion.2
  185.3 3.5 fusion.47
  190.2 4.0 collective-permute-done.20
  208.2 9.2 %multiply_convert_fusion.1 = (bf16[1024,704]{0,1:T(8,128)(2,1)S(1)}, bf16[1024,704]{0,1:T(8,128)(2,1)S(1)}) fusion(f32[1024,704]{0,1:T(8,128)} %copy-done.11, f32[1024,704]{0,1:T(8,128)} %fusion.46, bf16[1024,2048]{1,0:T(8,128)(2,1)} %copy-done.34, bf16[2048,704]{0,1:T(8,128)(2,1)} %all-gather.11.cloned.1.call-done), kind=kOutput, calls=%fused_computation.7 | convolution fusion | flops 2962161664 | bytes 15728640 | tf_op jit(solution)/shard_map/dot_general | solution.py:19
  217.5 3.7 fusion.48
  221.2 5.8 %fusion.44 = (bf16[1024,2048]{1,0:T(8,128)(2,1)S(1)}, f32[1024,2048]{1,0:T(8,128)}) fusion(f32[1024,2048]{1,0:T(8,128)S(1)} %fusion.48, bf16[1024,704]{0,1:T(8,128)(2,1)S(1)} %get-tuple-element.195, bf16[2048,704]{1,0:T(8,128)(2,1)S(1)} %copy-done.10), kind=kOutput, calls=%fused_computation.142 | convolution fusion | flops 2956984320 | bytes 25296896 | tf_op jit(solution)/shard_map/dot_general | solution.py:23
  230.5 4.1 all-to-all-start.2
  234.7 2.9 fusion.5
  241.4 6.7 %convolution_convert_fusion.3 = bf16[2048,704]{0,1:T(8,128)(2,1)} fusion(bf16[1024,704]{0,1:T(8,128)(2,1)S(1)} %copy-done.17, bf16[1024,2048]{1,0:T(8,128)(2,1)} %copy-done.34), kind=kOutput, calls=%fused_computation.5 | convolution fusion | flops 2954231808 | bytes 8519680 | tf_op jit(solution)/shard_map/dot_general | solution.py:29
  248.1 9.6 %collective-permute-done.36 = bf16[128,2048]{1,0:T(8,128)(2,1)} collective-permute-done((bf16[128,2048]{1,0:T(8,128)(2,1)}, bf16[128,2048]{1,0:T(8,128)(2,1)}, u32[]{:S(2)}, u32[]{:S(2)}) %collective-permute-start.36) | collective-permute-done | bytes 524320 | tf_op jit(solution)/shard_map/ppermute | solution.py:634
  259.5 2.8 add_convert_fusion.2
  262.4 3.4 collective-permute-start.39
  267.1 6.7 %convolution_convert_fusion.2 = bf16[2048,704]{0,1:T(8,128)(2,1)} fusion(bf16[1024,704]{0,1:T(8,128)(2,1)S(1)} %get-tuple-element.195, bf16[1024,2048]{1,0:T(8,128)(2,1)} %select_dynamic-update-slice_fusion.6), kind=kOutput, calls=%fused_computation.4 | convolution fusion | flops 2954231808 | bytes 8519680 | tf_op jit(solution)/shard_map/dot_general | solution.py:29
  273.7 3.6 collective-permute-done.39
  277.3 4.1 collective-permute-done.40
  281.6 4.1 add_convert_fusion
  285.6 3.4 collective-permute-start.41
  290.6 4.5 convolution_convert_fusion.1
  295.1 4.4 collective-permute-done.41.refs_1_
  299.5 4.0 collective-permute-done.42.refs_2_
  304.3 4.0 second_norm_back.1
  310.5 4.3 convolution_convert_fusion.5.do_ref
  314.8 11.4 %slot_backward.1 = (bf16[256,1024]{1,0:T(8,128)(2,1)}, bf16[256,1024]{1,0:T(8,128)(2,1)}, bf16[256,1024]{1,0:T(8,128)(2,1)}, bf16[256,128]{1,0:T(8,128)(2,1)}, bf16[4,256,896]{2,1,0:T(8,128)(2,1)}) custom-call(s32[1,3]{1,0:T(1,128)} %starts_ref.3, bf16[256,1024]{1,0:T(8,128)(2,1)} %get-tuple-element.224.q_ref, bf16[256,1024]{1,0:T(8,128)(2,1)} %get-tuple-element.226.k_ref, ...), custom_call_target="tpu_custom_call" | custom-call | flops 12000000000 | bytes 8000000 | tf_op jit(solution)/shard_map/slot_backward/pallas_call | solution.py:403
  326.2 4.5 all-to-all-start.3
  331.2 3.8 fusion.16
  348.3 3.0 constant_dynamic-slice_fusion
  352.6 3.3 collective-permute-start.49
  357.6 3.0 collective-permute-done.47
  362.2 6.4 %collective-permute-done.48 = bf16[1,128,704]{1,2,0:T(8,128)(2,1)S(1)} collective-permute-done((bf16[1,128,704]{1,2,0:T(8,128)(2,1)S(1)}, bf16[1,128,704]{1,2,0:T(8,128)(2,1)S(1)}, u32[]{:S(2)}, u32[]{:S(2)}) %collective-permute-start.48) | collective-permute-done | bytes 180256 | tf_op jit(solution)/shard_map/ppermute | solution.py:780
  369.9 14.1 %collective-permute-done.45 = bf16[1,128,704]{1,2,0:T(8,128)(2,1)S(1)} collective-permute-done((bf16[1,128,704]{1,2,0:T(8,128)(2,1)S(1)}, bf16[1,128,704]{1,2,0:T(8,128)(2,1)S(1)}, u32[]{:S(2)}, u32[]{:S(2)}) %collective-permute-start.45) | collective-permute-done | bytes 180256 | tf_op jit(solution)/shard_map/ppermute | solution.py:780
  385.3 9.2 %convolution_convert_fusion = bf16[2048,896]{1,0:T(8,128)(2,1)} fusion(bf16[1024,2048]{1,0:T(8,128)(2,1)} %bitcast.11, bf16[1024,896]{1,0:T(8,128)(2,1)} %bitcast.23), kind=kOutput, calls=%fused_computation.2 | convolution fusion | flops 3759931392 | bytes 9699328 | tf_op jit(solution)/shard_map/dot_general | solution.py:29
  395.7 2.7 collective-permute-done.50.other_ref
  399.3 3.9 first_norm_back.1
  407.0 11.1 %collective-permute-done.53 = bf16[128,2048]{1,0:T(8,128)(2,1)} collective-permute-done((bf16[128,2048]{1,0:T(8,128)(2,1)S(1)}, bf16[128,2048]{1,0:T(8,128)(2,1)}, u32[]{:S(2)}, u32[]{:S(2)}) %collective-permute-start.53) | collective-permute-done | bytes 524320 | tf_op jit(solution)/shard_map/ppermute | solution.py:648
  419.2 10.5 %collective-permute-done.54 = bf16[128,2048]{1,0:T(8,128)(2,1)S(1)} collective-permute-done((bf16[128,2048]{1,0:T(8,128)(2,1)S(1)}, bf16[128,2048]{1,0:T(8,128)(2,1)S(1)}, u32[]{:S(2)}, u32[]{:S(2)}) %collective-permute-start.54) | collective-permute-done | bytes 524320 | tf_op jit(solution)/shard_map/ppermute | solution.py:648
  432.0 5.3 all-to-all-start.7
  440.2 3.4 convolution_convert_fusion.4
  443.6 32.2 %reduce-scatter.13.cloned.1.call-done = bf16[512,896]{1,0:T(8,128)(2,1)} async-done(((bf16[2048,896]{1,0:T(8,128)(2,1)}), bf16[512,896]{1,0:T(8,128)(2,1)}) %reduce-scatter.13.cloned.1.call-update) | async-done | bytes 917520 | tf_op jit(solution)/shard_map/reduce_scatter | solution.py:723
  482.7 8.4 %all-to-all-start.4 = ((f32[16,2,128]{2,1,0:T(2,128)}), f32[16,2,128]{2,1,0:T(2,128)S(1)}, u32[]{:S(2)}, u32[]{:S(2)}) async-start(f32[16,2,128]{2,1,0:T(2,128)} %add_bitcast_fusion), calls=%async_computation.7 | async-start | bytes 32768 | tf_op jit(solution)/shard_map/all_to_all | solution.py:849
  500.1 4.1 all-to-all-start.5
  509.7 6.8 %all-to-all-done.5 = bf16[4,128,896]{1,2,0:T(8,128)(2,1)S(1)} async-done(((bf16[4,128,896]{1,2,0:T(8,128)(2,1)}), bf16[4,128,896]{1,2,0:T(8,128)(2,1)S(1)}, u32[]{:S(2)}, u32[]{:S(2)}) %all-to-all-start.5) | async-done | bytes 917536 | tf_op jit(solution)/shard_map/all_to_all | solution.py:585
  516.7 4.1 all-to-all-start.6
  (315 shorter events, 152.8 us)
Async XLA Ops:
  7.2 50.0 %all-gather.5.cloned.1.call-start = ((), (), s32[]{:S(2)}) async-start(), calls=%async_computation.14 | async-start | bytes 2621440 | tf_op jit(solution)/shard_map/all_gather | solution.py:697
  14.3 40.5 %all-to-all-start = ((bf16[128,4,1408]{0,2,1:T(8,128)(2,1)}), bf16[128,4,1408]{0,2,1:T(8,128)(2,1)S(1)}, u32[]{:S(2)}, u32[]{:S(2)}) async-start(bf16[128,4,1408]{0,2,1:T(8,128)(2,1)} %pad_maximum_fusion), calls=%async_computation | async-start | bytes 2883584 | tf_op jit(solution)/shard_map/all_to_all | solution.py:585
  20.7 110.3 %all-gather.7.cloned.1.call-start = ((), (), s32[]{:S(2)}) async-start(), calls=%async_computation.15 | async-start | bytes 3932160 | tf_op jit(solution)/shard_map/all_gather | solution.py:677
  57.2 103.1 %all-gather.9.cloned.1.call-start = ((), (), s32[]{:S(2)}) async-start(), calls=%async_computation.16 | async-start | bytes 3932160 | tf_op jit(solution)/shard_map/all_gather | solution.py:677
  58.0 43.4 %collective-permute-start.7 = (bf16[4,1,128,2048]{3,2,0,1:T(8,128)(2,1)}, bf16[4,1,128,2048]{3,2,0,1:T(8,128)(2,1)}, u32[]{:S(2)}, u32[]{:S(2)}) collective-permute-start(bf16[4,1,128,2048]{3,2,0,1:T(8,128)(2,1)} %bitcast.145), channel_id=1, source_target_pairs={{0,1},{1,0},{2,3},{3,2},{4,5},{5,4},{6,7},{7,6},{8,9},{9,8},{10,11... | collective-permute-start | bytes 6291464 | tf_op jit(solution)/shard_map/ppermute | solution.py:464
  61.8 7.1 %collective-permute-start = (f32[128,2048]{1,0:T(8,128)S(1)}, f32[128,2048]{1,0:T(8,128)S(1)}, u32[]{:S(2)}, u32[]{:S(2)}) collective-permute-start(f32[128,2048]{1,0:T(8,128)S(1)} %fusion.22), channel_id=1, source_target_pairs={{0,1},{1,0},{2,3},{3,2},{4,5},{5,4},{6,7},{7,6},{8,9},{9,8},{10,11... | collective-permute-start | bytes 3145736 | tf_op jit(solution)/shard_map/ppermute | solution.py:464
  63.5 23.6 %all-to-all-start.1 = ((bf16[128,4,704]{0,2,1:T(8,128)(2,1)}), bf16[128,4,704]{0,2,1:T(8,128)(2,1)S(1)}, u32[]{:S(2)}, u32[]{:S(2)}) async-start(bf16[128,4,704]{0,2,1:T(8,128)(2,1)} %bitcast.6), calls=%async_computation.1 | async-start | bytes 1441792 | tf_op jit(solution)/shard_map/all_to_all | solution.py:585
  67.0 111.1 %all-gather.11.cloned.1.call-start = ((), (), s32[]{:S(2)}) async-start(), calls=%async_computation.17 | async-start | bytes 3604480 | tf_op jit(solution)/shard_map/all_gather | solution.py:677
  73.1 17.5 %collective-permute-start.1 = (bf16[128,2048]{1,0:T(8,128)(2,1)}, bf16[128,2048]{1,0:T(8,128)(2,1)}, u32[]{:S(2)}, u32[]{:S(2)}) collective-permute-start(bf16[128,2048]{1,0:T(8,128)(2,1)} %get-tuple-element.91), channel_id=1, source_target_pairs={{0,8},{2,10},{4,12},{6,14},{8,16},{10,18},{12,20},{14,22},{16,24},... | collective-permute-start | bytes 1572872 | tf_op jit(solution)/shard_map/ppermute | solution.py:598
  77.7 18.3 %collective-permute-start.2 = (bf16[128,2048]{1,0:T(8,128)(2,1)}, bf16[128,2048]{1,0:T(8,128)(2,1)}, u32[]{:S(2)}, u32[]{:S(2)}) collective-permute-start(bf16[128,2048]{1,0:T(8,128)(2,1)} %get-tuple-element.91), channel_id=1, source_target_pairs={{8,0},{10,2},{12,4},{14,6},{16,8},{18,10},{20,12},{22,14},{24,16},... | collective-permute-start | bytes 1572872 | tf_op jit(solution)/shard_map/ppermute | solution.py:599
  96.1 14.8 %collective-permute-start.5 = (bf16[128,2048]{1,0:T(8,128)(2,1)}, bf16[128,2048]{1,0:T(8,128)(2,1)S(1)}, u32[]{:S(2)}, u32[]{:S(2)}) collective-permute-start(bf16[128,2048]{1,0:T(8,128)(2,1)} %collective-permute-done.1), channel_id=1, source_target_pairs={{0,8},{2,10},{4,12},{6,14},{8,16},{10,18},{12,20},{14,22},{16,24},... | collective-permute-start | bytes 1572872 | tf_op jit(solution)/shard_map/ppermute | solution.py:598
  100.0 14.9 %collective-permute-start.6 = (bf16[128,2048]{1,0:T(8,128)(2,1)}, bf16[128,2048]{1,0:T(8,128)(2,1)S(1)}, u32[]{:S(2)}, u32[]{:S(2)}) collective-permute-start(bf16[128,2048]{1,0:T(8,128)(2,1)} %collective-permute-done.2), channel_id=1, source_target_pairs={{8,0},{10,2},{12,4},{14,6},{16,8},{18,10},{20,12},{22,14},{24,16},... | collective-permute-start | bytes 1572872 | tf_op jit(solution)/shard_map/ppermute | solution.py:599
  114.9 11.9 %collective-permute-start.8 = (bf16[128,2048]{1,0:T(8,128)(2,1)S(1)}, bf16[128,2048]{1,0:T(8,128)(2,1)S(1)}, u32[]{:S(2)}, u32[]{:S(2)}) collective-permute-start(bf16[128,2048]{1,0:T(8,128)(2,1)S(1)} %collective-permute-done.5), channel_id=1, source_target_pairs={{0,8},{2,10},{4,12},{6,14},{8,16},{10,18},{12,20},{14,22},{16,24},... | collective-permute-start | bytes 1572872 | tf_op jit(solution)/shard_map/ppermute | solution.py:598
  117.3 13.6 %collective-permute-start.9 = (bf16[128,2048]{1,0:T(8,128)(2,1)S(1)}, bf16[128,2048]{1,0:T(8,128)(2,1)S(1)}, u32[]{:S(2)}, u32[]{:S(2)}) collective-permute-start(bf16[128,2048]{1,0:T(8,128)(2,1)S(1)} %collective-permute-done.6), channel_id=1, source_target_pairs={{8,0},{10,2},{12,4},{14,6},{16,8},{18,10},{20,12},{22,14},{24,16},... | collective-permute-start | bytes 1572872 | tf_op jit(solution)/shard_map/ppermute | solution.py:599
  118.8 16.1 %collective-permute-start.10 = (bf16[128,2048]{1,0:T(8,128)(2,1)S(1)}, bf16[128,2048]{1,0:T(8,128)(2,1)}, u32[]{:S(2)}, u32[]{:S(2)}) collective-permute-start(bf16[128,2048]{1,0:T(8,128)(2,1)S(1)} %copy-done.29), channel_id=1, source_target_pairs={{0,1},{1,0},{2,3},{3,2},{4,5},{5,4},{6,7},{7,6},{8,9},{9,8},{10,11... | collective-permute-start | bytes 1572872 | tf_op jit(solution)/shard_map/ppermute | solution.py:464
  119.7 17.8 %collective-permute-start.11 = (bf16[128,2048]{1,0:T(8,128)(2,1)}, bf16[128,2048]{1,0:T(8,128)(2,1)}, u32[]{:S(2)}, u32[]{:S(2)}) collective-permute-start(bf16[128,2048]{1,0:T(8,128)(2,1)} %collective-permute-done.2), channel_id=1, source_target_pairs={{0,1},{1,0},{2,3},{3,2},{4,5},{5,4},{6,7},{7,6},{8,9},{9,8},{10,11... | collective-permute-start | bytes 1572872 | tf_op jit(solution)/shard_map/ppermute | solution.py:464
  120.2 27.5 %collective-permute-start.16 = (bf16[128,2048]{1,0:T(8,128)(2,1)}, bf16[128,2048]{1,0:T(8,128)(2,1)}, u32[]{:S(2)}, u32[]{:S(2)}) collective-permute-start(bf16[128,2048]{1,0:T(8,128)(2,1)} %collective-permute-done.1), channel_id=1, source_target_pairs={{0,1},{1,0},{2,3},{3,2},{4,5},{5,4},{6,7},{7,6},{8,9},{9,8},{10,11... | collective-permute-start | bytes 1572872 | tf_op jit(solution)/shard_map/ppermute | solution.py:464
  120.2 139.2 %reduce-scatter.7.cloned.1.call-start = ((), (), s32[]{:S(2)}) async-start(), calls=%async_computation.18 | async-start | bytes 2621440 | tf_op jit(solution)/shard_map/reduce_scatter | solution.py:758
  126.8 17.0 %collective-permute-start.13 = (bf16[128,2048]{1,0:T(8,128)(2,1)S(1)}, bf16[128,2048]{1,0:T(8,128)(2,1)}, u32[]{:S(2)}, u32[]{:S(2)}) collective-permute-start(bf16[128,2048]{1,0:T(8,128)(2,1)S(1)} %collective-permute-done.6), channel_id=1, source_target_pairs={{0,1},{1,0},{2,3},{3,2},{4,5},{5,4},{6,7},{7,6},{8,9},{9,8},{10,11... | collective-permute-start | bytes 1572872 | tf_op jit(solution)/shard_map/ppermute | solution.py:464
  131.0 10.8 %collective-permute-start.12 = (bf16[128,2048]{1,0:T(8,128)(2,1)S(1)}, bf16[128,2048]{1,0:T(8,128)(2,1)S(1)}, u32[]{:S(2)}, u32[]{:S(2)}) collective-permute-start(bf16[128,2048]{1,0:T(8,128)(2,1)S(1)} %collective-permute-done.8), channel_id=1, source_target_pairs={{0,1},{1,0},{2,3},{3,2},{4,5},{5,4},{6,7},{7,6},{8,9},{9,8},{10,11... | collective-permute-start | bytes 1572872 | tf_op jit(solution)/shard_map/ppermute | solution.py:464
  134.8 10.3 %collective-permute-start.14 = (bf16[128,2048]{1,0:T(8,128)(2,1)S(1)}, bf16[128,2048]{1,0:T(8,128)(2,1)S(1)}, u32[]{:S(2)}, u32[]{:S(2)}) collective-permute-start(bf16[128,2048]{1,0:T(8,128)(2,1)S(1)} %collective-permute-done.5), channel_id=1, source_target_pairs={{0,1},{1,0},{2,3},{3,2},{4,5},{5,4},{6,7},{7,6},{8,9},{9,8},{10,11... | collective-permute-start | bytes 1572872 | tf_op jit(solution)/shard_map/ppermute | solution.py:464
  137.5 16.2 %collective-permute-start.3 = (bf16[128,2048]{1,0:T(8,128)(2,1)}, bf16[128,2048]{1,0:T(8,128)(2,1)}, u32[]{:S(2)}, u32[]{:S(2)}) collective-permute-start(bf16[128,2048]{1,0:T(8,128)(2,1)} %cotangent_rows.1), channel_id=1, source_target_pairs={{0,8},{2,10},{4,12},{6,14},{8,16},{10,18},{12,20},{14,22},{16,24},... | collective-permute-start | bytes 1572872 | tf_op jit(solution)/shard_map/ppermute | solution.py:598
  141.8 5.9 %collective-permute-start.15 = (bf16[128,2048]{1,0:T(8,128)(2,1)S(1)}, bf16[128,2048]{1,0:T(8,128)(2,1)S(1)}, u32[]{:S(2)}, u32[]{:S(2)}) collective-permute-start(bf16[128,2048]{1,0:T(8,128)(2,1)S(1)} %collective-permute-done.9), channel_id=1, source_target_pairs={{0,1},{1,0},{2,3},{3,2},{4,5},{5,4},{6,7},{7,6},{8,9},{9,8},{10,11... | collective-permute-start | bytes 1572872 | tf_op jit(solution)/shard_map/ppermute | solution.py:464
  143.8 16.5 %collective-permute-start.4 = (bf16[128,2048]{1,0:T(8,128)(2,1)}, bf16[128,2048]{1,0:T(8,128)(2,1)}, u32[]{:S(2)}, u32[]{:S(2)}) collective-permute-start(bf16[128,2048]{1,0:T(8,128)(2,1)} %cotangent_rows.1), channel_id=1, source_target_pairs={{8,0},{10,2},{12,4},{14,6},{16,8},{18,10},{20,12},{22,14},{24,16},... | collective-permute-start | bytes 1572872 | tf_op jit(solution)/shard_map/ppermute | solution.py:599
  145.1 53.0 %collective-permute-start.25 = (bf16[128,2048]{1,0:T(8,128)(2,1)}, bf16[128,2048]{1,0:T(8,128)(2,1)}, u32[]{:S(2)}, u32[]{:S(2)}) collective-permute-start(bf16[128,2048]{1,0:T(8,128)(2,1)} %cotangent_rows.1), channel_id=1, source_target_pairs={{0,1},{1,0},{2,3},{3,2},{4,5},{5,4},{6,7},{7,6},{8,9},{9,8},{10,11... | collective-permute-start | bytes 1572872 | tf_op jit(solution)/shard_map/ppermute | solution.py:464
  160.3 12.9 %collective-permute-start.17 = (bf16[128,2048]{1,0:T(8,128)(2,1)}, bf16[128,2048]{1,0:T(8,128)(2,1)}, u32[]{:S(2)}, u32[]{:S(2)}) collective-permute-start(bf16[128,2048]{1,0:T(8,128)(2,1)} %collective-permute-done.3), channel_id=1, source_target_pairs={{0,8},{2,10},{4,12},{6,14},{8,16},{10,18},{12,20},{14,22},{16,24},... | collective-permute-start | bytes 1572872 | tf_op jit(solution)/shard_map/ppermute | solution.py:598
  162.6 15.5 %collective-permute-start.18 = (bf16[128,2048]{1,0:T(8,128)(2,1)}, bf16[128,2048]{1,0:T(8,128)(2,1)}, u32[]{:S(2)}, u32[]{:S(2)}) collective-permute-start(bf16[128,2048]{1,0:T(8,128)(2,1)} %collective-permute-done.4), channel_id=1, source_target_pairs={{8,0},{10,2},{12,4},{14,6},{16,8},{18,10},{20,12},{22,14},{24,16},... | collective-permute-start | bytes 1572872 | tf_op jit(solution)/shard_map/ppermute | solution.py:599
  178.1 12.1 %collective-permute-start.19 = (bf16[128,2048]{1,0:T(8,128)(2,1)}, bf16[128,2048]{1,0:T(8,128)(2,1)S(1)}, u32[]{:S(2)}, u32[]{:S(2)}) collective-permute-start(bf16[128,2048]{1,0:T(8,128)(2,1)} %collective-permute-done.17), channel_id=1, source_target_pairs={{0,8},{2,10},{4,12},{6,14},{8,16},{10,18},{12,20},{14,22},{16,24},... | collective-permute-start | bytes 1572872 | tf_op jit(solution)/shard_map/ppermute | solution.py:598
  179.8 14.4 %collective-permute-start.20 = (bf16[128,2048]{1,0:T(8,128)(2,1)}, bf16[128,2048]{1,0:T(8,128)(2,1)S(1)}, u32[]{:S(2)}, u32[]{:S(2)}) collective-permute-start(bf16[128,2048]{1,0:T(8,128)(2,1)} %collective-permute-done.18), channel_id=1, source_target_pairs={{8,0},{10,2},{12,4},{14,6},{16,8},{18,10},{20,12},{22,14},{24,16},... | collective-permute-start | bytes 1572872 | tf_op jit(solution)/shard_map/ppermute | solution.py:599
  199.3 6.2 %collective-permute-start.31 = (bf16[128,2048]{1,0:T(8,128)(2,1)}, bf16[128,2048]{1,0:T(8,128)(2,1)S(1)}, u32[]{:S(2)}, u32[]{:S(2)}) collective-permute-start(bf16[128,2048]{1,0:T(8,128)(2,1)} %collective-permute-done.3), channel_id=1, source_target_pairs={{0,1},{1,0},{2,3},{3,2},{4,5},{5,4},{6,7},{7,6},{8,9},{9,8},{10,11... | collective-permute-start | bytes 1572872 | tf_op jit(solution)/shard_map/ppermute | solution.py:464
  199.8 5.3 collective-permute-start.28
  228.6 6.1 %collective-permute-start.32 = (bf16[128,2048]{1,0:T(8,128)(2,1)}, bf16[128,2048]{1,0:T(8,128)(2,1)}, u32[]{:S(2)}, u32[]{:S(2)}) collective-permute-start(bf16[128,2048]{1,0:T(8,128)(2,1)} %get-tuple-element.200), channel_id=1, source_target_pairs={{0,1},{1,0},{2,3},{3,2},{4,5},{5,4},{6,7},{7,6},{8,9},{9,8},{10,11... | collective-permute-start | bytes 1572872 | tf_op jit(solution)/shard_map/ppermute | solution.py:464
  228.6 6.1 %collective-permute-start.33 = (bf16[128,2048]{1,0:T(8,128)(2,1)}, bf16[128,2048]{1,0:T(8,128)(2,1)S(1)}, u32[]{:S(2)}, u32[]{:S(2)}) collective-permute-start(bf16[128,2048]{1,0:T(8,128)(2,1)} %get-tuple-element.199), channel_id=1, source_target_pairs={{0,1},{1,0},{2,3},{3,2},{4,5},{5,4},{6,7},{7,6},{8,9},{9,8},{10,11... | collective-permute-start | bytes 1572872 | tf_op jit(solution)/shard_map/ppermute | solution.py:464
  229.1 5.7 %collective-permute-start.34 = (bf16[128,2048]{1,0:T(8,128)(2,1)}, bf16[128,2048]{1,0:T(8,128)(2,1)S(1)}, u32[]{:S(2)}, u32[]{:S(2)}) collective-permute-start(bf16[128,2048]{1,0:T(8,128)(2,1)} %get-tuple-element.198), channel_id=1, source_target_pairs={{0,1},{1,0},{2,3},{3,2},{4,5},{5,4},{6,7},{7,6},{8,9},{9,8},{10,11... | collective-permute-start | bytes 1572872 | tf_op jit(solution)/shard_map/ppermute | solution.py:464
  229.1 5.6 %collective-permute-start.35 = (bf16[128,2048]{1,0:T(8,128)(2,1)}, bf16[128,2048]{1,0:T(8,128)(2,1)S(1)}, u32[]{:S(2)}, u32[]{:S(2)}) collective-permute-start(bf16[128,2048]{1,0:T(8,128)(2,1)} %get-tuple-element.197), channel_id=1, source_target_pairs={{0,1},{1,0},{2,3},{3,2},{4,5},{5,4},{6,7},{7,6},{8,9},{9,8},{10,11... | collective-permute-start | bytes 1572872 | tf_op jit(solution)/shard_map/ppermute | solution.py:464
  230.5 17.6 %all-to-all-start.2 = ((bf16[4,256,256]{2,1,0:T(8,128)(2,1)}), bf16[4,256,256]{2,1,0:T(8,128)(2,1)}, u32[]{:S(2)}, u32[]{:S(2)}) async-start(bf16[4,256,256]{2,1,0:T(8,128)(2,1)} %pad_maximum_fusion.1), calls=%async_computation.3 | async-start | bytes 1048576 | tf_op jit(solution)/shard_map/all_to_all | solution.py:585
  234.6 80.2 %reduce-scatter.9.cloned.1.call-start = ((), (), s32[]{:S(2)}) async-start(), calls=%async_computation.19 | async-start | bytes 3604480 | tf_op jit(solution)/shard_map/reduce_scatter | solution.py:763
  237.7 20.0 %collective-permute-start.36 = (bf16[128,2048]{1,0:T(8,128)(2,1)}, bf16[128,2048]{1,0:T(8,128)(2,1)}, u32[]{:S(2)}, u32[]{:S(2)}) collective-permute-start(bf16[128,2048]{1,0:T(8,128)(2,1)} %get-tuple-element.194), channel_id=1, source_target_pairs={{0,8},{2,10},{4,12},{6,14},{8,16},{10,18},{12,20},{14,22},{16,24},... | collective-permute-start | bytes 1572872 | tf_op jit(solution)/shard_map/ppermute | solution.py:634
  240.1 19.3 %collective-permute-start.37 = (bf16[128,2048]{1,0:T(8,128)(2,1)}, bf16[128,2048]{1,0:T(8,128)(2,1)}, u32[]{:S(2)}, u32[]{:S(2)}) collective-permute-start(bf16[128,2048]{1,0:T(8,128)(2,1)} %get-tuple-element.193), channel_id=1, source_target_pairs={{8,0},{10,2},{12,4},{14,6},{16,8},{18,10},{20,12},{22,14},{24,16},... | collective-permute-start | bytes 1572872 | tf_op jit(solution)/shard_map/ppermute | solution.py:635
  259.5 86.9 %reduce-scatter.11.cloned.1.call-start = ((), (), s32[]{:S(2)}) async-start(), calls=%async_computation.20 | async-start | bytes 3604480 | tf_op jit(solution)/shard_map/reduce_scatter | solution.py:763
  262.4 15.0 %collective-permute-start.39 = (bf16[128,2048]{1,0:T(8,128)(2,1)}, bf16[128,2048]{1,0:T(8,128)(2,1)S(1)}, u32[]{:S(2)}, u32[]{:S(2)}) collective-permute-start(bf16[128,2048]{1,0:T(8,128)(2,1)} %get-tuple-element.189), channel_id=1, source_target_pairs={{0,8},{2,10},{4,12},{6,14},{8,16},{10,18},{12,20},{14,22},{16,24},... | collective-permute-start | bytes 1572872 | tf_op jit(solution)/shard_map/ppermute | solution.py:634
  265.8 15.7 %collective-permute-start.40 = (bf16[128,2048]{1,0:T(8,128)(2,1)}, bf16[128,2048]{1,0:T(8,128)(2,1)}, u32[]{:S(2)}, u32[]{:S(2)}) collective-permute-start(bf16[128,2048]{1,0:T(8,128)(2,1)} %get-tuple-element.188), channel_id=1, source_target_pairs={{8,0},{10,2},{12,4},{14,6},{16,8},{18,10},{20,12},{22,14},{24,16},... | collective-permute-start | bytes 1572872 | tf_op jit(solution)/shard_map/ppermute | solution.py:635
  281.5 148.4 %reduce-scatter.17.cloned.1.call-start = ((), (), s32[]{:S(2)}) async-start(), calls=%async_computation.23 | async-start | bytes 3604480 | tf_op jit(solution)/shard_map/reduce_scatter | solution.py:763
  285.6 13.8 %collective-permute-start.41 = (bf16[128,2048]{1,0:T(8,128)(2,1)}, bf16[128,2048]{1,0:T(8,128)(2,1)S(1)}, u32[]{:S(2)}, u32[]{:S(2)}) collective-permute-start(bf16[128,2048]{1,0:T(8,128)(2,1)} %get-tuple-element.191), channel_id=1, source_target_pairs={{0,8},{2,10},{4,12},{6,14},{8,16},{10,18},{12,20},{14,22},{16,24},... | collective-permute-start | bytes 1572872 | tf_op jit(solution)/shard_map/ppermute | solution.py:634
  289.1 14.4 %collective-permute-start.42 = (bf16[128,2048]{1,0:T(8,128)(2,1)}, bf16[128,2048]{1,0:T(8,128)(2,1)S(1)}, u32[]{:S(2)}, u32[]{:S(2)}) collective-permute-start(bf16[128,2048]{1,0:T(8,128)(2,1)} %get-tuple-element.190), channel_id=1, source_target_pairs={{8,0},{10,2},{12,4},{14,6},{16,8},{18,10},{20,12},{22,14},{24,16},... | collective-permute-start | bytes 1572872 | tf_op jit(solution)/shard_map/ppermute | solution.py:635
  326.2 59.1 %all-to-all-start.3 = ((bf16[4,256,896]{2,1,0:T(8,128)(2,1)}), bf16[4,256,896]{2,1,0:T(8,128)(2,1)}, u32[]{:S(2)}, u32[]{:S(2)}) async-start(bf16[4,256,896]{2,1,0:T(8,128)(2,1)} %get-tuple-element.142), calls=%async_computation.5 | async-start | bytes 3670016 | tf_op jit(solution)/shard_map/all_to_all | solution.py:585
  330.8 145.1 %reduce-scatter.13.cloned.1.call-start = ((), (), s32[]{:S(2)}) async-start(), calls=%async_computation.21 | async-start | bytes 4587520 | tf_op jit(solution)/shard_map/reduce_scatter | solution.py:723
  351.3 9.4 %collective-permute-start.47 = (bf16[1,128,704]{1,2,0:T(8,128)(2,1)S(1)}, bf16[1,128,704]{1,2,0:T(8,128)(2,1)S(1)}, u32[]{:S(2)}, u32[]{:S(2)}) collective-permute-start(bf16[1,128,704]{1,2,0:T(8,128)(2,1)S(1)} %copy.97), channel_id=1, source_target_pairs={{0,8},{2,10},{4,12},{6,14},{8,0},{10,2},{12,4},{14,6},{16,24},{18,... | collective-permute-start | bytes 540680 | tf_op jit(solution)/shard_map/ppermute | solution.py:780
  352.5 16.1 %collective-permute-start.48 = (bf16[1,128,704]{1,2,0:T(8,128)(2,1)S(1)}, bf16[1,128,704]{1,2,0:T(8,128)(2,1)S(1)}, u32[]{:S(2)}, u32[]{:S(2)}) collective-permute-start(bf16[1,128,704]{1,2,0:T(8,128)(2,1)S(1)} %copy.98), channel_id=1, source_target_pairs={{0,16},{2,18},{4,20},{6,22},{8,24},{10,26},{12,28},{14,30},{16,0},... | collective-permute-start | bytes 540680 | tf_op jit(solution)/shard_map/ppermute | solution.py:780
  352.6 16.0 %collective-permute-start.49 = (bf16[1,128,704]{1,2,0:T(8,128)(2,1)S(1)}, bf16[1,128,704]{1,2,0:T(8,128)(2,1)S(1)}, u32[]{:S(2)}, u32[]{:S(2)}) collective-permute-start(bf16[1,128,704]{1,2,0:T(8,128)(2,1)S(1)} %copy.99), channel_id=1, source_target_pairs={{0,24},{2,26},{4,28},{6,30},{8,16},{10,18},{12,20},{14,22},{16,8},... | collective-permute-start | bytes 540680 | tf_op jit(solution)/shard_map/ppermute | solution.py:780
  355.9 14.0 %collective-permute-start.44 = (bf16[1,128,704]{1,2,0:T(8,128)(2,1)S(1)}, bf16[1,128,704]{1,2,0:T(8,128)(2,1)S(1)}, u32[]{:S(2)}, u32[]{:S(2)}) collective-permute-start(bf16[1,128,704]{1,2,0:T(8,128)(2,1)S(1)} %copy.93), channel_id=1, source_target_pairs={{0,8},{2,10},{4,12},{6,14},{8,0},{10,2},{12,4},{14,6},{16,24},{18,... | collective-permute-start | bytes 540680 | tf_op jit(solution)/shard_map/ppermute | solution.py:780
  356.3 27.7 %collective-permute-start.45 = (bf16[1,128,704]{1,2,0:T(8,128)(2,1)S(1)}, bf16[1,128,704]{1,2,0:T(8,128)(2,1)S(1)}, u32[]{:S(2)}, u32[]{:S(2)}) collective-permute-start(bf16[1,128,704]{1,2,0:T(8,128)(2,1)S(1)} %copy.94), channel_id=1, source_target_pairs={{0,16},{2,18},{4,20},{6,22},{8,24},{10,26},{12,28},{14,30},{16,0},... | collective-permute-start | bytes 540680 | tf_op jit(solution)/shard_map/ppermute | solution.py:780
  360.7 23.4 %collective-permute-start.46 = (bf16[1,128,704]{1,2,0:T(8,128)(2,1)S(1)}, bf16[1,128,704]{1,2,0:T(8,128)(2,1)S(1)}, u32[]{:S(2)}, u32[]{:S(2)}) collective-permute-start(bf16[1,128,704]{1,2,0:T(8,128)(2,1)S(1)} %copy.95), channel_id=1, source_target_pairs={{0,24},{2,26},{4,28},{6,30},{8,16},{10,18},{12,20},{14,22},{16,8},... | collective-permute-start | bytes 540680 | tf_op jit(solution)/shard_map/ppermute | solution.py:780
  403.2 14.9 %collective-permute-start.53 = (bf16[128,2048]{1,0:T(8,128)(2,1)S(1)}, bf16[128,2048]{1,0:T(8,128)(2,1)}, u32[]{:S(2)}, u32[]{:S(2)}) collective-permute-start(bf16[128,2048]{1,0:T(8,128)(2,1)S(1)} %copy-done.15), channel_id=1, source_target_pairs={{0,2},{2,0},{4,6},{6,4},{8,10},{10,8},{12,14},{14,12},{16,18},{18,... | collective-permute-start | bytes 1572872 | tf_op jit(solution)/shard_map/ppermute | solution.py:648
  404.7 24.9 %collective-permute-start.54 = (bf16[128,2048]{1,0:T(8,128)(2,1)S(1)}, bf16[128,2048]{1,0:T(8,128)(2,1)S(1)}, u32[]{:S(2)}, u32[]{:S(2)}) collective-permute-start(bf16[128,2048]{1,0:T(8,128)(2,1)S(1)} %copy-done.15), channel_id=1, source_target_pairs={{0,4},{2,6},{4,0},{6,2},{8,12},{10,14},{12,8},{14,10},{16,20},{18,... | collective-permute-start | bytes 1572872 | tf_op jit(solution)/shard_map/ppermute | solution.py:648
  406.2 23.5 %collective-permute-start.55 = (bf16[128,2048]{1,0:T(8,128)(2,1)S(1)}, bf16[128,2048]{1,0:T(8,128)(2,1)S(1)}, u32[]{:S(2)}, u32[]{:S(2)}) collective-permute-start(bf16[128,2048]{1,0:T(8,128)(2,1)S(1)} %copy-done.15), channel_id=1, source_target_pairs={{0,6},{2,4},{4,2},{6,0},{8,14},{10,12},{12,10},{14,8},{16,22},{18,... | collective-permute-start | bytes 1572872 | tf_op jit(solution)/shard_map/ppermute | solution.py:648
  429.8 8.6 %collective-permute-start.56 = (bf16[4,1,128,2048]{3,2,1,0:T(8,128)(2,1)S(1)}, bf16[4,1,128,2048]{3,2,1,0:T(8,128)(2,1)}, u32[]{:S(2)}, u32[]{:S(2)}) collective-permute-start(bf16[4,1,128,2048]{3,2,1,0:T(8,128)(2,1)S(1)} %bitcast_dynamic-update-slice_fusion.1), channel_id=1, source_target_pairs={{0,1},{1,0},{2,3},{3,2},{4,5},{5,4},{6,7},{7,6},{8,9},{9,8},{10,11... | collective-permute-start | bytes 6291464 | tf_op jit(solution)/shard_map/ppermute | solution.py:464
  432.0 50.7 %all-to-all-start.7 = ((bf16[4,128,704]{1,2,0:T(8,128)(2,1)}), bf16[4,128,704]{1,2,0:T(8,128)(2,1)}, u32[]{:S(2)}, u32[]{:S(2)}) async-start(bf16[4,128,704]{1,2,0:T(8,128)(2,1)} %copy_bitcast_fusion.1), calls=%async_computation.13 | async-start | bytes 1441792 | tf_op jit(solution)/shard_map/all_to_all | solution.py:585
  437.3 79.3 %reduce-scatter.15.cloned.1.call-start = ((), (), s32[]{:S(2)}) async-start(), calls=%async_computation.22 | async-start | bytes 1310720 | tf_op jit(solution)/shard_map/reduce_scatter | solution.py:723
  478.4 12.7 %collective-permute-start.38 = (bf16[128,2048]{1,0:T(8,128)(2,1)}, bf16[128,2048]{1,0:T(8,128)(2,1)}, u32[]{:S(2)}, u32[]{:S(2)}) collective-permute-start(bf16[128,2048]{1,0:T(8,128)(2,1)} %block_result.1), channel_id=1, source_target_pairs={{0,1},{1,0},{2,3},{3,2},{4,5},{5,4},{6,7},{7,6},{8,9},{9,8},{10,11... | collective-permute-start | bytes 1572872 | tf_op jit(solution)/shard_map/ppermute | solution.py:464
  479.0 28.4 %collective-permute-start.51 = (f32[128,2048]{1,0:T(8,128)}, f32[128,2048]{1,0:T(8,128)}, u32[]{:S(2)}, u32[]{:S(2)}) collective-permute-start(f32[128,2048]{1,0:T(8,128)} %get-tuple-element.151), channel_id=1, source_target_pairs={{0,1},{1,0},{2,3},{3,2},{4,5},{5,4},{6,7},{7,6},{8,9},{9,8},{10,11... | collective-permute-start | bytes 3145736 | tf_op jit(solution)/shard_map/ppermute | solution.py:464
  482.7 17.5 %all-to-all-start.4 = ((f32[16,2,128]{2,1,0:T(2,128)}), f32[16,2,128]{2,1,0:T(2,128)S(1)}, u32[]{:S(2)}, u32[]{:S(2)}) async-start(f32[16,2,128]{2,1,0:T(2,128)} %add_bitcast_fusion), calls=%async_computation.7 | async-start | bytes 32768 | tf_op jit(solution)/shard_map/all_to_all | solution.py:849
  500.1 16.4 %all-to-all-start.5 = ((bf16[4,128,896]{1,2,0:T(8,128)(2,1)}), bf16[4,128,896]{1,2,0:T(8,128)(2,1)S(1)}, u32[]{:S(2)}, u32[]{:S(2)}) async-start(bf16[4,128,896]{1,2,0:T(8,128)(2,1)} %copy.82), calls=%async_computation.9 | async-start | bytes 1835008 | tf_op jit(solution)/shard_map/all_to_all | solution.py:585
  516.7 9.7 %all-to-all-start.6 = ((bf16[4,128,256]{2,1,0:T(8,128)(2,1)}), bf16[4,128,256]{2,1,0:T(8,128)(2,1)}, u32[]{:S(2)}, u32[]{:S(2)}) async-start(bf16[4,128,256]{2,1,0:T(8,128)(2,1)} %bitcast.152), calls=%async_computation.11 | async-start | bytes 524288 | tf_op jit(solution)/shard_map/all_to_all | solution.py:585
  (53 other events, 372.9 us)
Sparse Core Ops, SparseCore 0:
  11.4 37.9 all-gather.4
  57.3 35.2 all-gather.6
  94.8 36.1 all-gather.8
  133.0 33.9 all-gather.10
  208.3 46.9 reduce-scatter.6
  259.6 32.4 reduce-scatter.8
  294.4 32.3 reduce-scatter.10
  329.0 48.6 reduce-scatter.16
  394.6 81.1 reduce-scatter.12
  478.0 30.2 reduce-scatter.14

commit v11 on v10

--- a/solution.py
+++ b/solution.py
@@ -785,15 +785,11 @@
     gate_grad = (inner_grad * up_act * silu_slope(gate_act)).astype(bf16)
     up_grad = (inner_grad * jax.nn.silu(gate_act)).astype(bf16)
     inner_act = gated(gate_act, up_act)
-    back_parts, (down_rows, out_sum, mixed_plane, gate_rows, up_rows) = scatter_along(
+    back_parts, (down_rows, out_sum, gate_rows, up_rows) = scatter_along(
         add_other_core(*by_core(nt(gate_grad, full_gate) + nt(up_grad, full_up)), grid),
         grid,
         (
-            (
-                tn(cot_all, inner_act).astype(bf16),
-                out_sum,
-                plane_columns(jnp.stack(jnp.split(mixed, INNER, axis=1))),
-            ),
+            (tn(cot_all, inner_act).astype(bf16), out_sum),
             (tn(tokens, gate_grad).astype(bf16),),
             (tn(tokens, up_grad).astype(bf16),),
         ),
@@ -825,9 +821,15 @@
     input_grad, attn_gain_part = first_norm_back(
         block_in, hidden_grad, attn_gain, part_mine, swap(part_other), core
     )
-    _, low_half, attn_gain_part = tie(pre_grad, low_half, attn_gain_part)
+    _, low_half, attn_gain_part, mixed = tie(pre_grad, low_half, attn_gain_part, mixed)
+    mixed_plane = plane_columns(jnp.stack(jnp.split(mixed, INNER, axis=1)))
     low_plane = plane_tokens(plane_gather(low_half, grid, inner))
-    sums, output_grad = tie(plane_sum(pre_grad), plane_product(low_plane, mixed_plane))
+    gains = jnp.concatenate([attn_gain_part, mlp_gain_part], axis=0)
+    gains = gains + swap(gains)
+    gains = jnp.swapaxes(gains.reshape(2, grid.dp, -1), 0, 1)
+    gains = jnp.sum(lax.all_to_all(gains, "dp", 0, 0, tiled=True), axis=0)
+    output_grad, gains = tie(plane_product(low_plane, mixed_plane), gains)
+    sums, output_grad = tie(plane_sum(pre_grad), output_grad)
     output_sum = plane_sum(output_grad)
     result = block_result(block_in, hidden, [out_sum], core, grid)
     result = join(result, swap(result), core)
@@ -842,11 +844,6 @@
     )
 
     input_grad = join(input_grad, swap(input_grad), core)
-
-    gains = jnp.concatenate([attn_gain_part, mlp_gain_part], axis=0)
-    gains = gains + swap(gains)
-    gains = jnp.swapaxes(gains.reshape(2, grid.dp, -1), 0, 1)
-    gains = jnp.sum(lax.all_to_all(gains, "dp", 0, 0, tiled=True), axis=0)
 
     return (
         result,

time: 546 us -> 534 us (0.978)
  waiting for transfers between devices: 180 us -> 174 us
    reduce_scatter x2, waiting for transfers between devices: 32.2 us -> 0.02 us  [plane_sum(): lax.psum_scatter(g, 'dp', scatter_dimension=0, tiled=True, axis_index_gro...]
    all_to_all x7, waiting for transfers between devices: 22.7 us -> 32 us  [exchange(): lax.all_to_all(x, 'dp', split, concat, tiled=True, axis_index_groups=groups)]
    all_to_all x1, waiting for transfers between devices: 0.01 us -> 5.85 us  [on_device(): gains = jnp.sum(lax.all_to_all(gains, 'dp', 0, 0, tiled=True), axis=0)]
    ppermute x3, waiting for transfers between devices: 17.6 us -> 23.1 us  [scatter_along(): up = lax.ppermute(up.astype(bf16), 'dp', grid.up)]
    unnamed x103 -> x107, local copies, waits for them, and re-layouts: 26.6 us -> 25.8 us
  transfers between devices with their start and end apart: 75 -> 75, of which waited for: 33 -> 40; matrix products, arithmetic and copies ran while one was open for 36% -> 37% of each run, Pallas kernels for 6% -> 6%
where the time goes in v11:
time: 534 us; the launch traced here: 524 us
  waiting for transfers between devices  174 us (33%)
  matrix products  102 us (19%)
  starting transfers between devices  94.9 us (18%)
  local copies, waits for them, and re-layouts  69.6 us (13%)
  other arithmetic  34.9 us (7%)
  Pallas kernels  33.2 us (6%)
  between operations  15.7 us (3%)
    dot_general x8, matrix products, nn(): return jnp.dot(a.astype(bf16), b.astype(bf16), preferred_element_type=f32)  37.6 us
    dot_general x13, matrix products, nt(): lax.dot_general(a.astype(bf16), b.astype(bf16), (((1,), (1,)), ((), ())),...  34 us
    all_to_all x7, waiting for transfers between devices, exchange(): lax.all_to_all(x, 'dp', split, concat, tiled=True, axis_index_groups=groups)  32 us
    all_to_all x7, starting transfers between devices, exchange(): lax.all_to_all(x, 'dp', split, concat, tiled=True, axis_index_groups=groups)  30.4 us
    dot_general x5, matrix products, tn(): lax.dot_general(a.astype(bf16), b.astype(bf16), (((0,), (0,)), ((), ())),...  30 us
    ppermute x6, waiting for transfers between devices, gather_along(): above = lax.ppermute(above, 'dp', grid.down)  29.2 us
    unnamed x107, local copies, waits for them, and re-layouts  25.8 us
    ppermute x6, waiting for transfers between devices, to_columns_beside(): piece = lax.ppermute(piece, 'dp', pairs)  24.1 us
  transfers between devices with their start and end apart: 75, of which 40 were waited for; matrix products, arithmetic and copies ran while one was open for 37% of the time, Pallas kernels for 6%

profile of v11, /device:TPU:0, one launch (start us, length us, event | category | flops | bytes accessed | tf_op | source)
XLA Modules:
  0.0 523.8 jit_solution(15167339203414283147)
XLA Ops:
  14.3 6.3 %all-to-all-start = ((bf16[128,4,1408]{0,2,1:T(8,128)(2,1)}), bf16[128,4,1408]{0,2,1:T(8,128)(2,1)S(1)}, u32[]{:S(2)}, u32[]{:S(2)}) async-start(bf16[128,4,1408]{0,2,1:T(8,128)(2,1)} %pad_maximum_fusion), calls=%async_computation | async-start | bytes 2883584 | tf_op jit(solution)/shard_map/all_to_all | solution.py:585
  20.7 5.0 multiply_convert_fusion.5
  31.8 6.4 %slot_forward.1 = (bf16[256,1024]{1,0:T(8,128)(2,1)}, f32[256,128]{1,0:T(8,128)}, f32[4,256,128]{2,1,0:T(8,128)}, bf16[2,256,256]{2,1,0:T(8,128)(2,1)}, bf16[2,256,16]{2,1,0:T(8,128)(2,1)}) custom-call(s32[1,3]{1,0:T(1,128)} %starts_ref.3, bf16[256,1024]{1,0:T(8,128)(2,1)} %get-tuple-element.228.q_ref, bf16[256,1024]{1,0:T(8,128)(2,1)} %get-tuple-element.230.k_ref, ...), custom_call_target="tpu_custom_call" | custom-call | flops 4000000000 | bytes 4000000 | tf_op jit(solution)/shard_map/slot_forward/pallas_call | solution.py:383
  38.2 4.8 fusion.24.mine_ref
  42.9 11.9 %all-to-all-done = bf16[128,4,1408]{0,2,1:T(8,128)(2,1)S(1)} async-done(((bf16[128,4,1408]{0,2,1:T(8,128)(2,1)}), bf16[128,4,1408]{0,2,1:T(8,128)(2,1)S(1)}, u32[]{:S(2)}, u32[]{:S(2)}) %all-to-all-start) | async-done | bytes 1441824 | tf_op jit(solution)/shard_map/all_to_all | solution.py:585
  58.1 3.7 fusion.22
  63.5 3.5 all-to-all-start.1
  69.9 3.3 second_norm.1
  73.1 4.6 collective-permute-start.1
  83.1 4.0 all-to-all-done.1
  90.6 5.5 %collective-permute-done.2 = bf16[128,2048]{1,0:T(8,128)(2,1)} collective-permute-done((bf16[128,2048]{1,0:T(8,128)(2,1)}, bf16[128,2048]{1,0:T(8,128)(2,1)}, u32[]{:S(2)}, u32[]{:S(2)}) %collective-permute-start.2) | collective-permute-done | bytes 524320 | tf_op jit(solution)/shard_map/ppermute | solution.py:599
  96.1 3.9 collective-permute-start.5
  101.3 3.4 bitcast_dynamic-update-slice_fusion
  104.7 6.1 %collective-permute-done.5 = bf16[128,2048]{1,0:T(8,128)(2,1)S(1)} collective-permute-done((bf16[128,2048]{1,0:T(8,128)(2,1)}, bf16[128,2048]{1,0:T(8,128)(2,1)S(1)}, u32[]{:S(2)}, u32[]{:S(2)}) %collective-permute-start.5) | collective-permute-done | bytes 524320 | tf_op jit(solution)/shard_map/ppermute | solution.py:598
  110.8 4.0 collective-permute-done.6
  122.2 4.6 collective-permute-done.8
  126.8 4.1 collective-permute-done.9
  137.5 4.3 collective-permute-start.3
  148.6 5.1 fusion.45
  153.7 6.6 %collective-permute-done.4 = bf16[128,2048]{1,0:T(8,128)(2,1)} collective-permute-done((bf16[128,2048]{1,0:T(8,128)(2,1)}, bf16[128,2048]{1,0:T(8,128)(2,1)}, u32[]{:S(2)}, u32[]{:S(2)}) %collective-permute-start.4) | collective-permute-done | bytes 524320 | tf_op jit(solution)/shard_map/ppermute | solution.py:599
  163.9 7.9 %fusion.46 = f32[1024,704]{0,1:T(8,128)} fusion(bf16[1024,2048]{1,0:T(8,128)(2,1)} %select_dynamic-update-slice_fusion.6, bf16[2048,704]{1,0:T(8,128)(2,1)} %all-gather.9.cloned.1.call-done), kind=kOutput, calls=%fused_computation.144 | convolution fusion | flops 2952790016 | bytes 9961472 | tf_op jit(solution)/shard_map/dot_general | solution.py:19
  173.2 4.9 collective-permute-done.18
  181.7 2.7 multiply_convert_fusion.2
  185.4 3.5 fusion.47
  190.2 4.0 collective-permute-done.20
  208.4 9.3 %multiply_convert_fusion.1 = (bf16[1024,704]{0,1:T(8,128)(2,1)S(1)}, bf16[1024,704]{0,1:T(8,128)(2,1)S(1)}) fusion(f32[1024,704]{0,1:T(8,128)} %copy-done.11, f32[1024,704]{0,1:T(8,128)} %fusion.46, bf16[1024,2048]{1,0:T(8,128)(2,1)} %copy-done.35, bf16[2048,704]{0,1:T(8,128)(2,1)} %all-gather.11.cloned.1.call-done), kind=kOutput, calls=%fused_computation.7 | convolution fusion | flops 2962161664 | bytes 15728640 | tf_op jit(solution)/shard_map/dot_general | solution.py:19
  217.7 3.5 fusion.48
  221.2 5.5 %fusion.44 = (bf16[1024,2048]{1,0:T(8,128)(2,1)S(1)}, f32[1024,2048]{1,0:T(8,128)S(1)}) fusion(f32[1024,2048]{1,0:T(8,128)S(1)} %fusion.48, bf16[1024,704]{0,1:T(8,128)(2,1)S(1)} %get-tuple-element.199, bf16[2048,704]{1,0:T(8,128)(2,1)} %all-gather.7.cloned.1.call-done), kind=kOutput, calls=%fused_computation.142 | convolution fusion | flops 2956984320 | bytes 25296896 | tf_op jit(solution)/shard_map/dot_general | solution.py:23
  236.5 4.6 convolution_convert_fusion.3
  241.1 16.5 %collective-permute-done.36 = bf16[128,2048]{1,0:T(8,128)(2,1)} collective-permute-done((bf16[128,2048]{1,0:T(8,128)(2,1)}, bf16[128,2048]{1,0:T(8,128)(2,1)}, u32[]{:S(2)}, u32[]{:S(2)}) %collective-permute-start.36) | collective-permute-done | bytes 524320 | tf_op jit(solution)/shard_map/ppermute | solution.py:634
  260.5 3.0 add_convert_fusion.2
  263.5 3.2 collective-permute-start.39
  267.9 7.2 %convolution_convert_fusion.2 = bf16[2048,704]{0,1:T(8,128)(2,1)} fusion(bf16[1024,704]{0,1:T(8,128)(2,1)S(1)} %get-tuple-element.199, bf16[1024,2048]{1,0:T(8,128)(2,1)} %select_dynamic-update-slice_fusion.6), kind=kOutput, calls=%fused_computation.4 | convolution fusion | flops 2954231808 | bytes 8519680 | tf_op jit(solution)/shard_map/dot_general | solution.py:29
  277.5 4.9 collective-permute-done.40
  282.5 4.1 add_convert_fusion
  286.6 3.3 collective-permute-start.41
  291.3 4.5 convolution_convert_fusion.1
  295.8 4.2 collective-permute-done.41.refs_1_
  300.0 3.8 collective-permute-done.42.refs_2_
  304.6 3.9 second_norm_back.1
  310.7 4.3 convolution_convert_fusion.5.do_ref
  315.0 11.3 %slot_backward.1 = (bf16[256,1024]{1,0:T(8,128)(2,1)}, bf16[256,1024]{1,0:T(8,128)(2,1)}, bf16[256,1024]{1,0:T(8,128)(2,1)}, bf16[256,128]{1,0:T(8,128)(2,1)}, bf16[4,256,896]{2,1,0:T(8,128)(2,1)}) custom-call(s32[1,3]{1,0:T(1,128)} %starts_ref.3, bf16[256,1024]{1,0:T(8,128)(2,1)} %get-tuple-element.228.q_ref, bf16[256,1024]{1,0:T(8,128)(2,1)} %get-tuple-element.230.k_ref, ...), custom_call_target="tpu_custom_call" | custom-call | flops 12000000000 | bytes 8000000 | tf_op jit(solution)/shard_map/slot_backward/pallas_call | solution.py:403
  326.4 4.5 all-to-all-start.2
  331.4 3.8 fusion.16
  347.4 3.0 constant_dynamic-slice_fusion
  351.8 3.2 collective-permute-start.49
  356.8 3.9 collective-permute-done.47
  361.6 6.1 %collective-permute-done.48 = bf16[1,128,704]{1,2,0:T(8,128)(2,1)S(1)} collective-permute-done((bf16[1,128,704]{1,2,0:T(8,128)(2,1)S(1)}, bf16[1,128,704]{1,2,0:T(8,128)(2,1)S(1)}, u32[]{:S(2)}, u32[]{:S(2)}) %collective-permute-start.48) | collective-permute-done | bytes 180256 | tf_op jit(solution)/shard_map/ppermute | solution.py:780
  369.0 14.1 %collective-permute-done.45 = bf16[1,128,704]{1,2,0:T(8,128)(2,1)S(1)} collective-permute-done((bf16[1,128,704]{1,2,0:T(8,128)(2,1)S(1)}, bf16[1,128,704]{1,2,0:T(8,128)(2,1)S(1)}, u32[]{:S(2)}, u32[]{:S(2)}) %collective-permute-start.45) | collective-permute-done | bytes 180256 | tf_op jit(solution)/shard_map/ppermute | solution.py:780
  384.4 9.2 %convolution_convert_fusion = bf16[2048,896]{1,0:T(8,128)(2,1)} fusion(bf16[1024,2048]{1,0:T(8,128)(2,1)} %bitcast.11, bf16[1024,896]{1,0:T(8,128)(2,1)} %bitcast.18), kind=kOutput, calls=%fused_computation.2 | convolution fusion | flops 3759931392 | bytes 9699328 | tf_op jit(solution)/shard_map/dot_general | solution.py:29
  393.7 2.6 collective-permute-done.50.other_ref
  397.3 3.9 first_norm_back.1
  406.1 10.2 %collective-permute-done.52 = bf16[128,2048]{1,0:T(8,128)(2,1)} collective-permute-done((bf16[128,2048]{1,0:T(8,128)(2,1)}, bf16[128,2048]{1,0:T(8,128)(2,1)}, u32[]{:S(2)}, u32[]{:S(2)}) %collective-permute-start.52) | collective-permute-done | bytes 524320 | tf_op jit(solution)/shard_map/ppermute | solution.py:648
  417.4 10.9 %collective-permute-done.53 = bf16[128,2048]{1,0:T(8,128)(2,1)S(1)} collective-permute-done((bf16[128,2048]{1,0:T(8,128)(2,1)}, bf16[128,2048]{1,0:T(8,128)(2,1)S(1)}, u32[]{:S(2)}, u32[]{:S(2)}) %collective-permute-start.53) | collective-permute-done | bytes 524320 | tf_op jit(solution)/shard_map/ppermute | solution.py:648
  433.4 5.5 %all-to-all-start.4 = ((f32[16,2,128]{2,1,0:T(2,128)}), f32[16,2,128]{2,1,0:T(2,128)S(1)}, u32[]{:S(2)}, u32[]{:S(2)}) async-start(f32[16,2,128]{2,1,0:T(2,128)} %add_bitcast_fusion), calls=%async_computation.7 | async-start | bytes 32768 | tf_op jit(solution)/shard_map/all_to_all | solution.py:830
  440.6 5.8 %all-to-all-done.4 = f32[16,2,128]{2,1,0:T(2,128)S(1)} async-done(((f32[16,2,128]{2,1,0:T(2,128)}), f32[16,2,128]{2,1,0:T(2,128)S(1)}, u32[]{:S(2)}, u32[]{:S(2)}) %all-to-all-start.4) | async-done | bytes 16416 | tf_op jit(solution)/shard_map/all_to_all | solution.py:830
  446.5 3.7 all-to-all-start.3
  454.2 3.2 constant_dynamic-update-slice_fusion.4
  457.5 4.2 all-to-all-start.7
  461.7 4.5 convolution_convert_fusion.4
  476.1 12.0 %all-to-all-done.7 = bf16[4,128,704]{1,2,0:T(8,128)(2,1)} async-done(((bf16[4,128,704]{1,2,0:T(8,128)(2,1)}), bf16[4,128,704]{1,2,0:T(8,128)(2,1)}, u32[]{:S(2)}, u32[]{:S(2)}) %all-to-all-start.7) | async-done | bytes 720928 | tf_op jit(solution)/shard_map/all_to_all | solution.py:585
  492.1 4.1 all-to-all-start.5
  501.0 4.1 all-to-all-done.5
  505.2 4.0 all-to-all-start.6
  (319 shorter events, 160.0 us)
Async XLA Ops:
  7.2 50.0 %all-gather.5.cloned.1.call-start = ((), (), s32[]{:S(2)}) async-start(), calls=%async_computation.14 | async-start | bytes 2621440 | tf_op jit(solution)/shard_map/all_gather | solution.py:697
  14.3 40.5 %all-to-all-start = ((bf16[128,4,1408]{0,2,1:T(8,128)(2,1)}), bf16[128,4,1408]{0,2,1:T(8,128)(2,1)S(1)}, u32[]{:S(2)}, u32[]{:S(2)}) async-start(bf16[128,4,1408]{0,2,1:T(8,128)(2,1)} %pad_maximum_fusion), calls=%async_computation | async-start | bytes 2883584 | tf_op jit(solution)/shard_map/all_to_all | solution.py:585
  20.7 110.3 %all-gather.7.cloned.1.call-start = ((), (), s32[]{:S(2)}) async-start(), calls=%async_computation.15 | async-start | bytes 3932160 | tf_op jit(solution)/shard_map/all_gather | solution.py:677
  57.2 103.1 %all-gather.9.cloned.1.call-start = ((), (), s32[]{:S(2)}) async-start(), calls=%async_computation.16 | async-start | bytes 3932160 | tf_op jit(solution)/shard_map/all_gather | solution.py:677
  58.0 43.3 %collective-permute-start.7 = (bf16[4,1,128,2048]{3,2,0,1:T(8,128)(2,1)}, bf16[4,1,128,2048]{3,2,0,1:T(8,128)(2,1)}, u32[]{:S(2)}, u32[]{:S(2)}) collective-permute-start(bf16[4,1,128,2048]{3,2,0,1:T(8,128)(2,1)} %bitcast.144), channel_id=1, source_target_pairs={{0,1},{1,0},{2,3},{3,2},{4,5},{5,4},{6,7},{7,6},{8,9},{9,8},{10,11... | collective-permute-start | bytes 6291464 | tf_op jit(solution)/shard_map/ppermute | solution.py:464
  61.8 7.1 %collective-permute-start = (f32[128,2048]{1,0:T(8,128)S(1)}, f32[128,2048]{1,0:T(8,128)S(1)}, u32[]{:S(2)}, u32[]{:S(2)}) collective-permute-start(f32[128,2048]{1,0:T(8,128)S(1)} %fusion.22), channel_id=1, source_target_pairs={{0,1},{1,0},{2,3},{3,2},{4,5},{5,4},{6,7},{7,6},{8,9},{9,8},{10,11... | collective-permute-start | bytes 3145736 | tf_op jit(solution)/shard_map/ppermute | solution.py:464
  63.5 23.6 %all-to-all-start.1 = ((bf16[128,4,704]{0,2,1:T(8,128)(2,1)}), bf16[128,4,704]{0,2,1:T(8,128)(2,1)S(1)}, u32[]{:S(2)}, u32[]{:S(2)}) async-start(bf16[128,4,704]{0,2,1:T(8,128)(2,1)} %bitcast.6), calls=%async_computation.1 | async-start | bytes 1441792 | tf_op jit(solution)/shard_map/all_to_all | solution.py:585
  67.0 111.1 %all-gather.11.cloned.1.call-start = ((), (), s32[]{:S(2)}) async-start(), calls=%async_computation.17 | async-start | bytes 3604480 | tf_op jit(solution)/shard_map/all_gather | solution.py:677
  73.1 17.4 %collective-permute-start.1 = (bf16[128,2048]{1,0:T(8,128)(2,1)}, bf16[128,2048]{1,0:T(8,128)(2,1)}, u32[]{:S(2)}, u32[]{:S(2)}) collective-permute-start(bf16[128,2048]{1,0:T(8,128)(2,1)} %get-tuple-element.93), channel_id=1, source_target_pairs={{0,8},{2,10},{4,12},{6,14},{8,16},{10,18},{12,20},{14,22},{16,24},... | collective-permute-start | bytes 1572872 | tf_op jit(solution)/shard_map/ppermute | solution.py:598
  77.7 18.3 %collective-permute-start.2 = (bf16[128,2048]{1,0:T(8,128)(2,1)}, bf16[128,2048]{1,0:T(8,128)(2,1)}, u32[]{:S(2)}, u32[]{:S(2)}) collective-permute-start(bf16[128,2048]{1,0:T(8,128)(2,1)} %get-tuple-element.93), channel_id=1, source_target_pairs={{8,0},{10,2},{12,4},{14,6},{16,8},{18,10},{20,12},{22,14},{24,16},... | collective-permute-start | bytes 1572872 | tf_op jit(solution)/shard_map/ppermute | solution.py:599
  96.1 14.8 %collective-permute-start.5 = (bf16[128,2048]{1,0:T(8,128)(2,1)}, bf16[128,2048]{1,0:T(8,128)(2,1)S(1)}, u32[]{:S(2)}, u32[]{:S(2)}) collective-permute-start(bf16[128,2048]{1,0:T(8,128)(2,1)} %collective-permute-done.1), channel_id=1, source_target_pairs={{0,8},{2,10},{4,12},{6,14},{8,16},{10,18},{12,20},{14,22},{16,24},... | collective-permute-start | bytes 1572872 | tf_op jit(solution)/shard_map/ppermute | solution.py:598
  100.0 14.9 %collective-permute-start.6 = (bf16[128,2048]{1,0:T(8,128)(2,1)}, bf16[128,2048]{1,0:T(8,128)(2,1)S(1)}, u32[]{:S(2)}, u32[]{:S(2)}) collective-permute-start(bf16[128,2048]{1,0:T(8,128)(2,1)} %collective-permute-done.2), channel_id=1, source_target_pairs={{8,0},{10,2},{12,4},{14,6},{16,8},{18,10},{20,12},{22,14},{24,16},... | collective-permute-start | bytes 1572872 | tf_op jit(solution)/shard_map/ppermute | solution.py:599
  114.9 11.9 %collective-permute-start.8 = (bf16[128,2048]{1,0:T(8,128)(2,1)S(1)}, bf16[128,2048]{1,0:T(8,128)(2,1)S(1)}, u32[]{:S(2)}, u32[]{:S(2)}) collective-permute-start(bf16[128,2048]{1,0:T(8,128)(2,1)S(1)} %collective-permute-done.5), channel_id=1, source_target_pairs={{0,8},{2,10},{4,12},{6,14},{8,16},{10,18},{12,20},{14,22},{16,24},... | collective-permute-start | bytes 1572872 | tf_op jit(solution)/shard_map/ppermute | solution.py:598
  117.3 13.6 %collective-permute-start.9 = (bf16[128,2048]{1,0:T(8,128)(2,1)S(1)}, bf16[128,2048]{1,0:T(8,128)(2,1)S(1)}, u32[]{:S(2)}, u32[]{:S(2)}) collective-permute-start(bf16[128,2048]{1,0:T(8,128)(2,1)S(1)} %collective-permute-done.6), channel_id=1, source_target_pairs={{8,0},{10,2},{12,4},{14,6},{16,8},{18,10},{20,12},{22,14},{24,16},... | collective-permute-start | bytes 1572872 | tf_op jit(solution)/shard_map/ppermute | solution.py:599
  118.8 16.1 %collective-permute-start.10 = (bf16[128,2048]{1,0:T(8,128)(2,1)S(1)}, bf16[128,2048]{1,0:T(8,128)(2,1)}, u32[]{:S(2)}, u32[]{:S(2)}) collective-permute-start(bf16[128,2048]{1,0:T(8,128)(2,1)S(1)} %copy-done.28), channel_id=1, source_target_pairs={{0,1},{1,0},{2,3},{3,2},{4,5},{5,4},{6,7},{7,6},{8,9},{9,8},{10,11... | collective-permute-start | bytes 1572872 | tf_op jit(solution)/shard_map/ppermute | solution.py:464
  119.7 17.8 %collective-permute-start.11 = (bf16[128,2048]{1,0:T(8,128)(2,1)}, bf16[128,2048]{1,0:T(8,128)(2,1)}, u32[]{:S(2)}, u32[]{:S(2)}) collective-permute-start(bf16[128,2048]{1,0:T(8,128)(2,1)} %collective-permute-done.2), channel_id=1, source_target_pairs={{0,1},{1,0},{2,3},{3,2},{4,5},{5,4},{6,7},{7,6},{8,9},{9,8},{10,11... | collective-permute-start | bytes 1572872 | tf_op jit(solution)/shard_map/ppermute | solution.py:464
  120.2 27.5 %collective-permute-start.16 = (bf16[128,2048]{1,0:T(8,128)(2,1)}, bf16[128,2048]{1,0:T(8,128)(2,1)}, u32[]{:S(2)}, u32[]{:S(2)}) collective-permute-start(bf16[128,2048]{1,0:T(8,128)(2,1)} %collective-permute-done.1), channel_id=1, source_target_pairs={{0,1},{1,0},{2,3},{3,2},{4,5},{5,4},{6,7},{7,6},{8,9},{9,8},{10,11... | collective-permute-start | bytes 1572872 | tf_op jit(solution)/shard_map/ppermute | solution.py:464
  120.2 140.2 %reduce-scatter.7.cloned.1.call-start = ((), (), s32[]{:S(2)}) async-start(), calls=%async_computation.18 | async-start | bytes 2621440 | tf_op jit(solution)/shard_map/reduce_scatter | solution.py:758
  126.8 17.0 %collective-permute-start.13 = (bf16[128,2048]{1,0:T(8,128)(2,1)S(1)}, bf16[128,2048]{1,0:T(8,128)(2,1)}, u32[]{:S(2)}, u32[]{:S(2)}) collective-permute-start(bf16[128,2048]{1,0:T(8,128)(2,1)S(1)} %collective-permute-done.6), channel_id=1, source_target_pairs={{0,1},{1,0},{2,3},{3,2},{4,5},{5,4},{6,7},{7,6},{8,9},{9,8},{10,11... | collective-permute-start | bytes 1572872 | tf_op jit(solution)/shard_map/ppermute | solution.py:464
  131.0 10.8 %collective-permute-start.12 = (bf16[128,2048]{1,0:T(8,128)(2,1)S(1)}, bf16[128,2048]{1,0:T(8,128)(2,1)S(1)}, u32[]{:S(2)}, u32[]{:S(2)}) collective-permute-start(bf16[128,2048]{1,0:T(8,128)(2,1)S(1)} %collective-permute-done.8), channel_id=1, source_target_pairs={{0,1},{1,0},{2,3},{3,2},{4,5},{5,4},{6,7},{7,6},{8,9},{9,8},{10,11... | collective-permute-start | bytes 1572872 | tf_op jit(solution)/shard_map/ppermute | solution.py:464
  134.9 10.2 %collective-permute-start.14 = (bf16[128,2048]{1,0:T(8,128)(2,1)S(1)}, bf16[128,2048]{1,0:T(8,128)(2,1)S(1)}, u32[]{:S(2)}, u32[]{:S(2)}) collective-permute-start(bf16[128,2048]{1,0:T(8,128)(2,1)S(1)} %collective-permute-done.5), channel_id=1, source_target_pairs={{0,1},{1,0},{2,3},{3,2},{4,5},{5,4},{6,7},{7,6},{8,9},{9,8},{10,11... | collective-permute-start | bytes 1572872 | tf_op jit(solution)/shard_map/ppermute | solution.py:464
  137.5 16.2 %collective-permute-start.3 = (bf16[128,2048]{1,0:T(8,128)(2,1)}, bf16[128,2048]{1,0:T(8,128)(2,1)}, u32[]{:S(2)}, u32[]{:S(2)}) collective-permute-start(bf16[128,2048]{1,0:T(8,128)(2,1)} %cotangent_rows.1), channel_id=1, source_target_pairs={{0,8},{2,10},{4,12},{6,14},{8,16},{10,18},{12,20},{14,22},{16,24},... | collective-permute-start | bytes 1572872 | tf_op jit(solution)/shard_map/ppermute | solution.py:598
  141.8 5.9 %collective-permute-start.15 = (bf16[128,2048]{1,0:T(8,128)(2,1)S(1)}, bf16[128,2048]{1,0:T(8,128)(2,1)S(1)}, u32[]{:S(2)}, u32[]{:S(2)}) collective-permute-start(bf16[128,2048]{1,0:T(8,128)(2,1)S(1)} %collective-permute-done.9), channel_id=1, source_target_pairs={{0,1},{1,0},{2,3},{3,2},{4,5},{5,4},{6,7},{7,6},{8,9},{9,8},{10,11... | collective-permute-start | bytes 1572872 | tf_op jit(solution)/shard_map/ppermute | solution.py:464
  143.8 16.5 %collective-permute-start.4 = (bf16[128,2048]{1,0:T(8,128)(2,1)}, bf16[128,2048]{1,0:T(8,128)(2,1)}, u32[]{:S(2)}, u32[]{:S(2)}) collective-permute-start(bf16[128,2048]{1,0:T(8,128)(2,1)} %cotangent_rows.1), channel_id=1, source_target_pairs={{8,0},{10,2},{12,4},{14,6},{16,8},{18,10},{20,12},{22,14},{24,16},... | collective-permute-start | bytes 1572872 | tf_op jit(solution)/shard_map/ppermute | solution.py:599
  145.1 53.0 %collective-permute-start.25 = (bf16[128,2048]{1,0:T(8,128)(2,1)}, bf16[128,2048]{1,0:T(8,128)(2,1)}, u32[]{:S(2)}, u32[]{:S(2)}) collective-permute-start(bf16[128,2048]{1,0:T(8,128)(2,1)} %cotangent_rows.1), channel_id=1, source_target_pairs={{0,1},{1,0},{2,3},{3,2},{4,5},{5,4},{6,7},{7,6},{8,9},{9,8},{10,11... | collective-permute-start | bytes 1572872 | tf_op jit(solution)/shard_map/ppermute | solution.py:464
  160.3 12.9 %collective-permute-start.17 = (bf16[128,2048]{1,0:T(8,128)(2,1)}, bf16[128,2048]{1,0:T(8,128)(2,1)}, u32[]{:S(2)}, u32[]{:S(2)}) collective-permute-start(bf16[128,2048]{1,0:T(8,128)(2,1)} %collective-permute-done.3), channel_id=1, source_target_pairs={{0,8},{2,10},{4,12},{6,14},{8,16},{10,18},{12,20},{14,22},{16,24},... | collective-permute-start | bytes 1572872 | tf_op jit(solution)/shard_map/ppermute | solution.py:598
  162.6 15.5 %collective-permute-start.18 = (bf16[128,2048]{1,0:T(8,128)(2,1)}, bf16[128,2048]{1,0:T(8,128)(2,1)}, u32[]{:S(2)}, u32[]{:S(2)}) collective-permute-start(bf16[128,2048]{1,0:T(8,128)(2,1)} %collective-permute-done.4), channel_id=1, source_target_pairs={{8,0},{10,2},{12,4},{14,6},{16,8},{18,10},{20,12},{22,14},{24,16},... | collective-permute-start | bytes 1572872 | tf_op jit(solution)/shard_map/ppermute | solution.py:599
  178.1 12.1 %collective-permute-start.19 = (bf16[128,2048]{1,0:T(8,128)(2,1)}, bf16[128,2048]{1,0:T(8,128)(2,1)S(1)}, u32[]{:S(2)}, u32[]{:S(2)}) collective-permute-start(bf16[128,2048]{1,0:T(8,128)(2,1)} %collective-permute-done.17), channel_id=1, source_target_pairs={{0,8},{2,10},{4,12},{6,14},{8,16},{10,18},{12,20},{14,22},{16,24},... | collective-permute-start | bytes 1572872 | tf_op jit(solution)/shard_map/ppermute | solution.py:598
  179.8 14.4 %collective-permute-start.20 = (bf16[128,2048]{1,0:T(8,128)(2,1)}, bf16[128,2048]{1,0:T(8,128)(2,1)S(1)}, u32[]{:S(2)}, u32[]{:S(2)}) collective-permute-start(bf16[128,2048]{1,0:T(8,128)(2,1)} %collective-permute-done.18), channel_id=1, source_target_pairs={{8,0},{10,2},{12,4},{14,6},{16,8},{18,10},{20,12},{22,14},{24,16},... | collective-permute-start | bytes 1572872 | tf_op jit(solution)/shard_map/ppermute | solution.py:599
  197.5 3.6 collective-permute-start.24
  198.0 3.7 collective-permute-start.26
  199.3 6.1 %collective-permute-start.31 = (bf16[128,2048]{1,0:T(8,128)(2,1)}, bf16[128,2048]{1,0:T(8,128)(2,1)S(1)}, u32[]{:S(2)}, u32[]{:S(2)}) collective-permute-start(bf16[128,2048]{1,0:T(8,128)(2,1)} %collective-permute-done.3), channel_id=1, source_target_pairs={{0,1},{1,0},{2,3},{3,2},{4,5},{5,4},{6,7},{7,6},{8,9},{9,8},{10,11... | collective-permute-start | bytes 1572872 | tf_op jit(solution)/shard_map/ppermute | solution.py:464
  199.8 5.3 %collective-permute-start.28 = (bf16[128,2048]{1,0:T(8,128)(2,1)}, bf16[128,2048]{1,0:T(8,128)(2,1)S(1)}, u32[]{:S(2)}, u32[]{:S(2)}) collective-permute-start(bf16[128,2048]{1,0:T(8,128)(2,1)} %collective-permute-done.18), channel_id=1, source_target_pairs={{0,1},{1,0},{2,3},{3,2},{4,5},{5,4},{6,7},{7,6},{8,9},{9,8},{10,11... | collective-permute-start | bytes 1572872 | tf_op jit(solution)/shard_map/ppermute | solution.py:464
  200.3 4.8 collective-permute-start.29
  201.0 3.7 collective-permute-start.27
  201.8 3.7 collective-permute-start.30
  208.1 106.9 %reduce-scatter.9.cloned.1.call-start = ((), (), s32[]{:S(2)}) async-start(), calls=%async_computation.19 | async-start | bytes 3604480 | tf_op jit(solution)/shard_map/reduce_scatter | solution.py:763
  232.6 25.1 %collective-permute-start.36 = (bf16[128,2048]{1,0:T(8,128)(2,1)}, bf16[128,2048]{1,0:T(8,128)(2,1)}, u32[]{:S(2)}, u32[]{:S(2)}) collective-permute-start(bf16[128,2048]{1,0:T(8,128)(2,1)} %get-tuple-element.198), channel_id=1, source_target_pairs={{0,8},{2,10},{4,12},{6,14},{8,16},{10,18},{12,20},{14,22},{16,24},... | collective-permute-start | bytes 1572872 | tf_op jit(solution)/shard_map/ppermute | solution.py:634
  235.0 24.4 %collective-permute-start.37 = (bf16[128,2048]{1,0:T(8,128)(2,1)}, bf16[128,2048]{1,0:T(8,128)(2,1)}, u32[]{:S(2)}, u32[]{:S(2)}) collective-permute-start(bf16[128,2048]{1,0:T(8,128)(2,1)} %get-tuple-element.197), channel_id=1, source_target_pairs={{8,0},{10,2},{12,4},{14,6},{16,8},{18,10},{20,12},{22,14},{24,16},... | collective-permute-start | bytes 1572872 | tf_op jit(solution)/shard_map/ppermute | solution.py:635
  260.4 85.1 %reduce-scatter.11.cloned.1.call-start = ((), (), s32[]{:S(2)}) async-start(), calls=%async_computation.20 | async-start | bytes 3604480 | tf_op jit(solution)/shard_map/reduce_scatter | solution.py:763
  263.5 14.0 %collective-permute-start.39 = (bf16[128,2048]{1,0:T(8,128)(2,1)}, bf16[128,2048]{1,0:T(8,128)(2,1)}, u32[]{:S(2)}, u32[]{:S(2)}) collective-permute-start(bf16[128,2048]{1,0:T(8,128)(2,1)} %get-tuple-element.193), channel_id=1, source_target_pairs={{0,8},{2,10},{4,12},{6,14},{8,16},{10,18},{12,20},{14,22},{16,24},... | collective-permute-start | bytes 1572872 | tf_op jit(solution)/shard_map/ppermute | solution.py:634
  266.7 15.7 %collective-permute-start.40 = (bf16[128,2048]{1,0:T(8,128)(2,1)}, bf16[128,2048]{1,0:T(8,128)(2,1)}, u32[]{:S(2)}, u32[]{:S(2)}) collective-permute-start(bf16[128,2048]{1,0:T(8,128)(2,1)} %get-tuple-element.192), channel_id=1, source_target_pairs={{8,0},{10,2},{12,4},{14,6},{16,8},{18,10},{20,12},{22,14},{24,16},... | collective-permute-start | bytes 1572872 | tf_op jit(solution)/shard_map/ppermute | solution.py:635
  282.4 146.1 %reduce-scatter.17.cloned.1.call-start = ((), (), s32[]{:S(2)}) async-start(), calls=%async_computation.23 | async-start | bytes 3604480 | tf_op jit(solution)/shard_map/reduce_scatter | solution.py:763
  286.6 13.4 %collective-permute-start.41 = (bf16[128,2048]{1,0:T(8,128)(2,1)}, bf16[128,2048]{1,0:T(8,128)(2,1)S(1)}, u32[]{:S(2)}, u32[]{:S(2)}) collective-permute-start(bf16[128,2048]{1,0:T(8,128)(2,1)} %get-tuple-element.195), channel_id=1, source_target_pairs={{0,8},{2,10},{4,12},{6,14},{8,16},{10,18},{12,20},{14,22},{16,24},... | collective-permute-start | bytes 1572872 | tf_op jit(solution)/shard_map/ppermute | solution.py:634
  290.0 13.9 %collective-permute-start.42 = (bf16[128,2048]{1,0:T(8,128)(2,1)S(1)}, bf16[128,2048]{1,0:T(8,128)(2,1)S(1)}, u32[]{:S(2)}, u32[]{:S(2)}) collective-permute-start(bf16[128,2048]{1,0:T(8,128)(2,1)S(1)} %get-tuple-element.194), channel_id=1, source_target_pairs={{8,0},{10,2},{12,4},{14,6},{16,8},{18,10},{20,12},{22,14},{24,16},... | collective-permute-start | bytes 1572872 | tf_op jit(solution)/shard_map/ppermute | solution.py:635
  326.4 58.0 %all-to-all-start.2 = ((bf16[4,256,896]{2,1,0:T(8,128)(2,1)}), bf16[4,256,896]{2,1,0:T(8,128)(2,1)}, u32[]{:S(2)}, u32[]{:S(2)}) async-start(bf16[4,256,896]{2,1,0:T(8,128)(2,1)} %get-tuple-element.144), calls=%async_computation.4 | async-start | bytes 3670016 | tf_op jit(solution)/shard_map/all_to_all | solution.py:585
  330.9 135.3 %reduce-scatter.13.cloned.1.call-start = ((), (), s32[]{:S(2)}) async-start(), calls=%async_computation.21 | async-start | bytes 4587520 | tf_op jit(solution)/shard_map/reduce_scatter | solution.py:723
  350.4 10.3 %collective-permute-start.47 = (bf16[1,128,704]{1,2,0:T(8,128)(2,1)S(1)}, bf16[1,128,704]{1,2,0:T(8,128)(2,1)S(1)}, u32[]{:S(2)}, u32[]{:S(2)}) collective-permute-start(bf16[1,128,704]{1,2,0:T(8,128)(2,1)S(1)} %copy.97), channel_id=1, source_target_pairs={{0,8},{2,10},{4,12},{6,14},{8,0},{10,2},{12,4},{14,6},{16,24},{18,... | collective-permute-start | bytes 540680 | tf_op jit(solution)/shard_map/ppermute | solution.py:780
  351.5 16.2 %collective-permute-start.48 = (bf16[1,128,704]{1,2,0:T(8,128)(2,1)S(1)}, bf16[1,128,704]{1,2,0:T(8,128)(2,1)S(1)}, u32[]{:S(2)}, u32[]{:S(2)}) collective-permute-start(bf16[1,128,704]{1,2,0:T(8,128)(2,1)S(1)} %copy.98), channel_id=1, source_target_pairs={{0,16},{2,18},{4,20},{6,22},{8,24},{10,26},{12,28},{14,30},{16,0},... | collective-permute-start | bytes 540680 | tf_op jit(solution)/shard_map/ppermute | solution.py:780
  351.8 15.9 %collective-permute-start.49 = (bf16[1,128,704]{1,2,0:T(8,128)(2,1)S(1)}, bf16[1,128,704]{1,2,0:T(8,128)(2,1)S(1)}, u32[]{:S(2)}, u32[]{:S(2)}) collective-permute-start(bf16[1,128,704]{1,2,0:T(8,128)(2,1)S(1)} %copy.99), channel_id=1, source_target_pairs={{0,24},{2,26},{4,28},{6,30},{8,16},{10,18},{12,20},{14,22},{16,8},... | collective-permute-start | bytes 540680 | tf_op jit(solution)/shard_map/ppermute | solution.py:780
  355.1 13.9 %collective-permute-start.44 = (bf16[1,128,704]{1,2,0:T(8,128)(2,1)S(1)}, bf16[1,128,704]{1,2,0:T(8,128)(2,1)S(1)}, u32[]{:S(2)}, u32[]{:S(2)}) collective-permute-start(bf16[1,128,704]{1,2,0:T(8,128)(2,1)S(1)} %copy.93), channel_id=1, source_target_pairs={{0,8},{2,10},{4,12},{6,14},{8,0},{10,2},{12,4},{14,6},{16,24},{18,... | collective-permute-start | bytes 540680 | tf_op jit(solution)/shard_map/ppermute | solution.py:780
  355.3 27.8 %collective-permute-start.45 = (bf16[1,128,704]{1,2,0:T(8,128)(2,1)S(1)}, bf16[1,128,704]{1,2,0:T(8,128)(2,1)S(1)}, u32[]{:S(2)}, u32[]{:S(2)}) collective-permute-start(bf16[1,128,704]{1,2,0:T(8,128)(2,1)S(1)} %copy.94), channel_id=1, source_target_pairs={{0,16},{2,18},{4,20},{6,22},{8,24},{10,26},{12,28},{14,30},{16,0},... | collective-permute-start | bytes 540680 | tf_op jit(solution)/shard_map/ppermute | solution.py:780
  360.7 22.5 %collective-permute-start.46 = (bf16[1,128,704]{1,2,0:T(8,128)(2,1)S(1)}, bf16[1,128,704]{1,2,0:T(8,128)(2,1)S(1)}, u32[]{:S(2)}, u32[]{:S(2)}) collective-permute-start(bf16[1,128,704]{1,2,0:T(8,128)(2,1)S(1)} %copy.95), channel_id=1, source_target_pairs={{0,24},{2,26},{4,28},{6,30},{8,16},{10,18},{12,20},{14,22},{16,8},... | collective-permute-start | bytes 540680 | tf_op jit(solution)/shard_map/ppermute | solution.py:780
  401.2 15.1 %collective-permute-start.52 = (bf16[128,2048]{1,0:T(8,128)(2,1)}, bf16[128,2048]{1,0:T(8,128)(2,1)}, u32[]{:S(2)}, u32[]{:S(2)}) collective-permute-start(bf16[128,2048]{1,0:T(8,128)(2,1)} %get-tuple-element.157), channel_id=1, source_target_pairs={{0,2},{2,0},{4,6},{6,4},{8,10},{10,8},{12,14},{14,12},{16,18},{18,... | collective-permute-start | bytes 1572872 | tf_op jit(solution)/shard_map/ppermute | solution.py:648
  403.1 25.1 %collective-permute-start.53 = (bf16[128,2048]{1,0:T(8,128)(2,1)}, bf16[128,2048]{1,0:T(8,128)(2,1)S(1)}, u32[]{:S(2)}, u32[]{:S(2)}) collective-permute-start(bf16[128,2048]{1,0:T(8,128)(2,1)} %get-tuple-element.157), channel_id=1, source_target_pairs={{0,4},{2,6},{4,0},{6,2},{8,12},{10,14},{12,8},{14,10},{16,20},{18,... | collective-permute-start | bytes 1572872 | tf_op jit(solution)/shard_map/ppermute | solution.py:648
  404.6 23.7 %collective-permute-start.54 = (bf16[128,2048]{1,0:T(8,128)(2,1)}, bf16[128,2048]{1,0:T(8,128)(2,1)S(1)}, u32[]{:S(2)}, u32[]{:S(2)}) collective-permute-start(bf16[128,2048]{1,0:T(8,128)(2,1)} %get-tuple-element.157), channel_id=1, source_target_pairs={{0,6},{2,4},{4,2},{6,0},{8,14},{10,12},{12,10},{14,8},{16,22},{18,... | collective-permute-start | bytes 1572872 | tf_op jit(solution)/shard_map/ppermute | solution.py:648
  428.4 25.9 %collective-permute-start.55 = (bf16[4,1,128,2048]{3,2,1,0:T(8,128)(2,1)S(1)}, bf16[4,1,128,2048]{3,2,1,0:T(8,128)(2,1)}, u32[]{:S(2)}, u32[]{:S(2)}) collective-permute-start(bf16[4,1,128,2048]{3,2,1,0:T(8,128)(2,1)S(1)} %bitcast_dynamic-update-slice_fusion.1), channel_id=1, source_target_pairs={{0,1},{1,0},{2,3},{3,2},{4,5},{5,4},{6,7},{7,6},{8,9},{9,8},{10,11... | collective-permute-start | bytes 6291464 | tf_op jit(solution)/shard_map/ppermute | solution.py:464
  433.4 13.1 %all-to-all-start.4 = ((f32[16,2,128]{2,1,0:T(2,128)}), f32[16,2,128]{2,1,0:T(2,128)S(1)}, u32[]{:S(2)}, u32[]{:S(2)}) async-start(f32[16,2,128]{2,1,0:T(2,128)} %add_bitcast_fusion), calls=%async_computation.7 | async-start | bytes 32768 | tf_op jit(solution)/shard_map/all_to_all | solution.py:830
  446.5 11.0 %all-to-all-start.3 = ((bf16[4,256,256]{2,1,0:T(8,128)(2,1)}), bf16[4,256,256]{2,1,0:T(8,128)(2,1)S(1)}, u32[]{:S(2)}, u32[]{:S(2)}) async-start(bf16[4,256,256]{2,1,0:T(8,128)(2,1)} %pad_maximum_fusion.1), calls=%async_computation.6 | async-start | bytes 1048576 | tf_op jit(solution)/shard_map/all_to_all | solution.py:585
  457.5 30.7 %all-to-all-start.7 = ((bf16[4,128,704]{1,2,0:T(8,128)(2,1)}), bf16[4,128,704]{1,2,0:T(8,128)(2,1)}, u32[]{:S(2)}, u32[]{:S(2)}) async-start(bf16[4,128,704]{1,2,0:T(8,128)(2,1)} %copy_bitcast_fusion.1), calls=%async_computation.13 | async-start | bytes 1441792 | tf_op jit(solution)/shard_map/all_to_all | solution.py:585
  461.6 43.6 %reduce-scatter.15.cloned.1.call-start = ((), (), s32[]{:S(2)}) async-start(), calls=%async_computation.22 | async-start | bytes 1310720 | tf_op jit(solution)/shard_map/reduce_scatter | solution.py:723
  466.2 31.6 %collective-permute-start.51 = (f32[128,2048]{1,0:T(8,128)}, f32[128,2048]{1,0:T(8,128)}, u32[]{:S(2)}, u32[]{:S(2)}) collective-permute-start(f32[128,2048]{1,0:T(8,128)} %get-tuple-element.153), channel_id=1, source_target_pairs={{0,1},{1,0},{2,3},{3,2},{4,5},{5,4},{6,7},{7,6},{8,9},{9,8},{10,11... | collective-permute-start | bytes 3145736 | tf_op jit(solution)/shard_map/ppermute | solution.py:464
  492.1 12.9 %all-to-all-start.5 = ((bf16[4,128,896]{1,2,0:T(8,128)(2,1)}), bf16[4,128,896]{1,2,0:T(8,128)(2,1)S(1)}, u32[]{:S(2)}, u32[]{:S(2)}) async-start(bf16[4,128,896]{1,2,0:T(8,128)(2,1)} %copy.82), calls=%async_computation.9 | async-start | bytes 1835008 | tf_op jit(solution)/shard_map/all_to_all | solution.py:585
  505.2 9.7 %all-to-all-start.6 = ((bf16[4,128,256]{2,1,0:T(8,128)(2,1)}), bf16[4,128,256]{2,1,0:T(8,128)(2,1)}, u32[]{:S(2)}, u32[]{:S(2)}) async-start(bf16[4,128,256]{2,1,0:T(8,128)(2,1)} %bitcast.152), calls=%async_computation.11 | async-start | bytes 524288 | tf_op jit(solution)/shard_map/all_to_all | solution.py:585
  (55 other events, 383.4 us)
Sparse Core Ops, SparseCore 0:
  11.4 37.9 all-gather.4
  57.4 35.2 all-gather.6
  94.8 36.1 all-gather.8
  133.0 33.9 all-gather.10
  208.2 52.1 reduce-scatter.6
  262.6 32.4 reduce-scatter.8
  297.3 32.3 reduce-scatter.10
  332.1 45.9 reduce-scatter.16
  393.7 69.9 reduce-scatter.12
  466.3 30.5 reduce-scatter.14

commit v12 on v11

--- a/solution.py
+++ b/solution.py
@@ -821,14 +821,18 @@
     input_grad, attn_gain_part = first_norm_back(
         block_in, hidden_grad, attn_gain, part_mine, swap(part_other), core
     )
-    _, low_half, attn_gain_part, mixed = tie(pre_grad, low_half, attn_gain_part, mixed)
+    _, low_half, attn_gain_part, mixed, up_rows = tie(
+        pre_grad, low_half, attn_gain_part, mixed, up_rows
+    )
     mixed_plane = plane_columns(jnp.stack(jnp.split(mixed, INNER, axis=1)))
     low_plane = plane_tokens(plane_gather(low_half, grid, inner))
     gains = jnp.concatenate([attn_gain_part, mlp_gain_part], axis=0)
     gains = gains + swap(gains)
     gains = jnp.swapaxes(gains.reshape(2, grid.dp, -1), 0, 1)
     gains = jnp.sum(lax.all_to_all(gains, "dp", 0, 0, tiled=True), axis=0)
-    output_grad, gains = tie(plane_product(low_plane, mixed_plane), gains)
+    output_grad, gains, up_sum = tie(
+        plane_product(low_plane, mixed_plane), gains, to_columns_beside(up_rows)
+    )
     sums, output_grad = tie(plane_sum(pre_grad), output_grad)
     output_sum = plane_sum(output_grad)
     result = block_result(block_in, hidden, [out_sum], core, grid)
@@ -856,7 +860,7 @@
         forget_sum,
         output_sum,
         gate_sum,
-        to_columns(up_rows),
+        up_sum,
         down_sum,
     )
 

time: 534 us -> 556 us (1.041)
  waiting for transfers between devices: 174 us -> 187 us
  local copies, waits for them, and re-layouts: 69.6 us -> 77.9 us
    all_to_all x1, waiting for transfers between devices: 5.85 us -> 29.8 us  [on_device(): gains = jnp.sum(lax.all_to_all(gains, 'dp', 0, 0, tiled=True), axis=0)]
    all_to_all x7 -> x6, waiting for transfers between devices: 32 us -> 20.2 us  [exchange(): lax.all_to_all(x, 'dp', split, concat, tiled=True, axis_index_groups=groups)]
    ppermute x6 -> x9, starting transfers between devices: 6.83 us -> 12.6 us  [to_columns_beside(): piece = lax.ppermute(piece, 'dp', pairs)]
    all_to_all x7 -> x6, starting transfers between devices: 30.4 us -> 26.7 us  [exchange(): lax.all_to_all(x, 'dp', split, concat, tiled=True, axis_index_groups=groups)]
    unnamed x107 -> x114, local copies, waits for them, and re-layouts: 25.8 us -> 28.6 us
    ppermute x6 -> x9, waiting for transfers between devices: 24.1 us -> 24.3 us  [to_columns_beside(): piece = lax.ppermute(piece, 'dp', pairs)]
  transfers between devices with their start and end apart: 75 -> 77, of which waited for: 40 -> 39; matrix products, arithmetic and copies ran while one was open for 37% -> 37% of each run, Pallas kernels for 6% -> 6%
where the time goes in v12:
time: 556 us; the launch traced here: 546 us
  waiting for transfers between devices  187 us (34%)
  matrix products  103 us (19%)
  starting transfers between devices  94.6 us (17%)
  local copies, waits for them, and re-layouts  77.9 us (14%)
  other arithmetic  35 us (6%)
  Pallas kernels  33.2 us (6%)
  between operations  16 us (3%)
    dot_general x8, matrix products, nn(): return jnp.dot(a.astype(bf16), b.astype(bf16), preferred_element_type=f32)  37.6 us
    dot_general x13, matrix products, nt(): lax.dot_general(a.astype(bf16), b.astype(bf16), (((1,), (1,)), ((), ())),...  35 us
    dot_general x5, matrix products, tn(): lax.dot_general(a.astype(bf16), b.astype(bf16), (((0,), (0,)), ((), ())),...  30.1 us
    all_to_all x1, waiting for transfers between devices, on_device(): gains = jnp.sum(lax.all_to_all(gains, 'dp', 0, 0, tiled=True), axis=0)  29.8 us
    ppermute x6, waiting for transfers between devices, gather_along(): above = lax.ppermute(above, 'dp', grid.down)  29.3 us
    unnamed x114, local copies, waits for them, and re-layouts  28.6 us
    all_to_all x6, starting transfers between devices, exchange(): lax.all_to_all(x, 'dp', split, concat, tiled=True, axis_index_groups=groups)  26.7 us
    ppermute x9, waiting for transfers between devices, to_columns_beside(): piece = lax.ppermute(piece, 'dp', pairs)  24.3 us
  transfers between devices with their start and end apart: 77, of which 39 were waited for; matrix products, arithmetic and copies ran while one was open for 37% of the time, Pallas kernels for 6%

profile of v12, /device:TPU:0, one launch (start us, length us, event | category | flops | bytes accessed | tf_op | source)
XLA Modules:
  0.0 545.9 jit_solution(15420109446060993892)
XLA Ops:
  14.3 6.3 %all-to-all-start = ((bf16[128,4,1408]{0,2,1:T(8,128)(2,1)}), bf16[128,4,1408]{0,2,1:T(8,128)(2,1)S(1)}, u32[]{:S(2)}, u32[]{:S(2)}) async-start(bf16[128,4,1408]{0,2,1:T(8,128)(2,1)} %pad_maximum_fusion), calls=%async_computation | async-start | bytes 2883584 | tf_op jit(solution)/shard_map/all_to_all | solution.py:585
  20.7 5.0 multiply_convert_fusion.5
  31.8 6.4 %slot_forward.1 = (bf16[256,1024]{1,0:T(8,128)(2,1)}, f32[256,128]{1,0:T(8,128)}, f32[4,256,128]{2,1,0:T(8,128)}, bf16[2,256,256]{2,1,0:T(8,128)(2,1)}, bf16[2,256,16]{2,1,0:T(8,128)(2,1)}) custom-call(s32[1,3]{1,0:T(1,128)} %starts_ref.3, bf16[256,1024]{1,0:T(8,128)(2,1)} %get-tuple-element.236.q_ref, bf16[256,1024]{1,0:T(8,128)(2,1)} %get-tuple-element.238.k_ref, ...), custom_call_target="tpu_custom_call" | custom-call | flops 4000000000 | bytes 4000000 | tf_op jit(solution)/shard_map/slot_forward/pallas_call | solution.py:383
  38.1 4.8 fusion.24.mine_ref
  42.9 11.9 %all-to-all-done = bf16[128,4,1408]{0,2,1:T(8,128)(2,1)S(1)} async-done(((bf16[128,4,1408]{0,2,1:T(8,128)(2,1)}), bf16[128,4,1408]{0,2,1:T(8,128)(2,1)S(1)}, u32[]{:S(2)}, u32[]{:S(2)}) %all-to-all-start) | async-done | bytes 1441824 | tf_op jit(solution)/shard_map/all_to_all | solution.py:585
  58.1 3.7 fusion.22
  63.5 3.5 all-to-all-start.1
  69.8 3.3 second_norm.1
  73.1 4.6 collective-permute-start.1
  83.1 4.0 all-to-all-done.1
  90.6 5.5 %collective-permute-done.2 = bf16[128,2048]{1,0:T(8,128)(2,1)} collective-permute-done((bf16[128,2048]{1,0:T(8,128)(2,1)}, bf16[128,2048]{1,0:T(8,128)(2,1)}, u32[]{:S(2)}, u32[]{:S(2)}) %collective-permute-start.2) | collective-permute-done | bytes 524320 | tf_op jit(solution)/shard_map/ppermute | solution.py:599
  96.1 3.9 collective-permute-start.5
  101.3 3.3 bitcast_dynamic-update-slice_fusion
  104.7 6.2 %collective-permute-done.5 = bf16[128,2048]{1,0:T(8,128)(2,1)S(1)} collective-permute-done((bf16[128,2048]{1,0:T(8,128)(2,1)}, bf16[128,2048]{1,0:T(8,128)(2,1)S(1)}, u32[]{:S(2)}, u32[]{:S(2)}) %collective-permute-start.5) | collective-permute-done | bytes 524320 | tf_op jit(solution)/shard_map/ppermute | solution.py:598
  110.8 4.0 collective-permute-done.6
  122.1 4.7 collective-permute-done.8
  126.8 4.1 collective-permute-done.9
  137.4 4.3 collective-permute-start.3
  148.5 5.1 fusion.45
  153.6 6.6 %collective-permute-done.4 = bf16[128,2048]{1,0:T(8,128)(2,1)} collective-permute-done((bf16[128,2048]{1,0:T(8,128)(2,1)}, bf16[128,2048]{1,0:T(8,128)(2,1)}, u32[]{:S(2)}, u32[]{:S(2)}) %collective-permute-start.4) | collective-permute-done | bytes 524320 | tf_op jit(solution)/shard_map/ppermute | solution.py:599
  163.8 7.9 %fusion.46 = f32[1024,704]{0,1:T(8,128)} fusion(bf16[1024,2048]{1,0:T(8,128)(2,1)} %select_dynamic-update-slice_fusion.6, bf16[2048,704]{1,0:T(8,128)(2,1)} %all-gather.9.cloned.1.call-done), kind=kOutput, calls=%fused_computation.151 | convolution fusion | flops 2952790016 | bytes 9961472 | tf_op jit(solution)/shard_map/dot_general | solution.py:19
  173.1 4.9 collective-permute-done.18
  181.2 2.7 multiply_convert_fusion.2
  185.0 3.5 fusion.47
  190.1 4.0 collective-permute-done.20
  202.1 2.6 collective-permute-done.27
  208.3 9.3 %multiply_convert_fusion.1 = (bf16[1024,704]{0,1:T(8,128)(2,1)S(1)}, bf16[1024,704]{0,1:T(8,128)(2,1)S(1)}) fusion(f32[1024,704]{0,1:T(8,128)} %copy-done.12, f32[1024,704]{0,1:T(8,128)} %fusion.46, bf16[1024,2048]{1,0:T(8,128)(2,1)} %copy-done.37, bf16[2048,704]{0,1:T(8,128)(2,1)} %all-gather.11.cloned.1.call-done), kind=kOutput, calls=%fused_computation.7 | convolution fusion | flops 2962161664 | bytes 15728640 | tf_op jit(solution)/shard_map/dot_general | solution.py:19
  217.6 3.5 fusion.48
  221.2 5.5 %fusion.44 = (bf16[1024,2048]{1,0:T(8,128)(2,1)S(1)}, f32[1024,2048]{1,0:T(8,128)S(1)}) fusion(f32[1024,2048]{1,0:T(8,128)S(1)} %fusion.48, bf16[1024,704]{0,1:T(8,128)(2,1)S(1)} %get-tuple-element.203, bf16[2048,704]{1,0:T(8,128)(2,1)} %all-gather.7.cloned.1.call-done), kind=kOutput, calls=%fused_computation.149 | convolution fusion | flops 2956984320 | bytes 25296896 | tf_op jit(solution)/shard_map/dot_general | solution.py:23
  236.7 4.6 convolution_convert_fusion.3
  241.2 16.2 %collective-permute-done.36 = bf16[128,2048]{1,0:T(8,128)(2,1)} collective-permute-done((bf16[128,2048]{1,0:T(8,128)(2,1)}, bf16[128,2048]{1,0:T(8,128)(2,1)}, u32[]{:S(2)}, u32[]{:S(2)}) %collective-permute-start.36) | collective-permute-done | bytes 524320 | tf_op jit(solution)/shard_map/ppermute | solution.py:634
  260.2 3.0 add_convert_fusion.2
  263.2 3.3 collective-permute-start.39
  267.8 7.2 %convolution_convert_fusion.2 = bf16[2048,704]{0,1:T(8,128)(2,1)} fusion(bf16[1024,704]{0,1:T(8,128)(2,1)S(1)} %get-tuple-element.203, bf16[1024,2048]{1,0:T(8,128)(2,1)} %select_dynamic-update-slice_fusion.6), kind=kOutput, calls=%fused_computation.4 | convolution fusion | flops 2954231808 | bytes 8519680 | tf_op jit(solution)/shard_map/dot_general | solution.py:29
  277.4 4.9 collective-permute-done.40
  282.4 4.1 add_convert_fusion
  286.5 3.3 collective-permute-start.41
  291.1 4.5 convolution_convert_fusion.1
  295.6 4.2 collective-permute-done.41.refs_1_
  299.8 3.8 collective-permute-done.42.refs_2_
  304.4 3.9 second_norm_back.1
  310.5 4.3 convolution_convert_fusion.5.do_ref
  314.8 11.3 %slot_backward.1 = (bf16[256,1024]{1,0:T(8,128)(2,1)}, bf16[256,1024]{1,0:T(8,128)(2,1)}, bf16[256,1024]{1,0:T(8,128)(2,1)}, bf16[256,128]{1,0:T(8,128)(2,1)}, bf16[4,256,896]{2,1,0:T(8,128)(2,1)}) custom-call(s32[1,3]{1,0:T(1,128)} %starts_ref.3, bf16[256,1024]{1,0:T(8,128)(2,1)} %get-tuple-element.236.q_ref, bf16[256,1024]{1,0:T(8,128)(2,1)} %get-tuple-element.238.k_ref, ...), custom_call_target="tpu_custom_call" | custom-call | flops 12000000000 | bytes 8000000 | tf_op jit(solution)/shard_map/slot_backward/pallas_call | solution.py:403
  326.1 4.5 all-to-all-start.2
  330.9 3.8 fusion.16
  347.9 3.0 constant_dynamic-slice_fusion.4
  352.2 3.4 collective-permute-start.49
  357.2 4.0 collective-permute-done.47
  362.0 6.1 %collective-permute-done.48 = bf16[1,128,704]{1,2,0:T(8,128)(2,1)S(1)} collective-permute-done((bf16[1,128,704]{1,2,0:T(8,128)(2,1)S(1)}, bf16[1,128,704]{1,2,0:T(8,128)(2,1)S(1)}, u32[]{:S(2)}, u32[]{:S(2)}) %collective-permute-start.48) | collective-permute-done | bytes 180256 | tf_op jit(solution)/shard_map/ppermute | solution.py:780
  369.4 14.1 %collective-permute-done.45 = bf16[1,128,704]{1,2,0:T(8,128)(2,1)S(1)} collective-permute-done((bf16[1,128,704]{1,2,0:T(8,128)(2,1)S(1)}, bf16[1,128,704]{1,2,0:T(8,128)(2,1)S(1)}, u32[]{:S(2)}, u32[]{:S(2)}) %collective-permute-start.45) | collective-permute-done | bytes 180256 | tf_op jit(solution)/shard_map/ppermute | solution.py:780
  384.8 9.2 %convolution_convert_fusion = bf16[2048,896]{1,0:T(8,128)(2,1)} fusion(bf16[1024,2048]{1,0:T(8,128)(2,1)} %bitcast.11, bf16[1024,896]{1,0:T(8,128)(2,1)} %bitcast.18), kind=kOutput, calls=%fused_computation.2 | convolution fusion | flops 3759931392 | bytes 9699328 | tf_op jit(solution)/shard_map/dot_general | solution.py:29
  395.3 2.7 collective-permute-done.50.other_ref
  398.9 3.9 first_norm_back.1
  406.6 11.1 %collective-permute-done.52 = bf16[128,2048]{1,0:T(8,128)(2,1)} collective-permute-done((bf16[128,2048]{1,0:T(8,128)(2,1)S(1)}, bf16[128,2048]{1,0:T(8,128)(2,1)}, u32[]{:S(2)}, u32[]{:S(2)}) %collective-permute-start.52) | collective-permute-done | bytes 524320 | tf_op jit(solution)/shard_map/ppermute | solution.py:648
  418.8 10.9 %collective-permute-done.53 = bf16[128,2048]{1,0:T(8,128)(2,1)S(1)} collective-permute-done((bf16[128,2048]{1,0:T(8,128)(2,1)S(1)}, bf16[128,2048]{1,0:T(8,128)(2,1)S(1)}, u32[]{:S(2)}, u32[]{:S(2)}) %collective-permute-start.53) | collective-permute-done | bytes 524320 | tf_op jit(solution)/shard_map/ppermute | solution.py:648
  434.0 3.6 collective-permute-start.57
  443.3 3.8 all-to-all-start.4
  449.0 29.8 %all-to-all-done.4 = f32[16,2,128]{2,1,0:T(2,128)S(1)} async-done(((f32[16,2,128]{2,1,0:T(2,128)}), f32[16,2,128]{2,1,0:T(2,128)S(1)}, u32[]{:S(2)}, u32[]{:S(2)}) %all-to-all-start.4) | async-done | bytes 16416 | tf_op jit(solution)/shard_map/all_to_all | solution.py:832
  478.8 4.2 all-to-all-start.3
  491.3 3.2 constant_dynamic-update-slice_fusion.7
  494.4 4.6 convolution_convert_fusion.4
  510.2 4.1 all-to-all-start.5
  522.6 4.3 all-to-all-done.5
  527.0 4.1 all-to-all-start.6
  (336 shorter events, 167.8 us)
Async XLA Ops:
  7.2 50.0 %all-gather.5.cloned.1.call-start = ((), (), s32[]{:S(2)}) async-start(), calls=%async_computation.13 | async-start | bytes 2621440 | tf_op jit(solution)/shard_map/all_gather | solution.py:697
  14.3 40.5 %all-to-all-start = ((bf16[128,4,1408]{0,2,1:T(8,128)(2,1)}), bf16[128,4,1408]{0,2,1:T(8,128)(2,1)S(1)}, u32[]{:S(2)}, u32[]{:S(2)}) async-start(bf16[128,4,1408]{0,2,1:T(8,128)(2,1)} %pad_maximum_fusion), calls=%async_computation | async-start | bytes 2883584 | tf_op jit(solution)/shard_map/all_to_all | solution.py:585
  20.7 110.3 %all-gather.7.cloned.1.call-start = ((), (), s32[]{:S(2)}) async-start(), calls=%async_computation.14 | async-start | bytes 3932160 | tf_op jit(solution)/shard_map/all_gather | solution.py:677
  57.2 103.0 %all-gather.9.cloned.1.call-start = ((), (), s32[]{:S(2)}) async-start(), calls=%async_computation.15 | async-start | bytes 3932160 | tf_op jit(solution)/shard_map/all_gather | solution.py:677
  58.0 43.3 %collective-permute-start.7 = (bf16[4,1,128,2048]{3,2,0,1:T(8,128)(2,1)}, bf16[4,1,128,2048]{3,2,0,1:T(8,128)(2,1)}, u32[]{:S(2)}, u32[]{:S(2)}) collective-permute-start(bf16[4,1,128,2048]{3,2,0,1:T(8,128)(2,1)} %bitcast.141), channel_id=1, source_target_pairs={{0,1},{1,0},{2,3},{3,2},{4,5},{5,4},{6,7},{7,6},{8,9},{9,8},{10,11... | collective-permute-start | bytes 6291464 | tf_op jit(solution)/shard_map/ppermute | solution.py:464
  61.8 7.1 %collective-permute-start = (f32[128,2048]{1,0:T(8,128)S(1)}, f32[128,2048]{1,0:T(8,128)S(1)}, u32[]{:S(2)}, u32[]{:S(2)}) collective-permute-start(f32[128,2048]{1,0:T(8,128)S(1)} %fusion.22), channel_id=1, source_target_pairs={{0,1},{1,0},{2,3},{3,2},{4,5},{5,4},{6,7},{7,6},{8,9},{9,8},{10,11... | collective-permute-start | bytes 3145736 | tf_op jit(solution)/shard_map/ppermute | solution.py:464
  63.5 23.6 %all-to-all-start.1 = ((bf16[128,4,704]{0,2,1:T(8,128)(2,1)}), bf16[128,4,704]{0,2,1:T(8,128)(2,1)S(1)}, u32[]{:S(2)}, u32[]{:S(2)}) async-start(bf16[128,4,704]{0,2,1:T(8,128)(2,1)} %bitcast.6), calls=%async_computation.1 | async-start | bytes 1441792 | tf_op jit(solution)/shard_map/all_to_all | solution.py:585
  67.0 111.0 %all-gather.11.cloned.1.call-start = ((), (), s32[]{:S(2)}) async-start(), calls=%async_computation.16 | async-start | bytes 3604480 | tf_op jit(solution)/shard_map/all_gather | solution.py:677
  73.1 17.4 %collective-permute-start.1 = (bf16[128,2048]{1,0:T(8,128)(2,1)}, bf16[128,2048]{1,0:T(8,128)(2,1)}, u32[]{:S(2)}, u32[]{:S(2)}) collective-permute-start(bf16[128,2048]{1,0:T(8,128)(2,1)} %get-tuple-element.95), channel_id=1, source_target_pairs={{0,8},{2,10},{4,12},{6,14},{8,16},{10,18},{12,20},{14,22},{16,24},... | collective-permute-start | bytes 1572872 | tf_op jit(solution)/shard_map/ppermute | solution.py:598
  77.7 18.3 %collective-permute-start.2 = (bf16[128,2048]{1,0:T(8,128)(2,1)}, bf16[128,2048]{1,0:T(8,128)(2,1)}, u32[]{:S(2)}, u32[]{:S(2)}) collective-permute-start(bf16[128,2048]{1,0:T(8,128)(2,1)} %get-tuple-element.95), channel_id=1, source_target_pairs={{8,0},{10,2},{12,4},{14,6},{16,8},{18,10},{20,12},{22,14},{24,16},... | collective-permute-start | bytes 1572872 | tf_op jit(solution)/shard_map/ppermute | solution.py:599
  96.1 14.8 %collective-permute-start.5 = (bf16[128,2048]{1,0:T(8,128)(2,1)}, bf16[128,2048]{1,0:T(8,128)(2,1)S(1)}, u32[]{:S(2)}, u32[]{:S(2)}) collective-permute-start(bf16[128,2048]{1,0:T(8,128)(2,1)} %collective-permute-done.1), channel_id=1, source_target_pairs={{0,8},{2,10},{4,12},{6,14},{8,16},{10,18},{12,20},{14,22},{16,24},... | collective-permute-start | bytes 1572872 | tf_op jit(solution)/shard_map/ppermute | solution.py:598
  100.0 14.9 %collective-permute-start.6 = (bf16[128,2048]{1,0:T(8,128)(2,1)}, bf16[128,2048]{1,0:T(8,128)(2,1)S(1)}, u32[]{:S(2)}, u32[]{:S(2)}) collective-permute-start(bf16[128,2048]{1,0:T(8,128)(2,1)} %collective-permute-done.2), channel_id=1, source_target_pairs={{8,0},{10,2},{12,4},{14,6},{16,8},{18,10},{20,12},{22,14},{24,16},... | collective-permute-start | bytes 1572872 | tf_op jit(solution)/shard_map/ppermute | solution.py:599
  114.9 11.9 %collective-permute-start.8 = (bf16[128,2048]{1,0:T(8,128)(2,1)S(1)}, bf16[128,2048]{1,0:T(8,128)(2,1)S(1)}, u32[]{:S(2)}, u32[]{:S(2)}) collective-permute-start(bf16[128,2048]{1,0:T(8,128)(2,1)S(1)} %collective-permute-done.5), channel_id=1, source_target_pairs={{0,8},{2,10},{4,12},{6,14},{8,16},{10,18},{12,20},{14,22},{16,24},... | collective-permute-start | bytes 1572872 | tf_op jit(solution)/shard_map/ppermute | solution.py:598
  117.3 13.6 %collective-permute-start.9 = (bf16[128,2048]{1,0:T(8,128)(2,1)S(1)}, bf16[128,2048]{1,0:T(8,128)(2,1)S(1)}, u32[]{:S(2)}, u32[]{:S(2)}) collective-permute-start(bf16[128,2048]{1,0:T(8,128)(2,1)S(1)} %collective-permute-done.6), channel_id=1, source_target_pairs={{8,0},{10,2},{12,4},{14,6},{16,8},{18,10},{20,12},{22,14},{24,16},... | collective-permute-start | bytes 1572872 | tf_op jit(solution)/shard_map/ppermute | solution.py:599
  118.7 16.0 %collective-permute-start.10 = (bf16[128,2048]{1,0:T(8,128)(2,1)S(1)}, bf16[128,2048]{1,0:T(8,128)(2,1)}, u32[]{:S(2)}, u32[]{:S(2)}) collective-permute-start(bf16[128,2048]{1,0:T(8,128)(2,1)S(1)} %copy-done.30), channel_id=1, source_target_pairs={{0,1},{1,0},{2,3},{3,2},{4,5},{5,4},{6,7},{7,6},{8,9},{9,8},{10,11... | collective-permute-start | bytes 1572872 | tf_op jit(solution)/shard_map/ppermute | solution.py:464
  119.7 17.8 %collective-permute-start.11 = (bf16[128,2048]{1,0:T(8,128)(2,1)}, bf16[128,2048]{1,0:T(8,128)(2,1)}, u32[]{:S(2)}, u32[]{:S(2)}) collective-permute-start(bf16[128,2048]{1,0:T(8,128)(2,1)} %collective-permute-done.2), channel_id=1, source_target_pairs={{0,1},{1,0},{2,3},{3,2},{4,5},{5,4},{6,7},{7,6},{8,9},{9,8},{10,11... | collective-permute-start | bytes 1572872 | tf_op jit(solution)/shard_map/ppermute | solution.py:464
  120.2 27.4 %collective-permute-start.16 = (bf16[128,2048]{1,0:T(8,128)(2,1)}, bf16[128,2048]{1,0:T(8,128)(2,1)}, u32[]{:S(2)}, u32[]{:S(2)}) collective-permute-start(bf16[128,2048]{1,0:T(8,128)(2,1)} %collective-permute-done.1), channel_id=1, source_target_pairs={{0,1},{1,0},{2,3},{3,2},{4,5},{5,4},{6,7},{7,6},{8,9},{9,8},{10,11... | collective-permute-start | bytes 1572872 | tf_op jit(solution)/shard_map/ppermute | solution.py:464
  120.2 140.0 %reduce-scatter.7.cloned.1.call-start = ((), (), s32[]{:S(2)}) async-start(), calls=%async_computation.17 | async-start | bytes 2621440 | tf_op jit(solution)/shard_map/reduce_scatter | solution.py:758
  126.8 16.9 %collective-permute-start.13 = (bf16[128,2048]{1,0:T(8,128)(2,1)S(1)}, bf16[128,2048]{1,0:T(8,128)(2,1)}, u32[]{:S(2)}, u32[]{:S(2)}) collective-permute-start(bf16[128,2048]{1,0:T(8,128)(2,1)S(1)} %collective-permute-done.6), channel_id=1, source_target_pairs={{0,1},{1,0},{2,3},{3,2},{4,5},{5,4},{6,7},{7,6},{8,9},{9,8},{10,11... | collective-permute-start | bytes 1572872 | tf_op jit(solution)/shard_map/ppermute | solution.py:464
  130.9 10.8 %collective-permute-start.12 = (bf16[128,2048]{1,0:T(8,128)(2,1)S(1)}, bf16[128,2048]{1,0:T(8,128)(2,1)S(1)}, u32[]{:S(2)}, u32[]{:S(2)}) collective-permute-start(bf16[128,2048]{1,0:T(8,128)(2,1)S(1)} %collective-permute-done.8), channel_id=1, source_target_pairs={{0,1},{1,0},{2,3},{3,2},{4,5},{5,4},{6,7},{7,6},{8,9},{9,8},{10,11... | collective-permute-start | bytes 1572872 | tf_op jit(solution)/shard_map/ppermute | solution.py:464
  134.8 10.2 %collective-permute-start.14 = (bf16[128,2048]{1,0:T(8,128)(2,1)S(1)}, bf16[128,2048]{1,0:T(8,128)(2,1)S(1)}, u32[]{:S(2)}, u32[]{:S(2)}) collective-permute-start(bf16[128,2048]{1,0:T(8,128)(2,1)S(1)} %collective-permute-done.5), channel_id=1, source_target_pairs={{0,1},{1,0},{2,3},{3,2},{4,5},{5,4},{6,7},{7,6},{8,9},{9,8},{10,11... | collective-permute-start | bytes 1572872 | tf_op jit(solution)/shard_map/ppermute | solution.py:464
  137.4 16.1 %collective-permute-start.3 = (bf16[128,2048]{1,0:T(8,128)(2,1)}, bf16[128,2048]{1,0:T(8,128)(2,1)}, u32[]{:S(2)}, u32[]{:S(2)}) collective-permute-start(bf16[128,2048]{1,0:T(8,128)(2,1)} %cotangent_rows.1), channel_id=1, source_target_pairs={{0,8},{2,10},{4,12},{6,14},{8,16},{10,18},{12,20},{14,22},{16,24},... | collective-permute-start | bytes 1572872 | tf_op jit(solution)/shard_map/ppermute | solution.py:598
  141.7 5.8 %collective-permute-start.15 = (bf16[128,2048]{1,0:T(8,128)(2,1)S(1)}, bf16[128,2048]{1,0:T(8,128)(2,1)S(1)}, u32[]{:S(2)}, u32[]{:S(2)}) collective-permute-start(bf16[128,2048]{1,0:T(8,128)(2,1)S(1)} %collective-permute-done.9), channel_id=1, source_target_pairs={{0,1},{1,0},{2,3},{3,2},{4,5},{5,4},{6,7},{7,6},{8,9},{9,8},{10,11... | collective-permute-start | bytes 1572872 | tf_op jit(solution)/shard_map/ppermute | solution.py:464
  143.7 16.5 %collective-permute-start.4 = (bf16[128,2048]{1,0:T(8,128)(2,1)}, bf16[128,2048]{1,0:T(8,128)(2,1)}, u32[]{:S(2)}, u32[]{:S(2)}) collective-permute-start(bf16[128,2048]{1,0:T(8,128)(2,1)} %cotangent_rows.1), channel_id=1, source_target_pairs={{8,0},{10,2},{12,4},{14,6},{16,8},{18,10},{20,12},{22,14},{24,16},... | collective-permute-start | bytes 1572872 | tf_op jit(solution)/shard_map/ppermute | solution.py:599
  145.0 53.0 %collective-permute-start.25 = (bf16[128,2048]{1,0:T(8,128)(2,1)}, bf16[128,2048]{1,0:T(8,128)(2,1)}, u32[]{:S(2)}, u32[]{:S(2)}) collective-permute-start(bf16[128,2048]{1,0:T(8,128)(2,1)} %cotangent_rows.1), channel_id=1, source_target_pairs={{0,1},{1,0},{2,3},{3,2},{4,5},{5,4},{6,7},{7,6},{8,9},{9,8},{10,11... | collective-permute-start | bytes 1572872 | tf_op jit(solution)/shard_map/ppermute | solution.py:464
  160.2 12.9 %collective-permute-start.17 = (bf16[128,2048]{1,0:T(8,128)(2,1)}, bf16[128,2048]{1,0:T(8,128)(2,1)}, u32[]{:S(2)}, u32[]{:S(2)}) collective-permute-start(bf16[128,2048]{1,0:T(8,128)(2,1)} %collective-permute-done.3), channel_id=1, source_target_pairs={{0,8},{2,10},{4,12},{6,14},{8,16},{10,18},{12,20},{14,22},{16,24},... | collective-permute-start | bytes 1572872 | tf_op jit(solution)/shard_map/ppermute | solution.py:598
  162.5 15.5 %collective-permute-start.18 = (bf16[128,2048]{1,0:T(8,128)(2,1)}, bf16[128,2048]{1,0:T(8,128)(2,1)}, u32[]{:S(2)}, u32[]{:S(2)}) collective-permute-start(bf16[128,2048]{1,0:T(8,128)(2,1)} %collective-permute-done.4), channel_id=1, source_target_pairs={{8,0},{10,2},{12,4},{14,6},{16,8},{18,10},{20,12},{22,14},{24,16},... | collective-permute-start | bytes 1572872 | tf_op jit(solution)/shard_map/ppermute | solution.py:599
  178.0 12.1 %collective-permute-start.19 = (bf16[128,2048]{1,0:T(8,128)(2,1)}, bf16[128,2048]{1,0:T(8,128)(2,1)S(1)}, u32[]{:S(2)}, u32[]{:S(2)}) collective-permute-start(bf16[128,2048]{1,0:T(8,128)(2,1)} %collective-permute-done.17), channel_id=1, source_target_pairs={{0,8},{2,10},{4,12},{6,14},{8,16},{10,18},{12,20},{14,22},{16,24},... | collective-permute-start | bytes 1572872 | tf_op jit(solution)/shard_map/ppermute | solution.py:598
  179.7 14.4 %collective-permute-start.20 = (bf16[128,2048]{1,0:T(8,128)(2,1)}, bf16[128,2048]{1,0:T(8,128)(2,1)S(1)}, u32[]{:S(2)}, u32[]{:S(2)}) collective-permute-start(bf16[128,2048]{1,0:T(8,128)(2,1)} %collective-permute-done.18), channel_id=1, source_target_pairs={{8,0},{10,2},{12,4},{14,6},{16,8},{18,10},{20,12},{22,14},{24,16},... | collective-permute-start | bytes 1572872 | tf_op jit(solution)/shard_map/ppermute | solution.py:599
  199.2 6.1 %collective-permute-start.31 = (bf16[128,2048]{1,0:T(8,128)(2,1)}, bf16[128,2048]{1,0:T(8,128)(2,1)S(1)}, u32[]{:S(2)}, u32[]{:S(2)}) collective-permute-start(bf16[128,2048]{1,0:T(8,128)(2,1)} %collective-permute-done.3), channel_id=1, source_target_pairs={{0,1},{1,0},{2,3},{3,2},{4,5},{5,4},{6,7},{7,6},{8,9},{9,8},{10,11... | collective-permute-start | bytes 1572872 | tf_op jit(solution)/shard_map/ppermute | solution.py:464
  199.7 5.3 collective-permute-start.28
  200.2 4.8 collective-permute-start.29
  201.0 3.7 collective-permute-start.27
  201.7 3.7 collective-permute-start.30
  208.1 106.7 %reduce-scatter.9.cloned.1.call-start = ((), (), s32[]{:S(2)}) async-start(), calls=%async_computation.18 | async-start | bytes 3604480 | tf_op jit(solution)/shard_map/reduce_scatter | solution.py:763
  232.5 24.9 %collective-permute-start.36 = (bf16[128,2048]{1,0:T(8,128)(2,1)}, bf16[128,2048]{1,0:T(8,128)(2,1)}, u32[]{:S(2)}, u32[]{:S(2)}) collective-permute-start(bf16[128,2048]{1,0:T(8,128)(2,1)} %get-tuple-element.202), channel_id=1, source_target_pairs={{0,8},{2,10},{4,12},{6,14},{8,16},{10,18},{12,20},{14,22},{16,24},... | collective-permute-start | bytes 1572872 | tf_op jit(solution)/shard_map/ppermute | solution.py:634
  235.0 24.3 %collective-permute-start.37 = (bf16[128,2048]{1,0:T(8,128)(2,1)}, bf16[128,2048]{1,0:T(8,128)(2,1)}, u32[]{:S(2)}, u32[]{:S(2)}) collective-permute-start(bf16[128,2048]{1,0:T(8,128)(2,1)} %get-tuple-element.201), channel_id=1, source_target_pairs={{8,0},{10,2},{12,4},{14,6},{16,8},{18,10},{20,12},{22,14},{24,16},... | collective-permute-start | bytes 1572872 | tf_op jit(solution)/shard_map/ppermute | solution.py:635
  260.2 85.8 %reduce-scatter.11.cloned.1.call-start = ((), (), s32[]{:S(2)}) async-start(), calls=%async_computation.19 | async-start | bytes 3604480 | tf_op jit(solution)/shard_map/reduce_scatter | solution.py:763
  263.2 14.1 %collective-permute-start.39 = (bf16[128,2048]{1,0:T(8,128)(2,1)}, bf16[128,2048]{1,0:T(8,128)(2,1)}, u32[]{:S(2)}, u32[]{:S(2)}) collective-permute-start(bf16[128,2048]{1,0:T(8,128)(2,1)} %get-tuple-element.197), channel_id=1, source_target_pairs={{0,8},{2,10},{4,12},{6,14},{8,16},{10,18},{12,20},{14,22},{16,24},... | collective-permute-start | bytes 1572872 | tf_op jit(solution)/shard_map/ppermute | solution.py:634
  266.5 15.7 %collective-permute-start.40 = (bf16[128,2048]{1,0:T(8,128)(2,1)}, bf16[128,2048]{1,0:T(8,128)(2,1)}, u32[]{:S(2)}, u32[]{:S(2)}) collective-permute-start(bf16[128,2048]{1,0:T(8,128)(2,1)} %get-tuple-element.196), channel_id=1, source_target_pairs={{8,0},{10,2},{12,4},{14,6},{16,8},{18,10},{20,12},{22,14},{24,16},... | collective-permute-start | bytes 1572872 | tf_op jit(solution)/shard_map/ppermute | solution.py:635
  282.3 120.5 %reduce-scatter.13.cloned.1.call-start = ((), (), s32[]{:S(2)}) async-start(), calls=%async_computation.20 | async-start | bytes 3604480 | tf_op jit(solution)/shard_map/reduce_scatter | solution.py:763
  286.5 13.2 %collective-permute-start.41 = (bf16[128,2048]{1,0:T(8,128)(2,1)}, bf16[128,2048]{1,0:T(8,128)(2,1)S(1)}, u32[]{:S(2)}, u32[]{:S(2)}) collective-permute-start(bf16[128,2048]{1,0:T(8,128)(2,1)} %get-tuple-element.199), channel_id=1, source_target_pairs={{0,8},{2,10},{4,12},{6,14},{8,16},{10,18},{12,20},{14,22},{16,24},... | collective-permute-start | bytes 1572872 | tf_op jit(solution)/shard_map/ppermute | solution.py:634
  289.8 13.8 %collective-permute-start.42 = (bf16[128,2048]{1,0:T(8,128)(2,1)S(1)}, bf16[128,2048]{1,0:T(8,128)(2,1)S(1)}, u32[]{:S(2)}, u32[]{:S(2)}) collective-permute-start(bf16[128,2048]{1,0:T(8,128)(2,1)S(1)} %get-tuple-element.198), channel_id=1, source_target_pairs={{8,0},{10,2},{12,4},{14,6},{16,8},{18,10},{20,12},{22,14},{24,16},... | collective-permute-start | bytes 1572872 | tf_op jit(solution)/shard_map/ppermute | solution.py:635
  326.1 58.7 %all-to-all-start.2 = ((bf16[4,256,896]{2,1,0:T(8,128)(2,1)}), bf16[4,256,896]{2,1,0:T(8,128)(2,1)}, u32[]{:S(2)}, u32[]{:S(2)}) async-start(bf16[4,256,896]{2,1,0:T(8,128)(2,1)} %get-tuple-element.146), calls=%async_computation.4 | async-start | bytes 3670016 | tf_op jit(solution)/shard_map/all_to_all | solution.py:585
  330.7 168.3 %reduce-scatter.15.cloned.1.call-start = ((), (), s32[]{:S(2)}) async-start(), calls=%async_computation.21 | async-start | bytes 4587520 | tf_op jit(solution)/shard_map/reduce_scatter | solution.py:723
  350.9 10.3 %collective-permute-start.47 = (bf16[1,128,704]{1,2,0:T(8,128)(2,1)S(1)}, bf16[1,128,704]{1,2,0:T(8,128)(2,1)S(1)}, u32[]{:S(2)}, u32[]{:S(2)}) collective-permute-start(bf16[1,128,704]{1,2,0:T(8,128)(2,1)S(1)} %copy.106), channel_id=1, source_target_pairs={{0,8},{2,10},{4,12},{6,14},{8,0},{10,2},{12,4},{14,6},{16,24},{18,... | collective-permute-start | bytes 540680 | tf_op jit(solution)/shard_map/ppermute | solution.py:780
  351.9 16.2 %collective-permute-start.48 = (bf16[1,128,704]{1,2,0:T(8,128)(2,1)S(1)}, bf16[1,128,704]{1,2,0:T(8,128)(2,1)S(1)}, u32[]{:S(2)}, u32[]{:S(2)}) collective-permute-start(bf16[1,128,704]{1,2,0:T(8,128)(2,1)S(1)} %copy.107), channel_id=1, source_target_pairs={{0,16},{2,18},{4,20},{6,22},{8,24},{10,26},{12,28},{14,30},{16,0},... | collective-permute-start | bytes 540680 | tf_op jit(solution)/shard_map/ppermute | solution.py:780
  352.2 15.9 %collective-permute-start.49 = (bf16[1,128,704]{1,2,0:T(8,128)(2,1)S(1)}, bf16[1,128,704]{1,2,0:T(8,128)(2,1)S(1)}, u32[]{:S(2)}, u32[]{:S(2)}) collective-permute-start(bf16[1,128,704]{1,2,0:T(8,128)(2,1)S(1)} %copy.108), channel_id=1, source_target_pairs={{0,24},{2,26},{4,28},{6,30},{8,16},{10,18},{12,20},{14,22},{16,8},... | collective-permute-start | bytes 540680 | tf_op jit(solution)/shard_map/ppermute | solution.py:780
  355.6 13.8 %collective-permute-start.44 = (bf16[1,128,704]{1,2,0:T(8,128)(2,1)S(1)}, bf16[1,128,704]{1,2,0:T(8,128)(2,1)S(1)}, u32[]{:S(2)}, u32[]{:S(2)}) collective-permute-start(bf16[1,128,704]{1,2,0:T(8,128)(2,1)S(1)} %copy.102), channel_id=1, source_target_pairs={{0,8},{2,10},{4,12},{6,14},{8,0},{10,2},{12,4},{14,6},{16,24},{18,... | collective-permute-start | bytes 540680 | tf_op jit(solution)/shard_map/ppermute | solution.py:780
  355.7 27.8 %collective-permute-start.45 = (bf16[1,128,704]{1,2,0:T(8,128)(2,1)S(1)}, bf16[1,128,704]{1,2,0:T(8,128)(2,1)S(1)}, u32[]{:S(2)}, u32[]{:S(2)}) collective-permute-start(bf16[1,128,704]{1,2,0:T(8,128)(2,1)S(1)} %copy.103), channel_id=1, source_target_pairs={{0,16},{2,18},{4,20},{6,22},{8,24},{10,26},{12,28},{14,30},{16,0},... | collective-permute-start | bytes 540680 | tf_op jit(solution)/shard_map/ppermute | solution.py:780
  361.2 22.4 %collective-permute-start.46 = (bf16[1,128,704]{1,2,0:T(8,128)(2,1)S(1)}, bf16[1,128,704]{1,2,0:T(8,128)(2,1)S(1)}, u32[]{:S(2)}, u32[]{:S(2)}) collective-permute-start(bf16[1,128,704]{1,2,0:T(8,128)(2,1)S(1)} %copy.104), channel_id=1, source_target_pairs={{0,24},{2,26},{4,28},{6,30},{8,16},{10,18},{12,20},{14,22},{16,8},... | collective-permute-start | bytes 540680 | tf_op jit(solution)/shard_map/ppermute | solution.py:780
  402.8 14.9 %collective-permute-start.52 = (bf16[128,2048]{1,0:T(8,128)(2,1)S(1)}, bf16[128,2048]{1,0:T(8,128)(2,1)}, u32[]{:S(2)}, u32[]{:S(2)}) collective-permute-start(bf16[128,2048]{1,0:T(8,128)(2,1)S(1)} %copy-done.16), channel_id=1, source_target_pairs={{0,2},{2,0},{4,6},{6,4},{8,10},{10,8},{12,14},{14,12},{16,18},{18,... | collective-permute-start | bytes 1572872 | tf_op jit(solution)/shard_map/ppermute | solution.py:648
  404.7 24.9 %collective-permute-start.53 = (bf16[128,2048]{1,0:T(8,128)(2,1)S(1)}, bf16[128,2048]{1,0:T(8,128)(2,1)S(1)}, u32[]{:S(2)}, u32[]{:S(2)}) collective-permute-start(bf16[128,2048]{1,0:T(8,128)(2,1)S(1)} %copy-done.16), channel_id=1, source_target_pairs={{0,4},{2,6},{4,0},{6,2},{8,12},{10,14},{12,8},{14,10},{16,20},{18,... | collective-permute-start | bytes 1572872 | tf_op jit(solution)/shard_map/ppermute | solution.py:648
  406.2 23.5 %collective-permute-start.54 = (bf16[128,2048]{1,0:T(8,128)(2,1)S(1)}, bf16[128,2048]{1,0:T(8,128)(2,1)S(1)}, u32[]{:S(2)}, u32[]{:S(2)}) collective-permute-start(bf16[128,2048]{1,0:T(8,128)(2,1)S(1)} %copy-done.16), channel_id=1, source_target_pairs={{0,6},{2,4},{4,2},{6,0},{8,14},{10,12},{12,10},{14,8},{16,22},{18,... | collective-permute-start | bytes 1572872 | tf_op jit(solution)/shard_map/ppermute | solution.py:648
  429.8 61.5 %collective-permute-start.55 = (bf16[4,1,128,2048]{3,2,1,0:T(8,128)(2,1)S(1)}, bf16[4,1,128,2048]{3,2,1,0:T(8,128)(2,1)}, u32[]{:S(2)}, u32[]{:S(2)}) collective-permute-start(bf16[4,1,128,2048]{3,2,1,0:T(8,128)(2,1)S(1)} %bitcast_dynamic-update-slice_fusion.1), channel_id=1, source_target_pairs={{0,1},{1,0},{2,3},{3,2},{4,5},{5,4},{6,7},{7,6},{8,9},{9,8},{10,11... | collective-permute-start | bytes 6291464 | tf_op jit(solution)/shard_map/ppermute | solution.py:464
  434.0 49.0 %collective-permute-start.57 = (bf16[1,128,704]{1,2,0:T(8,128)(2,1)}, bf16[1,128,704]{1,2,0:T(8,128)(2,1)}, u32[]{:S(2)}, u32[]{:S(2)}) collective-permute-start(bf16[1,128,704]{1,2,0:T(8,128)(2,1)} %copy.110), channel_id=1, source_target_pairs={{0,8},{2,10},{4,12},{6,14},{8,0},{10,2},{12,4},{14,6},{16,24},{18,... | collective-permute-start | bytes 540680 | tf_op jit(solution)/shard_map/ppermute | solution.py:780
  438.3 45.6 %collective-permute-start.58 = (bf16[1,128,704]{1,2,0:T(8,128)(2,1)}, bf16[1,128,704]{1,2,0:T(8,128)(2,1)}, u32[]{:S(2)}, u32[]{:S(2)}) collective-permute-start(bf16[1,128,704]{1,2,0:T(8,128)(2,1)} %copy.111), channel_id=1, source_target_pairs={{0,16},{2,18},{4,20},{6,22},{8,24},{10,26},{12,28},{14,30},{16,0},... | collective-permute-start | bytes 540680 | tf_op jit(solution)/shard_map/ppermute | solution.py:780
  439.1 45.9 %collective-permute-start.59 = (bf16[1,128,704]{1,2,0:T(8,128)(2,1)}, bf16[1,128,704]{1,2,0:T(8,128)(2,1)}, u32[]{:S(2)}, u32[]{:S(2)}) collective-permute-start(bf16[1,128,704]{1,2,0:T(8,128)(2,1)} %copy.112), channel_id=1, source_target_pairs={{0,24},{2,26},{4,28},{6,30},{8,16},{10,18},{12,20},{14,22},{16,8},... | collective-permute-start | bytes 540680 | tf_op jit(solution)/shard_map/ppermute | solution.py:780
  443.3 35.5 %all-to-all-start.4 = ((f32[16,2,128]{2,1,0:T(2,128)}), f32[16,2,128]{2,1,0:T(2,128)S(1)}, u32[]{:S(2)}, u32[]{:S(2)}) async-start(f32[16,2,128]{2,1,0:T(2,128)} %add_bitcast_fusion), calls=%async_computation.8 | async-start | bytes 32768 | tf_op jit(solution)/shard_map/all_to_all | solution.py:832
  478.8 15.6 %all-to-all-start.3 = ((bf16[4,256,256]{2,1,0:T(8,128)(2,1)}), bf16[4,256,256]{2,1,0:T(8,128)(2,1)}, u32[]{:S(2)}, u32[]{:S(2)}) async-start(bf16[4,256,256]{2,1,0:T(8,128)(2,1)} %pad_maximum_fusion.1), calls=%async_computation.7 | async-start | bytes 1048576 | tf_op jit(solution)/shard_map/all_to_all | solution.py:585
  482.9 44.0 %reduce-scatter.17.cloned.1.call-start = ((), (), s32[]{:S(2)}) async-start(), calls=%async_computation.22 | async-start | bytes 1310720 | tf_op jit(solution)/shard_map/reduce_scatter | solution.py:723
  499.1 19.1 %collective-permute-start.51 = (f32[128,2048]{1,0:T(8,128)}, f32[128,2048]{1,0:T(8,128)}, u32[]{:S(2)}, u32[]{:S(2)}) collective-permute-start(f32[128,2048]{1,0:T(8,128)} %get-tuple-element.155), channel_id=1, source_target_pairs={{0,1},{1,0},{2,3},{3,2},{4,5},{5,4},{6,7},{7,6},{8,9},{9,8},{10,11... | collective-permute-start | bytes 3145736 | tf_op jit(solution)/shard_map/ppermute | solution.py:464
  510.2 16.6 %all-to-all-start.5 = ((bf16[4,128,896]{1,2,0:T(8,128)(2,1)}), bf16[4,128,896]{1,2,0:T(8,128)(2,1)S(1)}, u32[]{:S(2)}, u32[]{:S(2)}) async-start(bf16[4,128,896]{1,2,0:T(8,128)(2,1)} %copy.92), calls=%async_computation.10 | async-start | bytes 1835008 | tf_op jit(solution)/shard_map/all_to_all | solution.py:585
  527.0 9.7 %all-to-all-start.6 = ((bf16[4,128,256]{2,1,0:T(8,128)(2,1)}), bf16[4,128,256]{2,1,0:T(8,128)(2,1)}, u32[]{:S(2)}, u32[]{:S(2)}) async-start(bf16[4,128,256]{2,1,0:T(8,128)(2,1)} %bitcast.148), calls=%async_computation.12 | async-start | bytes 524288 | tf_op jit(solution)/shard_map/all_to_all | solution.py:585
  (59 other events, 339.4 us)
Sparse Core Ops, SparseCore 0:
  11.4 37.8 all-gather.4
  57.3 35.2 all-gather.6
  94.8 36.1 all-gather.8
  133.0 33.9 all-gather.10
  208.2 51.9 reduce-scatter.6
  262.3 32.5 reduce-scatter.8
  297.2 32.3 reduce-scatter.10
  331.9 45.7 reduce-scatter.12
  394.2 81.4 reduce-scatter.14
  499.2 27.5 reduce-scatter.16
